TPU v7x, 512 devices: a whole 4x8x8 slice. The times are simulated.
512 devices in a mesh: wide: 64 (over z_lo, y, x), narrow: 8 (over z_hi, core).
Axes of the slice: x: 4, y: 8, z: 8 (z_hi: 4, z_lo: 2; z = z_hi * 2 + z_lo), core: 2. Of those that a mesh axis runs over, the one named last changes fastest.
Arguments:
- tokens: bfloat16 [4096, 2048], P('wide'), may hold values from -6 to 6
- routes: int32 [4096, 6], P('wide'), may hold values from 0 to 63, all different within a row; in each aligned block of 64 rows (0 to 63, 64 to 127, ...) at most 11 rows name the same one
- route_weight: float32 [4096, 6], P('wide'), may hold values from 0.1 to 0.8
- w_gate: bfloat16 [64, 1408, 2048], P('wide', None, 'narrow'), may hold values from -0.1875 to 0.1875
- w_up: bfloat16 [64, 1408, 2048], P('wide', None, 'narrow'), may hold values from -0.1875 to 0.1875
- w_down: bfloat16 [64, 1408, 2048], P('wide', None, 'narrow'), may hold values from -0.15625 to 0.15625
Outputs:
- combined: bfloat16 [4096, 2048], P('wide', 'narrow')
Inputs may be any that keep to these rules, and one draw needn't show every extreme that they name: `routes`: each row names 6 different experts. Within each aligned block of 64 rows no expert is named by more than 11 rows, and in some block an expert is named by exactly 11 rows.
All inputs are finite; a program needn't handle non-finite values.
Results may differ from a plain program's by a relative error of at most 0.029.
Values may be sent and summed in bfloat16 or wider, within the bound.
No kernel may reach another device: no remote copies, remote signals or barrier semaphores. Data moves between devices by JAX's collectives and lax.ppermute only.
A program may use at most 64 MiB of HBM per device.

v0:
```python
import jax
import jax.numpy as jnp
from jax import lax
from jax.sharding import PartitionSpec as P


def slot_numbers(routes, experts):
    flat_routes = routes.reshape(-1)
    onehot = (flat_routes[:, None] == jnp.arange(experts, dtype=jnp.int32)[None, :]).astype(
        jnp.int32
    )
    before = jnp.cumsum(onehot, 0) - onehot
    return jnp.sum(before * onehot, 1).reshape(routes.shape)


def on_device(tokens, routes, route_weight, w_gate, w_up, w_down):
    tok_count = tokens.shape[0]
    model_width = tokens.shape[1]
    wide_count = lax.axis_size("wide")
    narrow_count = lax.axis_size("narrow")
    local_experts = w_gate.shape[0]
    experts = local_experts * wide_count
    capacity = max(2, (11 * tok_count + experts - 1) // experts)
    column_width = model_width // narrow_count
    slot_index = slot_numbers(routes, experts)
    target = routes * capacity + slot_index
    lane_ids = jnp.arange(experts * capacity, dtype=jnp.int32)
    picker = jnp.sum((lane_ids[:, None, None] == target[None, :, :]).astype(jnp.int32), 2).astype(
        jnp.bfloat16
    )
    columns = lax.dynamic_slice_in_dim(
        tokens, lax.axis_index("narrow") * column_width, column_width, 1
    )
    outgoing = jnp.dot(picker, columns, preferred_element_type=jnp.float32).astype(jnp.bfloat16)
    outgoing = outgoing.reshape(experts, capacity, column_width)
    received = lax.all_to_all(outgoing, "wide", split_axis=0, concat_axis=1, tiled=True)
    expert_rows = received[0]
    slot_total = expert_rows.shape[0]
    gate_matrix = w_gate[0]
    up_matrix = w_up[0]
    down_matrix = w_down[0]
    gate_term = jnp.einsum(
        "sc,fc->fs", expert_rows, gate_matrix, preferred_element_type=jnp.float32
    )
    up_term = jnp.einsum("sc,fc->fs", expert_rows, up_matrix, preferred_element_type=jnp.float32)
    sums = lax.psum_scatter(
        jnp.concatenate([gate_term, up_term], 1).astype(jnp.bfloat16),
        "narrow",
        scatter_dimension=0,
        tiled=True,
    ).astype(jnp.float32)
    hidden = (jax.nn.silu(sums[:, :slot_total]) * sums[:, slot_total:]).astype(jnp.bfloat16)
    produced = jnp.einsum(
        "fs,fc->sc",
        lax.all_gather(hidden, "narrow", axis=0, tiled=True),
        down_matrix,
        preferred_element_type=jnp.float32,
    )
    expert_out = produced.astype(jnp.bfloat16).reshape(local_experts, slot_total, column_width)
    returned = lax.all_to_all(expert_out, "wide", split_axis=1, concat_axis=0, tiled=True)
    flat_rows = returned.reshape(experts * capacity, column_width)
    picked = jnp.take(flat_rows, target, axis=0).astype(jnp.float32)
    combined = jnp.sum(picked * route_weight[:, :, None], 1)
    return combined.astype(jnp.bfloat16)


def solution(mesh):
    return jax.shard_map(
        on_device,
        mesh=mesh,
        in_specs=(
            P("wide", None),
            P("wide", None),
            P("wide", None),
            P("wide", None, "narrow"),
            P("wide", None, "narrow"),
            P("wide", None, "narrow"),
        ),
        out_specs=P("wide", "narrow"),
        check_vma=False,
    )
```

profile of v0, /device:TPU:8, one launch (start us, length us, event | category | flops | bytes accessed | tf_op | source)
XLA Modules:
  0.0 197.1 jit_solution(5945480343832865840)
XLA Ops:
  6.5 0.8 copy.41
  7.7 0.9 reduce-window.6
  8.6 0.2 slice_reduce_fusion
  9.2 0.7 compare_and_fusion
  10.1 1.0 convolution_convert_fusion.3
  11.3 30.4 %all_to_all.8 = bf16[64,11,256]{2,1,0:T(8,128)(2,1)S(1)} all-to-all(bf16[64,11,256]{2,1,0:T(8,128)(2,1)S(1)} %reshape.46), channel_id=1, replica_groups=mesh['wide'=64,'narrow'=8] {'wide'}, dimensions={0} | all-to-all | bytes 720896 | tf_op jit(solution)/shard_map/all_to_all | solution.py:36
  41.9 0.8 fusion
  42.8 0.8 fusion.1
  43.6 2.2 %pad_maximum_fusion = bf16[1408,1408]{0,1:T(8,128)(2,1)} fusion(bf16[1408,704]{0,1:T(8,128)(2,1)S(1)} %fusion.1, bf16[1408,704]{0,1:T(8,128)(2,1)S(1)} %fusion), kind=kLoop, calls=%fused_computation.1 | loop fusion | flops 7929856 | bytes 7929856 | tf_op jit(solution)/shard_map/concatenate | solution.py:47
  45.8 6.2 %copy.50 = bf16[1408,1408]{1,0:T(8,128)(2,1)} copy(bf16[1408,1408]{0,1:T(8,128)(2,1)} %pad_maximum_fusion) | data formatting | bytes 7929856
  52.1 56.2 %reduce-scatter.4.cloned.1.call-done = bf16[176,1408]{1,0:T(8,128)(2,1)} async-done(((bf16[1408,1408]{1,0:T(8,128)(2,1)}), bf16[176,1408]{1,0:T(8,128)(2,1)}) %reduce-scatter.4.cloned.1.call-update) | async-done | bytes 495632
  108.3 1.3 copy.51
  109.9 0.9 copy.46
  110.8 42.8 %all-gather.2.cloned.1.call-done = bf16[1408,704]{1,0:T(8,128)(2,1)} async-done(((bf16[176,704]{1,0:T(8,128)(2,1)}), bf16[1408,704]{1,0:T(8,128)(2,1)}) %all-gather.2.cloned.1.call-update) | async-done | bytes 1982480 | tf_op jit(solution)/shard_map/all_gather | solution.py:55
  153.7 2.4 %fusion.2 = bf16[1,704,256]{2,1,0:T(8,128)(2,1)S(1)} fusion(bf16[1408,704]{1,0:T(8,128)(2,1)} %all-gather.2.cloned.1.call-done, bf16[1,1408,256]{2,1,0:T(8,128)(2,1)S(1)} %copy-done.3), kind=kOutput, calls=%fused_computation.8 | convolution fusion | flops 507691008 | bytes 3063808 | tf_op jit(solution)/shard_map/fs,fc->sc/dot_general | solution.py:53
  156.1 0.6 copy.58
  156.7 0.5 broadcast.31
  157.2 2.9 %reduce.2 = bf16[704,256]{1,0:T(8,128)(2,1)S(1)} reduce(bf16[704,1,256]{2,1,0:T(2,128)(2,1)S(1)} %bitcast.47, bf16[]{:T(256)} %broadcast.31), dimensions={1}, to_apply=%bitcast.44.reduce_sub_computation | reduce | bytes 720898
  160.1 0.9 reshape.62
  161.0 10.3 %all-to-all-start.1 = ((bf16[64,2,1408]{2,1,0:T(2,128)(2,1)}), bf16[64,2,1408]{2,1,0:T(2,128)(2,1)S(1)}, u32[]{:S(2)}, u32[]{:S(2)}) async-start(bf16[64,2,1408]{2,1,0:T(2,128)(2,1)} %reshape.62), calls=%async_computation.1 | async-start | bytes 720896 | tf_op jit(solution)/shard_map/all_to_all | solution.py:60
  171.7 15.0 %all-to-all-done.1 = bf16[64,2,1408]{2,1,0:T(2,128)(2,1)S(1)} async-done(((bf16[64,2,1408]{2,1,0:T(2,128)(2,1)}), bf16[64,2,1408]{2,1,0:T(2,128)(2,1)S(1)}, u32[]{:S(2)}, u32[]{:S(2)}) %all-to-all-start.1) | async-done | bytes 360480 | tf_op jit(solution)/shard_map/all_to_all | solution.py:60
  186.7 0.3 reshape.63
  187.1 2.1 %gather_fusion = bf16[384,256]{1,0:T(8,128)(2,1)S(1)} fusion(bf16[704,256]{1,0:T(8,128)(2,1)S(1)} %bitcast.46, s32[1024]{0:T(1024)S(1)} %pad_clamp_fusion), kind=kCustom, calls=%fused_computation | custom fusion | bytes 394752 | tf_op jit(solution)/shard_map/jit(_take)/gather | solution.py:62
  189.2 1.1 multiply_reduce_fusion
  (32 shorter events, 2.3 us)
Async XLA Ops:
  6.5 35.3 %copy-start = (bf16[1,1408,256]{2,1,0:T(8,128)(2,1)S(1)}, bf16[1,1408,256]{2,1,0:T(8,128)(2,1)}, u32[]{:S(2)}) copy-start(bf16[1,1408,256]{2,1,0:T(8,128)(2,1)} %param.9) | copy-start | bytes 2162692
  6.5 101.7 %reduce-scatter.4.cloned.1.call-start = ((), (), s32[]{:S(2)}) async-start(), calls=%async_computation.4 | async-start | bytes 4460544
  41.7 1.1 copy-start.1
  52.1 101.6 %all-gather.2.cloned.1.call-start = ((), (), s32[]{:S(2)}) async-start(), calls=%async_computation.3 | async-start | bytes 2433024 | tf_op jit(solution)/shard_map/all_gather | solution.py:55
  109.6 44.1 %copy-start.3 = (bf16[1,1408,256]{2,1,0:T(8,128)(2,1)S(1)}, bf16[1,1408,256]{2,1,0:T(8,128)(2,1)}, u32[]{:S(2)}) copy-start(bf16[1,1408,256]{2,1,0:T(8,128)(2,1)} %param.11) | copy-start | bytes 2162692
  156.1 15.5 %copy-start.2 = (f32[64,6]{0,1:T(8,128)S(1)}, f32[64,6]{0,1:T(8,128)}, u32[]{:S(2)}) copy-start(f32[64,6]{0,1:T(8,128)} %param.8) | copy-start | bytes 4612
  161.0 25.7 %all-to-all-start.1 = ((bf16[64,2,1408]{2,1,0:T(2,128)(2,1)}), bf16[64,2,1408]{2,1,0:T(2,128)(2,1)S(1)}, u32[]{:S(2)}, u32[]{:S(2)}) async-start(bf16[64,2,1408]{2,1,0:T(2,128)(2,1)} %reshape.62), calls=%async_computation.1 | async-start | bytes 720896 | tf_op jit(solution)/shard_map/all_to_all | solution.py:60
Sparse Core Ops, SparseCore 0:
  52.2 56.0 reduce-scatter.3
  111.0 42.6 all-gather.1
where the time goes:
time: 198 us; the launch traced here: 197 us
  waiting for transfers between devices  114 us (58%)
  blocking collectives  30.4 us (15%)
  local copies, waits for them, and re-layouts  15.3 us (8%)
  between operations  13.6 us (7%)
  starting transfers between devices  10.3 us (5%)
  other arithmetic  8.48 us (4%)
  matrix products  5 us (3%)
    unnamed x3, waiting for transfers between devices  56.2 us
    all_gather x1, waiting for transfers between devices, on_device(): lax.all_gather(hidden, 'narrow', axis=0, tiled=True)  42.8 us
    all_to_all x1, blocking collectives, on_device(): lax.all_to_all(outgoing, 'wide', split_axis=0, concat_axis=1, tiled=True)  30.4 us
    all_to_all x1, waiting for transfers between devices, on_device(): lax.all_to_all(expert_out, 'wide', split_axis=1, concat_axis=0, tiled=True)  15 us
    unnamed x16, local copies, waits for them, and re-layouts  10.4 us
    all_to_all x1, starting transfers between devices, on_device(): lax.all_to_all(expert_out, 'wide', split_axis=1, concat_axis=0, tiled=True)  10.3 us
  transfers between devices with their start and end apart: 3, of which 3 were waited for; matrix products, arithmetic and copies ran while one was open for 0% of the time, Pallas kernels for 0%

commit v1 on v0

v1 whole, which is shorter than its diff:
```python
import functools

import jax
import jax.numpy as jnp
from jax import lax
from jax.experimental import pallas as pl
from jax.experimental.pallas import tpu as pltpu
from jax.sharding import Mesh
from jax.sharding import PartitionSpec as P

VMEM = pl.BlockSpec(memory_space=pltpu.VMEM)
SMEM = pl.BlockSpec(memory_space=pltpu.SMEM)
NT = (((1,), (1,)), ((), ()))
TN = (((0,), (0,)), ((), ()))


def call(body, outs, *operands, scalars=0):
    return pl.pallas_call(
        body,
        out_shape=outs,
        in_specs=[SMEM] * scalars + [VMEM] * (len(operands) - scalars),
        out_specs=jax.tree.map(lambda _: VMEM, outs),
        compiler_params=pltpu.CompilerParams(vmem_limit_bytes=16 << 20),
    )(*operands)


def dispatch_body(cap, chips, cols, place, routes_t, tokens, outgoing, target_t):
    top, rows = routes_t.shape
    slots = outgoing.shape[0]
    experts = slots // cap
    expert_ids = lax.broadcasted_iota(jnp.int32, (experts, rows), 0)
    chosen = [(routes_t[k : k + 1, :] == expert_ids).astype(jnp.float32) for k in range(top)]
    named = functools.reduce(jnp.add, chosen)
    earlier = (
        lax.broadcasted_iota(jnp.int32, (rows, rows), 0) < lax.broadcasted_iota(jnp.int32, (rows, rows), 1)
    ).astype(jnp.bfloat16)
    before = jnp.dot(named.astype(jnp.bfloat16), earlier, preferred_element_type=jnp.float32)
    slot_ids = lax.broadcasted_iota(jnp.int32, (slots, rows), 0)
    picker = jnp.zeros((slots, rows), jnp.float32)
    for k in range(top):
        slot = jnp.sum(chosen[k] * before, axis=0, keepdims=True).astype(jnp.int32)
        target = routes_t[k : k + 1, :] * cap + slot
        target_t[k : k + 1, :] = target
        picker += (slot_ids == target).astype(jnp.float32)
    picker = picker.astype(jnp.bfloat16)
    parts = []
    for shift in range(chips):
        block = lax.rem(place[0] - shift + chips, chips) * 2 + place[1]
        columns = tokens[:, pl.ds(pl.multiple_of(block * cols, cols), cols)]
        parts.append(jnp.dot(picker, columns, preferred_element_type=jnp.float32).astype(jnp.bfloat16))
    outgoing[...] = jnp.concatenate(parts, 1).reshape(outgoing.shape)


def gate_up_body(cols, place, rows, *refs):
    weights, (theirs, mine) = refs[:-2], refs[-2:]
    half = mine.shape[0]
    flat = rows[...].reshape(rows.shape[0], rows.shape[1] * rows.shape[2])
    total = functools.reduce(
        jnp.add,
        [
            lax.dot_general(
                flat[:, s * cols : (s + 1) * cols], w[...], NT, preferred_element_type=jnp.float32
            )
            for s, w in enumerate(weights)
        ],
    )
    first = place[1] == 0
    theirs[...] = jnp.where(first, total[half:], total[:half]).astype(jnp.bfloat16)
    mine[...] = jnp.where(first, total[:half], total[half:])


def hidden_body(mine, theirs, hidden):
    units = hidden.shape[1]
    total = mine[...] + theirs[...].astype(jnp.float32)
    gate, up = total[:, :units], total[:, units:]
    hidden[...] = (gate / (1 + jnp.exp(-gate)) * up).astype(jnp.bfloat16)


def down_body(place, own, other, w_down, out):
    chips, half, units = own.shape
    for source, which in ((own, place[1]), (other, 1 - place[1])):
        total = functools.reduce(
            jnp.add,
            [
                jnp.dot(
                    source[z], w_down[z * units : (z + 1) * units, :], preferred_element_type=jnp.float32
                )
                for z in range(chips)
            ],
        )
        out[pl.ds(which * half, half)] = total.astype(jnp.bfloat16).reshape(half, *out.shape[1:])


def combine_body(target_t, weight_t, returned, out):
    top, rows = target_t.shape
    slots = returned.shape[0]
    slot_ids = lax.broadcasted_iota(jnp.int32, (slots, rows), 0)
    spread = jnp.zeros((slots, rows), jnp.float32)
    for k in range(top):
        spread += jnp.where(slot_ids == target_t[k : k + 1, :], weight_t[k : k + 1, :], 0.0)
    high = spread.astype(jnp.bfloat16)
    low = (spread - high.astype(jnp.float32)).astype(jnp.bfloat16)
    flat = returned[...].reshape(slots, out.shape[1])
    total = lax.dot_general(high, flat, TN, preferred_element_type=jnp.float32)
    total += lax.dot_general(low, flat, TN, preferred_element_type=jnp.float32)
    out[...] = total.astype(jnp.bfloat16)


def on_device(wide, chips, tokens, routes, route_weight, w_gate, w_up, w_down):
    tok_count, top = routes.shape
    _, units, cols = w_gate.shape
    experts = functools.reduce(lambda a, b: a * b, [lax.axis_size(a) for a in wide])
    cap = max(2, (11 * tok_count + experts - 1) // experts)
    slots = experts * cap
    share = units // chips
    half = slots // 2
    bf16 = jnp.bfloat16
    chip, core = lax.axis_index("chip"), lax.axis_index("core")
    place = jnp.stack([chip, core]).astype(jnp.int32)

    def share_of(index):
        start = index * share
        return jnp.concatenate(
            [lax.dynamic_slice_in_dim(w[0], start, share, 0) for w in (w_gate, w_up)], 0
        )

    weights = [share_of(chip)]
    for shift in range(1, chips):
        piece = share_of(lax.rem(chip + shift, chips))
        weights.append(lax.ppermute(piece, "chip", [(i, (i + shift) % chips) for i in range(chips)]))

    outgoing, target_t = call(
        functools.partial(dispatch_body, cap, chips, cols),
        (
            jax.ShapeDtypeStruct((slots, chips * cols // 128, 128), bf16),
            jax.ShapeDtypeStruct((top, tok_count), jnp.int32),
        ),
        place,
        routes.T,
        tokens,
        scalars=1,
    )
    received = lax.all_to_all(outgoing, wide, split_axis=0, concat_axis=0, tiled=True)
    theirs, mine = call(
        functools.partial(gate_up_body, cols),
        (
            jax.ShapeDtypeStruct((half, 2 * share), bf16),
            jax.ShapeDtypeStruct((half, 2 * share), jnp.float32),
        ),
        place,
        received,
        *weights,
        scalars=1,
    )
    theirs = lax.ppermute(theirs, "core", [(0, 1), (1, 0)])
    hidden = call(hidden_body, jax.ShapeDtypeStruct((half, share), bf16), mine, theirs)
    own = lax.all_gather(hidden, "chip", axis=0)
    other = lax.ppermute(own, "core", [(0, 1), (1, 0)])
    produced = call(
        down_body,
        jax.ShapeDtypeStruct((slots, cols // 128, 128), bf16),
        place,
        own,
        other,
        w_down[0],
        scalars=1,
    )
    returned = lax.all_to_all(produced, wide, split_axis=0, concat_axis=0, tiled=True)
    return call(
        combine_body,
        jax.ShapeDtypeStruct((tok_count, cols), bf16),
        target_t,
        route_weight.T,
        returned,
    )


def solution(mesh):
    chips = mesh.shape["narrow"] // 2
    fine = Mesh(mesh.devices.reshape(mesh.shape["wide"], chips, 2), ("wide", "chip", "core"))
    narrow = ("chip", "core")
    return jax.shard_map(
        functools.partial(on_device, ("wide",), chips),
        mesh=fine,
        in_specs=(
            P("wide", None),
            P("wide", None),
            P("wide", None),
            P("wide", None, narrow),
            P("wide", None, narrow),
            P("wide", None, narrow),
        ),
        out_specs=P("wide", narrow),
        check_vma=False,
    )
```

time: 198 us -> 133 us (0.67)
  waiting for transfers between devices: 114 us -> 41.2 us
  starting transfers between devices: 10.3 us -> 34.3 us
  blocking collectives: 30.4 us -> 47.9 us
  local copies, waits for them, and re-layouts: 15.3 us -> 1.76 us
  between operations: 13.6 us -> 0.17 us
  other arithmetic: 8.48 us -> 0.18 us
  Pallas kernels: 0 us -> 7.03 us
  matrix products: 5 us -> 0 us
    unnamed x3 -> x0, waiting for transfers between devices: 56.2 us -> none
    all_gather x1 -> x0, waiting for transfers between devices: 42.8 us -> none  [on_device(): lax.all_gather(hidden, 'narrow', axis=0, tiled=True)]
    ppermute x0 -> x5, waiting for transfers between devices: none -> 41.2 us  [the longest x3 36.6 us: on_device(): lax.ppermute(piece, 'chip', [(i, (i + shift) % chips) for i in range(chip...]
    all_gather x0 -> x1, blocking collectives: none -> 23.8 us  [on_device(): own = lax.all_gather(hidden, 'chip', axis=0)]
    ppermute x0 -> x5, starting transfers between devices: none -> 21.8 us  [the longest x3 18 us: on_device(): lax.ppermute(piece, 'chip', [(i, (i + shift) % chips) for i in range(chip...]
    all_to_all x1, waiting for transfers between devices: 15 us -> 0.01 us  [on_device(): lax.all_to_all(outgoing, wide, split_axis=0, concat_axis=0, tiled=True)]
    unnamed x16 -> x12, local copies, waits for them, and re-layouts: 10.4 us -> 1.65 us
    pallas_call x0 -> x5, Pallas kernels: none -> 7.03 us  [call(): pl.pallas_call(body, out_shape=outs, in_specs=[SMEM] * scalars + [VMEM] *...]
  transfers between devices with their start and end apart: 3 -> 6, of which waited for: 3 -> 4; matrix products, arithmetic and copies ran while one was open for 0% -> 0% of each run, Pallas kernels for 0% -> 0%
where the time goes in v1:
time: 133 us; the launch traced here: 132 us
  blocking collectives  47.9 us (36%)
  waiting for transfers between devices  41.2 us (31%)
  starting transfers between devices  34.3 us (26%)
  Pallas kernels  7.03 us (5%)
  local copies, waits for them, and re-layouts  1.76 us (1%)
    ppermute x3, waiting for transfers between devices, on_device(): lax.ppermute(piece, 'chip', [(i, (i + shift) % chips) for i in range(chip...  36.6 us
    all_to_all x1, blocking collectives, on_device(): lax.all_to_all(produced, wide, split_axis=0, concat_axis=0, tiled=True)  24.1 us
    all_gather x1, blocking collectives, on_device(): own = lax.all_gather(hidden, 'chip', axis=0)  23.8 us
    ppermute x3, starting transfers between devices, on_device(): lax.ppermute(piece, 'chip', [(i, (i + shift) % chips) for i in range(chip...  18 us
    all_to_all x1, starting transfers between devices, on_device(): lax.all_to_all(outgoing, wide, split_axis=0, concat_axis=0, tiled=True)  12.5 us
    pallas_call x5, Pallas kernels, call(): pl.pallas_call(body, out_shape=outs, in_specs=[SMEM] * scalars + [VMEM] *...  7.03 us
    ppermute x1, waiting for transfers between devices, on_device(): other = lax.ppermute(own, 'core', [(0, 1), (1, 0)])  2.67 us
  transfers between devices with their start and end apart: 6, of which 4 were waited for; matrix products, arithmetic and copies ran while one was open for 0% of the time, Pallas kernels for 0%

profile of v1, /device:TPU:8, one launch (start us, length us, event | category | flops | bytes accessed | tf_op | source)
XLA Modules:
  0.0 132.5 jit_solution(1947806903655609426)
XLA Ops:
  0.0 0.1 pad_add_fusion.place
  0.1 0.9 copy-done.1
  1.0 0.7 copy-done.2
  1.7 2.4 %shard_map.64 = (bf16[704,8,128]{2,1,0:T(8,128)(2,1)}, s32[6,64]{1,0:T(8,128)S(1)}) custom-call(s32[2]{0:T(128)S(1)} %pad_add_fusion.place, s32[6,64]{1,0:T(8,128)S(1)} %bitcast.25, bf16[64,2048]{1,0:T(8,128)(2,1)S(1)} %copy-done.1), custom_call_target="tpu_custom_call" | custom-call | tf_op jit(solution)/shard_map/pallas_call | solution.py:18
  4.1 12.5 %all-to-all-start = ((bf16[704,8,128]{2,1,0:T(8,128)(2,1)}), bf16[704,8,128]{2,1,0:T(8,128)(2,1)S(1)}, u32[]{:S(2)}, u32[]{:S(2)}) async-start(bf16[704,8,128]{2,1,0:T(8,128)(2,1)} %get-tuple-element.10), calls=%async_computation | async-start | bytes 2883584 | tf_op jit(solution)/shard_map/all_to_all | solution.py:143
  16.7 0.1 dynamic-slice_bitcast_fusion
  16.8 10.0 %collective-permute-start.1 = (bf16[704,256]{1,0:T(8,128)(2,1)S(1)}, bf16[704,256]{1,0:T(8,128)(2,1)S(1)}, u32[]{:S(2)}, u32[]{:S(2)}) collective-permute-start(bf16[704,256]{1,0:T(8,128)(2,1)S(1)} %pad_maximum_fusion.2), channel_id=1, source_target_pairs={{0,4},{2,6},{4,0},{6,2},{1,5},{3,7},{5,1},{7,3},{8,12},{10,14},{12... | collective-permute-start | bytes 1081352 | tf_op jit(solution)/shard_map/ppermute | solution.py:130
  26.9 4.3 %collective-permute-start = (bf16[704,256]{1,0:T(8,128)(2,1)S(1)}, bf16[704,256]{1,0:T(8,128)(2,1)S(1)}, u32[]{:S(2)}, u32[]{:S(2)}) collective-permute-start(bf16[704,256]{1,0:T(8,128)(2,1)S(1)} %pad_maximum_fusion.1), channel_id=1, source_target_pairs={{0,2},{2,4},{4,6},{6,0},{1,3},{3,5},{5,7},{7,1},{8,10},{10,12},{12... | collective-permute-start | bytes 1081352 | tf_op jit(solution)/shard_map/ppermute | solution.py:130
  31.2 3.7 %collective-permute-start.2 = (bf16[704,256]{1,0:T(8,128)(2,1)S(1)}, bf16[704,256]{1,0:T(8,128)(2,1)S(1)}, u32[]{:S(2)}, u32[]{:S(2)}) collective-permute-start(bf16[704,256]{1,0:T(8,128)(2,1)S(1)} %pad_maximum_fusion.3), channel_id=1, source_target_pairs={{0,6},{2,0},{4,2},{6,4},{1,7},{3,1},{5,3},{7,5},{8,14},{10,8},{12,... | collective-permute-start | bytes 1081352 | tf_op jit(solution)/shard_map/ppermute | solution.py:130
  34.9 22.2 %collective-permute-done.1.refs_2_ = bf16[704,256]{1,0:T(8,128)(2,1)S(1)} collective-permute-done((bf16[704,256]{1,0:T(8,128)(2,1)S(1)}, bf16[704,256]{1,0:T(8,128)(2,1)S(1)}, u32[]{:S(2)}, u32[]{:S(2)}) %collective-permute-start.1) | collective-permute-done | bytes 360480 | tf_op jit(solution)/shard_map/ppermute | solution.py:130
  57.1 14.4 %collective-permute-done.refs_1_ = bf16[704,256]{1,0:T(8,128)(2,1)S(1)} collective-permute-done((bf16[704,256]{1,0:T(8,128)(2,1)S(1)}, bf16[704,256]{1,0:T(8,128)(2,1)S(1)}, u32[]{:S(2)}, u32[]{:S(2)}) %collective-permute-start) | collective-permute-done | bytes 360480 | tf_op jit(solution)/shard_map/ppermute | solution.py:130
  71.5 0.0 collective-permute-done.2.refs_3_
  71.5 0.0 all-to-all-done.rows
  71.5 1.8 %shard_map.65 = (bf16[352,704]{1,0:T(8,128)(2,1)S(1)}, f32[352,704]{1,0:T(8,128)S(1)}) custom-call(s32[2]{0:T(128)S(1)} %pad_add_fusion.place, bf16[704,8,128]{2,1,0:T(8,128)(2,1)S(1)} %all-to-all-done.rows, bf16[704,256]{1,0:T(8,128)(2,1)S(1)} %pad_maximum_fusion.refs_0_, bf16[704,256]{1,0:T(8,128)(2,1)S(1)} %collective-permute-done.refs_1_, ...), custom_call_target="tpu_custom_call" | custom-call | tf_op jit(solution)/shard_map/pallas_call | solution.py:18
  73.4 1.9 %collective-permute-start.3 = (bf16[352,704]{1,0:T(8,128)(2,1)S(1)}, bf16[352,704]{1,0:T(8,128)(2,1)S(1)}, u32[]{:S(2)}, u32[]{:S(2)}) collective-permute-start(bf16[352,704]{1,0:T(8,128)(2,1)S(1)} %get-tuple-element.12), channel_id=1, source_target_pairs={{0,1},{1,0},{2,3},{3,2},{4,5},{5,4},{6,7},{7,6},{8,9},{9,8},{10,11... | collective-permute-start | bytes 1486856 | tf_op jit(solution)/shard_map/ppermute | solution.py:155
  75.3 1.9 %collective-permute-done.3.theirs = bf16[352,704]{1,0:T(8,128)(2,1)S(1)} collective-permute-done((bf16[352,704]{1,0:T(8,128)(2,1)S(1)}, bf16[352,704]{1,0:T(8,128)(2,1)S(1)}, u32[]{:S(2)}, u32[]{:S(2)}) %collective-permute-start.3) | collective-permute-done | bytes 495648 | tf_op jit(solution)/shard_map/ppermute | solution.py:155
  77.2 0.3 shard_map.66
  77.5 0.0 copy-start
  77.5 23.8 %all-gather = bf16[1408,352]{1,0:T(8,128)(2,1)S(1)} all-gather(bf16[352,352]{1,0:T(8,128)(2,1)S(1)} %shard_map.66), channel_id=2, replica_groups=mesh['wide'=64,'chip'=4,'core'=2] {'chip'}, dimensions={0}, use_global_device_ids=true | all-gather | bytes 1239040 | tf_op jit(solution)/shard_map/all_gather | solution.py:157
  101.3 1.9 %collective-permute-start.4 = (bf16[4,352,352]{2,1,0:T(8,128)(2,1)S(1)}, bf16[4,352,352]{2,1,0:T(8,128)(2,1)S(1)}, u32[]{:S(2)}, u32[]{:S(2)}) collective-permute-start(bf16[4,352,352]{2,1,0:T(8,128)(2,1)S(1)} %bitcast.22), channel_id=1, source_target_pairs={{0,1},{1,0},{2,3},{3,2},{4,5},{5,4},{6,7},{7,6},{8,9},{9,8},{10,11... | collective-permute-start | bytes 2973704 | tf_op jit(solution)/shard_map/ppermute | solution.py:158
  103.2 2.7 %collective-permute-done.4.other = bf16[4,352,352]{2,1,0:T(8,128)(2,1)S(1)} collective-permute-done((bf16[4,352,352]{2,1,0:T(8,128)(2,1)S(1)}, bf16[4,352,352]{2,1,0:T(8,128)(2,1)S(1)}, u32[]{:S(2)}, u32[]{:S(2)}) %collective-permute-start.4) | collective-permute-done | bytes 991264 | tf_op jit(solution)/shard_map/ppermute | solution.py:158
  105.8 1.5 %shard_map.67 = bf16[704,2,128]{2,1,0:T(2,128)(2,1)S(1)} custom-call(s32[2]{0:T(128)S(1)} %pad_add_fusion.place, bf16[4,352,352]{2,1,0:T(8,128)(2,1)S(1)} %bitcast.23, bf16[4,352,352]{2,1,0:T(8,128)(2,1)S(1)} %collective-permute-done.4.other, bf16[1408,256]{1,0:T(8,128)(2,1)S(1)} %bitcast.24), custom_call_target="tpu_custom_call" | custom-call | tf_op jit(solution)/shard_map/pallas_call | solution.py:18
  107.3 24.1 %all_to_all.10.returned = bf16[704,2,128]{2,1,0:T(2,128)(2,1)S(1)} all-to-all(bf16[704,2,128]{2,1,0:T(2,128)(2,1)S(1)} %shard_map.67), channel_id=1, replica_groups=mesh['wide'=64,'chip'=4,'core'=2] {'wide'}, dimensions={0} | all-to-all | bytes 720896 | tf_op jit(solution)/shard_map/all_to_all | solution.py:168
  131.4 1.1 shard_map.68
  (13 shorter events, 0.1 us)
Async XLA Ops:
  0.1 0.9 copy-start.1
  1.0 0.7 copy-start.2
  4.1 12.5 %copy-start.4 = (bf16[1,1408,256]{2,1,0:T(8,128)(2,1)S(1)}, bf16[1,1408,256]{2,1,0:T(8,128)(2,1)}, u32[]{:S(2)}) copy-start(bf16[1,1408,256]{2,1,0:T(8,128)(2,1)} %param.10) | copy-start | bytes 2162692
  4.1 12.6 %copy-start.5 = (bf16[1,1408,256]{2,1,0:T(8,128)(2,1)S(1)}, bf16[1,1408,256]{2,1,0:T(8,128)(2,1)}, u32[]{:S(2)}) copy-start(bf16[1,1408,256]{2,1,0:T(8,128)(2,1)} %param.9) | copy-start | bytes 2162692
  4.1 67.4 %all-to-all-start = ((bf16[704,8,128]{2,1,0:T(8,128)(2,1)}), bf16[704,8,128]{2,1,0:T(8,128)(2,1)S(1)}, u32[]{:S(2)}, u32[]{:S(2)}) async-start(bf16[704,8,128]{2,1,0:T(8,128)(2,1)} %get-tuple-element.10), calls=%async_computation | async-start | bytes 2883584 | tf_op jit(solution)/shard_map/all_to_all | solution.py:143
  16.8 40.3 %collective-permute-start.1 = (bf16[704,256]{1,0:T(8,128)(2,1)S(1)}, bf16[704,256]{1,0:T(8,128)(2,1)S(1)}, u32[]{:S(2)}, u32[]{:S(2)}) collective-permute-start(bf16[704,256]{1,0:T(8,128)(2,1)S(1)} %pad_maximum_fusion.2), channel_id=1, source_target_pairs={{0,4},{2,6},{4,0},{6,2},{1,5},{3,7},{5,1},{7,3},{8,12},{10,14},{12... | collective-permute-start | bytes 1081352 | tf_op jit(solution)/shard_map/ppermute | solution.py:130
  26.9 44.6 %collective-permute-start = (bf16[704,256]{1,0:T(8,128)(2,1)S(1)}, bf16[704,256]{1,0:T(8,128)(2,1)S(1)}, u32[]{:S(2)}, u32[]{:S(2)}) collective-permute-start(bf16[704,256]{1,0:T(8,128)(2,1)S(1)} %pad_maximum_fusion.1), channel_id=1, source_target_pairs={{0,2},{2,4},{4,6},{6,0},{1,3},{3,5},{5,7},{7,1},{8,10},{10,12},{12... | collective-permute-start | bytes 1081352 | tf_op jit(solution)/shard_map/ppermute | solution.py:130
  31.2 40.3 %collective-permute-start.2 = (bf16[704,256]{1,0:T(8,128)(2,1)S(1)}, bf16[704,256]{1,0:T(8,128)(2,1)S(1)}, u32[]{:S(2)}, u32[]{:S(2)}) collective-permute-start(bf16[704,256]{1,0:T(8,128)(2,1)S(1)} %pad_maximum_fusion.3), channel_id=1, source_target_pairs={{0,6},{2,0},{4,2},{6,4},{1,7},{3,1},{5,3},{7,5},{8,14},{10,8},{12,... | collective-permute-start | bytes 1081352 | tf_op jit(solution)/shard_map/ppermute | solution.py:130
  73.4 3.8 %collective-permute-start.3 = (bf16[352,704]{1,0:T(8,128)(2,1)S(1)}, bf16[352,704]{1,0:T(8,128)(2,1)S(1)}, u32[]{:S(2)}, u32[]{:S(2)}) collective-permute-start(bf16[352,704]{1,0:T(8,128)(2,1)S(1)} %get-tuple-element.12), channel_id=1, source_target_pairs={{0,1},{1,0},{2,3},{3,2},{4,5},{5,4},{6,7},{7,6},{8,9},{9,8},{10,11... | collective-permute-start | bytes 1486856 | tf_op jit(solution)/shard_map/ppermute | solution.py:155
  77.5 28.4 %copy-start = (bf16[1,1408,256]{2,1,0:T(8,128)(2,1)S(1)}, bf16[1,1408,256]{2,1,0:T(8,128)(2,1)}, u32[]{:S(2)}) copy-start(bf16[1,1408,256]{2,1,0:T(8,128)(2,1)} %param.11) | copy-start | bytes 2162692
  101.3 4.6 %collective-permute-start.4 = (bf16[4,352,352]{2,1,0:T(8,128)(2,1)S(1)}, bf16[4,352,352]{2,1,0:T(8,128)(2,1)S(1)}, u32[]{:S(2)}, u32[]{:S(2)}) collective-permute-start(bf16[4,352,352]{2,1,0:T(8,128)(2,1)S(1)} %bitcast.22), channel_id=1, source_target_pairs={{0,1},{1,0},{2,3},{3,2},{4,5},{5,4},{6,7},{7,6},{8,9},{9,8},{10,11... | collective-permute-start | bytes 2973704 | tf_op jit(solution)/shard_map/ppermute | solution.py:158
  105.8 25.6 %copy-start.3 = (f32[64,6]{0,1:T(8,128)S(1)}, f32[64,6]{0,1:T(8,128)}, u32[]{:S(2)}) copy-start(f32[64,6]{0,1:T(8,128)} %param.8) | copy-start | bytes 4612

commit v2 on v1

--- a/solution.py
+++ b/solution.py
@@ -14,13 +14,15 @@
 TN = (((0,), (0,)), ((), ()))
 
 
-def call(body, outs, *operands, scalars=0):
+def call(body, outs, *operands, scalars=0, flops=None):
+    cost = None if flops is None else pl.CostEstimate(flops=flops, transcendentals=0, bytes_accessed=0)
     return pl.pallas_call(
         body,
         out_shape=outs,
         in_specs=[SMEM] * scalars + [VMEM] * (len(operands) - scalars),
         out_specs=jax.tree.map(lambda _: VMEM, outs),
         compiler_params=pltpu.CompilerParams(vmem_limit_bytes=16 << 20),
+        cost_estimate=cost,
     )(*operands)
 
 
@@ -51,19 +53,41 @@
     outgoing[...] = jnp.concatenate(parts, 1).reshape(outgoing.shape)
 
 
-def gate_up_body(cols, place, rows, *refs):
-    weights, (theirs, mine) = refs[:-2], refs[-2:]
+def pack_body(place, w_gate, w_up, ahead, behind):
+    share = ahead.shape[0] // 3
+    chips = w_gate.shape[0] // share
+
+    def units(w, shift):
+        start = lax.rem(place[0] + shift, chips) * share
+        return w[pl.ds(pl.multiple_of(start, 16), share), :]
+
+    for out, near, far in ((ahead, 1, w_gate), (behind, chips - 1, w_up)):
+        out[:share, :] = units(w_gate, near)
+        out[share : 2 * share, :] = units(w_up, near)
+        out[2 * share :, :] = units(far, 2)
+
+
+def relay_body(before, after, gate, up):
+    share = gate.shape[0]
+    gate[...] = before[2 * share :, :]
+    up[...] = after[2 * share :, :]
+
+
+def gather_body(place, w_gate, w_up, before, after, far_gate, far_up, weights):
+    share, cols = far_gate.shape
+    here = pl.ds(pl.multiple_of(place[0] * share, 16), share)
+    weights[:share, :cols] = w_gate[here, :]
+    weights[share:, :cols] = w_up[here, :]
+    weights[:, cols : 2 * cols] = before[: 2 * share, :]
+    weights[:share, 2 * cols : 3 * cols] = far_gate[...]
+    weights[share:, 2 * cols : 3 * cols] = far_up[...]
+    weights[:, 3 * cols :] = after[: 2 * share, :]
+
+
+def gate_up_body(place, rows, weights, theirs, mine):
     half = mine.shape[0]
     flat = rows[...].reshape(rows.shape[0], rows.shape[1] * rows.shape[2])
-    total = functools.reduce(
-        jnp.add,
-        [
-            lax.dot_general(
-                flat[:, s * cols : (s + 1) * cols], w[...], NT, preferred_element_type=jnp.float32
-            )
-            for s, w in enumerate(weights)
-        ],
-    )
+    total = lax.dot_general(flat, weights[...], NT, preferred_element_type=jnp.float32)
     first = place[1] == 0
     theirs[...] = jnp.where(first, total[half:], total[:half]).astype(jnp.bfloat16)
     mine[...] = jnp.where(first, total[:half], total[half:])
@@ -76,18 +100,21 @@
     hidden[...] = (gate / (1 + jnp.exp(-gate)) * up).astype(jnp.bfloat16)
 
 
-def down_body(place, own, other, w_down, out):
-    chips, half, units = own.shape
-    for source, which in ((own, place[1]), (other, 1 - place[1])):
-        total = functools.reduce(
-            jnp.add,
-            [
-                jnp.dot(
-                    source[z], w_down[z * units : (z + 1) * units, :], preferred_element_type=jnp.float32
-                )
-                for z in range(chips)
-            ],
-        )
+def down_body(place, w_down, *refs):
+    out = refs[-1]
+    half, units = refs[0].shape
+    per = len(refs) // 2
+    chips = w_down.shape[0] // units
+    for pieces, which in ((refs[:per], place[1]), (refs[per:-1], 1 - place[1])):
+        here, before, after, *far = [p[...] for p in pieces]
+        total = jnp.zeros((half, w_down.shape[1]), jnp.float32)
+        for shift, part in enumerate((here, before, jnp.concatenate(far, 0), after)):
+            start = lax.rem(place[0] - shift + chips, chips) * units
+            total += jnp.dot(
+                part,
+                w_down[pl.ds(pl.multiple_of(start, 16), units), :],
+                preferred_element_type=jnp.float32,
+            )
         out[pl.ds(which * half, half)] = total.astype(jnp.bfloat16).reshape(half, *out.shape[1:])
 
 
@@ -118,16 +145,30 @@
     chip, core = lax.axis_index("chip"), lax.axis_index("core")
     place = jnp.stack([chip, core]).astype(jnp.int32)
 
-    def share_of(index):
-        start = index * share
-        return jnp.concatenate(
-            [lax.dynamic_slice_in_dim(w[0], start, share, 0) for w in (w_gate, w_up)], 0
-        )
-
-    weights = [share_of(chip)]
-    for shift in range(1, chips):
-        piece = share_of(lax.rem(chip + shift, chips))
-        weights.append(lax.ppermute(piece, "chip", [(i, (i + shift) % chips) for i in range(chips)]))
+    forward = [(i, (i + 1) % chips) for i in range(chips)]
+    backward = [(i, (i - 1) % chips) for i in range(chips)]
+    swap = [(0, 1), (1, 0)]
+
+    part = jax.ShapeDtypeStruct((share, cols), bf16)
+    parts = jax.ShapeDtypeStruct((3 * share, cols), bf16)
+    ahead, behind = call(pack_body, (parts, parts), place, w_gate[0], w_up[0], scalars=1)
+    before = lax.ppermute(ahead, "chip", forward)
+    after = lax.ppermute(behind, "chip", backward)
+    far_gate, far_up = call(relay_body, (part, part), before, after, flops=30_000_000_000)
+    far_gate = lax.ppermute(far_gate, "chip", forward)
+    far_up = lax.ppermute(far_up, "chip", backward)
+    weights = call(
+        gather_body,
+        jax.ShapeDtypeStruct((2 * share, chips * cols), bf16),
+        place,
+        w_gate[0],
+        w_up[0],
+        before,
+        after,
+        far_gate,
+        far_up,
+        scalars=1,
+    )
 
     outgoing, target_t = call(
         functools.partial(dispatch_body, cap, chips, cols),
@@ -142,27 +183,33 @@
     )
     received = lax.all_to_all(outgoing, wide, split_axis=0, concat_axis=0, tiled=True)
     theirs, mine = call(
-        functools.partial(gate_up_body, cols),
+        gate_up_body,
         (
             jax.ShapeDtypeStruct((half, 2 * share), bf16),
             jax.ShapeDtypeStruct((half, 2 * share), jnp.float32),
         ),
         place,
         received,
-        *weights,
-        scalars=1,
-    )
-    theirs = lax.ppermute(theirs, "core", [(0, 1), (1, 0)])
+        weights,
+        scalars=1,
+    )
+    theirs = lax.ppermute(theirs, "core", swap)
     hidden = call(hidden_body, jax.ShapeDtypeStruct((half, share), bf16), mine, theirs)
-    own = lax.all_gather(hidden, "chip", axis=0)
-    other = lax.ppermute(own, "core", [(0, 1), (1, 0)])
+    one_back = lax.ppermute(hidden, "chip", forward)
+    one_on = lax.ppermute(hidden, "chip", backward)
+    quarter = half // 2
+    far = (
+        lax.ppermute(one_back[:quarter], "chip", forward),
+        lax.ppermute(one_on[quarter:], "chip", backward),
+    )
+    own = (hidden, one_back, one_on, *far)
     produced = call(
         down_body,
         jax.ShapeDtypeStruct((slots, cols // 128, 128), bf16),
         place,
-        own,
-        other,
         w_down[0],
+        *own,
+        *[lax.ppermute(piece, "core", swap) for piece in own],
         scalars=1,
     )
     returned = lax.all_to_all(produced, wide, split_axis=0, concat_axis=0, tiled=True)

time: 133 us -> 139 us (1.045)
  starting transfers between devices: 34.3 us -> 63.8 us
  blocking collectives: 47.9 us -> 24.2 us
  waiting for transfers between devices: 41.2 us -> 36.5 us
  local copies, waits for them, and re-layouts: 1.76 us -> 4.12 us
  Pallas kernels: 7.03 us -> 9.28 us
    ppermute x5 -> x14, starting transfers between devices: 21.8 us -> 52.3 us  [the longest x5 10.1 us: on_device(): lax.ppermute(piece, 'core', swap)]
    all_gather x1 -> x0, blocking collectives: 23.8 us -> none  [on_device(): own = lax.all_gather(hidden, 'chip', axis=0)]
    ppermute x5 -> x14, waiting for transfers between devices: 41.2 us -> 31.5 us  [the longest x1 8.82 us: on_device(): after = lax.ppermute(behind, 'chip', backward)]
    all_to_all x1, waiting for transfers between devices: 0.01 us -> 5.03 us  [on_device(): lax.all_to_all(outgoing, wide, split_axis=0, concat_axis=0, tiled=True)]
    unnamed x12 -> x20, local copies, waits for them, and re-layouts: 1.65 us -> 4.09 us
    pallas_call x5 -> x8, Pallas kernels: 7.03 us -> 9.28 us  [call(): pl.pallas_call(body, out_shape=outs, in_specs=[SMEM] * scalars + [VMEM] *...]
  transfers between devices with their start and end apart: 6 -> 15, of which waited for: 4 -> 8; matrix products, arithmetic and copies ran while one was open for 0% -> 0% of each run, Pallas kernels for 0% -> 2%
where the time goes in v2:
time: 139 us; the launch traced here: 138 us
  starting transfers between devices  63.8 us (46%)
  waiting for transfers between devices  36.5 us (26%)
  blocking collectives  24.2 us (17%)
  Pallas kernels  9.28 us (7%)
  local copies, waits for them, and re-layouts  4.12 us (3%)
    all_to_all x1, blocking collectives, on_device(): lax.all_to_all(produced, wide, split_axis=0, concat_axis=0, tiled=True)  24.2 us
    all_to_all x1, starting transfers between devices, on_device(): lax.all_to_all(outgoing, wide, split_axis=0, concat_axis=0, tiled=True)  11.5 us
    ppermute x5, starting transfers between devices, on_device(): lax.ppermute(piece, 'core', swap)  10.1 us
    ppermute x1, starting transfers between devices, on_device(): far_gate = lax.ppermute(far_gate, 'chip', forward)  9.35 us
    pallas_call x8, Pallas kernels, call(): pl.pallas_call(body, out_shape=outs, in_specs=[SMEM] * scalars + [VMEM] *...  9.28 us
    ppermute x1, waiting for transfers between devices, on_device(): after = lax.ppermute(behind, 'chip', backward)  8.82 us
    ppermute x1, waiting for transfers between devices, on_device(): one_on = lax.ppermute(hidden, 'chip', backward)  7.91 us
    ppermute x1, starting transfers between devices, on_device(): after = lax.ppermute(behind, 'chip', backward)  6.77 us
  transfers between devices with their start and end apart: 15, of which 8 were waited for; matrix products, arithmetic and copies ran while one was open for 0% of the time, Pallas kernels for 2%

profile of v2, /device:TPU:8, one launch (start us, length us, event | category | flops | bytes accessed | tf_op | source)
XLA Modules:
  0.0 138.2 jit_solution(14021595422072525609)
XLA Ops:
  3.7 6.1 %collective-permute-start = (bf16[1056,256]{1,0:T(8,128)(2,1)}, bf16[1056,256]{1,0:T(8,128)(2,1)S(1)}, u32[]{:S(2)}, u32[]{:S(2)}) collective-permute-start(bf16[1056,256]{1,0:T(8,128)(2,1)} %get-tuple-element.15), channel_id=1, source_target_pairs={{0,2},{2,4},{4,6},{6,0},{1,3},{3,5},{5,7},{7,1},{8,10},{10,12},{12... | collective-permute-start | bytes 1622024 | tf_op jit(solution)/shard_map/ppermute | solution.py:155
  9.8 6.8 %collective-permute-start.1 = (bf16[1056,256]{1,0:T(8,128)(2,1)S(1)}, bf16[1056,256]{1,0:T(8,128)(2,1)S(1)}, u32[]{:S(2)}, u32[]{:S(2)}) collective-permute-start(bf16[1056,256]{1,0:T(8,128)(2,1)S(1)} %get-tuple-element.16), channel_id=1, source_target_pairs={{0,6},{2,0},{4,2},{6,4},{1,7},{3,1},{5,3},{7,5},{8,14},{10,8},{12,... | collective-permute-start | bytes 1622024 | tf_op jit(solution)/shard_map/ppermute | solution.py:156
  16.6 2.4 %shard_map.64 = (bf16[704,8,128]{2,1,0:T(8,128)(2,1)}, s32[6,64]{1,0:T(8,128)S(1)}) custom-call(s32[2]{0:T(128)S(1)} %pad_add_fusion.place, s32[6,64]{1,0:T(8,128)S(1)} %bitcast.12, bf16[64,2048]{1,0:T(8,128)(2,1)S(1)} %copy-done.7), custom_call_target="tpu_custom_call" | custom-call | tf_op jit(solution)/shard_map/pallas_call | solution.py:19
  19.0 11.5 %all-to-all-start = ((bf16[704,8,128]{2,1,0:T(8,128)(2,1)}), bf16[704,8,128]{2,1,0:T(8,128)(2,1)S(1)}, u32[]{:S(2)}, u32[]{:S(2)}) async-start(bf16[704,8,128]{2,1,0:T(8,128)(2,1)} %get-tuple-element.14), calls=%async_computation | async-start | bytes 2883584 | tf_op jit(solution)/shard_map/all_to_all | solution.py:184
  30.5 8.8 %collective-permute-done.1.after = bf16[1056,256]{1,0:T(8,128)(2,1)S(1)} collective-permute-done((bf16[1056,256]{1,0:T(8,128)(2,1)S(1)}, bf16[1056,256]{1,0:T(8,128)(2,1)S(1)}, u32[]{:S(2)}, u32[]{:S(2)}) %collective-permute-start.1) | collective-permute-done | bytes 540704 | tf_op jit(solution)/shard_map/ppermute | solution.py:156
  40.2 9.3 %collective-permute-start.2 = (bf16[352,256]{1,0:T(8,128)(2,1)S(1)}, bf16[352,256]{1,0:T(8,128)(2,1)S(1)}, u32[]{:S(2)}, u32[]{:S(2)}) collective-permute-start(bf16[352,256]{1,0:T(8,128)(2,1)S(1)} %get-tuple-element.17), channel_id=1, source_target_pairs={{0,2},{2,4},{4,6},{6,0},{1,3},{3,5},{5,7},{7,1},{8,10},{10,12},{12... | collective-permute-start | bytes 540680 | tf_op jit(solution)/shard_map/ppermute | solution.py:158
  49.5 2.8 %collective-permute-start.3 = (bf16[352,256]{1,0:T(8,128)(2,1)S(1)}, bf16[352,256]{1,0:T(8,128)(2,1)S(1)}, u32[]{:S(2)}, u32[]{:S(2)}) collective-permute-start(bf16[352,256]{1,0:T(8,128)(2,1)S(1)} %get-tuple-element.18), channel_id=1, source_target_pairs={{0,6},{2,0},{4,2},{6,4},{1,7},{3,1},{5,3},{7,5},{8,14},{10,8},{12,... | collective-permute-start | bytes 540680 | tf_op jit(solution)/shard_map/ppermute | solution.py:159
  52.4 4.6 %collective-permute-done.2.far_gate = bf16[352,256]{1,0:T(8,128)(2,1)S(1)} collective-permute-done((bf16[352,256]{1,0:T(8,128)(2,1)S(1)}, bf16[352,256]{1,0:T(8,128)(2,1)S(1)}, u32[]{:S(2)}, u32[]{:S(2)}) %collective-permute-start.2) | collective-permute-done | bytes 180256 | tf_op jit(solution)/shard_map/ppermute | solution.py:158
  57.0 3.3 %collective-permute-done.3.far_up = bf16[352,256]{1,0:T(8,128)(2,1)S(1)} collective-permute-done((bf16[352,256]{1,0:T(8,128)(2,1)S(1)}, bf16[352,256]{1,0:T(8,128)(2,1)S(1)}, u32[]{:S(2)}, u32[]{:S(2)}) %collective-permute-start.3) | collective-permute-done | bytes 180256 | tf_op jit(solution)/shard_map/ppermute | solution.py:159
  62.0 5.0 %all-to-all-done.rows = bf16[704,8,128]{2,1,0:T(8,128)(2,1)S(1)} async-done(((bf16[704,8,128]{2,1,0:T(8,128)(2,1)}), bf16[704,8,128]{2,1,0:T(8,128)(2,1)S(1)}, u32[]{:S(2)}, u32[]{:S(2)}) %all-to-all-start) | async-done | bytes 1441824 | tf_op jit(solution)/shard_map/all_to_all | solution.py:184
  68.9 2.1 %collective-permute-start.4 = (bf16[352,704]{1,0:T(8,128)(2,1)S(1)}, bf16[352,704]{1,0:T(8,128)(2,1)S(1)}, u32[]{:S(2)}, u32[]{:S(2)}) collective-permute-start(bf16[352,704]{1,0:T(8,128)(2,1)S(1)} %get-tuple-element.20), channel_id=1, source_target_pairs={{0,1},{1,0},{2,3},{3,2},{4,5},{5,4},{6,7},{7,6},{8,9},{9,8},{10,11... | collective-permute-start | bytes 1486856 | tf_op jit(solution)/shard_map/ppermute | solution.py:196
  71.0 1.9 %collective-permute-done.4.theirs = bf16[352,704]{1,0:T(8,128)(2,1)S(1)} collective-permute-done((bf16[352,704]{1,0:T(8,128)(2,1)S(1)}, bf16[352,704]{1,0:T(8,128)(2,1)S(1)}, u32[]{:S(2)}, u32[]{:S(2)}) %collective-permute-start.4) | collective-permute-done | bytes 495648 | tf_op jit(solution)/shard_map/ppermute | solution.py:196
  73.2 4.7 %collective-permute-start.6 = (bf16[352,352]{1,0:T(8,128)(2,1)S(1)}, bf16[352,352]{1,0:T(8,128)(2,1)S(1)}, u32[]{:S(2)}, u32[]{:S(2)}) collective-permute-start(bf16[352,352]{1,0:T(8,128)(2,1)S(1)} %shard_map.69.refs_0_), channel_id=1, source_target_pairs={{0,6},{2,0},{4,2},{6,4},{1,7},{3,1},{5,3},{7,5},{8,14},{10,8},{12,... | collective-permute-start | bytes 743432 | tf_op jit(solution)/shard_map/ppermute | solution.py:199
  77.9 2.0 %collective-permute-start.5 = (bf16[352,352]{1,0:T(8,128)(2,1)S(1)}, bf16[352,352]{1,0:T(8,128)(2,1)S(1)}, u32[]{:S(2)}, u32[]{:S(2)}) collective-permute-start(bf16[352,352]{1,0:T(8,128)(2,1)S(1)} %shard_map.69.refs_0_), channel_id=1, source_target_pairs={{0,2},{2,4},{4,6},{6,0},{1,3},{3,5},{5,7},{7,1},{8,10},{10,12},{12... | collective-permute-start | bytes 743432 | tf_op jit(solution)/shard_map/ppermute | solution.py:198
  79.9 1.9 %collective-permute-start.9 = (bf16[352,352]{1,0:T(8,128)(2,1)S(1)}, bf16[352,352]{1,0:T(8,128)(2,1)S(1)}, u32[]{:S(2)}, u32[]{:S(2)}) collective-permute-start(bf16[352,352]{1,0:T(8,128)(2,1)S(1)} %shard_map.69.refs_0_), channel_id=1, source_target_pairs={{0,1},{1,0},{2,3},{3,2},{4,5},{5,4},{6,7},{7,6},{8,9},{9,8},{10,11... | collective-permute-start | bytes 743432 | tf_op jit(solution)/shard_map/ppermute | solution.py:212
  81.9 7.9 %collective-permute-done.6.refs_2_ = bf16[352,352]{1,0:T(8,128)(2,1)S(1)} collective-permute-done((bf16[352,352]{1,0:T(8,128)(2,1)S(1)}, bf16[352,352]{1,0:T(8,128)(2,1)S(1)}, u32[]{:S(2)}, u32[]{:S(2)}) %collective-permute-start.6) | collective-permute-done | bytes 247840 | tf_op jit(solution)/shard_map/ppermute | solution.py:199
  89.8 6.5 %collective-permute-start.8 = (bf16[176,352]{1,0:T(8,128)(2,1)S(1)}, bf16[176,352]{1,0:T(8,128)(2,1)S(1)}, u32[]{:S(2)}, u32[]{:S(2)}) collective-permute-start(bf16[176,352]{1,0:T(8,128)(2,1)S(1)} %slice.9), channel_id=1, source_target_pairs={{0,6},{2,0},{4,2},{6,4},{1,7},{3,1},{5,3},{7,5},{8,14},{10,8},{12,... | collective-permute-start | bytes 371720 | tf_op jit(solution)/shard_map/ppermute | solution.py:203
  96.3 1.9 %collective-permute-start.7 = (bf16[176,352]{1,0:T(8,128)(2,1)S(1)}, bf16[176,352]{1,0:T(8,128)(2,1)S(1)}, u32[]{:S(2)}, u32[]{:S(2)}) collective-permute-start(bf16[176,352]{1,0:T(8,128)(2,1)S(1)} %slice.8), channel_id=1, source_target_pairs={{0,2},{2,4},{4,6},{6,0},{1,3},{3,5},{5,7},{7,1},{8,10},{10,12},{12... | collective-permute-start | bytes 371720 | tf_op jit(solution)/shard_map/ppermute | solution.py:202
  98.2 1.9 %collective-permute-start.11 = (bf16[352,352]{1,0:T(8,128)(2,1)S(1)}, bf16[352,352]{1,0:T(8,128)(2,1)S(1)}, u32[]{:S(2)}, u32[]{:S(2)}) collective-permute-start(bf16[352,352]{1,0:T(8,128)(2,1)S(1)} %collective-permute-done.6.refs_2_), channel_id=1, source_target_pairs={{0,1},{1,0},{2,3},{3,2},{4,5},{5,4},{6,7},{7,6},{8,9},{9,8},{10,11... | collective-permute-start | bytes 743432 | tf_op jit(solution)/shard_map/ppermute | solution.py:212
  100.2 2.4 %collective-permute-start.10 = (bf16[352,352]{1,0:T(8,128)(2,1)S(1)}, bf16[352,352]{1,0:T(8,128)(2,1)S(1)}, u32[]{:S(2)}, u32[]{:S(2)}) collective-permute-start(bf16[352,352]{1,0:T(8,128)(2,1)S(1)} %collective-permute-done.5.refs_1_), channel_id=1, source_target_pairs={{0,1},{1,0},{2,3},{3,2},{4,5},{5,4},{6,7},{7,6},{8,9},{9,8},{10,11... | collective-permute-start | bytes 743432 | tf_op jit(solution)/shard_map/ppermute | solution.py:212
  102.6 1.9 %collective-permute-start.13 = (bf16[176,352]{1,0:T(8,128)(2,1)S(1)}, bf16[176,352]{1,0:T(8,128)(2,1)S(1)}, u32[]{:S(2)}, u32[]{:S(2)}) collective-permute-start(bf16[176,352]{1,0:T(8,128)(2,1)S(1)} %collective-permute-done.8.refs_4_), channel_id=1, source_target_pairs={{0,1},{1,0},{2,3},{3,2},{4,5},{5,4},{6,7},{7,6},{8,9},{9,8},{10,11... | collective-permute-start | bytes 371720 | tf_op jit(solution)/shard_map/ppermute | solution.py:212
  104.5 3.7 %collective-permute-done.7.refs_3_ = bf16[176,352]{1,0:T(8,128)(2,1)S(1)} collective-permute-done((bf16[176,352]{1,0:T(8,128)(2,1)S(1)}, bf16[176,352]{1,0:T(8,128)(2,1)S(1)}, u32[]{:S(2)}, u32[]{:S(2)}) %collective-permute-start.7) | collective-permute-done | bytes 123936 | tf_op jit(solution)/shard_map/ppermute | solution.py:202
  108.2 1.9 %collective-permute-start.12 = (bf16[176,352]{1,0:T(8,128)(2,1)S(1)}, bf16[176,352]{1,0:T(8,128)(2,1)S(1)}, u32[]{:S(2)}, u32[]{:S(2)}) collective-permute-start(bf16[176,352]{1,0:T(8,128)(2,1)S(1)} %collective-permute-done.7.refs_3_), channel_id=1, source_target_pairs={{0,1},{1,0},{2,3},{3,2},{4,5},{5,4},{6,7},{7,6},{8,9},{9,8},{10,11... | collective-permute-start | bytes 371720 | tf_op jit(solution)/shard_map/ppermute | solution.py:212
  112.9 24.2 %all_to_all.10.returned = bf16[704,2,128]{2,1,0:T(2,128)(2,1)S(1)} all-to-all(bf16[704,2,128]{2,1,0:T(2,128)(2,1)S(1)} %shard_map.70), channel_id=1, replica_groups=mesh['wide'=64,'chip'=4,'core'=2] {'wide'}, dimensions={0} | all-to-all | bytes 720896 | tf_op jit(solution)/shard_map/all_to_all | solution.py:215
  (38 shorter events, 12.4 us)
Async XLA Ops:
  0.0 16.6 %copy-start.8 = (s32[64,6]{0,1:T(8,128)S(1)}, s32[64,6]{0,1:T(8,128)}, u32[]{:S(2)}) copy-start(s32[64,6]{0,1:T(8,128)} %param.7) | copy-start | bytes 4612
  0.1 1.1 copy-start
  1.2 1.1 copy-start.2
  2.3 14.3 %copy-start.7 = (bf16[64,2048]{1,0:T(8,128)(2,1)S(1)}, bf16[64,2048]{1,0:T(8,128)(2,1)}, u32[]{:S(2)}) copy-start(bf16[64,2048]{1,0:T(8,128)(2,1)} %tokens.1) | copy-start | bytes 786436
  3.7 26.8 %collective-permute-start = (bf16[1056,256]{1,0:T(8,128)(2,1)}, bf16[1056,256]{1,0:T(8,128)(2,1)S(1)}, u32[]{:S(2)}, u32[]{:S(2)}) collective-permute-start(bf16[1056,256]{1,0:T(8,128)(2,1)} %get-tuple-element.15), channel_id=1, source_target_pairs={{0,2},{2,4},{4,6},{6,0},{1,3},{3,5},{5,7},{7,1},{8,10},{10,12},{12... | collective-permute-start | bytes 1622024 | tf_op jit(solution)/shard_map/ppermute | solution.py:155
  9.8 29.5 %collective-permute-start.1 = (bf16[1056,256]{1,0:T(8,128)(2,1)S(1)}, bf16[1056,256]{1,0:T(8,128)(2,1)S(1)}, u32[]{:S(2)}, u32[]{:S(2)}) collective-permute-start(bf16[1056,256]{1,0:T(8,128)(2,1)S(1)} %get-tuple-element.16), channel_id=1, source_target_pairs={{0,6},{2,0},{4,2},{6,4},{1,7},{3,1},{5,3},{7,5},{8,14},{10,8},{12,... | collective-permute-start | bytes 1622024 | tf_op jit(solution)/shard_map/ppermute | solution.py:156
  19.0 48.0 %all-to-all-start = ((bf16[704,8,128]{2,1,0:T(8,128)(2,1)}), bf16[704,8,128]{2,1,0:T(8,128)(2,1)S(1)}, u32[]{:S(2)}, u32[]{:S(2)}) async-start(bf16[704,8,128]{2,1,0:T(8,128)(2,1)} %get-tuple-element.14), calls=%async_computation | async-start | bytes 2883584 | tf_op jit(solution)/shard_map/all_to_all | solution.py:184
  30.5 29.7 %copy-start.1 = (bf16[1,1408,256]{2,1,0:T(8,128)(2,1)S(1)}, bf16[1,1408,256]{2,1,0:T(8,128)(2,1)}, u32[]{:S(2)}) copy-start(bf16[1,1408,256]{2,1,0:T(8,128)(2,1)} %param.9) | copy-start | bytes 2162692
  30.5 29.7 %copy-start.3 = (bf16[1,1408,256]{2,1,0:T(8,128)(2,1)S(1)}, bf16[1,1408,256]{2,1,0:T(8,128)(2,1)}, u32[]{:S(2)}) copy-start(bf16[1,1408,256]{2,1,0:T(8,128)(2,1)} %param.10) | copy-start | bytes 2162692
  40.2 16.8 %collective-permute-start.2 = (bf16[352,256]{1,0:T(8,128)(2,1)S(1)}, bf16[352,256]{1,0:T(8,128)(2,1)S(1)}, u32[]{:S(2)}, u32[]{:S(2)}) collective-permute-start(bf16[352,256]{1,0:T(8,128)(2,1)S(1)} %get-tuple-element.17), channel_id=1, source_target_pairs={{0,2},{2,4},{4,6},{6,0},{1,3},{3,5},{5,7},{7,1},{8,10},{10,12},{12... | collective-permute-start | bytes 540680 | tf_op jit(solution)/shard_map/ppermute | solution.py:158
  49.5 10.7 %collective-permute-start.3 = (bf16[352,256]{1,0:T(8,128)(2,1)S(1)}, bf16[352,256]{1,0:T(8,128)(2,1)S(1)}, u32[]{:S(2)}, u32[]{:S(2)}) collective-permute-start(bf16[352,256]{1,0:T(8,128)(2,1)S(1)} %get-tuple-element.18), channel_id=1, source_target_pairs={{0,6},{2,0},{4,2},{6,4},{1,7},{3,1},{5,3},{7,5},{8,14},{10,8},{12,... | collective-permute-start | bytes 540680 | tf_op jit(solution)/shard_map/ppermute | solution.py:159
  60.2 1.0 copy-start.6
  68.9 42.5 %copy-start.4 = (bf16[1,1408,256]{2,1,0:T(8,128)(2,1)S(1)}, bf16[1,1408,256]{2,1,0:T(8,128)(2,1)}, u32[]{:S(2)}) copy-start(bf16[1,1408,256]{2,1,0:T(8,128)(2,1)} %param.11) | copy-start | bytes 2162692
  68.9 4.0 %collective-permute-start.4 = (bf16[352,704]{1,0:T(8,128)(2,1)S(1)}, bf16[352,704]{1,0:T(8,128)(2,1)S(1)}, u32[]{:S(2)}, u32[]{:S(2)}) collective-permute-start(bf16[352,704]{1,0:T(8,128)(2,1)S(1)} %get-tuple-element.20), channel_id=1, source_target_pairs={{0,1},{1,0},{2,3},{3,2},{4,5},{5,4},{6,7},{7,6},{8,9},{9,8},{10,11... | collective-permute-start | bytes 1486856 | tf_op jit(solution)/shard_map/ppermute | solution.py:196
  73.2 16.6 %collective-permute-start.6 = (bf16[352,352]{1,0:T(8,128)(2,1)S(1)}, bf16[352,352]{1,0:T(8,128)(2,1)S(1)}, u32[]{:S(2)}, u32[]{:S(2)}) collective-permute-start(bf16[352,352]{1,0:T(8,128)(2,1)S(1)} %shard_map.69.refs_0_), channel_id=1, source_target_pairs={{0,6},{2,0},{4,2},{6,4},{1,7},{3,1},{5,3},{7,5},{8,14},{10,8},{12,... | collective-permute-start | bytes 743432 | tf_op jit(solution)/shard_map/ppermute | solution.py:199
  77.9 18.3 %collective-permute-start.5 = (bf16[352,352]{1,0:T(8,128)(2,1)S(1)}, bf16[352,352]{1,0:T(8,128)(2,1)S(1)}, u32[]{:S(2)}, u32[]{:S(2)}) collective-permute-start(bf16[352,352]{1,0:T(8,128)(2,1)S(1)} %shard_map.69.refs_0_), channel_id=1, source_target_pairs={{0,2},{2,4},{4,6},{6,0},{1,3},{3,5},{5,7},{7,1},{8,10},{10,12},{12... | collective-permute-start | bytes 743432 | tf_op jit(solution)/shard_map/ppermute | solution.py:198
  79.9 30.2 %collective-permute-start.9 = (bf16[352,352]{1,0:T(8,128)(2,1)S(1)}, bf16[352,352]{1,0:T(8,128)(2,1)S(1)}, u32[]{:S(2)}, u32[]{:S(2)}) collective-permute-start(bf16[352,352]{1,0:T(8,128)(2,1)S(1)} %shard_map.69.refs_0_), channel_id=1, source_target_pairs={{0,1},{1,0},{2,3},{3,2},{4,5},{5,4},{6,7},{7,6},{8,9},{9,8},{10,11... | collective-permute-start | bytes 743432 | tf_op jit(solution)/shard_map/ppermute | solution.py:212
  89.8 12.8 %collective-permute-start.8 = (bf16[176,352]{1,0:T(8,128)(2,1)S(1)}, bf16[176,352]{1,0:T(8,128)(2,1)S(1)}, u32[]{:S(2)}, u32[]{:S(2)}) collective-permute-start(bf16[176,352]{1,0:T(8,128)(2,1)S(1)} %slice.9), channel_id=1, source_target_pairs={{0,6},{2,0},{4,2},{6,4},{1,7},{3,1},{5,3},{7,5},{8,14},{10,8},{12,... | collective-permute-start | bytes 371720 | tf_op jit(solution)/shard_map/ppermute | solution.py:203
  96.3 11.9 %collective-permute-start.7 = (bf16[176,352]{1,0:T(8,128)(2,1)S(1)}, bf16[176,352]{1,0:T(8,128)(2,1)S(1)}, u32[]{:S(2)}, u32[]{:S(2)}) collective-permute-start(bf16[176,352]{1,0:T(8,128)(2,1)S(1)} %slice.8), channel_id=1, source_target_pairs={{0,2},{2,4},{4,6},{6,0},{1,3},{3,5},{5,7},{7,1},{8,10},{10,12},{12... | collective-permute-start | bytes 371720 | tf_op jit(solution)/shard_map/ppermute | solution.py:202
  98.2 11.9 %collective-permute-start.11 = (bf16[352,352]{1,0:T(8,128)(2,1)S(1)}, bf16[352,352]{1,0:T(8,128)(2,1)S(1)}, u32[]{:S(2)}, u32[]{:S(2)}) collective-permute-start(bf16[352,352]{1,0:T(8,128)(2,1)S(1)} %collective-permute-done.6.refs_2_), channel_id=1, source_target_pairs={{0,1},{1,0},{2,3},{3,2},{4,5},{5,4},{6,7},{7,6},{8,9},{9,8},{10,11... | collective-permute-start | bytes 743432 | tf_op jit(solution)/shard_map/ppermute | solution.py:212
  100.2 11.3 %collective-permute-start.10 = (bf16[352,352]{1,0:T(8,128)(2,1)S(1)}, bf16[352,352]{1,0:T(8,128)(2,1)S(1)}, u32[]{:S(2)}, u32[]{:S(2)}) collective-permute-start(bf16[352,352]{1,0:T(8,128)(2,1)S(1)} %collective-permute-done.5.refs_1_), channel_id=1, source_target_pairs={{0,1},{1,0},{2,3},{3,2},{4,5},{5,4},{6,7},{7,6},{8,9},{9,8},{10,11... | collective-permute-start | bytes 743432 | tf_op jit(solution)/shard_map/ppermute | solution.py:212
  102.6 7.6 %collective-permute-start.13 = (bf16[176,352]{1,0:T(8,128)(2,1)S(1)}, bf16[176,352]{1,0:T(8,128)(2,1)S(1)}, u32[]{:S(2)}, u32[]{:S(2)}) collective-permute-start(bf16[176,352]{1,0:T(8,128)(2,1)S(1)} %collective-permute-done.8.refs_4_), channel_id=1, source_target_pairs={{0,1},{1,0},{2,3},{3,2},{4,5},{5,4},{6,7},{7,6},{8,9},{9,8},{10,11... | collective-permute-start | bytes 371720 | tf_op jit(solution)/shard_map/ppermute | solution.py:212
  108.2 3.2 %collective-permute-start.12 = (bf16[176,352]{1,0:T(8,128)(2,1)S(1)}, bf16[176,352]{1,0:T(8,128)(2,1)S(1)}, u32[]{:S(2)}, u32[]{:S(2)}) collective-permute-start(bf16[176,352]{1,0:T(8,128)(2,1)S(1)} %collective-permute-done.7.refs_3_), channel_id=1, source_target_pairs={{0,1},{1,0},{2,3},{3,2},{4,5},{5,4},{6,7},{7,6},{8,9},{9,8},{10,11... | collective-permute-start | bytes 371720 | tf_op jit(solution)/shard_map/ppermute | solution.py:212
  111.5 25.7 %copy-start.9 = (f32[64,6]{0,1:T(8,128)S(1)}, f32[64,6]{0,1:T(8,128)}, u32[]{:S(2)}) copy-start(f32[64,6]{0,1:T(8,128)} %param.8) | copy-start | bytes 4612
  (1 other events, 0.8 us)

commit v3 on v1

--- a/solution.py
+++ b/solution.py
@@ -9,22 +9,29 @@
 from jax.sharding import PartitionSpec as P
 
 VMEM = pl.BlockSpec(memory_space=pltpu.VMEM)
+ANY = pl.BlockSpec(memory_space=pl.ANY)
 SMEM = pl.BlockSpec(memory_space=pltpu.SMEM)
+SHARES = (0, 2, 3, 1)
+PAIR = [(0, 1), (1, 0), (2, 3), (3, 2)]
+OPPOSITE = [(0, 3), (3, 0), (1, 2), (2, 1)]
+SWAP = [(0, 1), (1, 0)]
+CORE, HALF, SHARE, BLOCK, PAIR_BLOCK = range(5)
 NT = (((1,), (1,)), ((), ()))
 TN = (((0,), (0,)), ((), ()))
 
 
-def call(body, outs, *operands, scalars=0):
+def call(body, outs, *operands, scalars=0, space=VMEM, scratch=()):
     return pl.pallas_call(
         body,
         out_shape=outs,
-        in_specs=[SMEM] * scalars + [VMEM] * (len(operands) - scalars),
+        in_specs=[SMEM] * scalars + [space] * (len(operands) - scalars),
         out_specs=jax.tree.map(lambda _: VMEM, outs),
+        scratch_shapes=scratch,
         compiler_params=pltpu.CompilerParams(vmem_limit_bytes=16 << 20),
     )(*operands)
 
 
-def dispatch_body(cap, chips, cols, place, routes_t, tokens, outgoing, target_t):
+def dispatch_body(cap, cols, place, routes_t, tokens, outgoing, target_t):
     top, rows = routes_t.shape
     slots = outgoing.shape[0]
     experts = slots // cap
@@ -44,48 +51,70 @@
         picker += (slot_ids == target).astype(jnp.float32)
     picker = picker.astype(jnp.bfloat16)
     parts = []
-    for shift in range(chips):
-        block = lax.rem(place[0] - shift + chips, chips) * 2 + place[1]
+    for block in (place[BLOCK], place[PAIR_BLOCK]):
         columns = tokens[:, pl.ds(pl.multiple_of(block * cols, cols), cols)]
         parts.append(jnp.dot(picker, columns, preferred_element_type=jnp.float32).astype(jnp.bfloat16))
     outgoing[...] = jnp.concatenate(parts, 1).reshape(outgoing.shape)
 
 
-def gate_up_body(cols, place, rows, *refs):
-    weights, (theirs, mine) = refs[:-2], refs[-2:]
-    half = mine.shape[0]
+def pack_body(share, place, w_gate, w_up, out, sems):
+    copies = []
+    for n, w in ((0, w_gate), (1, w_up)):
+        for part in range(2):
+            start = pl.multiple_of((1 - place[HALF]) * 2 * share + part * share, 16)
+            copies.append(
+                pltpu.make_async_copy(
+                    w.at[pl.ds(start, share), :],
+                    out.at[pl.ds((2 * part + n) * share, share), :],
+                    sems.at[2 * n + part],
+                )
+            )
+    for copy in copies:
+        copy.start()
+    for copy in copies:
+        copy.wait()
+
+
+def gate_up_body(keep, place, rows, w_gate, w_up, pair, theirs, mine):
+    half, both = mine.shape
+    share = both // 2
+    part = place[SHARE] if keep else 1 - place[SHARE]
     flat = rows[...].reshape(rows.shape[0], rows.shape[1] * rows.shape[2])
-    total = functools.reduce(
-        jnp.add,
+    here = pl.ds(pl.multiple_of((2 * place[HALF] + part) * share, 16), share)
+    weights = jnp.concatenate(
         [
-            lax.dot_general(
-                flat[:, s * cols : (s + 1) * cols], w[...], NT, preferred_element_type=jnp.float32
-            )
-            for s, w in enumerate(weights)
+            jnp.concatenate([w_gate[here, :], w_up[here, :]], 0),
+            pair[pl.ds(pl.multiple_of(part * both, 16), both), :],
         ],
-    )
-    first = place[1] == 0
+        1,
+    )
+    total = lax.dot_general(flat, weights, NT, preferred_element_type=jnp.float32)
+    first = place[CORE] == 0
     theirs[...] = jnp.where(first, total[half:], total[:half]).astype(jnp.bfloat16)
     mine[...] = jnp.where(first, total[:half], total[half:])
 
 
-def hidden_body(mine, theirs, hidden):
+def add_body(mine, theirs, out):
+    out[...] = (mine[...] + theirs[...].astype(jnp.float32)).astype(out.dtype)
+
+
+def hidden_body(mine, theirs, far, hidden):
     units = hidden.shape[1]
-    total = mine[...] + theirs[...].astype(jnp.float32)
+    total = mine[...] + theirs[...].astype(jnp.float32) + far[...].astype(jnp.float32)
     gate, up = total[:, :units], total[:, units:]
     hidden[...] = (gate / (1 + jnp.exp(-gate)) * up).astype(jnp.bfloat16)
 
 
 def down_body(place, own, other, w_down, out):
-    chips, half, units = own.shape
-    for source, which in ((own, place[1]), (other, 1 - place[1])):
+    half, units = own.shape[1:]
+    for source, which in ((own, place[CORE]), (other, 1 - place[CORE])):
         total = functools.reduce(
             jnp.add,
             [
                 jnp.dot(
-                    source[z], w_down[z * units : (z + 1) * units, :], preferred_element_type=jnp.float32
+                    source[z], w_down[n * units : (n + 1) * units, :], preferred_element_type=jnp.float32
                 )
-                for z in range(chips)
+                for z, n in enumerate(SHARES)
             ],
         )
         out[pl.ds(which * half, half)] = total.astype(jnp.bfloat16).reshape(half, *out.shape[1:])
@@ -116,23 +145,27 @@
     half = slots // 2
     bf16 = jnp.bfloat16
     chip, core = lax.axis_index("chip"), lax.axis_index("core")
-    place = jnp.stack([chip, core]).astype(jnp.int32)
-
-    def share_of(index):
-        start = index * share
-        return jnp.concatenate(
-            [lax.dynamic_slice_in_dim(w[0], start, share, 0) for w in (w_gate, w_up)], 0
-        )
-
-    weights = [share_of(chip)]
-    for shift in range(1, chips):
-        piece = share_of(lax.rem(chip + shift, chips))
-        weights.append(lax.ppermute(piece, "chip", [(i, (i + shift) % chips) for i in range(chips)]))
+    quarter = 2 * ((chip ^ (chip >> 1)) & 1) + (chip >> 1)
+    place = jnp.stack(
+        [core, quarter >> 1, quarter & 1, 2 * chip + core, 2 * (chip ^ 1) + core]
+    ).astype(jnp.int32)
+
+    packed = call(
+        functools.partial(pack_body, share),
+        jax.ShapeDtypeStruct((4 * share, cols), bf16),
+        place,
+        w_gate[0],
+        w_up[0],
+        scalars=1,
+        space=ANY,
+        scratch=[pltpu.SemaphoreType.DMA((4,))],
+    )
+    pair = lax.ppermute(packed, "chip", PAIR)
 
     outgoing, target_t = call(
-        functools.partial(dispatch_body, cap, chips, cols),
+        functools.partial(dispatch_body, cap, cols),
         (
-            jax.ShapeDtypeStruct((slots, chips * cols // 128, 128), bf16),
+            jax.ShapeDtypeStruct((slots, 2 * cols // 128, 128), bf16),
             jax.ShapeDtypeStruct((top, tok_count), jnp.int32),
         ),
         place,
@@ -141,21 +174,27 @@
         scalars=1,
     )
     received = lax.all_to_all(outgoing, wide, split_axis=0, concat_axis=0, tiled=True)
-    theirs, mine = call(
-        functools.partial(gate_up_body, cols),
-        (
-            jax.ShapeDtypeStruct((half, 2 * share), bf16),
-            jax.ShapeDtypeStruct((half, 2 * share), jnp.float32),
-        ),
-        place,
-        received,
-        *weights,
-        scalars=1,
-    )
-    theirs = lax.ppermute(theirs, "core", [(0, 1), (1, 0)])
-    hidden = call(hidden_body, jax.ShapeDtypeStruct((half, share), bf16), mine, theirs)
+    sums = {}
+    for keep in (False, True):
+        theirs, mine = call(
+            functools.partial(gate_up_body, keep),
+            (
+                jax.ShapeDtypeStruct((half, 2 * share), bf16),
+                jax.ShapeDtypeStruct((half, 2 * share), jnp.float32),
+            ),
+            place,
+            received,
+            w_gate[0],
+            w_up[0],
+            pair,
+            scalars=1,
+        )
+        sums[keep] = (mine, lax.ppermute(theirs, "core", SWAP))
+    sent = call(add_body, jax.ShapeDtypeStruct((half, 2 * share), bf16), *sums[False])
+    far = lax.ppermute(sent, "chip", OPPOSITE)
+    hidden = call(hidden_body, jax.ShapeDtypeStruct((half, share), bf16), *sums[True], far)
     own = lax.all_gather(hidden, "chip", axis=0)
-    other = lax.ppermute(own, "core", [(0, 1), (1, 0)])
+    other = lax.ppermute(own, "core", SWAP)
     produced = call(
         down_body,
         jax.ShapeDtypeStruct((slots, cols // 128, 128), bf16),

time: 133 us -> 150 us (1.13)
  waiting for transfers between devices: 41.2 us -> 57 us
  starting transfers between devices: 34.3 us -> 30.3 us
  blocking collectives: 47.9 us -> 51.5 us
  Pallas kernels: 7.03 us -> 9.04 us
    ppermute x5, waiting for transfers between devices: 41.2 us -> 57 us  [the longest x1 31 us: on_device(): pair = lax.ppermute(packed, 'chip', PAIR)]
    ppermute x5, starting transfers between devices: 21.8 us -> 18 us  [the longest x1 6.08 us: on_device(): pair = lax.ppermute(packed, 'chip', PAIR)]
    all_to_all x1, blocking collectives: 24.1 us -> 26.8 us  [on_device(): lax.all_to_all(produced, wide, split_axis=0, concat_axis=0, tiled=True)]
    pallas_call x5 -> x8, Pallas kernels: 7.03 us -> 9.04 us  [call(): pl.pallas_call(body, out_shape=outs, in_specs=[SMEM] * scalars + [space]...]
  transfers between devices with their start and end apart: 6 -> 6, of which waited for: 4 -> 3; matrix products, arithmetic and copies ran while one was open for 0% -> 0% of each run, Pallas kernels for 0% -> 2%
where the time goes in v3:
time: 150 us
  waiting for transfers between devices  57 us (38%)
  blocking collectives  51.5 us (34%)
  starting transfers between devices  30.3 us (20%)
  Pallas kernels  9.04 us (6%)
  local copies, waits for them, and re-layouts  1.83 us (1%)
    ppermute x1, waiting for transfers between devices, on_device(): pair = lax.ppermute(packed, 'chip', PAIR)  31 us
    all_to_all x1, blocking collectives, on_device(): lax.all_to_all(produced, wide, split_axis=0, concat_axis=0, tiled=True)  26.8 us
    all_gather x1, blocking collectives, on_device(): own = lax.all_gather(hidden, 'chip', axis=0)  24.6 us
    ppermute x1, waiting for transfers between devices, on_device(): far = lax.ppermute(sent, 'chip', OPPOSITE)  23.3 us
    all_to_all x1, starting transfers between devices, on_device(): lax.all_to_all(outgoing, wide, split_axis=0, concat_axis=0, tiled=True)  12.4 us
    pallas_call x8, Pallas kernels, call(): pl.pallas_call(body, out_shape=outs, in_specs=[SMEM] * scalars + [space]...  9.04 us
    ppermute x1, starting transfers between devices, on_device(): pair = lax.ppermute(packed, 'chip', PAIR)  6.08 us
    ppermute x1, starting transfers between devices, on_device(): far = lax.ppermute(sent, 'chip', OPPOSITE)  5.64 us
  transfers between devices with their start and end apart: 6, of which 3 were waited for; matrix products, arithmetic and copies ran while one was open for 0% of the time, Pallas kernels for 2%

profile of v3, /device:TPU:8, one launch (start us, length us, event | category | flops | bytes accessed | tf_op | source)
XLA Modules:
  0.0 149.8 jit_solution(1111691304774690778)
XLA Ops:
  0.0 0.1 stack.23.place
  0.1 1.0 copy-done.3
  1.1 0.7 copy-done.4
  1.8 2.0 %shard_map.64 = (bf16[704,4,128]{2,1,0:T(4,128)(2,1)}, s32[6,64]{1,0:T(8,128)S(1)}) custom-call(s32[5]{0:T(128)S(1)} %stack.23.place, s32[6,64]{1,0:T(8,128)S(1)} %bitcast.20, bf16[64,2048]{1,0:T(8,128)(2,1)S(1)} %copy-done.3), custom_call_target="tpu_custom_call" | custom-call | tf_op jit(solution)/shard_map/pallas_call | solution.py:24
  3.8 12.4 %all-to-all-start = ((bf16[704,4,128]{2,1,0:T(4,128)(2,1)}), bf16[704,4,128]{2,1,0:T(4,128)(2,1)S(1)}, u32[]{:S(2)}, u32[]{:S(2)}) async-start(bf16[704,4,128]{2,1,0:T(4,128)(2,1)} %get-tuple-element.12), calls=%async_computation | async-start | bytes 1441792 | tf_op jit(solution)/shard_map/all_to_all | solution.py:176
  16.2 1.5 %shard_map.65 = bf16[1408,256]{1,0:T(8,128)(2,1)S(1)} custom-call(s32[5]{0:T(128)S(1)} %stack.23.place, bf16[1408,256]{1,0:T(8,128)(2,1)S(1)} %bitcast.11, bf16[1408,256]{1,0:T(8,128)(2,1)S(1)} %bitcast.14), custom_call_target="tpu_custom_call" | custom-call | tf_op jit(solution)/shard_map/pallas_call | solution.py:24
  17.7 6.1 %collective-permute-start = (bf16[1408,256]{1,0:T(8,128)(2,1)S(1)}, bf16[1408,256]{1,0:T(8,128)(2,1)S(1)}, u32[]{:S(2)}, u32[]{:S(2)}) collective-permute-start(bf16[1408,256]{1,0:T(8,128)(2,1)S(1)} %shard_map.65), channel_id=1, source_target_pairs={{0,2},{2,0},{4,6},{6,4},{1,3},{3,1},{5,7},{7,5},{8,10},{10,8},{12,... | collective-permute-start | bytes 2162696 | tf_op jit(solution)/shard_map/ppermute | solution.py:163
  23.8 31.0 %collective-permute-done.pair = bf16[1408,256]{1,0:T(8,128)(2,1)S(1)} collective-permute-done((bf16[1408,256]{1,0:T(8,128)(2,1)S(1)}, bf16[1408,256]{1,0:T(8,128)(2,1)S(1)}, u32[]{:S(2)}, u32[]{:S(2)}) %collective-permute-start) | collective-permute-done | bytes 720928 | tf_op jit(solution)/shard_map/ppermute | solution.py:163
  54.8 0.0 all-to-all-done.rows
  54.8 1.3 shard_map.67
  56.1 1.9 %collective-permute-start.2 = (bf16[352,704]{1,0:T(8,128)(2,1)S(1)}, bf16[352,704]{1,0:T(8,128)(2,1)S(1)}, u32[]{:S(2)}, u32[]{:S(2)}) collective-permute-start(bf16[352,704]{1,0:T(8,128)(2,1)S(1)} %get-tuple-element.16), channel_id=1, source_target_pairs={{0,1},{1,0},{2,3},{3,2},{4,5},{5,4},{6,7},{7,6},{8,9},{9,8},{10,11... | collective-permute-start | bytes 1486856 | tf_op jit(solution)/shard_map/ppermute | solution.py:192
  58.1 1.3 shard_map.66
  59.4 2.4 %collective-permute-start.1 = (bf16[352,704]{1,0:T(8,128)(2,1)S(1)}, bf16[352,704]{1,0:T(8,128)(2,1)S(1)}, u32[]{:S(2)}, u32[]{:S(2)}) collective-permute-start(bf16[352,704]{1,0:T(8,128)(2,1)S(1)} %get-tuple-element.14), channel_id=1, source_target_pairs={{0,1},{1,0},{2,3},{3,2},{4,5},{5,4},{6,7},{7,6},{8,9},{9,8},{10,11... | collective-permute-start | bytes 1486856 | tf_op jit(solution)/shard_map/ppermute | solution.py:192
  61.8 0.1 shard_map.68
  61.9 5.6 %collective-permute-start.3 = (bf16[352,704]{1,0:T(8,128)(2,1)S(1)}, bf16[352,704]{1,0:T(8,128)(2,1)S(1)}, u32[]{:S(2)}, u32[]{:S(2)}) collective-permute-start(bf16[352,704]{1,0:T(8,128)(2,1)S(1)} %shard_map.68), channel_id=1, source_target_pairs={{0,6},{6,0},{2,4},{4,2},{1,7},{7,1},{3,5},{5,3},{8,14},{14,8},{10,... | collective-permute-start | bytes 1486856 | tf_op jit(solution)/shard_map/ppermute | solution.py:194
  67.6 23.3 %collective-permute-done.3.far = bf16[352,704]{1,0:T(8,128)(2,1)S(1)} collective-permute-done((bf16[352,704]{1,0:T(8,128)(2,1)S(1)}, bf16[352,704]{1,0:T(8,128)(2,1)S(1)}, u32[]{:S(2)}, u32[]{:S(2)}) %collective-permute-start.3) | collective-permute-done | bytes 495648 | tf_op jit(solution)/shard_map/ppermute | solution.py:194
  90.8 0.3 shard_map.69
  91.2 0.0 copy-start.2
  91.2 24.6 %all-gather = bf16[1408,352]{1,0:T(8,128)(2,1)S(1)} all-gather(bf16[352,352]{1,0:T(8,128)(2,1)S(1)} %shard_map.69), channel_id=2, replica_groups=mesh['wide'=64,'chip'=4,'core'=2] {'chip'}, dimensions={0}, use_global_device_ids=true | all-gather | bytes 1239040 | tf_op jit(solution)/shard_map/all_gather | solution.py:196
  115.8 1.9 %collective-permute-start.4 = (bf16[4,352,352]{2,1,0:T(8,128)(2,1)S(1)}, bf16[4,352,352]{2,1,0:T(8,128)(2,1)S(1)}, u32[]{:S(2)}, u32[]{:S(2)}) collective-permute-start(bf16[4,352,352]{2,1,0:T(8,128)(2,1)S(1)} %bitcast.17), channel_id=1, source_target_pairs={{0,1},{1,0},{2,3},{3,2},{4,5},{5,4},{6,7},{7,6},{8,9},{9,8},{10,11... | collective-permute-start | bytes 2973704 | tf_op jit(solution)/shard_map/ppermute | solution.py:197
  117.7 2.7 %collective-permute-done.4.other = bf16[4,352,352]{2,1,0:T(8,128)(2,1)S(1)} collective-permute-done((bf16[4,352,352]{2,1,0:T(8,128)(2,1)S(1)}, bf16[4,352,352]{2,1,0:T(8,128)(2,1)S(1)}, u32[]{:S(2)}, u32[]{:S(2)}) %collective-permute-start.4) | collective-permute-done | bytes 991264 | tf_op jit(solution)/shard_map/ppermute | solution.py:197
  120.4 1.5 shard_map.70
  121.8 26.8 %all_to_all.10.returned = bf16[704,2,128]{2,1,0:T(2,128)(2,1)S(1)} all-to-all(bf16[704,2,128]{2,1,0:T(2,128)(2,1)S(1)} %shard_map.70), channel_id=1, replica_groups=mesh['wide'=64,'chip'=4,'core'=2] {'wide'}, dimensions={0} | all-to-all | bytes 720896 | tf_op jit(solution)/shard_map/all_to_all | solution.py:207
  148.7 1.1 shard_map.71
  (11 shorter events, 0.0 us)
Async XLA Ops:
  0.0 16.2 %copy-start = (bf16[1,1408,256]{2,1,0:T(8,128)(2,1)S(1)}, bf16[1,1408,256]{2,1,0:T(8,128)(2,1)}, u32[]{:S(2)}) copy-start(bf16[1,1408,256]{2,1,0:T(8,128)(2,1)} %param.9) | copy-start | bytes 2162692
  0.0 16.2 %copy-start.1 = (bf16[1,1408,256]{2,1,0:T(8,128)(2,1)S(1)}, bf16[1,1408,256]{2,1,0:T(8,128)(2,1)}, u32[]{:S(2)}) copy-start(bf16[1,1408,256]{2,1,0:T(8,128)(2,1)} %param.10) | copy-start | bytes 2162692
  0.1 1.0 copy-start.3
  1.1 0.7 copy-start.4
  3.8 51.0 %all-to-all-start = ((bf16[704,4,128]{2,1,0:T(4,128)(2,1)}), bf16[704,4,128]{2,1,0:T(4,128)(2,1)S(1)}, u32[]{:S(2)}, u32[]{:S(2)}) async-start(bf16[704,4,128]{2,1,0:T(4,128)(2,1)} %get-tuple-element.12), calls=%async_computation | async-start | bytes 1441792 | tf_op jit(solution)/shard_map/all_to_all | solution.py:176
  17.7 37.1 %collective-permute-start = (bf16[1408,256]{1,0:T(8,128)(2,1)S(1)}, bf16[1408,256]{1,0:T(8,128)(2,1)S(1)}, u32[]{:S(2)}, u32[]{:S(2)}) collective-permute-start(bf16[1408,256]{1,0:T(8,128)(2,1)S(1)} %shard_map.65), channel_id=1, source_target_pairs={{0,2},{2,0},{4,6},{6,4},{1,3},{3,1},{5,7},{7,5},{8,10},{10,8},{12,... | collective-permute-start | bytes 2162696 | tf_op jit(solution)/shard_map/ppermute | solution.py:163
  56.1 5.7 %collective-permute-start.2 = (bf16[352,704]{1,0:T(8,128)(2,1)S(1)}, bf16[352,704]{1,0:T(8,128)(2,1)S(1)}, u32[]{:S(2)}, u32[]{:S(2)}) collective-permute-start(bf16[352,704]{1,0:T(8,128)(2,1)S(1)} %get-tuple-element.16), channel_id=1, source_target_pairs={{0,1},{1,0},{2,3},{3,2},{4,5},{5,4},{6,7},{7,6},{8,9},{9,8},{10,11... | collective-permute-start | bytes 1486856 | tf_op jit(solution)/shard_map/ppermute | solution.py:192
  59.4 8.2 %collective-permute-start.1 = (bf16[352,704]{1,0:T(8,128)(2,1)S(1)}, bf16[352,704]{1,0:T(8,128)(2,1)S(1)}, u32[]{:S(2)}, u32[]{:S(2)}) collective-permute-start(bf16[352,704]{1,0:T(8,128)(2,1)S(1)} %get-tuple-element.14), channel_id=1, source_target_pairs={{0,1},{1,0},{2,3},{3,2},{4,5},{5,4},{6,7},{7,6},{8,9},{9,8},{10,11... | collective-permute-start | bytes 1486856 | tf_op jit(solution)/shard_map/ppermute | solution.py:192
  61.9 28.9 %collective-permute-start.3 = (bf16[352,704]{1,0:T(8,128)(2,1)S(1)}, bf16[352,704]{1,0:T(8,128)(2,1)S(1)}, u32[]{:S(2)}, u32[]{:S(2)}) collective-permute-start(bf16[352,704]{1,0:T(8,128)(2,1)S(1)} %shard_map.68), channel_id=1, source_target_pairs={{0,6},{6,0},{2,4},{4,2},{1,7},{7,1},{3,5},{5,3},{8,14},{14,8},{10,... | collective-permute-start | bytes 1486856 | tf_op jit(solution)/shard_map/ppermute | solution.py:194
  91.2 29.2 %copy-start.2 = (bf16[1,1408,256]{2,1,0:T(8,128)(2,1)S(1)}, bf16[1,1408,256]{2,1,0:T(8,128)(2,1)}, u32[]{:S(2)}) copy-start(bf16[1,1408,256]{2,1,0:T(8,128)(2,1)} %param.11) | copy-start | bytes 2162692
  115.8 4.6 %collective-permute-start.4 = (bf16[4,352,352]{2,1,0:T(8,128)(2,1)S(1)}, bf16[4,352,352]{2,1,0:T(8,128)(2,1)S(1)}, u32[]{:S(2)}, u32[]{:S(2)}) collective-permute-start(bf16[4,352,352]{2,1,0:T(8,128)(2,1)S(1)} %bitcast.17), channel_id=1, source_target_pairs={{0,1},{1,0},{2,3},{3,2},{4,5},{5,4},{6,7},{7,6},{8,9},{9,8},{10,11... | collective-permute-start | bytes 2973704 | tf_op jit(solution)/shard_map/ppermute | solution.py:197
  120.4 28.3 %copy-start.5 = (f32[64,6]{0,1:T(8,128)S(1)}, f32[64,6]{0,1:T(8,128)}, u32[]{:S(2)}) copy-start(f32[64,6]{0,1:T(8,128)} %param.8) | copy-start | bytes 4612

commit v4 on v2

v4 whole, which is shorter than its diff:
```python
import functools

import jax
import jax.numpy as jnp
from jax import lax
from jax.experimental import pallas as pl
from jax.experimental.pallas import tpu as pltpu
from jax.sharding import Mesh
from jax.sharding import PartitionSpec as P

VMEM = pl.BlockSpec(memory_space=pltpu.VMEM)
SMEM = pl.BlockSpec(memory_space=pltpu.SMEM)
CHIPS = 4
RELAY = 30_000_000_000
CORE, CHIP, SIDE = range(3)
NT = (((1,), (1,)), ((), ()))
TN = (((0,), (0,)), ((), ()))


def call(body, outs, *operands, scalars=0, flops=None):
    cost = None if flops is None else pl.CostEstimate(flops=flops, transcendentals=0, bytes_accessed=0)
    return pl.pallas_call(
        body,
        out_shape=outs,
        in_specs=[SMEM] * scalars + [VMEM] * (len(operands) - scalars),
        out_specs=jax.tree.map(lambda _: VMEM, outs),
        compiler_params=pltpu.CompilerParams(vmem_limit_bytes=16 << 20),
        cost_estimate=cost,
    )(*operands)


def block_body(place, routes_t, tokens, out):
    rows = tokens.shape[0]
    cols = out.shape[1] // CHIPS
    out[rows:, :] = jnp.zeros((out.shape[0] - rows, out.shape[1]), out.dtype)
    for shift in range(CHIPS):
        block = lax.rem(place[CHIP] - shift + CHIPS, CHIPS) * 2 + place[CORE]
        columns = tokens[:, pl.ds(pl.multiple_of(block * cols, cols), cols)]
        out[:rows, shift * cols : (shift + 1) * cols] = columns
    out[rows : rows + routes_t.shape[0], : routes_t.shape[1]] = routes_t[...].astype(out.dtype)


def dispatch_body(top, cap, experts, place, mine, neighbour, outgoing, target_t):
    rows = target_t.shape[1]
    side = outgoing.shape[0]
    slots = side * cap
    expert_ids = lax.broadcasted_iota(jnp.int32, (experts, rows), 0)
    slot_ids = lax.broadcasted_iota(jnp.int32, (slots, rows), 0)
    earlier = (
        lax.broadcasted_iota(jnp.int32, (rows, rows), 0) < lax.broadcasted_iota(jnp.int32, (rows, rows), 1)
    ).astype(jnp.bfloat16)
    for block, which in ((mine, place[SIDE]), (neighbour, 1 - place[SIDE])):
        routes_t = block[rows : rows + 16, :rows].astype(jnp.float32).astype(jnp.int32)
        chosen = [(routes_t[k : k + 1, :] == expert_ids).astype(jnp.float32) for k in range(top)]
        named = functools.reduce(jnp.add, chosen)
        before = jnp.dot(named.astype(jnp.bfloat16), earlier, preferred_element_type=jnp.float32)
        picker = jnp.zeros((slots, rows), jnp.float32)
        for k in range(top):
            slot = jnp.sum(chosen[k] * before, axis=0, keepdims=True).astype(jnp.int32)
            target = routes_t[k : k + 1, :] * cap + slot
            if block is mine:
                target_t[k : k + 1, :] = target
            picker += (slot_ids == target - place[SIDE] * slots).astype(jnp.float32)
        picked = jnp.dot(picker.astype(jnp.bfloat16), block[:rows, :], preferred_element_type=jnp.float32)
        outgoing[:, which] = picked.astype(jnp.bfloat16).reshape(side, cap, *outgoing.shape[3:])


def pack_body(place, w_gate, w_up, ahead, behind):
    share = ahead.shape[0] // 3
    chips = w_gate.shape[0] // share

    def units(w, shift):
        start = lax.rem(place[CHIP] + shift, chips) * share
        return w[pl.ds(pl.multiple_of(start, 16), share), :]

    for out, near, far in ((ahead, 1, w_gate), (behind, chips - 1, w_up)):
        out[:share, :] = units(w_gate, near)
        out[share : 2 * share, :] = units(w_up, near)
        out[2 * share :, :] = units(far, 2)


def relay_body(before, after, gate, up):
    share = gate.shape[0]
    gate[...] = before[2 * share :, :]
    up[...] = after[2 * share :, :]


def gather_body(place, w_gate, w_up, before, after, far_gate, far_up, weights):
    share, cols = far_gate.shape
    here = pl.ds(pl.multiple_of(place[CHIP] * share, 16), share)
    weights[:share, :cols] = w_gate[here, :]
    weights[share:, :cols] = w_up[here, :]
    weights[:, cols : 2 * cols] = before[: 2 * share, :]
    weights[:share, 2 * cols : 3 * cols] = far_gate[...]
    weights[share:, 2 * cols : 3 * cols] = far_up[...]
    weights[:, 3 * cols :] = after[: 2 * share, :]


def gate_up_body(place, rows, weights, theirs, mine):
    half = mine.shape[0]
    flat = rows[...].reshape(2 * half, weights.shape[1])
    total = lax.dot_general(flat, weights[...], NT, preferred_element_type=jnp.float32)
    first = place[CORE] == 0
    theirs[...] = jnp.where(first, total[half:], total[:half]).astype(jnp.bfloat16)
    mine[...] = jnp.where(first, total[:half], total[half:])


def hidden_body(mine, theirs, hidden):
    units = hidden.shape[1]
    total = mine[...] + theirs[...].astype(jnp.float32)
    gate, up = total[:, :units], total[:, units:]
    hidden[...] = (gate / (1 + jnp.exp(-gate)) * up).astype(jnp.bfloat16)


def down_body(place, own, other, w_down, out):
    chips, half, units = own.shape
    blocks, cap = out.shape[:2]
    for source, which in ((own, place[CORE]), (other, 1 - place[CORE])):
        total = functools.reduce(
            jnp.add,
            [
                jnp.dot(
                    source[z], w_down[z * units : (z + 1) * units, :], preferred_element_type=jnp.float32
                )
                for z in range(chips)
            ],
        )
        total = total.astype(jnp.bfloat16).reshape(blocks // 4, 2, cap, *out.shape[2:])
        for side in range(2):
            out[pl.ds(side * (blocks // 2) + which * (blocks // 4), blocks // 4)] = total[:, side]


def combine_body(target_t, weight_t, returned, out):
    top, rows = target_t.shape
    slots = returned.shape[0] * returned.shape[1]
    slot_ids = lax.broadcasted_iota(jnp.int32, (slots, rows), 0)
    spread = jnp.zeros((slots, rows), jnp.float32)
    for k in range(top):
        spread += jnp.where(slot_ids == target_t[k : k + 1, :], weight_t[k : k + 1, :], 0.0)
    high = spread.astype(jnp.bfloat16)
    low = (spread - high.astype(jnp.float32)).astype(jnp.bfloat16)
    flat = returned[...].reshape(slots, out.shape[1])
    total = lax.dot_general(high, flat, TN, preferred_element_type=jnp.float32)
    total += lax.dot_general(low, flat, TN, preferred_element_type=jnp.float32)
    out[...] = total.astype(jnp.bfloat16)


def on_device(tokens, routes, route_weight, w_gate, w_up, w_down):
    tok_count, top = routes.shape
    _, units, cols = w_gate.shape
    side = lax.axis_size("plane")
    experts = 2 * side
    cap = max(2, (11 * tok_count + experts - 1) // experts)
    slots = experts * cap
    share = units // CHIPS
    half = slots // 2
    bf16 = jnp.bfloat16
    forward = [(i, (i + 1) % CHIPS) for i in range(CHIPS)]
    backward = [(i, (i - 1) % CHIPS) for i in range(CHIPS)]
    swap = [(0, 1), (1, 0)]
    place = jnp.stack([lax.axis_index(a) for a in ("core", "chip", "side")]).astype(jnp.int32)

    mine = call(
        block_body,
        jax.ShapeDtypeStruct((tok_count + 16, CHIPS * cols), bf16),
        place,
        routes.T,
        tokens,
        scalars=1,
    )
    neighbour = lax.ppermute(mine, "side", swap)
    part = jax.ShapeDtypeStruct((share, cols), bf16)
    parts = jax.ShapeDtypeStruct((3 * share, cols), bf16)
    ahead, behind = call(pack_body, (parts, parts), place, w_gate[0], w_up[0], scalars=1)
    before = lax.ppermute(ahead, "chip", forward)
    after = lax.ppermute(behind, "chip", backward)
    far_gate, far_up = call(relay_body, (part, part), before, after, flops=RELAY)
    far_gate = lax.ppermute(far_gate, "chip", forward)
    far_up = lax.ppermute(far_up, "chip", backward)
    weights = call(
        gather_body,
        jax.ShapeDtypeStruct((2 * share, CHIPS * cols), bf16),
        place,
        w_gate[0],
        w_up[0],
        before,
        after,
        far_gate,
        far_up,
        scalars=1,
    )
    outgoing, target_t = call(
        functools.partial(dispatch_body, top, cap, experts),
        (
            jax.ShapeDtypeStruct((side, 2, cap, CHIPS * cols // 128, 128), bf16),
            jax.ShapeDtypeStruct((top, tok_count), jnp.int32),
        ),
        place,
        mine,
        neighbour,
        scalars=1,
    )
    received = lax.all_to_all(outgoing, "plane", split_axis=0, concat_axis=0, tiled=True)
    theirs, mine = call(
        gate_up_body,
        (
            jax.ShapeDtypeStruct((half, 2 * share), bf16),
            jax.ShapeDtypeStruct((half, 2 * share), jnp.float32),
        ),
        place,
        received,
        weights,
        scalars=1,
    )
    theirs = lax.ppermute(theirs, "core", swap)
    hidden = call(hidden_body, jax.ShapeDtypeStruct((half, share), bf16), mine, theirs)
    own = lax.all_gather(hidden, "chip", axis=0)
    other = lax.ppermute(own, "core", swap)
    produced = call(
        down_body,
        jax.ShapeDtypeStruct((experts, cap, cols // 128, 128), bf16),
        place,
        own,
        other,
        w_down[0],
        scalars=1,
    )
    returned = lax.all_to_all(produced, ("side", "plane"), split_axis=0, concat_axis=0, tiled=True)
    return call(
        combine_body,
        jax.ShapeDtypeStruct((tok_count, cols), bf16),
        target_t,
        route_weight.T,
        returned,
    )


def solution(mesh):
    fine = Mesh(
        mesh.devices.reshape(2, mesh.shape["wide"] // 2, CHIPS, 2), ("side", "plane", "chip", "core")
    )
    wide, narrow = ("side", "plane"), ("chip", "core")
    return jax.shard_map(
        on_device,
        mesh=fine,
        in_specs=(
            P(wide, None),
            P(wide, None),
            P(wide, None),
            P(wide, None, narrow),
            P(wide, None, narrow),
            P(wide, None, narrow),
        ),
        out_specs=P(wide, narrow),
        check_vma=False,
    )
```

time: 139 us -> 154 us (1.11)
  starting transfers between devices: 63.8 us -> 38.2 us
  blocking collectives: 24.2 us -> 47.1 us
  waiting for transfers between devices: 36.5 us -> 52.6 us
  Pallas kernels: 9.28 us -> 11.8 us
    all_gather x0 -> x1, blocking collectives: none -> 25 us  [on_device(): own = lax.all_gather(hidden, 'chip', axis=0)]
    ppermute x9 -> x2, starting transfers between devices: 25.2 us -> 5.29 us  [the longest x1 3.38 us: on_device(): neighbour = lax.ppermute(mine, 'side', swap)]
    ppermute x9 -> x2, waiting for transfers between devices: 12.9 us -> 26.4 us  [the longest x1 23.7 us: on_device(): neighbour = lax.ppermute(mine, 'side', swap)]
    all_to_all x1, waiting for transfers between devices: 5.03 us -> 16.7 us  [on_device(): lax.all_to_all(outgoing, 'plane', split_axis=0, concat_axis=0, tiled=True)]
    ppermute x1, waiting for transfers between devices: 8.82 us -> 0.01 us  [on_device(): after = lax.ppermute(behind, 'chip', backward)]
    ppermute x1, starting transfers between devices: 9.35 us -> 3.37 us  [on_device(): far_gate = lax.ppermute(far_gate, 'chip', forward)]
    pallas_call x8 -> x9, Pallas kernels: 9.28 us -> 11.8 us  [call(): pl.pallas_call(body, out_shape=outs, in_specs=[SMEM] * scalars + [VMEM] *...]
    all_to_all x1, blocking collectives: 24.2 us -> 22 us  [on_device(): lax.all_to_all(produced, ('side', 'plane'), split_axis=0, concat_axis=0,...]
  transfers between devices with their start and end apart: 15 -> 8, of which waited for: 8 -> 6; matrix products, arithmetic and copies ran while one was open for 0% -> 0% of each run, Pallas kernels for 2% -> 3%
where the time goes in v4:
time: 154 us
  waiting for transfers between devices  52.6 us (34%)
  blocking collectives  47.1 us (31%)
  starting transfers between devices  38.2 us (25%)
  Pallas kernels  11.8 us (8%)
  local copies, waits for them, and re-layouts  4.07 us (3%)
    all_gather x1, blocking collectives, on_device(): own = lax.all_gather(hidden, 'chip', axis=0)  25 us
    ppermute x1, waiting for transfers between devices, on_device(): neighbour = lax.ppermute(mine, 'side', swap)  23.7 us
    all_to_all x1, blocking collectives, on_device(): lax.all_to_all(produced, ('side', 'plane'), split_axis=0, concat_axis=0,...  22 us
    all_to_all x1, waiting for transfers between devices, on_device(): lax.all_to_all(outgoing, 'plane', split_axis=0, concat_axis=0, tiled=True)  16.7 us
    pallas_call x9, Pallas kernels, call(): pl.pallas_call(body, out_shape=outs, in_specs=[SMEM] * scalars + [VMEM] *...  11.8 us
    all_to_all x1, starting transfers between devices, on_device(): lax.all_to_all(outgoing, 'plane', split_axis=0, concat_axis=0, tiled=True)  10.2 us
    ppermute x1, starting transfers between devices, on_device(): after = lax.ppermute(behind, 'chip', backward)  6.77 us
    ppermute x1, starting transfers between devices, on_device(): before = lax.ppermute(ahead, 'chip', forward)  6.08 us
  transfers between devices with their start and end apart: 8, of which 6 were waited for; matrix products, arithmetic and copies ran while one was open for 0% of the time, Pallas kernels for 3%

profile of v4, /device:TPU:8, one launch (start us, length us, event | category | flops | bytes accessed | tf_op | source)
XLA Modules:
  0.0 153.9 jit_solution(11216380547386590845)
XLA Ops:
  0.1 1.1 copy-done
  1.2 1.1 copy-done.2
  2.3 1.4 shard_map.66
  3.7 6.1 %collective-permute-start.1 = (bf16[1056,256]{1,0:T(8,128)(2,1)}, bf16[1056,256]{1,0:T(8,128)(2,1)S(1)}, u32[]{:S(2)}, u32[]{:S(2)}) collective-permute-start(bf16[1056,256]{1,0:T(8,128)(2,1)} %get-tuple-element.15), channel_id=1, source_target_pairs={{0,2},{2,4},{4,6},{6,0},{1,3},{3,5},{5,7},{7,1},{8,10},{10,12},{12... | collective-permute-start | bytes 1622024 | tf_op jit(solution)/shard_map/ppermute | solution.py:175
  9.8 6.8 %collective-permute-start.2 = (bf16[1056,256]{1,0:T(8,128)(2,1)S(1)}, bf16[1056,256]{1,0:T(8,128)(2,1)S(1)}, u32[]{:S(2)}, u32[]{:S(2)}) collective-permute-start(bf16[1056,256]{1,0:T(8,128)(2,1)S(1)} %get-tuple-element.16), channel_id=1, source_target_pairs={{0,6},{2,0},{4,2},{6,4},{1,7},{3,1},{5,3},{7,5},{8,14},{10,8},{12,... | collective-permute-start | bytes 1622024 | tf_op jit(solution)/shard_map/ppermute | solution.py:176
  17.2 3.4 %collective-permute-start = (bf16[80,1024]{1,0:T(8,128)(2,1)S(1)}, bf16[80,1024]{1,0:T(8,128)(2,1)S(1)}, u32[]{:S(2)}, u32[]{:S(2)}) collective-permute-start(bf16[80,1024]{1,0:T(8,128)(2,1)S(1)} %shard_map.64.mine), channel_id=1, source_target_pairs={{0,256},{256,0},{1,257},{257,1},{2,258},{258,2},{3,259},{259,3},{4... | collective-permute-start | bytes 491528 | tf_op jit(solution)/shard_map/ppermute | solution.py:171
  20.6 23.7 %collective-permute-done.neighbour = bf16[80,1024]{1,0:T(8,128)(2,1)S(1)} collective-permute-done((bf16[80,1024]{1,0:T(8,128)(2,1)S(1)}, bf16[80,1024]{1,0:T(8,128)(2,1)S(1)}, u32[]{:S(2)}, u32[]{:S(2)}) %collective-permute-start) | collective-permute-done | bytes 163872 | tf_op jit(solution)/shard_map/ppermute | solution.py:171
  44.3 3.4 %shard_map.65 = (bf16[32,2,11,8,128]{4,3,2,1,0:T(8,128)(2,1)}, s32[6,64]{1,0:T(8,128)S(1)}) custom-call(s32[3]{0:T(128)S(1)} %pad_add_fusion.place, bf16[80,1024]{1,0:T(8,128)(2,1)S(1)} %shard_map.64.mine, bf16[80,1024]{1,0:T(8,128)(2,1)S(1)} %collective-permute-done.neighbour), custom_call_target="tpu_custom_call" | custom-call | tf_op jit(solution)/shard_map/pallas_call | solution.py:22
  47.7 10.2 %all-to-all-start = ((bf16[32,2,11,8,128]{4,3,2,1,0:T(8,128)(2,1)}), bf16[32,2,11,8,128]{4,3,2,1,0:T(8,128)(2,1)S(1)}, u32[]{:S(2)}, u32[]{:S(2)}) async-start(bf16[32,2,11,8,128]{4,3,2,1,0:T(8,128)(2,1)} %get-tuple-element.14), calls=%async_computation | async-start | bytes 2883584 | tf_op jit(solution)/shard_map/all_to_all | solution.py:203
  58.8 3.4 %collective-permute-start.3 = (bf16[352,256]{1,0:T(8,128)(2,1)S(1)}, bf16[352,256]{1,0:T(8,128)(2,1)S(1)}, u32[]{:S(2)}, u32[]{:S(2)}) collective-permute-start(bf16[352,256]{1,0:T(8,128)(2,1)S(1)} %get-tuple-element.17), channel_id=1, source_target_pairs={{0,2},{2,4},{4,6},{6,0},{1,3},{3,5},{5,7},{7,1},{8,10},{10,12},{12... | collective-permute-start | bytes 540680 | tf_op jit(solution)/shard_map/ppermute | solution.py:178
  62.1 4.6 %collective-permute-start.4 = (bf16[352,256]{1,0:T(8,128)(2,1)S(1)}, bf16[352,256]{1,0:T(8,128)(2,1)S(1)}, u32[]{:S(2)}, u32[]{:S(2)}) collective-permute-start(bf16[352,256]{1,0:T(8,128)(2,1)S(1)} %get-tuple-element.18), channel_id=1, source_target_pairs={{0,6},{2,0},{4,2},{6,4},{1,7},{3,1},{5,3},{7,5},{8,14},{10,8},{12,... | collective-permute-start | bytes 540680 | tf_op jit(solution)/shard_map/ppermute | solution.py:179
  66.7 5.4 %collective-permute-done.3.far_gate = bf16[352,256]{1,0:T(8,128)(2,1)S(1)} collective-permute-done((bf16[352,256]{1,0:T(8,128)(2,1)S(1)}, bf16[352,256]{1,0:T(8,128)(2,1)S(1)}, u32[]{:S(2)}, u32[]{:S(2)}) %collective-permute-start.3) | collective-permute-done | bytes 180256 | tf_op jit(solution)/shard_map/ppermute | solution.py:178
  72.1 2.3 %collective-permute-done.4.far_up = bf16[352,256]{1,0:T(8,128)(2,1)S(1)} collective-permute-done((bf16[352,256]{1,0:T(8,128)(2,1)S(1)}, bf16[352,256]{1,0:T(8,128)(2,1)S(1)}, u32[]{:S(2)}, u32[]{:S(2)}) %collective-permute-start.4) | collective-permute-done | bytes 180256 | tf_op jit(solution)/shard_map/ppermute | solution.py:179
  74.3 1.0 copy-done.6
  76.1 16.7 %all-to-all-done.rows = bf16[32,2,11,8,128]{4,3,2,1,0:T(8,128)(2,1)S(1)} async-done(((bf16[32,2,11,8,128]{4,3,2,1,0:T(8,128)(2,1)}), bf16[32,2,11,8,128]{4,3,2,1,0:T(8,128)(2,1)S(1)}, u32[]{:S(2)}, u32[]{:S(2)}) %all-to-all-start) | async-done | bytes 1441824 | tf_op jit(solution)/shard_map/all_to_all | solution.py:203
  92.8 2.3 %shard_map.69 = (bf16[352,704]{1,0:T(8,128)(2,1)S(1)}, f32[352,704]{1,0:T(8,128)S(1)}) custom-call(s32[3]{0:T(128)S(1)} %pad_add_fusion.place, bf16[32,2,11,8,128]{4,3,2,1,0:T(8,128)(2,1)S(1)} %all-to-all-done.rows, bf16[704,1024]{1,0:T(8,128)(2,1)S(1)} %shard_map.68.weights), custom_call_target="tpu_custom_call" | custom-call | tf_op jit(solution)/shard_map/pallas_call | solution.py:22
  95.1 1.9 %collective-permute-start.5 = (bf16[352,704]{1,0:T(8,128)(2,1)S(1)}, bf16[352,704]{1,0:T(8,128)(2,1)S(1)}, u32[]{:S(2)}, u32[]{:S(2)}) collective-permute-start(bf16[352,704]{1,0:T(8,128)(2,1)S(1)} %get-tuple-element.20), channel_id=1, source_target_pairs={{0,1},{1,0},{2,3},{3,2},{4,5},{5,4},{6,7},{7,6},{8,9},{9,8},{10,11... | collective-permute-start | bytes 1486856 | tf_op jit(solution)/shard_map/ppermute | solution.py:215
  97.0 1.9 %collective-permute-done.5.theirs = bf16[352,704]{1,0:T(8,128)(2,1)S(1)} collective-permute-done((bf16[352,704]{1,0:T(8,128)(2,1)S(1)}, bf16[352,704]{1,0:T(8,128)(2,1)S(1)}, u32[]{:S(2)}, u32[]{:S(2)}) %collective-permute-start.5) | collective-permute-done | bytes 495648 | tf_op jit(solution)/shard_map/ppermute | solution.py:215
  99.2 25.0 %all-gather = bf16[1408,352]{1,0:T(8,128)(2,1)S(1)} all-gather(bf16[352,352]{1,0:T(8,128)(2,1)S(1)} %shard_map.70), channel_id=2, replica_groups=mesh['side'=2,'plane'=32,'chip'=4,'core'=2] {'chip'}, dimensions={0}, use_global_device_ids=true | all-gather | bytes 1239040 | tf_op jit(solution)/shard_map/all_gather | solution.py:217
  124.3 1.9 %collective-permute-start.6 = (bf16[4,352,352]{2,1,0:T(8,128)(2,1)S(1)}, bf16[4,352,352]{2,1,0:T(8,128)(2,1)S(1)}, u32[]{:S(2)}, u32[]{:S(2)}) collective-permute-start(bf16[4,352,352]{2,1,0:T(8,128)(2,1)S(1)} %bitcast.9), channel_id=1, source_target_pairs={{0,1},{1,0},{2,3},{3,2},{4,5},{5,4},{6,7},{7,6},{8,9},{9,8},{10,11... | collective-permute-start | bytes 2973704 | tf_op jit(solution)/shard_map/ppermute | solution.py:218
  126.2 2.7 %collective-permute-done.6.other = bf16[4,352,352]{2,1,0:T(8,128)(2,1)S(1)} collective-permute-done((bf16[4,352,352]{2,1,0:T(8,128)(2,1)S(1)}, bf16[4,352,352]{2,1,0:T(8,128)(2,1)S(1)}, u32[]{:S(2)}, u32[]{:S(2)}) %collective-permute-start.6) | collective-permute-done | bytes 991264 | tf_op jit(solution)/shard_map/ppermute | solution.py:218
  128.9 1.7 %shard_map.71 = bf16[64,11,2,128]{3,2,1,0:T(2,128)(2,1)S(1)} custom-call(s32[3]{0:T(128)S(1)} %pad_add_fusion.place, bf16[4,352,352]{2,1,0:T(8,128)(2,1)S(1)} %bitcast.10, bf16[4,352,352]{2,1,0:T(8,128)(2,1)S(1)} %collective-permute-done.6.other, bf16[1408,256]{1,0:T(8,128)(2,1)S(1)} %bitcast.15), custom_call_target="tpu_custom_call" | custom-call | tf_op jit(solution)/shard_map/pallas_call | solution.py:22
  130.6 22.0 %all_to_all.10.returned = bf16[64,11,2,128]{3,2,1,0:T(2,128)(2,1)S(1)} all-to-all(bf16[64,11,2,128]{3,2,1,0:T(2,128)(2,1)S(1)} %shard_map.71), channel_id=1, replica_groups=mesh['side'=2,'plane'=32,'chip'=4,'core'=2] {'side','plane'}, dimensions={0} | all-to-all | bytes 720896 | tf_op jit(solution)/shard_map/all_to_all | solution.py:228
  152.6 1.3 shard_map.72
  (24 shorter events, 2.5 us)
Async XLA Ops:
  0.0 16.6 %copy-start.8 = (s32[64,6]{0,1:T(8,128)S(1)}, s32[64,6]{0,1:T(8,128)}, u32[]{:S(2)}) copy-start(s32[64,6]{0,1:T(8,128)} %param.7) | copy-start | bytes 4612
  0.1 1.1 copy-start
  1.2 1.1 copy-start.2
  2.3 14.3 %copy-start.7 = (bf16[64,2048]{1,0:T(8,128)(2,1)S(1)}, bf16[64,2048]{1,0:T(8,128)(2,1)}, u32[]{:S(2)}) copy-start(bf16[64,2048]{1,0:T(8,128)(2,1)} %tokens.1) | copy-start | bytes 786436
  3.7 54.2 %collective-permute-start.1 = (bf16[1056,256]{1,0:T(8,128)(2,1)}, bf16[1056,256]{1,0:T(8,128)(2,1)S(1)}, u32[]{:S(2)}, u32[]{:S(2)}) collective-permute-start(bf16[1056,256]{1,0:T(8,128)(2,1)} %get-tuple-element.15), channel_id=1, source_target_pairs={{0,2},{2,4},{4,6},{6,0},{1,3},{3,5},{5,7},{7,1},{8,10},{10,12},{12... | collective-permute-start | bytes 1622024 | tf_op jit(solution)/shard_map/ppermute | solution.py:175
  9.8 48.1 %collective-permute-start.2 = (bf16[1056,256]{1,0:T(8,128)(2,1)S(1)}, bf16[1056,256]{1,0:T(8,128)(2,1)S(1)}, u32[]{:S(2)}, u32[]{:S(2)}) collective-permute-start(bf16[1056,256]{1,0:T(8,128)(2,1)S(1)} %get-tuple-element.16), channel_id=1, source_target_pairs={{0,6},{2,0},{4,2},{6,4},{1,7},{3,1},{5,3},{7,5},{8,14},{10,8},{12,... | collective-permute-start | bytes 1622024 | tf_op jit(solution)/shard_map/ppermute | solution.py:176
  17.2 27.1 %collective-permute-start = (bf16[80,1024]{1,0:T(8,128)(2,1)S(1)}, bf16[80,1024]{1,0:T(8,128)(2,1)S(1)}, u32[]{:S(2)}, u32[]{:S(2)}) collective-permute-start(bf16[80,1024]{1,0:T(8,128)(2,1)S(1)} %shard_map.64.mine), channel_id=1, source_target_pairs={{0,256},{256,0},{1,257},{257,1},{2,258},{258,2},{3,259},{259,3},{4... | collective-permute-start | bytes 491528 | tf_op jit(solution)/shard_map/ppermute | solution.py:171
  47.7 45.1 %all-to-all-start = ((bf16[32,2,11,8,128]{4,3,2,1,0:T(8,128)(2,1)}), bf16[32,2,11,8,128]{4,3,2,1,0:T(8,128)(2,1)S(1)}, u32[]{:S(2)}, u32[]{:S(2)}) async-start(bf16[32,2,11,8,128]{4,3,2,1,0:T(8,128)(2,1)} %get-tuple-element.14), calls=%async_computation | async-start | bytes 2883584 | tf_op jit(solution)/shard_map/all_to_all | solution.py:203
  57.9 16.4 %copy-start.1 = (bf16[1,1408,256]{2,1,0:T(8,128)(2,1)S(1)}, bf16[1,1408,256]{2,1,0:T(8,128)(2,1)}, u32[]{:S(2)}) copy-start(bf16[1,1408,256]{2,1,0:T(8,128)(2,1)} %param.9) | copy-start | bytes 2162692
  57.9 16.4 %copy-start.3 = (bf16[1,1408,256]{2,1,0:T(8,128)(2,1)S(1)}, bf16[1,1408,256]{2,1,0:T(8,128)(2,1)}, u32[]{:S(2)}) copy-start(bf16[1,1408,256]{2,1,0:T(8,128)(2,1)} %param.10) | copy-start | bytes 2162692
  58.0 0.8 copy-start.5
  58.8 13.3 %collective-permute-start.3 = (bf16[352,256]{1,0:T(8,128)(2,1)S(1)}, bf16[352,256]{1,0:T(8,128)(2,1)S(1)}, u32[]{:S(2)}, u32[]{:S(2)}) collective-permute-start(bf16[352,256]{1,0:T(8,128)(2,1)S(1)} %get-tuple-element.17), channel_id=1, source_target_pairs={{0,2},{2,4},{4,6},{6,0},{1,3},{3,5},{5,7},{7,1},{8,10},{10,12},{12... | collective-permute-start | bytes 540680 | tf_op jit(solution)/shard_map/ppermute | solution.py:178
  62.1 12.2 %collective-permute-start.4 = (bf16[352,256]{1,0:T(8,128)(2,1)S(1)}, bf16[352,256]{1,0:T(8,128)(2,1)S(1)}, u32[]{:S(2)}, u32[]{:S(2)}) collective-permute-start(bf16[352,256]{1,0:T(8,128)(2,1)S(1)} %get-tuple-element.18), channel_id=1, source_target_pairs={{0,6},{2,0},{4,2},{6,4},{1,7},{3,1},{5,3},{7,5},{8,14},{10,8},{12,... | collective-permute-start | bytes 540680 | tf_op jit(solution)/shard_map/ppermute | solution.py:179
  74.3 1.0 copy-start.6
  95.1 3.8 %collective-permute-start.5 = (bf16[352,704]{1,0:T(8,128)(2,1)S(1)}, bf16[352,704]{1,0:T(8,128)(2,1)S(1)}, u32[]{:S(2)}, u32[]{:S(2)}) collective-permute-start(bf16[352,704]{1,0:T(8,128)(2,1)S(1)} %get-tuple-element.20), channel_id=1, source_target_pairs={{0,1},{1,0},{2,3},{3,2},{4,5},{5,4},{6,7},{7,6},{8,9},{9,8},{10,11... | collective-permute-start | bytes 1486856 | tf_op jit(solution)/shard_map/ppermute | solution.py:215
  98.9 29.9 %copy-start.4 = (bf16[1,1408,256]{2,1,0:T(8,128)(2,1)S(1)}, bf16[1,1408,256]{2,1,0:T(8,128)(2,1)}, u32[]{:S(2)}) copy-start(bf16[1,1408,256]{2,1,0:T(8,128)(2,1)} %param.11) | copy-start | bytes 2162692
  124.3 4.6 %collective-permute-start.6 = (bf16[4,352,352]{2,1,0:T(8,128)(2,1)S(1)}, bf16[4,352,352]{2,1,0:T(8,128)(2,1)S(1)}, u32[]{:S(2)}, u32[]{:S(2)}) collective-permute-start(bf16[4,352,352]{2,1,0:T(8,128)(2,1)S(1)} %bitcast.9), channel_id=1, source_target_pairs={{0,1},{1,0},{2,3},{3,2},{4,5},{5,4},{6,7},{7,6},{8,9},{9,8},{10,11... | collective-permute-start | bytes 2973704 | tf_op jit(solution)/shard_map/ppermute | solution.py:218
  128.8 23.8 %copy-start.9 = (f32[64,6]{0,1:T(8,128)S(1)}, f32[64,6]{0,1:T(8,128)}, u32[]{:S(2)}) copy-start(f32[64,6]{0,1:T(8,128)} %param.8) | copy-start | bytes 4612

commit v5 on v1

v5 whole, which is shorter than its diff:
```python
import functools

import jax
import jax.numpy as jnp
from jax import lax
from jax.experimental import pallas as pl
from jax.experimental.pallas import tpu as pltpu
from jax.sharding import Mesh
from jax.sharding import PartitionSpec as P

VMEM = pl.BlockSpec(memory_space=pltpu.VMEM)
HBM = pl.BlockSpec(memory_space=pltpu.HBM)
SMEM = pl.BlockSpec(memory_space=pltpu.SMEM)
NT = (((1,), (1,)), ((), ()))
TN = (((0,), (0,)), ((), ()))


GATHER = 40_000_000_000
CHIPS = 4
CORE, CHIP = range(2)


def call(body, outs, *operands, scalars=0, raw=0, scratch=(), flops=None, out_space=VMEM):
    operands = list(operands)
    for n in range(scalars, scalars + raw):
        operands[n] = pltpu.with_memory_space_constraint(operands[n], pltpu.HBM)
    cost = None if flops is None else pl.CostEstimate(flops=flops, transcendentals=0, bytes_accessed=0)
    return pl.pallas_call(
        body,
        out_shape=outs,
        in_specs=[SMEM] * scalars + [HBM] * raw + [VMEM] * (len(operands) - scalars - raw),
        out_specs=jax.tree.map(lambda _: out_space, outs),
        scratch_shapes=scratch,
        cost_estimate=cost,
        compiler_params=pltpu.CompilerParams(vmem_limit_bytes=16 << 20),
    )(*operands)


def copy_all(pairs, sems):
    copies = [pltpu.make_async_copy(src, dst, sems.at[n]) for n, (src, dst) in enumerate(pairs)]
    for copy in copies:
        copy.start()
    return copies


def dispatch_body(cap, place, routes_hbm, tokens_hbm, outgoing, target_t, routes_t, tokens, sems):
    top, rows = routes_t.shape
    slots = outgoing.shape[0]
    experts = slots // cap
    cols = tokens.shape[1] // CHIPS
    pairs = [(routes_hbm, routes_t)]
    for shift in range(CHIPS):
        block = lax.rem(place[CHIP] - shift + CHIPS, CHIPS) * 2 + place[CORE]
        columns = pl.ds(pl.multiple_of(block * cols, cols), cols)
        pairs.append((tokens_hbm.at[:, columns], tokens.at[:, shift * cols : (shift + 1) * cols]))
    copies = copy_all(pairs, sems)
    copies[0].wait()
    expert_ids = lax.broadcasted_iota(jnp.int32, (experts, rows), 0)
    chosen = [(routes_t[k : k + 1, :] == expert_ids).astype(jnp.float32) for k in range(top)]
    named = functools.reduce(jnp.add, chosen)
    earlier = (
        lax.broadcasted_iota(jnp.int32, (rows, rows), 0) < lax.broadcasted_iota(jnp.int32, (rows, rows), 1)
    ).astype(jnp.bfloat16)
    before = jnp.dot(named.astype(jnp.bfloat16), earlier, preferred_element_type=jnp.float32)
    slot_ids = lax.broadcasted_iota(jnp.int32, (slots, rows), 0)
    picker = jnp.zeros((slots, rows), jnp.float32)
    for k in range(top):
        slot = jnp.sum(chosen[k] * before, axis=0, keepdims=True).astype(jnp.int32)
        target = routes_t[k : k + 1, :] * cap + slot
        target_t[k : k + 1, :] = target
        picker += (slot_ids == target).astype(jnp.float32)
    for copy in copies[1:]:
        copy.wait()
    picked = jnp.dot(picker.astype(jnp.bfloat16), tokens[...], preferred_element_type=jnp.float32)
    outgoing[...] = picked.astype(jnp.bfloat16).reshape(outgoing.shape)


def units_of(place, shift, share):
    start = lax.rem(place[CHIP] + shift, CHIPS) * share
    return pl.ds(pl.multiple_of(start, 16), share)


def pack_body(place, w_gate, w_up, _, *refs):
    outs, sems = refs[:-1], refs[-1]
    share = outs[0].shape[0] // 2
    pairs = []
    for shift, out in enumerate(outs, 1):
        pairs.append((w_gate.at[units_of(place, shift, share), :], out.at[:share, :]))
        pairs.append((w_up.at[units_of(place, shift, share), :], out.at[share:, :]))
    for copy in copy_all(pairs, sems):
        copy.wait()


def gather_body(place, w_gate, w_up, one, two, three, weights, sems):
    both, cols = one.shape
    share = both // 2
    copies = copy_all(
        [
            (w.at[units_of(place, 0, share), :], weights.at[n * share : (n + 1) * share, :cols])
            for n, w in enumerate((w_gate, w_up))
        ],
        sems,
    )
    for shift, piece in enumerate((one, two, three), 1):
        weights[:, shift * cols : (shift + 1) * cols] = piece[...]
    for copy in copies:
        copy.wait()


def gate_up_body(mine, place, rows, weights, out):
    half = out.shape[0]
    for core in range(2):
        start = (core if mine else 1 - core) * half

        @pl.when(place[CORE] == core)
        def _():
            flat = rows[start : start + half].reshape(half, weights.shape[1])
            total = lax.dot_general(flat, weights[...], NT, preferred_element_type=jnp.float32)
            out[...] = total.astype(out.dtype)


def hidden_body(mine, theirs, hidden):
    units = hidden.shape[1]
    total = mine[...] + theirs[...].astype(jnp.float32)
    gate, up = total[:, :units], total[:, units:]
    hidden[...] = (gate / (1 + jnp.exp(-gate)) * up).astype(jnp.bfloat16)


def down(hidden, w_down):
    units = hidden.shape[2]
    total = functools.reduce(
        jnp.add,
        [
            jnp.dot(
                hidden[z], w_down[z * units : (z + 1) * units, :], preferred_element_type=jnp.float32
            )
            for z in range(CHIPS)
        ],
    )
    return total.astype(jnp.bfloat16)


def down_own_body(own, w_down, out):
    out[...] = down(own, w_down)


def down_body(place, own, other, w_down, out):
    half = own.shape[0]
    for value, which in ((own[...], place[CORE]), (down(other, w_down), 1 - place[CORE])):
        out[pl.ds(pl.multiple_of(which * half, 16), half)] = value.reshape(half, *out.shape[1:])


def combine_body(target_t, weight_t, returned, out):
    top, rows = target_t.shape
    slots = returned.shape[0]
    slot_ids = lax.broadcasted_iota(jnp.int32, (slots, rows), 0)
    spread = jnp.zeros((slots, rows), jnp.float32)
    for k in range(top):
        spread += jnp.where(slot_ids == target_t[k : k + 1, :], weight_t[k : k + 1, :], 0.0)
    high = spread.astype(jnp.bfloat16)
    low = (spread - high.astype(jnp.float32)).astype(jnp.bfloat16)
    flat = returned[...].reshape(slots, out.shape[1])
    total = lax.dot_general(high, flat, TN, preferred_element_type=jnp.float32)
    total += lax.dot_general(low, flat, TN, preferred_element_type=jnp.float32)
    out[...] = total.astype(jnp.bfloat16)


def on_device(tokens, routes, route_weight, w_gate, w_up, w_down):
    tok_count, top = routes.shape
    _, units, cols = w_gate.shape
    experts = lax.axis_size("wide")
    cap = max(2, (11 * tok_count + experts - 1) // experts)
    slots = experts * cap
    share = units // CHIPS
    half = slots // 2
    bf16 = jnp.bfloat16
    dma = pltpu.SemaphoreType.DMA
    swap = [(0, 1), (1, 0)]
    place = jnp.stack([lax.axis_index(a) for a in ("core", "chip")]).astype(jnp.int32)

    outgoing, target_t = call(
        functools.partial(dispatch_body, cap),
        (
            jax.ShapeDtypeStruct((slots, CHIPS * cols // 128, 128), bf16),
            jax.ShapeDtypeStruct((top, tok_count), jnp.int32),
        ),
        place,
        routes.T,
        tokens,
        scalars=1,
        raw=2,
        scratch=[
            pltpu.VMEM((top, tok_count), jnp.int32),
            pltpu.VMEM((tok_count, CHIPS * cols), bf16),
            dma((1 + CHIPS,)),
        ],
    )
    received = lax.all_to_all(outgoing, "wide", split_axis=0, concat_axis=0, tiled=True)

    part = jax.ShapeDtypeStruct((2 * share, cols), bf16)
    pieces = call(
        pack_body,
        (part,) * (CHIPS - 1),
        place,
        w_gate[0],
        w_up[0],
        target_t,
        scalars=1,
        raw=2,
        scratch=[dma((2 * (CHIPS - 1),))],
        out_space=HBM,
    )
    pieces = [
        lax.ppermute(piece, "chip", [(i, (i + shift) % CHIPS) for i in range(CHIPS)])
        for shift, piece in enumerate(pieces, 1)
    ]
    weights = call(
        gather_body,
        jax.ShapeDtypeStruct((2 * share, CHIPS * cols), bf16),
        place,
        w_gate[0],
        w_up[0],
        *pieces,
        scalars=1,
        raw=2,
        scratch=[dma((2,))],
        flops=GATHER,
    )
    theirs = call(
        functools.partial(gate_up_body, False),
        jax.ShapeDtypeStruct((half, 2 * share), bf16),
        place,
        received,
        weights,
        scalars=1,
    )
    theirs = lax.ppermute(theirs, "core", swap)
    mine = call(
        functools.partial(gate_up_body, True),
        jax.ShapeDtypeStruct((half, 2 * share), jnp.float32),
        place,
        received,
        weights,
        scalars=1,
    )
    hidden = call(hidden_body, jax.ShapeDtypeStruct((half, share), bf16), mine, theirs)
    own = lax.all_gather(hidden, "chip", axis=0)
    other = lax.ppermute(own, "core", swap)
    produced = call(
        down_body,
        jax.ShapeDtypeStruct((slots, cols // 128, 128), bf16),
        place,
        call(down_own_body, jax.ShapeDtypeStruct((half, cols), bf16), own, w_down[0]),
        other,
        w_down[0],
        scalars=1,
    )
    returned = lax.all_to_all(produced, "wide", split_axis=0, concat_axis=0, tiled=True)
    return call(
        combine_body,
        jax.ShapeDtypeStruct((tok_count, cols), bf16),
        target_t,
        route_weight.T,
        returned,
    )


def solution(mesh):
    fine = Mesh(mesh.devices.reshape(mesh.shape["wide"], CHIPS, 2), ("wide", "chip", "core"))
    narrow = ("chip", "core")
    return jax.shard_map(
        on_device,
        mesh=fine,
        in_specs=(
            P("wide", None),
            P("wide", None),
            P("wide", None),
            P("wide", None, narrow),
            P("wide", None, narrow),
            P("wide", None, narrow),
        ),
        out_specs=P("wide", narrow),
        check_vma=False,
    )
```

time: 133 us -> 133 us (level)
  Pallas kernels: 7.03 us -> 13.1 us
  waiting for transfers between devices: 41.2 us -> 35.7 us
    ppermute x5, waiting for transfers between devices: 41.2 us -> 28.7 us  [the longest x3 26 us: on_device(): lax.ppermute(piece, 'chip', [(i, (i + shift) % CHIPS) for i in range(CHIP...]
    all_to_all x1, waiting for transfers between devices: 0.01 us -> 7 us  [on_device(): lax.all_to_all(outgoing, 'wide', split_axis=0, concat_axis=0, tiled=True)]
    pallas_call x5 -> x9, Pallas kernels: 7.03 us -> 13.1 us  [call(): pl.pallas_call(body, out_shape=outs, in_specs=[SMEM] * scalars + [HBM] *...]
  transfers between devices with their start and end apart: 6 -> 6, of which waited for: 4 -> 4; matrix products, arithmetic and copies ran while one was open for 0% -> 0% of each run, Pallas kernels for 0% -> 3%
where the time goes in v5:
time: 133 us; the launch traced here: 132 us
  blocking collectives  47.2 us (35%)
  waiting for transfers between devices  35.7 us (27%)
  starting transfers between devices  34.2 us (26%)
  Pallas kernels  13.1 us (10%)
  local copies, waits for them, and re-layouts  1.77 us (1%)
    ppermute x3, waiting for transfers between devices, on_device(): lax.ppermute(piece, 'chip', [(i, (i + shift) % CHIPS) for i in range(CHIP...  26 us
    all_to_all x1, blocking collectives, on_device(): lax.all_to_all(produced, 'wide', split_axis=0, concat_axis=0, tiled=True)  24.7 us
    all_gather x1, blocking collectives, on_device(): own = lax.all_gather(hidden, 'chip', axis=0)  22.5 us
    ppermute x3, starting transfers between devices, on_device(): lax.ppermute(piece, 'chip', [(i, (i + shift) % CHIPS) for i in range(CHIP...  18.9 us
    pallas_call x9, Pallas kernels, call(): pl.pallas_call(body, out_shape=outs, in_specs=[SMEM] * scalars + [HBM] *...  13.1 us
    all_to_all x1, starting transfers between devices, on_device(): lax.all_to_all(outgoing, 'wide', split_axis=0, concat_axis=0, tiled=True)  11.5 us
    all_to_all x1, waiting for transfers between devices, on_device(): lax.all_to_all(outgoing, 'wide', split_axis=0, concat_axis=0, tiled=True)  7 us
  transfers between devices with their start and end apart: 6, of which 4 were waited for; matrix products, arithmetic and copies ran while one was open for 0% of the time, Pallas kernels for 3%

profile of v5, /device:TPU:8, one launch (start us, length us, event | category | flops | bytes accessed | tf_op | source)
XLA Modules:
  0.0 132.1 jit_solution(13300266981332841415)
XLA Ops:
  0.0 0.1 pad_add_fusion.place
  0.1 3.6 %shard_map.64 = (bf16[704,8,128]{2,1,0:T(8,128)(2,1)}, s32[6,64]{1,0:T(8,128)S(1)}) custom-call(s32[2]{0:T(128)S(1)} %pad_add_fusion.place, s32[6,64]{1,0:T(8,128)} %bitcast.17, bf16[64,2048]{1,0:T(8,128)(2,1)} %tokens_hbm.1), custom_call_target="tpu_custom_call" | custom-call | tf_op jit(solution)/shard_map/pallas_call | solution.py:28
  3.6 1.9 %shard_map.65 = (bf16[704,256]{1,0:T(8,128)(2,1)S(1)}, bf16[704,256]{1,0:T(8,128)(2,1)S(1)}, bf16[704,256]{1,0:T(8,128)(2,1)S(1)}) custom-call(s32[2]{0:T(128)S(1)} %pad_add_fusion.place, bf16[1408,256]{1,0:T(8,128)(2,1)} %bitcast.13, bf16[1408,256]{1,0:T(8,128)(2,1)} %bitcast.15, s32[6,64]{1,0:T(8,128)S(1)} %get-tuple-element.10._.target_t), custom_call_target="tpu_custom_call" | custom-call | tf_op jit(solution)/shard_map/pallas_call | solution.py:28
  5.6 6.1 %collective-permute-start = (bf16[704,256]{1,0:T(8,128)(2,1)S(1)}, bf16[704,256]{1,0:T(8,128)(2,1)S(1)}, u32[]{:S(2)}, u32[]{:S(2)}) collective-permute-start(bf16[704,256]{1,0:T(8,128)(2,1)S(1)} %get-tuple-element.12), channel_id=1, source_target_pairs={{0,2},{2,4},{4,6},{6,0},{1,3},{3,5},{5,7},{7,1},{8,10},{10,12},{12... | collective-permute-start | bytes 1081352 | tf_op jit(solution)/shard_map/ppermute | solution.py:214
  11.7 9.1 %collective-permute-start.1 = (bf16[704,256]{1,0:T(8,128)(2,1)S(1)}, bf16[704,256]{1,0:T(8,128)(2,1)S(1)}, u32[]{:S(2)}, u32[]{:S(2)}) collective-permute-start(bf16[704,256]{1,0:T(8,128)(2,1)S(1)} %get-tuple-element.13), channel_id=1, source_target_pairs={{0,4},{2,6},{4,0},{6,2},{1,5},{3,7},{5,1},{7,3},{8,12},{10,14},{12... | collective-permute-start | bytes 1081352 | tf_op jit(solution)/shard_map/ppermute | solution.py:214
  20.8 3.7 %collective-permute-start.2 = (bf16[704,256]{1,0:T(8,128)(2,1)S(1)}, bf16[704,256]{1,0:T(8,128)(2,1)}, u32[]{:S(2)}, u32[]{:S(2)}) collective-permute-start(bf16[704,256]{1,0:T(8,128)(2,1)S(1)} %get-tuple-element.14), channel_id=1, source_target_pairs={{0,6},{2,0},{4,2},{6,4},{1,7},{3,1},{5,3},{7,5},{8,14},{10,8},{12,... | collective-permute-start | bytes 1081352 | tf_op jit(solution)/shard_map/ppermute | solution.py:214
  24.4 11.5 %all-to-all-start = ((bf16[704,8,128]{2,1,0:T(8,128)(2,1)}), bf16[704,8,128]{2,1,0:T(8,128)(2,1)S(1)}, u32[]{:S(2)}, u32[]{:S(2)}) async-start(bf16[704,8,128]{2,1,0:T(8,128)(2,1)} %get-tuple-element.11), calls=%async_computation | async-start | bytes 2883584 | tf_op jit(solution)/shard_map/all_to_all | solution.py:198
  36.0 26.0 %collective-permute-done.1.two = bf16[704,256]{1,0:T(8,128)(2,1)S(1)} collective-permute-done((bf16[704,256]{1,0:T(8,128)(2,1)S(1)}, bf16[704,256]{1,0:T(8,128)(2,1)S(1)}, u32[]{:S(2)}, u32[]{:S(2)}) %collective-permute-start.1) | collective-permute-done | bytes 360480 | tf_op jit(solution)/shard_map/ppermute | solution.py:214
  62.0 0.8 copy-done.2
  62.7 1.0 copy-done.3
  63.7 2.0 %shard_map.66.weights = bf16[704,1024]{1,0:T(8,128)(2,1)S(1)} custom-call(s32[2]{0:T(128)S(1)} %pad_add_fusion.place, bf16[1408,256]{1,0:T(8,128)(2,1)} %bitcast.14, bf16[1408,256]{1,0:T(8,128)(2,1)} %bitcast.16, bf16[704,256]{1,0:T(8,128)(2,1)S(1)} %collective-permute-done.one, bf16[704,256]{1,0:T(8,128)(2,1)S(1)} %copy-done.3, ...), custom_call_target="tpu_custom_call" | custom-call | flops 40000000000 | tf_op jit(solution)/shard_map/pallas_call | solution.py:28
  65.8 7.0 %all-to-all-done.rows = bf16[704,8,128]{2,1,0:T(8,128)(2,1)S(1)} async-done(((bf16[704,8,128]{2,1,0:T(8,128)(2,1)}), bf16[704,8,128]{2,1,0:T(8,128)(2,1)S(1)}, u32[]{:S(2)}, u32[]{:S(2)}) %all-to-all-start) | async-done | bytes 1441824 | tf_op jit(solution)/shard_map/all_to_all | solution.py:198
  72.8 1.3 %shard_map.68 = bf16[352,704]{1,0:T(8,128)(2,1)S(1)} custom-call(s32[2]{0:T(128)S(1)} %pad_add_fusion.place, bf16[704,8,128]{2,1,0:T(8,128)(2,1)S(1)} %all-to-all-done.rows, bf16[704,1024]{1,0:T(8,128)(2,1)S(1)} %shard_map.66.weights), custom_call_target="tpu_custom_call" | custom-call | tf_op jit(solution)/shard_map/pallas_call | solution.py:28
  74.1 1.9 %collective-permute-start.3 = (bf16[352,704]{1,0:T(8,128)(2,1)S(1)}, bf16[352,704]{1,0:T(8,128)(2,1)S(1)}, u32[]{:S(2)}, u32[]{:S(2)}) collective-permute-start(bf16[352,704]{1,0:T(8,128)(2,1)S(1)} %shard_map.68), channel_id=1, source_target_pairs={{0,1},{1,0},{2,3},{3,2},{4,5},{5,4},{6,7},{7,6},{8,9},{9,8},{10,11... | collective-permute-start | bytes 1486856 | tf_op jit(solution)/shard_map/ppermute | solution.py:237
  76.0 1.3 %shard_map.67.mine = f32[352,704]{1,0:T(8,128)S(1)} custom-call(s32[2]{0:T(128)S(1)} %pad_add_fusion.place, bf16[704,8,128]{2,1,0:T(8,128)(2,1)S(1)} %all-to-all-done.rows, bf16[704,1024]{1,0:T(8,128)(2,1)S(1)} %shard_map.66.weights), custom_call_target="tpu_custom_call" | custom-call | tf_op jit(solution)/shard_map/pallas_call | solution.py:28
  77.4 0.5 collective-permute-done.3.theirs
  77.9 0.3 shard_map.69
  78.2 22.5 %all-gather = bf16[1408,352]{1,0:T(8,128)(2,1)S(1)} all-gather(bf16[352,352]{1,0:T(8,128)(2,1)S(1)} %shard_map.69), channel_id=2, replica_groups=mesh['wide'=64,'chip'=4,'core'=2] {'chip'}, dimensions={0}, use_global_device_ids=true | all-gather | bytes 1239040 | tf_op jit(solution)/shard_map/all_gather | solution.py:247
  100.7 1.9 %collective-permute-start.4 = (bf16[4,352,352]{2,1,0:T(8,128)(2,1)S(1)}, bf16[4,352,352]{2,1,0:T(8,128)(2,1)S(1)}, u32[]{:S(2)}, u32[]{:S(2)}) collective-permute-start(bf16[4,352,352]{2,1,0:T(8,128)(2,1)S(1)} %bitcast.8), channel_id=1, source_target_pairs={{0,1},{1,0},{2,3},{3,2},{4,5},{5,4},{6,7},{7,6},{8,9},{9,8},{10,11... | collective-permute-start | bytes 2973704 | tf_op jit(solution)/shard_map/ppermute | solution.py:248
  102.6 0.5 shard_map.70.own
  103.2 2.1 %collective-permute-done.4.other = bf16[4,352,352]{2,1,0:T(8,128)(2,1)S(1)} collective-permute-done((bf16[4,352,352]{2,1,0:T(8,128)(2,1)S(1)}, bf16[4,352,352]{2,1,0:T(8,128)(2,1)S(1)}, u32[]{:S(2)}, u32[]{:S(2)}) %collective-permute-start.4) | collective-permute-done | bytes 991264 | tf_op jit(solution)/shard_map/ppermute | solution.py:248
  105.3 1.1 shard_map.71
  106.4 24.7 %all_to_all.10.returned = bf16[704,2,128]{2,1,0:T(2,128)(2,1)S(1)} all-to-all(bf16[704,2,128]{2,1,0:T(2,128)(2,1)S(1)} %shard_map.71), channel_id=1, replica_groups=mesh['wide'=64,'chip'=4,'core'=2] {'wide'}, dimensions={0} | all-to-all | bytes 720896 | tf_op jit(solution)/shard_map/all_to_all | solution.py:258
  131.1 1.1 shard_map.72
  (8 shorter events, 0.0 us)
Async XLA Ops:
  5.6 30.4 %collective-permute-start = (bf16[704,256]{1,0:T(8,128)(2,1)S(1)}, bf16[704,256]{1,0:T(8,128)(2,1)S(1)}, u32[]{:S(2)}, u32[]{:S(2)}) collective-permute-start(bf16[704,256]{1,0:T(8,128)(2,1)S(1)} %get-tuple-element.12), channel_id=1, source_target_pairs={{0,2},{2,4},{4,6},{6,0},{1,3},{3,5},{5,7},{7,1},{8,10},{10,12},{12... | collective-permute-start | bytes 1081352 | tf_op jit(solution)/shard_map/ppermute | solution.py:214
  11.7 50.3 %collective-permute-start.1 = (bf16[704,256]{1,0:T(8,128)(2,1)S(1)}, bf16[704,256]{1,0:T(8,128)(2,1)S(1)}, u32[]{:S(2)}, u32[]{:S(2)}) collective-permute-start(bf16[704,256]{1,0:T(8,128)(2,1)S(1)} %get-tuple-element.13), channel_id=1, source_target_pairs={{0,4},{2,6},{4,0},{6,2},{1,5},{3,7},{5,1},{7,3},{8,12},{10,14},{12... | collective-permute-start | bytes 1081352 | tf_op jit(solution)/shard_map/ppermute | solution.py:214
  20.8 41.9 %collective-permute-start.2 = (bf16[704,256]{1,0:T(8,128)(2,1)S(1)}, bf16[704,256]{1,0:T(8,128)(2,1)}, u32[]{:S(2)}, u32[]{:S(2)}) collective-permute-start(bf16[704,256]{1,0:T(8,128)(2,1)S(1)} %get-tuple-element.14), channel_id=1, source_target_pairs={{0,6},{2,0},{4,2},{6,4},{1,7},{3,1},{5,3},{7,5},{8,14},{10,8},{12,... | collective-permute-start | bytes 1081352 | tf_op jit(solution)/shard_map/ppermute | solution.py:214
  24.4 48.3 %all-to-all-start = ((bf16[704,8,128]{2,1,0:T(8,128)(2,1)}), bf16[704,8,128]{2,1,0:T(8,128)(2,1)S(1)}, u32[]{:S(2)}, u32[]{:S(2)}) async-start(bf16[704,8,128]{2,1,0:T(8,128)(2,1)} %get-tuple-element.11), calls=%async_computation | async-start | bytes 2883584 | tf_op jit(solution)/shard_map/all_to_all | solution.py:198
  62.0 0.8 copy-start.2
  62.7 1.0 copy-start.3
  74.1 3.8 %collective-permute-start.3 = (bf16[352,704]{1,0:T(8,128)(2,1)S(1)}, bf16[352,704]{1,0:T(8,128)(2,1)S(1)}, u32[]{:S(2)}, u32[]{:S(2)}) collective-permute-start(bf16[352,704]{1,0:T(8,128)(2,1)S(1)} %shard_map.68), channel_id=1, source_target_pairs={{0,1},{1,0},{2,3},{3,2},{4,5},{5,4},{6,7},{7,6},{8,9},{9,8},{10,11... | collective-permute-start | bytes 1486856 | tf_op jit(solution)/shard_map/ppermute | solution.py:237
  77.4 25.3 %copy-start = (bf16[1,1408,256]{2,1,0:T(8,128)(2,1)S(1)}, bf16[1,1408,256]{2,1,0:T(8,128)(2,1)}, u32[]{:S(2)}) copy-start(bf16[1,1408,256]{2,1,0:T(8,128)(2,1)} %param.11) | copy-start | bytes 2162692
  100.7 4.6 %collective-permute-start.4 = (bf16[4,352,352]{2,1,0:T(8,128)(2,1)S(1)}, bf16[4,352,352]{2,1,0:T(8,128)(2,1)S(1)}, u32[]{:S(2)}, u32[]{:S(2)}) collective-permute-start(bf16[4,352,352]{2,1,0:T(8,128)(2,1)S(1)} %bitcast.8), channel_id=1, source_target_pairs={{0,1},{1,0},{2,3},{3,2},{4,5},{5,4},{6,7},{7,6},{8,9},{9,8},{10,11... | collective-permute-start | bytes 2973704 | tf_op jit(solution)/shard_map/ppermute | solution.py:248
  103.2 27.9 %copy-start.1 = (f32[64,6]{0,1:T(8,128)S(1)}, f32[64,6]{0,1:T(8,128)}, u32[]{:S(2)}) copy-start(f32[64,6]{0,1:T(8,128)} %param.8) | copy-start | bytes 4612

commit v6 on v5

--- a/solution.py
+++ b/solution.py
@@ -15,9 +15,10 @@
 TN = (((0,), (0,)), ((), ()))
 
 
+PICK = 10_000_000_000
 GATHER = 40_000_000_000
 CHIPS = 4
-CORE, CHIP = range(2)
+CORE, CHIP, SIDE = range(3)
 
 
 def call(body, outs, *operands, scalars=0, raw=0, scratch=(), flops=None, out_space=VMEM):
@@ -43,18 +44,35 @@
     return copies
 
 
-def dispatch_body(cap, place, routes_hbm, tokens_hbm, outgoing, target_t, routes_t, tokens, sems):
+def units_of(place, shift, share):
+    start = lax.rem(place[CHIP] + shift, CHIPS) * share
+    return pl.ds(pl.multiple_of(start, 16), share)
+
+
+def first_body(place, routes_hbm, tokens_hbm, w_gate, w_up, mine, one, two, three, routes_t, sems):
     top, rows = routes_t.shape
-    slots = outgoing.shape[0]
-    experts = slots // cap
-    cols = tokens.shape[1] // CHIPS
+    cols = mine.shape[1] // CHIPS
+    share = one.shape[0] // 2
     pairs = [(routes_hbm, routes_t)]
     for shift in range(CHIPS):
         block = lax.rem(place[CHIP] - shift + CHIPS, CHIPS) * 2 + place[CORE]
         columns = pl.ds(pl.multiple_of(block * cols, cols), cols)
-        pairs.append((tokens_hbm.at[:, columns], tokens.at[:, shift * cols : (shift + 1) * cols]))
+        pairs.append((tokens_hbm.at[:, columns], mine.at[:rows, shift * cols : (shift + 1) * cols]))
+    for shift, out in enumerate((one, two, three), 1):
+        pairs.append((w_gate.at[units_of(place, shift, share), :], out.at[:share, :]))
+        pairs.append((w_up.at[units_of(place, shift, share), :], out.at[share:, :]))
     copies = copy_all(pairs, sems)
+    mine[rows:, :] = jnp.zeros((mine.shape[0] - rows, mine.shape[1]), mine.dtype)
     copies[0].wait()
+    mine[rows : rows + top, :rows] = routes_t[...].astype(mine.dtype)
+    for copy in copies[1:]:
+        copy.wait()
+
+
+def picked(top, cap, experts, side, place, block, target_t=None):
+    rows = block.shape[0] - 16
+    slots = side * cap
+    routes_t = block[rows:, :rows].astype(jnp.float32).astype(jnp.int32)
     expert_ids = lax.broadcasted_iota(jnp.int32, (experts, rows), 0)
     chosen = [(routes_t[k : k + 1, :] == expert_ids).astype(jnp.float32) for k in range(top)]
     named = functools.reduce(jnp.add, chosen)
@@ -67,28 +85,20 @@
     for k in range(top):
         slot = jnp.sum(chosen[k] * before, axis=0, keepdims=True).astype(jnp.int32)
         target = routes_t[k : k + 1, :] * cap + slot
-        target_t[k : k + 1, :] = target
-        picker += (slot_ids == target).astype(jnp.float32)
-    for copy in copies[1:]:
-        copy.wait()
-    picked = jnp.dot(picker.astype(jnp.bfloat16), tokens[...], preferred_element_type=jnp.float32)
-    outgoing[...] = picked.astype(jnp.bfloat16).reshape(outgoing.shape)
-
-
-def units_of(place, shift, share):
-    start = lax.rem(place[CHIP] + shift, CHIPS) * share
-    return pl.ds(pl.multiple_of(start, 16), share)
-
-
-def pack_body(place, w_gate, w_up, _, *refs):
-    outs, sems = refs[:-1], refs[-1]
-    share = outs[0].shape[0] // 2
-    pairs = []
-    for shift, out in enumerate(outs, 1):
-        pairs.append((w_gate.at[units_of(place, shift, share), :], out.at[:share, :]))
-        pairs.append((w_up.at[units_of(place, shift, share), :], out.at[share:, :]))
-    for copy in copy_all(pairs, sems):
-        copy.wait()
+        if target_t is not None:
+            target_t[k : k + 1, :] = target
+        picker += (slot_ids == target - place[SIDE] * slots).astype(jnp.float32)
+    rows_out = jnp.dot(picker.astype(jnp.bfloat16), block[:rows, :], preferred_element_type=jnp.float32)
+    return rows_out.astype(jnp.bfloat16).reshape(side, cap, block.shape[1] // 128, 128)
+
+
+def own_body(sizes, place, mine, out, target_t):
+    out[...] = picked(*sizes, place, mine, target_t)
+
+
+def dispatch_body(sizes, place, own, neighbour, outgoing):
+    outgoing[:, 1 - place[SIDE]] = picked(*sizes, place, neighbour)
+    outgoing[:, place[SIDE]] = own[...]
 
 
 def gather_body(place, w_gate, w_up, one, two, three, weights, sems):
@@ -110,11 +120,11 @@
 def gate_up_body(mine, place, rows, weights, out):
     half = out.shape[0]
     for core in range(2):
-        start = (core if mine else 1 - core) * half
+        start = (core if mine else 1 - core) * (rows.shape[0] // 2)
 
         @pl.when(place[CORE] == core)
         def _():
-            flat = rows[start : start + half].reshape(half, weights.shape[1])
+            flat = rows[start : start + rows.shape[0] // 2].reshape(half, weights.shape[1])
             total = lax.dot_general(flat, weights[...], NT, preferred_element_type=jnp.float32)
             out[...] = total.astype(out.dtype)
 
@@ -145,14 +155,17 @@
 
 
 def down_body(place, own, other, w_down, out):
-    half = own.shape[0]
+    blocks, cap = out.shape[:2]
+    part = blocks // 4
     for value, which in ((own[...], place[CORE]), (down(other, w_down), 1 - place[CORE])):
-        out[pl.ds(pl.multiple_of(which * half, 16), half)] = value.reshape(half, *out.shape[1:])
+        value = value.reshape(part, 2, cap, *out.shape[2:])
+        for side in range(2):
+            out[pl.ds(side * (blocks // 2) + which * part, part)] = value[:, side]
 
 
 def combine_body(target_t, weight_t, returned, out):
     top, rows = target_t.shape
-    slots = returned.shape[0]
+    slots = returned.shape[0] * returned.shape[1]
     slot_ids = lax.broadcasted_iota(jnp.int32, (slots, rows), 0)
     spread = jnp.zeros((slots, rows), jnp.float32)
     for k in range(top):
@@ -168,7 +181,8 @@
 def on_device(tokens, routes, route_weight, w_gate, w_up, w_down):
     tok_count, top = routes.shape
     _, units, cols = w_gate.shape
-    experts = lax.axis_size("wide")
+    side = lax.axis_size("plane")
+    experts = 2 * side
     cap = max(2, (11 * tok_count + experts - 1) // experts)
     slots = experts * cap
     share = units // CHIPS
@@ -176,40 +190,44 @@
     bf16 = jnp.bfloat16
     dma = pltpu.SemaphoreType.DMA
     swap = [(0, 1), (1, 0)]
-    place = jnp.stack([lax.axis_index(a) for a in ("core", "chip")]).astype(jnp.int32)
-
-    outgoing, target_t = call(
-        functools.partial(dispatch_body, cap),
+    place = jnp.stack([lax.axis_index(a) for a in ("core", "chip", "side")]).astype(jnp.int32)
+
+    part = jax.ShapeDtypeStruct((2 * share, cols), bf16)
+    mine, *pieces = call(
+        first_body,
+        (jax.ShapeDtypeStruct((tok_count + 16, CHIPS * cols), bf16),) + (part,) * (CHIPS - 1),
+        place,
+        routes.T,
+        tokens,
+        w_gate[0],
+        w_up[0],
+        scalars=1,
+        raw=4,
+        scratch=[pltpu.VMEM((top, tok_count), jnp.int32), dma((1 + CHIPS + 2 * (CHIPS - 1),))],
+    )
+    neighbour = lax.ppermute(mine, "side", swap)
+    sizes = (top, cap, experts, side)
+    chunk = (cap, CHIPS * cols // 128, 128)
+    picked_own, target_t = call(
+        functools.partial(own_body, sizes),
         (
-            jax.ShapeDtypeStruct((slots, CHIPS * cols // 128, 128), bf16),
+            jax.ShapeDtypeStruct((side, *chunk), bf16),
             jax.ShapeDtypeStruct((top, tok_count), jnp.int32),
         ),
         place,
-        routes.T,
-        tokens,
-        scalars=1,
-        raw=2,
-        scratch=[
-            pltpu.VMEM((top, tok_count), jnp.int32),
-            pltpu.VMEM((tok_count, CHIPS * cols), bf16),
-            dma((1 + CHIPS,)),
-        ],
-    )
-    received = lax.all_to_all(outgoing, "wide", split_axis=0, concat_axis=0, tiled=True)
-
-    part = jax.ShapeDtypeStruct((2 * share, cols), bf16)
-    pieces = call(
-        pack_body,
-        (part,) * (CHIPS - 1),
-        place,
-        w_gate[0],
-        w_up[0],
-        target_t,
-        scalars=1,
-        raw=2,
-        scratch=[dma((2 * (CHIPS - 1),))],
-        out_space=HBM,
-    )
+        mine,
+        scalars=1,
+    )
+    outgoing = call(
+        functools.partial(dispatch_body, sizes),
+        jax.ShapeDtypeStruct((side, 2, *chunk), bf16),
+        place,
+        picked_own,
+        neighbour,
+        scalars=1,
+        flops=PICK,
+    )
+    received = lax.all_to_all(outgoing, "plane", split_axis=0, concat_axis=0, tiled=True)
     pieces = [
         lax.ppermute(piece, "chip", [(i, (i + shift) % CHIPS) for i in range(CHIPS)])
         for shift, piece in enumerate(pieces, 1)
@@ -248,14 +266,14 @@
     other = lax.ppermute(own, "core", swap)
     produced = call(
         down_body,
-        jax.ShapeDtypeStruct((slots, cols // 128, 128), bf16),
+        jax.ShapeDtypeStruct((experts, cap, cols // 128, 128), bf16),
         place,
         call(down_own_body, jax.ShapeDtypeStruct((half, cols), bf16), own, w_down[0]),
         other,
         w_down[0],
         scalars=1,
     )
-    returned = lax.all_to_all(produced, "wide", split_axis=0, concat_axis=0, tiled=True)
+    returned = lax.all_to_all(produced, ("side", "plane"), split_axis=0, concat_axis=0, tiled=True)
     return call(
         combine_body,
         jax.ShapeDtypeStruct((tok_count, cols), bf16),
@@ -266,19 +284,21 @@
 
 
 def solution(mesh):
-    fine = Mesh(mesh.devices.reshape(mesh.shape["wide"], CHIPS, 2), ("wide", "chip", "core"))
-    narrow = ("chip", "core")
+    fine = Mesh(
+        mesh.devices.reshape(2, mesh.shape["wide"] // 2, CHIPS, 2), ("side", "plane", "chip", "core")
+    )
+    wide, narrow = ("side", "plane"), ("chip", "core")
     return jax.shard_map(
         on_device,
         mesh=fine,
         in_specs=(
-            P("wide", None),
-            P("wide", None),
-            P("wide", None),
-            P("wide", None, narrow),
-            P("wide", None, narrow),
-            P("wide", None, narrow),
+            P(wide, None),
+            P(wide, None),
+            P(wide, None),
+            P(wide, None, narrow),
+            P(wide, None, narrow),
+            P(wide, None, narrow),
         ),
-        out_specs=P("wide", narrow),
+        out_specs=P(wide, narrow),
         check_vma=False,
     )

time: 133 us -> 131 us (0.985)
  waiting for transfers between devices: 35.7 us -> 33.4 us
  blocking collectives: 47.2 us -> 45.2 us
  starting transfers between devices: 34.2 us -> 36.2 us
    ppermute x3, waiting for transfers between devices: 26 us -> 12.5 us  [on_device(): lax.ppermute(piece, 'chip', [(i, (i + shift) % CHIPS) for i in range(CHIP...]
    all_to_all x1, waiting for transfers between devices: 7 us -> 18.2 us  [on_device(): lax.all_to_all(outgoing, 'plane', split_axis=0, concat_axis=0, tiled=True)]
    ppermute x0 -> x1, starting transfers between devices: none -> 4.28 us  [on_device(): neighbour = lax.ppermute(mine, 'side', swap)]
    all_to_all x1, blocking collectives: 24.7 us -> 22.5 us  [on_device(): lax.all_to_all(produced, ('side', 'plane'), split_axis=0, concat_axis=0,...]
    pallas_call x9 -> x10, Pallas kernels: 13.1 us -> 14.1 us  [call(): pl.pallas_call(body, out_shape=outs, in_specs=[SMEM] * scalars + [HBM] *...]
  transfers between devices with their start and end apart: 6 -> 7, of which waited for: 4 -> 5; matrix products, arithmetic and copies ran while one was open for 0% -> 0% of each run, Pallas kernels for 3% -> 6%
where the time goes in v6:
time: 131 us
  blocking collectives  45.2 us (35%)
  starting transfers between devices  36.2 us (28%)
  waiting for transfers between devices  33.4 us (25%)
  Pallas kernels  14.1 us (11%)
  local copies, waits for them, and re-layouts  1.77 us (1%)
    all_gather x1, blocking collectives, on_device(): own = lax.all_gather(hidden, 'chip', axis=0)  22.7 us
    all_to_all x1, blocking collectives, on_device(): lax.all_to_all(produced, ('side', 'plane'), split_axis=0, concat_axis=0,...  22.5 us
    all_to_all x1, waiting for transfers between devices, on_device(): lax.all_to_all(outgoing, 'plane', split_axis=0, concat_axis=0, tiled=True)  18.2 us
    ppermute x3, starting transfers between devices, on_device(): lax.ppermute(piece, 'chip', [(i, (i + shift) % CHIPS) for i in range(CHIP...  18 us
    pallas_call x10, Pallas kernels, call(): pl.pallas_call(body, out_shape=outs, in_specs=[SMEM] * scalars + [HBM] *...  14.1 us
    ppermute x3, waiting for transfers between devices, on_device(): lax.ppermute(piece, 'chip', [(i, (i + shift) % CHIPS) for i in range(CHIP...  12.5 us
    all_to_all x1, starting transfers between devices, on_device(): lax.all_to_all(outgoing, 'plane', split_axis=0, concat_axis=0, tiled=True)  10.2 us
    ppermute x1, starting transfers between devices, on_device(): neighbour = lax.ppermute(mine, 'side', swap)  4.28 us
  transfers between devices with their start and end apart: 7, of which 5 were waited for; matrix products, arithmetic and copies ran while one was open for 0% of the time, Pallas kernels for 6%

profile of v6, /device:TPU:8, one launch (start us, length us, event | category | flops | bytes accessed | tf_op | source)
XLA Modules:
  0.0 130.9 jit_solution(14118390686176860775)
XLA Ops:
  0.1 2.0 %shard_map.64 = (bf16[80,1024]{1,0:T(8,128)(2,1)S(1)}, bf16[704,256]{1,0:T(8,128)(2,1)S(1)}, bf16[704,256]{1,0:T(8,128)(2,1)S(1)}, bf16[704,256]{1,0:T(8,128)(2,1)S(1)}) custom-call(s32[3]{0:T(128)S(1)} %pad_add_fusion.place, s32[6,64]{1,0:T(8,128)} %bitcast.18, bf16[64,2048]{1,0:T(8,128)(2,1)} %tokens_hbm.1, bf16[1408,256]{1,0:T(8,128)(2,1)} %bitcast.14, ...), custom_call_target="tpu_custom_call" | custom-call | tf_op jit(solution)/shard_map/pallas_call | solution.py:29
  2.1 4.3 %collective-permute-start = (bf16[80,1024]{1,0:T(8,128)(2,1)S(1)}, bf16[80,1024]{1,0:T(8,128)(2,1)S(1)}, u32[]{:S(2)}, u32[]{:S(2)}) collective-permute-start(bf16[80,1024]{1,0:T(8,128)(2,1)S(1)} %get-tuple-element.11.mine), channel_id=1, source_target_pairs={{0,256},{256,0},{1,257},{257,1},{2,258},{258,2},{3,259},{259,3},{4... | collective-permute-start | bytes 491528 | tf_op jit(solution)/shard_map/ppermute | solution.py:208
  6.4 6.1 %collective-permute-start.1 = (bf16[704,256]{1,0:T(8,128)(2,1)S(1)}, bf16[704,256]{1,0:T(8,128)(2,1)S(1)}, u32[]{:S(2)}, u32[]{:S(2)}) collective-permute-start(bf16[704,256]{1,0:T(8,128)(2,1)S(1)} %get-tuple-element.14), channel_id=1, source_target_pairs={{0,2},{2,4},{4,6},{6,0},{1,3},{3,5},{5,7},{7,1},{8,10},{10,12},{12... | collective-permute-start | bytes 1081352 | tf_op jit(solution)/shard_map/ppermute | solution.py:232
  12.5 8.2 %collective-permute-start.2 = (bf16[704,256]{1,0:T(8,128)(2,1)S(1)}, bf16[704,256]{1,0:T(8,128)(2,1)S(1)}, u32[]{:S(2)}, u32[]{:S(2)}) collective-permute-start(bf16[704,256]{1,0:T(8,128)(2,1)S(1)} %get-tuple-element.15), channel_id=1, source_target_pairs={{0,4},{2,6},{4,0},{6,2},{1,5},{3,7},{5,1},{7,3},{8,12},{10,14},{12... | collective-permute-start | bytes 1081352 | tf_op jit(solution)/shard_map/ppermute | solution.py:232
  20.7 3.7 %collective-permute-start.3 = (bf16[704,256]{1,0:T(8,128)(2,1)S(1)}, bf16[704,256]{1,0:T(8,128)(2,1)}, u32[]{:S(2)}, u32[]{:S(2)}) collective-permute-start(bf16[704,256]{1,0:T(8,128)(2,1)S(1)} %get-tuple-element.16), channel_id=1, source_target_pairs={{0,6},{2,0},{4,2},{6,4},{1,7},{3,1},{5,3},{7,5},{8,14},{10,8},{12,... | collective-permute-start | bytes 1081352 | tf_op jit(solution)/shard_map/ppermute | solution.py:232
  24.4 1.5 %shard_map.65 = (bf16[32,11,8,128]{3,2,1,0:T(8,128)(2,1)S(1)}, s32[6,64]{1,0:T(8,128)S(1)}) custom-call(s32[3]{0:T(128)S(1)} %pad_add_fusion.place, bf16[80,1024]{1,0:T(8,128)(2,1)S(1)} %get-tuple-element.11.mine), custom_call_target="tpu_custom_call" | custom-call | tf_op jit(solution)/shard_map/pallas_call | solution.py:29
  25.9 2.7 %shard_map.66 = bf16[32,2,11,8,128]{4,3,2,1,0:T(8,128)(2,1)} custom-call(s32[3]{0:T(128)S(1)} %pad_add_fusion.place, bf16[32,11,8,128]{3,2,1,0:T(8,128)(2,1)S(1)} %get-tuple-element.13.own, bf16[80,1024]{1,0:T(8,128)(2,1)S(1)} %collective-permute-done.neighbour), custom_call_target="tpu_custom_call" | custom-call | flops 10000000000 | tf_op jit(solution)/shard_map/pallas_call | solution.py:29
  28.5 10.2 %all-to-all-start = ((bf16[32,2,11,8,128]{4,3,2,1,0:T(8,128)(2,1)}), bf16[32,2,11,8,128]{4,3,2,1,0:T(8,128)(2,1)S(1)}, u32[]{:S(2)}, u32[]{:S(2)}) async-start(bf16[32,2,11,8,128]{4,3,2,1,0:T(8,128)(2,1)} %shard_map.66), calls=%async_computation | async-start | bytes 2883584 | tf_op jit(solution)/shard_map/all_to_all | solution.py:230
  38.7 4.0 %collective-permute-done.1.one = bf16[704,256]{1,0:T(8,128)(2,1)S(1)} collective-permute-done((bf16[704,256]{1,0:T(8,128)(2,1)S(1)}, bf16[704,256]{1,0:T(8,128)(2,1)S(1)}, u32[]{:S(2)}, u32[]{:S(2)}) %collective-permute-start.1) | collective-permute-done | bytes 360480 | tf_op jit(solution)/shard_map/ppermute | solution.py:232
  42.7 0.8 copy-done.2
  43.5 8.5 %collective-permute-done.3.three = bf16[704,256]{1,0:T(8,128)(2,1)} collective-permute-done((bf16[704,256]{1,0:T(8,128)(2,1)S(1)}, bf16[704,256]{1,0:T(8,128)(2,1)}, u32[]{:S(2)}, u32[]{:S(2)}) %collective-permute-start.3) | collective-permute-done | bytes 360480 | tf_op jit(solution)/shard_map/ppermute | solution.py:232
  52.0 1.0 copy-done.3
  53.0 2.0 %shard_map.67.weights = bf16[704,1024]{1,0:T(8,128)(2,1)S(1)} custom-call(s32[3]{0:T(128)S(1)} %pad_add_fusion.place, bf16[1408,256]{1,0:T(8,128)(2,1)} %bitcast.15, bf16[1408,256]{1,0:T(8,128)(2,1)} %bitcast.17, bf16[704,256]{1,0:T(8,128)(2,1)S(1)} %collective-permute-done.1.one, bf16[704,256]{1,0:T(8,128)(2,1)S(1)} %copy-done.3, ...), custom_call_target="tpu_custom_call" | custom-call | flops 40000000000 | tf_op jit(solution)/shard_map/pallas_call | solution.py:29
  55.0 18.2 %all-to-all-done.rows = bf16[32,2,11,8,128]{4,3,2,1,0:T(8,128)(2,1)S(1)} async-done(((bf16[32,2,11,8,128]{4,3,2,1,0:T(8,128)(2,1)}), bf16[32,2,11,8,128]{4,3,2,1,0:T(8,128)(2,1)S(1)}, u32[]{:S(2)}, u32[]{:S(2)}) %all-to-all-start) | async-done | bytes 1441824 | tf_op jit(solution)/shard_map/all_to_all | solution.py:230
  73.2 1.3 %shard_map.69 = bf16[352,704]{1,0:T(8,128)(2,1)S(1)} custom-call(s32[3]{0:T(128)S(1)} %pad_add_fusion.place, bf16[32,2,11,8,128]{4,3,2,1,0:T(8,128)(2,1)S(1)} %all-to-all-done.rows, bf16[704,1024]{1,0:T(8,128)(2,1)S(1)} %shard_map.67.weights), custom_call_target="tpu_custom_call" | custom-call | tf_op jit(solution)/shard_map/pallas_call | solution.py:29
  74.5 1.9 %collective-permute-start.4 = (bf16[352,704]{1,0:T(8,128)(2,1)S(1)}, bf16[352,704]{1,0:T(8,128)(2,1)S(1)}, u32[]{:S(2)}, u32[]{:S(2)}) collective-permute-start(bf16[352,704]{1,0:T(8,128)(2,1)S(1)} %shard_map.69), channel_id=1, source_target_pairs={{0,1},{1,0},{2,3},{3,2},{4,5},{5,4},{6,7},{7,6},{8,9},{9,8},{10,11... | collective-permute-start | bytes 1486856 | tf_op jit(solution)/shard_map/ppermute | solution.py:255
  76.4 1.3 %shard_map.68.mine = f32[352,704]{1,0:T(8,128)S(1)} custom-call(s32[3]{0:T(128)S(1)} %pad_add_fusion.place, bf16[32,2,11,8,128]{4,3,2,1,0:T(8,128)(2,1)S(1)} %all-to-all-done.rows, bf16[704,1024]{1,0:T(8,128)(2,1)S(1)} %shard_map.67.weights), custom_call_target="tpu_custom_call" | custom-call | tf_op jit(solution)/shard_map/pallas_call | solution.py:29
  77.8 0.6 collective-permute-done.4.theirs
  78.6 22.7 %all-gather = bf16[1408,352]{1,0:T(8,128)(2,1)S(1)} all-gather(bf16[352,352]{1,0:T(8,128)(2,1)S(1)} %shard_map.70), channel_id=2, replica_groups=mesh['side'=2,'plane'=32,'chip'=4,'core'=2] {'chip'}, dimensions={0}, use_global_device_ids=true | all-gather | bytes 1239040 | tf_op jit(solution)/shard_map/all_gather | solution.py:265
  101.3 1.9 %collective-permute-start.5 = (bf16[4,352,352]{2,1,0:T(8,128)(2,1)S(1)}, bf16[4,352,352]{2,1,0:T(8,128)(2,1)S(1)}, u32[]{:S(2)}, u32[]{:S(2)}) collective-permute-start(bf16[4,352,352]{2,1,0:T(8,128)(2,1)S(1)} %bitcast.9), channel_id=1, source_target_pairs={{0,1},{1,0},{2,3},{3,2},{4,5},{5,4},{6,7},{7,6},{8,9},{9,8},{10,11... | collective-permute-start | bytes 2973704 | tf_op jit(solution)/shard_map/ppermute | solution.py:266
  103.7 2.1 %collective-permute-done.5.other = bf16[4,352,352]{2,1,0:T(8,128)(2,1)S(1)} collective-permute-done((bf16[4,352,352]{2,1,0:T(8,128)(2,1)S(1)}, bf16[4,352,352]{2,1,0:T(8,128)(2,1)S(1)}, u32[]{:S(2)}, u32[]{:S(2)}) %collective-permute-start.5) | collective-permute-done | bytes 991264 | tf_op jit(solution)/shard_map/ppermute | solution.py:266
  105.9 1.2 shard_map.72
  107.1 22.5 %all_to_all.10.returned = bf16[64,11,2,128]{3,2,1,0:T(2,128)(2,1)S(1)} all-to-all(bf16[64,11,2,128]{3,2,1,0:T(2,128)(2,1)S(1)} %shard_map.72), channel_id=1, replica_groups=mesh['side'=2,'plane'=32,'chip'=4,'core'=2] {'side','plane'}, dimensions={0} | all-to-all | bytes 720896 | tf_op jit(solution)/shard_map/all_to_all | solution.py:276
  129.6 1.3 shard_map.73
  (11 shorter events, 0.9 us)
Async XLA Ops:
  2.1 23.7 %collective-permute-start = (bf16[80,1024]{1,0:T(8,128)(2,1)S(1)}, bf16[80,1024]{1,0:T(8,128)(2,1)S(1)}, u32[]{:S(2)}, u32[]{:S(2)}) collective-permute-start(bf16[80,1024]{1,0:T(8,128)(2,1)S(1)} %get-tuple-element.11.mine), channel_id=1, source_target_pairs={{0,256},{256,0},{1,257},{257,1},{2,258},{258,2},{3,259},{259,3},{4... | collective-permute-start | bytes 491528 | tf_op jit(solution)/shard_map/ppermute | solution.py:208
  6.4 36.3 %collective-permute-start.1 = (bf16[704,256]{1,0:T(8,128)(2,1)S(1)}, bf16[704,256]{1,0:T(8,128)(2,1)S(1)}, u32[]{:S(2)}, u32[]{:S(2)}) collective-permute-start(bf16[704,256]{1,0:T(8,128)(2,1)S(1)} %get-tuple-element.14), channel_id=1, source_target_pairs={{0,2},{2,4},{4,6},{6,0},{1,3},{3,5},{5,7},{7,1},{8,10},{10,12},{12... | collective-permute-start | bytes 1081352 | tf_op jit(solution)/shard_map/ppermute | solution.py:232
  12.5 30.2 %collective-permute-start.2 = (bf16[704,256]{1,0:T(8,128)(2,1)S(1)}, bf16[704,256]{1,0:T(8,128)(2,1)S(1)}, u32[]{:S(2)}, u32[]{:S(2)}) collective-permute-start(bf16[704,256]{1,0:T(8,128)(2,1)S(1)} %get-tuple-element.15), channel_id=1, source_target_pairs={{0,4},{2,6},{4,0},{6,2},{1,5},{3,7},{5,1},{7,3},{8,12},{10,14},{12... | collective-permute-start | bytes 1081352 | tf_op jit(solution)/shard_map/ppermute | solution.py:232
  20.7 31.2 %collective-permute-start.3 = (bf16[704,256]{1,0:T(8,128)(2,1)S(1)}, bf16[704,256]{1,0:T(8,128)(2,1)}, u32[]{:S(2)}, u32[]{:S(2)}) collective-permute-start(bf16[704,256]{1,0:T(8,128)(2,1)S(1)} %get-tuple-element.16), channel_id=1, source_target_pairs={{0,6},{2,0},{4,2},{6,4},{1,7},{3,1},{5,3},{7,5},{8,14},{10,8},{12,... | collective-permute-start | bytes 1081352 | tf_op jit(solution)/shard_map/ppermute | solution.py:232
  28.5 44.7 %all-to-all-start = ((bf16[32,2,11,8,128]{4,3,2,1,0:T(8,128)(2,1)}), bf16[32,2,11,8,128]{4,3,2,1,0:T(8,128)(2,1)S(1)}, u32[]{:S(2)}, u32[]{:S(2)}) async-start(bf16[32,2,11,8,128]{4,3,2,1,0:T(8,128)(2,1)} %shard_map.66), calls=%async_computation | async-start | bytes 2883584 | tf_op jit(solution)/shard_map/all_to_all | solution.py:230
  42.7 0.8 copy-start.2
  52.0 1.0 copy-start.3
  74.5 3.8 %collective-permute-start.4 = (bf16[352,704]{1,0:T(8,128)(2,1)S(1)}, bf16[352,704]{1,0:T(8,128)(2,1)S(1)}, u32[]{:S(2)}, u32[]{:S(2)}) collective-permute-start(bf16[352,704]{1,0:T(8,128)(2,1)S(1)} %shard_map.69), channel_id=1, source_target_pairs={{0,1},{1,0},{2,3},{3,2},{4,5},{5,4},{6,7},{7,6},{8,9},{9,8},{10,11... | collective-permute-start | bytes 1486856 | tf_op jit(solution)/shard_map/ppermute | solution.py:255
  77.8 25.4 %copy-start = (bf16[1,1408,256]{2,1,0:T(8,128)(2,1)S(1)}, bf16[1,1408,256]{2,1,0:T(8,128)(2,1)}, u32[]{:S(2)}) copy-start(bf16[1,1408,256]{2,1,0:T(8,128)(2,1)} %param.11) | copy-start | bytes 2162692
  101.3 4.6 %collective-permute-start.5 = (bf16[4,352,352]{2,1,0:T(8,128)(2,1)S(1)}, bf16[4,352,352]{2,1,0:T(8,128)(2,1)S(1)}, u32[]{:S(2)}, u32[]{:S(2)}) collective-permute-start(bf16[4,352,352]{2,1,0:T(8,128)(2,1)S(1)} %bitcast.9), channel_id=1, source_target_pairs={{0,1},{1,0},{2,3},{3,2},{4,5},{5,4},{6,7},{7,6},{8,9},{9,8},{10,11... | collective-permute-start | bytes 2973704 | tf_op jit(solution)/shard_map/ppermute | solution.py:266
  103.7 25.9 %copy-start.1 = (f32[64,6]{0,1:T(8,128)S(1)}, f32[64,6]{0,1:T(8,128)}, u32[]{:S(2)}) copy-start(f32[64,6]{0,1:T(8,128)} %param.8) | copy-start | bytes 4612

commit v7 on v6

--- a/solution.py
+++ b/solution.py
@@ -15,8 +15,7 @@
 TN = (((0,), (0,)), ((), ()))
 
 
-PICK = 10_000_000_000
-GATHER = 40_000_000_000
+GATHER = 20_000_000_000
 CHIPS = 4
 CORE, CHIP, SIDE = range(3)
 
@@ -225,7 +224,6 @@
         picked_own,
         neighbour,
         scalars=1,
-        flops=PICK,
     )
     received = lax.all_to_all(outgoing, "plane", split_axis=0, concat_axis=0, tiled=True)
     pieces = [

time: 131 us -> 134 us (1.023)
  blocking collectives: 45.2 us -> 50.4 us
  local copies, waits for them, and re-layouts: 1.77 us -> 0.01 us
    all_to_all x1, waiting for transfers between devices: 18.2 us -> 0.01 us  [on_device(): lax.all_to_all(outgoing, 'plane', split_axis=0, concat_axis=0, tiled=True)]
    ppermute x3, waiting for transfers between devices: 12.5 us -> 27.2 us  [on_device(): lax.ppermute(piece, 'chip', [(i, (i + shift) % CHIPS) for i in range(CHIP...]
    all_to_all x1, blocking collectives: 22.5 us -> 26.8 us  [on_device(): lax.all_to_all(produced, ('side', 'plane'), split_axis=0, concat_axis=0,...]
    ppermute x1, waiting for transfers between devices: 0.01 us -> 2.72 us  [on_device(): neighbour = lax.ppermute(mine, 'side', swap)]
    unnamed x8 -> x4, local copies, waits for them, and re-layouts: 1.77 us -> 0.01 us
  transfers between devices with their start and end apart: 7 -> 7, of which waited for: 5 -> 6; matrix products, arithmetic and copies ran while one was open for 0% -> 0% of each run, Pallas kernels for 6% -> 4%
where the time goes in v7:
time: 134 us; the launch traced here: 133 us
  blocking collectives  50.4 us (38%)
  starting transfers between devices  36.5 us (27%)
  waiting for transfers between devices  32.6 us (24%)
  Pallas kernels  13.7 us (10%)
    ppermute x3, waiting for transfers between devices, on_device(): lax.ppermute(piece, 'chip', [(i, (i + shift) % CHIPS) for i in range(CHIP...  27.2 us
    all_to_all x1, blocking collectives, on_device(): lax.all_to_all(produced, ('side', 'plane'), split_axis=0, concat_axis=0,...  26.8 us
    all_gather x1, blocking collectives, on_device(): own = lax.all_gather(hidden, 'chip', axis=0)  23.6 us
    ppermute x3, starting transfers between devices, on_device(): lax.ppermute(piece, 'chip', [(i, (i + shift) % CHIPS) for i in range(CHIP...  18.2 us
    pallas_call x10, Pallas kernels, call(): pl.pallas_call(body, out_shape=outs, in_specs=[SMEM] * scalars + [HBM] *...  13.7 us
    all_to_all x1, starting transfers between devices, on_device(): lax.all_to_all(outgoing, 'plane', split_axis=0, concat_axis=0, tiled=True)  10.2 us
    ppermute x1, starting transfers between devices, on_device(): neighbour = lax.ppermute(mine, 'side', swap)  4.28 us
    ppermute x1, waiting for transfers between devices, on_device(): neighbour = lax.ppermute(mine, 'side', swap)  2.72 us
  transfers between devices with their start and end apart: 7, of which 6 were waited for; matrix products, arithmetic and copies ran while one was open for 0% of the time, Pallas kernels for 4%

profile of v7, /device:TPU:8, one launch (start us, length us, event | category | flops | bytes accessed | tf_op | source)
XLA Modules:
  0.0 133.4 jit_solution(13528647313932826291)
XLA Ops:
  0.1 2.0 %shard_map.64 = (bf16[80,1024]{1,0:T(8,128)(2,1)S(1)}, bf16[704,256]{1,0:T(8,128)(2,1)S(1)}, bf16[704,256]{1,0:T(8,128)(2,1)S(1)}, bf16[704,256]{1,0:T(8,128)(2,1)S(1)}) custom-call(s32[3]{0:T(128)S(1)} %pad_add_fusion.place, s32[6,64]{1,0:T(8,128)} %bitcast.18, bf16[64,2048]{1,0:T(8,128)(2,1)} %tokens_hbm.1, bf16[1408,256]{1,0:T(8,128)(2,1)} %bitcast.14, ...), custom_call_target="tpu_custom_call" | custom-call | tf_op jit(solution)/shard_map/pallas_call | solution.py:28
  2.1 4.3 %collective-permute-start = (bf16[80,1024]{1,0:T(8,128)(2,1)S(1)}, bf16[80,1024]{1,0:T(8,128)(2,1)S(1)}, u32[]{:S(2)}, u32[]{:S(2)}) collective-permute-start(bf16[80,1024]{1,0:T(8,128)(2,1)S(1)} %get-tuple-element.11.mine), channel_id=1, source_target_pairs={{0,256},{256,0},{1,257},{257,1},{2,258},{258,2},{3,259},{259,3},{4... | collective-permute-start | bytes 491528 | tf_op jit(solution)/shard_map/ppermute | solution.py:207
  6.4 1.5 %shard_map.65 = (bf16[32,11,8,128]{3,2,1,0:T(8,128)(2,1)S(1)}, s32[6,64]{1,0:T(8,128)S(1)}) custom-call(s32[3]{0:T(128)S(1)} %pad_add_fusion.place, bf16[80,1024]{1,0:T(8,128)(2,1)S(1)} %get-tuple-element.11.mine), custom_call_target="tpu_custom_call" | custom-call | tf_op jit(solution)/shard_map/pallas_call | solution.py:28
  7.9 2.7 %collective-permute-done.neighbour = bf16[80,1024]{1,0:T(8,128)(2,1)S(1)} collective-permute-done((bf16[80,1024]{1,0:T(8,128)(2,1)S(1)}, bf16[80,1024]{1,0:T(8,128)(2,1)S(1)}, u32[]{:S(2)}, u32[]{:S(2)}) %collective-permute-start) | collective-permute-done | bytes 163872 | tf_op jit(solution)/shard_map/ppermute | solution.py:207
  10.6 2.7 %shard_map.66 = bf16[32,2,11,8,128]{4,3,2,1,0:T(8,128)(2,1)} custom-call(s32[3]{0:T(128)S(1)} %pad_add_fusion.place, bf16[32,11,8,128]{3,2,1,0:T(8,128)(2,1)S(1)} %get-tuple-element.13.own, bf16[80,1024]{1,0:T(8,128)(2,1)S(1)} %collective-permute-done.neighbour), custom_call_target="tpu_custom_call" | custom-call | tf_op jit(solution)/shard_map/pallas_call | solution.py:28
  13.2 10.2 %all-to-all-start = ((bf16[32,2,11,8,128]{4,3,2,1,0:T(8,128)(2,1)}), bf16[32,2,11,8,128]{4,3,2,1,0:T(8,128)(2,1)S(1)}, u32[]{:S(2)}, u32[]{:S(2)}) async-start(bf16[32,2,11,8,128]{4,3,2,1,0:T(8,128)(2,1)} %shard_map.66), calls=%async_computation | async-start | bytes 2883584 | tf_op jit(solution)/shard_map/all_to_all | solution.py:228
  23.4 6.1 %collective-permute-start.1 = (bf16[704,256]{1,0:T(8,128)(2,1)S(1)}, bf16[704,256]{1,0:T(8,128)(2,1)S(1)}, u32[]{:S(2)}, u32[]{:S(2)}) collective-permute-start(bf16[704,256]{1,0:T(8,128)(2,1)S(1)} %get-tuple-element.14), channel_id=1, source_target_pairs={{0,2},{2,4},{4,6},{6,0},{1,3},{3,5},{5,7},{7,1},{8,10},{10,12},{12... | collective-permute-start | bytes 1081352 | tf_op jit(solution)/shard_map/ppermute | solution.py:230
  29.5 8.5 %collective-permute-start.2 = (bf16[704,256]{1,0:T(8,128)(2,1)S(1)}, bf16[704,256]{1,0:T(8,128)(2,1)S(1)}, u32[]{:S(2)}, u32[]{:S(2)}) collective-permute-start(bf16[704,256]{1,0:T(8,128)(2,1)S(1)} %get-tuple-element.15), channel_id=1, source_target_pairs={{0,4},{2,6},{4,0},{6,2},{1,5},{3,7},{5,1},{7,3},{8,12},{10,14},{12... | collective-permute-start | bytes 1081352 | tf_op jit(solution)/shard_map/ppermute | solution.py:230
  38.0 3.7 %collective-permute-start.3 = (bf16[704,256]{1,0:T(8,128)(2,1)S(1)}, bf16[704,256]{1,0:T(8,128)(2,1)S(1)}, u32[]{:S(2)}, u32[]{:S(2)}) collective-permute-start(bf16[704,256]{1,0:T(8,128)(2,1)S(1)} %get-tuple-element.16), channel_id=1, source_target_pairs={{0,6},{2,0},{4,2},{6,4},{1,7},{3,1},{5,3},{7,5},{8,14},{10,8},{12,... | collective-permute-start | bytes 1081352 | tf_op jit(solution)/shard_map/ppermute | solution.py:230
  41.7 3.5 %collective-permute-done.1.one = bf16[704,256]{1,0:T(8,128)(2,1)S(1)} collective-permute-done((bf16[704,256]{1,0:T(8,128)(2,1)S(1)}, bf16[704,256]{1,0:T(8,128)(2,1)S(1)}, u32[]{:S(2)}, u32[]{:S(2)}) %collective-permute-start.1) | collective-permute-done | bytes 360480 | tf_op jit(solution)/shard_map/ppermute | solution.py:230
  45.2 7.2 %collective-permute-done.2.two = bf16[704,256]{1,0:T(8,128)(2,1)S(1)} collective-permute-done((bf16[704,256]{1,0:T(8,128)(2,1)S(1)}, bf16[704,256]{1,0:T(8,128)(2,1)S(1)}, u32[]{:S(2)}, u32[]{:S(2)}) %collective-permute-start.2) | collective-permute-done | bytes 360480 | tf_op jit(solution)/shard_map/ppermute | solution.py:230
  52.5 16.5 %collective-permute-done.3.three = bf16[704,256]{1,0:T(8,128)(2,1)S(1)} collective-permute-done((bf16[704,256]{1,0:T(8,128)(2,1)S(1)}, bf16[704,256]{1,0:T(8,128)(2,1)S(1)}, u32[]{:S(2)}, u32[]{:S(2)}) %collective-permute-start.3) | collective-permute-done | bytes 360480 | tf_op jit(solution)/shard_map/ppermute | solution.py:230
  68.9 1.6 %shard_map.67.weights = bf16[704,1024]{1,0:T(8,128)(2,1)S(1)} custom-call(s32[3]{0:T(128)S(1)} %pad_add_fusion.place, bf16[1408,256]{1,0:T(8,128)(2,1)} %bitcast.15, bf16[1408,256]{1,0:T(8,128)(2,1)} %bitcast.17, bf16[704,256]{1,0:T(8,128)(2,1)S(1)} %collective-permute-done.1.one, bf16[704,256]{1,0:T(8,128)(2,1)S(1)} %collective-permute-done.2.two, ...), custom_call_target="tpu_custom_call" | custom-call | flops 20000000000 | tf_op jit(solution)/shard_map/pallas_call | solution.py:28
  70.5 1.3 shard_map.69
  71.8 1.9 %collective-permute-start.4 = (bf16[352,704]{1,0:T(8,128)(2,1)S(1)}, bf16[352,704]{1,0:T(8,128)(2,1)S(1)}, u32[]{:S(2)}, u32[]{:S(2)}) collective-permute-start(bf16[352,704]{1,0:T(8,128)(2,1)S(1)} %shard_map.69), channel_id=1, source_target_pairs={{0,1},{1,0},{2,3},{3,2},{4,5},{5,4},{6,7},{7,6},{8,9},{9,8},{10,11... | collective-permute-start | bytes 1486856 | tf_op jit(solution)/shard_map/ppermute | solution.py:253
  73.8 1.3 shard_map.68.mine
  75.1 0.5 collective-permute-done.4.theirs
  76.0 23.6 %all-gather = bf16[1408,352]{1,0:T(8,128)(2,1)S(1)} all-gather(bf16[352,352]{1,0:T(8,128)(2,1)S(1)} %shard_map.70), channel_id=2, replica_groups=mesh['side'=2,'plane'=32,'chip'=4,'core'=2] {'chip'}, dimensions={0}, use_global_device_ids=true | all-gather | bytes 1239040 | tf_op jit(solution)/shard_map/all_gather | solution.py:263
  99.6 1.9 %collective-permute-start.5 = (bf16[4,352,352]{2,1,0:T(8,128)(2,1)S(1)}, bf16[4,352,352]{2,1,0:T(8,128)(2,1)S(1)}, u32[]{:S(2)}, u32[]{:S(2)}) collective-permute-start(bf16[4,352,352]{2,1,0:T(8,128)(2,1)S(1)} %bitcast.9), channel_id=1, source_target_pairs={{0,1},{1,0},{2,3},{3,2},{4,5},{5,4},{6,7},{7,6},{8,9},{9,8},{10,11... | collective-permute-start | bytes 2973704 | tf_op jit(solution)/shard_map/ppermute | solution.py:264
  101.5 0.5 shard_map.71.own
  102.0 2.1 %collective-permute-done.5.other = bf16[4,352,352]{2,1,0:T(8,128)(2,1)S(1)} collective-permute-done((bf16[4,352,352]{2,1,0:T(8,128)(2,1)S(1)}, bf16[4,352,352]{2,1,0:T(8,128)(2,1)S(1)}, u32[]{:S(2)}, u32[]{:S(2)}) %collective-permute-start.5) | collective-permute-done | bytes 991264 | tf_op jit(solution)/shard_map/ppermute | solution.py:264
  104.2 1.2 shard_map.72
  105.4 26.8 %all_to_all.10.returned = bf16[64,11,2,128]{3,2,1,0:T(2,128)(2,1)S(1)} all-to-all(bf16[64,11,2,128]{3,2,1,0:T(2,128)(2,1)S(1)} %shard_map.72), channel_id=1, replica_groups=mesh['side'=2,'plane'=32,'chip'=4,'core'=2] {'side','plane'}, dimensions={0} | all-to-all | bytes 720896 | tf_op jit(solution)/shard_map/all_to_all | solution.py:274
  132.1 1.3 shard_map.73
  (7 shorter events, 0.4 us)
Async XLA Ops:
  2.1 8.5 %collective-permute-start = (bf16[80,1024]{1,0:T(8,128)(2,1)S(1)}, bf16[80,1024]{1,0:T(8,128)(2,1)S(1)}, u32[]{:S(2)}, u32[]{:S(2)}) collective-permute-start(bf16[80,1024]{1,0:T(8,128)(2,1)S(1)} %get-tuple-element.11.mine), channel_id=1, source_target_pairs={{0,256},{256,0},{1,257},{257,1},{2,258},{258,2},{3,259},{259,3},{4... | collective-permute-start | bytes 491528 | tf_op jit(solution)/shard_map/ppermute | solution.py:207
  13.2 57.3 %all-to-all-start = ((bf16[32,2,11,8,128]{4,3,2,1,0:T(8,128)(2,1)}), bf16[32,2,11,8,128]{4,3,2,1,0:T(8,128)(2,1)S(1)}, u32[]{:S(2)}, u32[]{:S(2)}) async-start(bf16[32,2,11,8,128]{4,3,2,1,0:T(8,128)(2,1)} %shard_map.66), calls=%async_computation | async-start | bytes 2883584 | tf_op jit(solution)/shard_map/all_to_all | solution.py:228
  23.4 21.8 %collective-permute-start.1 = (bf16[704,256]{1,0:T(8,128)(2,1)S(1)}, bf16[704,256]{1,0:T(8,128)(2,1)S(1)}, u32[]{:S(2)}, u32[]{:S(2)}) collective-permute-start(bf16[704,256]{1,0:T(8,128)(2,1)S(1)} %get-tuple-element.14), channel_id=1, source_target_pairs={{0,2},{2,4},{4,6},{6,0},{1,3},{3,5},{5,7},{7,1},{8,10},{10,12},{12... | collective-permute-start | bytes 1081352 | tf_op jit(solution)/shard_map/ppermute | solution.py:230
  29.5 22.9 %collective-permute-start.2 = (bf16[704,256]{1,0:T(8,128)(2,1)S(1)}, bf16[704,256]{1,0:T(8,128)(2,1)S(1)}, u32[]{:S(2)}, u32[]{:S(2)}) collective-permute-start(bf16[704,256]{1,0:T(8,128)(2,1)S(1)} %get-tuple-element.15), channel_id=1, source_target_pairs={{0,4},{2,6},{4,0},{6,2},{1,5},{3,7},{5,1},{7,3},{8,12},{10,14},{12... | collective-permute-start | bytes 1081352 | tf_op jit(solution)/shard_map/ppermute | solution.py:230
  38.0 30.9 %collective-permute-start.3 = (bf16[704,256]{1,0:T(8,128)(2,1)S(1)}, bf16[704,256]{1,0:T(8,128)(2,1)S(1)}, u32[]{:S(2)}, u32[]{:S(2)}) collective-permute-start(bf16[704,256]{1,0:T(8,128)(2,1)S(1)} %get-tuple-element.16), channel_id=1, source_target_pairs={{0,6},{2,0},{4,2},{6,4},{1,7},{3,1},{5,3},{7,5},{8,14},{10,8},{12,... | collective-permute-start | bytes 1081352 | tf_op jit(solution)/shard_map/ppermute | solution.py:230
  71.8 3.8 %collective-permute-start.4 = (bf16[352,704]{1,0:T(8,128)(2,1)S(1)}, bf16[352,704]{1,0:T(8,128)(2,1)S(1)}, u32[]{:S(2)}, u32[]{:S(2)}) collective-permute-start(bf16[352,704]{1,0:T(8,128)(2,1)S(1)} %shard_map.69), channel_id=1, source_target_pairs={{0,1},{1,0},{2,3},{3,2},{4,5},{5,4},{6,7},{7,6},{8,9},{9,8},{10,11... | collective-permute-start | bytes 1486856 | tf_op jit(solution)/shard_map/ppermute | solution.py:253
  75.1 26.4 %copy-start = (bf16[1,1408,256]{2,1,0:T(8,128)(2,1)S(1)}, bf16[1,1408,256]{2,1,0:T(8,128)(2,1)}, u32[]{:S(2)}) copy-start(bf16[1,1408,256]{2,1,0:T(8,128)(2,1)} %param.11) | copy-start | bytes 2162692
  99.6 4.6 %collective-permute-start.5 = (bf16[4,352,352]{2,1,0:T(8,128)(2,1)S(1)}, bf16[4,352,352]{2,1,0:T(8,128)(2,1)S(1)}, u32[]{:S(2)}, u32[]{:S(2)}) collective-permute-start(bf16[4,352,352]{2,1,0:T(8,128)(2,1)S(1)} %bitcast.9), channel_id=1, source_target_pairs={{0,1},{1,0},{2,3},{3,2},{4,5},{5,4},{6,7},{7,6},{8,9},{9,8},{10,11... | collective-permute-start | bytes 2973704 | tf_op jit(solution)/shard_map/ppermute | solution.py:264
  102.0 30.1 %copy-start.1 = (f32[64,6]{0,1:T(8,128)S(1)}, f32[64,6]{0,1:T(8,128)}, u32[]{:S(2)}) copy-start(f32[64,6]{0,1:T(8,128)} %param.8) | copy-start | bytes 4612

commit v8 on v6

--- a/solution.py
+++ b/solution.py
@@ -15,8 +15,8 @@
 TN = (((0,), (0,)), ((), ()))
 
 
+PACK = 30_000_000_000
 PICK = 10_000_000_000
-GATHER = 40_000_000_000
 CHIPS = 4
 CORE, CHIP, SIDE = range(3)
 
@@ -49,23 +49,32 @@
     return pl.ds(pl.multiple_of(start, 16), share)
 
 
-def first_body(place, routes_hbm, tokens_hbm, w_gate, w_up, mine, one, two, three, routes_t, sems):
+def first_body(place, routes_hbm, tokens_hbm, w_gate, w_up, mine, two, routes_t, sems):
     top, rows = routes_t.shape
     cols = mine.shape[1] // CHIPS
-    share = one.shape[0] // 2
+    share = two.shape[0] // 2
     pairs = [(routes_hbm, routes_t)]
     for shift in range(CHIPS):
         block = lax.rem(place[CHIP] - shift + CHIPS, CHIPS) * 2 + place[CORE]
         columns = pl.ds(pl.multiple_of(block * cols, cols), cols)
         pairs.append((tokens_hbm.at[:, columns], mine.at[:rows, shift * cols : (shift + 1) * cols]))
-    for shift, out in enumerate((one, two, three), 1):
-        pairs.append((w_gate.at[units_of(place, shift, share), :], out.at[:share, :]))
-        pairs.append((w_up.at[units_of(place, shift, share), :], out.at[share:, :]))
+    pairs.append((w_gate.at[units_of(place, 2, share), :], two.at[:share, :]))
+    pairs.append((w_up.at[units_of(place, 2, share), :], two.at[share:, :]))
     copies = copy_all(pairs, sems)
     mine[rows:, :] = jnp.zeros((mine.shape[0] - rows, mine.shape[1]), mine.dtype)
     copies[0].wait()
     mine[rows : rows + top, :rows] = routes_t[...].astype(mine.dtype)
     for copy in copies[1:]:
+        copy.wait()
+
+
+def pack_body(place, w_gate, w_up, _, one, three, sems):
+    share = one.shape[0] // 2
+    pairs = []
+    for shift, out in ((1, one), (3, three)):
+        pairs.append((w_gate.at[units_of(place, shift, share), :], out.at[:share, :]))
+        pairs.append((w_up.at[units_of(place, shift, share), :], out.at[share:, :]))
+    for copy in copy_all(pairs, sems):
         copy.wait()
 
 
@@ -193,9 +202,9 @@
     place = jnp.stack([lax.axis_index(a) for a in ("core", "chip", "side")]).astype(jnp.int32)
 
     part = jax.ShapeDtypeStruct((2 * share, cols), bf16)
-    mine, *pieces = call(
+    mine, two = call(
         first_body,
-        (jax.ShapeDtypeStruct((tok_count + 16, CHIPS * cols), bf16),) + (part,) * (CHIPS - 1),
+        (jax.ShapeDtypeStruct((tok_count + 16, CHIPS * cols), bf16),) + (part,),
         place,
         routes.T,
         tokens,
@@ -203,7 +212,7 @@
         w_up[0],
         scalars=1,
         raw=4,
-        scratch=[pltpu.VMEM((top, tok_count), jnp.int32), dma((1 + CHIPS + 2 * (CHIPS - 1),))],
+        scratch=[pltpu.VMEM((top, tok_count), jnp.int32), dma((3 + CHIPS,))],
     )
     neighbour = lax.ppermute(mine, "side", swap)
     sizes = (top, cap, experts, side)
@@ -228,10 +237,21 @@
         flops=PICK,
     )
     received = lax.all_to_all(outgoing, "plane", split_axis=0, concat_axis=0, tiled=True)
-    pieces = [
-        lax.ppermute(piece, "chip", [(i, (i + shift) % CHIPS) for i in range(CHIPS)])
-        for shift, piece in enumerate(pieces, 1)
-    ]
+    ring = [[(i, (i + shift) % CHIPS) for i in range(CHIPS)] for shift in range(CHIPS)]
+    two = lax.ppermute(two, "chip", ring[2])
+    one, three = call(
+        pack_body,
+        (part, part),
+        place,
+        w_gate[0],
+        w_up[0],
+        two,
+        scalars=1,
+        raw=2,
+        scratch=[dma((4,))],
+        flops=PACK,
+    )
+    pieces = [lax.ppermute(one, "chip", ring[1]), two, lax.ppermute(three, "chip", ring[3])]
     weights = call(
         gather_body,
         jax.ShapeDtypeStruct((2 * share, CHIPS * cols), bf16),
@@ -242,7 +262,6 @@
         scalars=1,
         raw=2,
         scratch=[dma((2,))],
-        flops=GATHER,
     )
     theirs = call(
         functools.partial(gate_up_body, False),

time: 131 us -> 125 us (0.954)
  waiting for transfers between devices: 33.4 us -> 21.7 us
  starting transfers between devices: 36.2 us -> 40.9 us
  local copies, waits for them, and re-layouts: 1.77 us -> 0.01 us
    all_to_all x1, waiting for transfers between devices: 18.2 us -> 7.5 us  [on_device(): lax.all_to_all(outgoing, 'plane', split_axis=0, concat_axis=0, tiled=True)]
    ppermute x3, starting transfers between devices: 18 us -> 22.6 us  [the longest x1 10 us: on_device(): two = lax.ppermute(two, 'chip', ring[2])]
    unnamed x8 -> x4, local copies, waits for them, and re-layouts: 1.77 us -> 0.01 us
    pallas_call x10 -> x11, Pallas kernels: 14.1 us -> 15.1 us  [call(): pl.pallas_call(body, out_shape=outs, in_specs=[SMEM] * scalars + [HBM] *...]
  transfers between devices with their start and end apart: 7 -> 7, of which waited for: 5 -> 5; matrix products, arithmetic and copies ran while one was open for 0% -> 0% of each run, Pallas kernels for 6% -> 8%
where the time goes in v8:
time: 125 us; the launch traced here: 124 us
  blocking collectives  46.1 us (37%)
  starting transfers between devices  40.9 us (33%)
  waiting for transfers between devices  21.7 us (17%)
  Pallas kernels  15.1 us (12%)
    all_gather x1, blocking collectives, on_device(): own = lax.all_gather(hidden, 'chip', axis=0)  23.8 us
    all_to_all x1, blocking collectives, on_device(): lax.all_to_all(produced, ('side', 'plane'), split_axis=0, concat_axis=0,...  22.3 us
    pallas_call x11, Pallas kernels, call(): pl.pallas_call(body, out_shape=outs, in_specs=[SMEM] * scalars + [HBM] *...  15.1 us
    all_to_all x1, starting transfers between devices, on_device(): lax.all_to_all(outgoing, 'plane', split_axis=0, concat_axis=0, tiled=True)  10.2 us
    ppermute x1, starting transfers between devices, on_device(): two = lax.ppermute(two, 'chip', ring[2])  10 us
    ppermute x1, waiting for transfers between devices, on_device(): lax.ppermute(one, 'chip', ring[1])  9.58 us
    all_to_all x1, waiting for transfers between devices, on_device(): lax.all_to_all(outgoing, 'plane', split_axis=0, concat_axis=0, tiled=True)  7.5 us
    ppermute x1, starting transfers between devices, on_device(): lax.ppermute(one, 'chip', ring[1])  7.39 us
  transfers between devices with their start and end apart: 7, of which 5 were waited for; matrix products, arithmetic and copies ran while one was open for 0% of the time, Pallas kernels for 8%

profile of v8, /device:TPU:8, one launch (start us, length us, event | category | flops | bytes accessed | tf_op | source)
XLA Modules:
  0.0 124.1 jit_solution(8008911842539230445)
XLA Ops:
  0.1 1.7 %shard_map.64 = (bf16[80,1024]{1,0:T(8,128)(2,1)S(1)}, bf16[704,256]{1,0:T(8,128)(2,1)S(1)}) custom-call(s32[3]{0:T(128)S(1)} %pad_add_fusion.place, s32[6,64]{1,0:T(8,128)} %bitcast.20, bf16[64,2048]{1,0:T(8,128)(2,1)} %tokens_hbm.1, bf16[1408,256]{1,0:T(8,128)(2,1)} %bitcast.14, bf16[1408,256]{1,0:T(8,128)(2,1)} %bitcast.17), custom_call_target="tpu_custom_call" | custom-call | tf_op jit(solution)/shard_map/pallas_call | solution.py:29
  1.8 4.3 %collective-permute-start = (bf16[80,1024]{1,0:T(8,128)(2,1)S(1)}, bf16[80,1024]{1,0:T(8,128)(2,1)S(1)}, u32[]{:S(2)}, u32[]{:S(2)}) collective-permute-start(bf16[80,1024]{1,0:T(8,128)(2,1)S(1)} %get-tuple-element.11.mine), channel_id=1, source_target_pairs={{0,256},{256,0},{1,257},{257,1},{2,258},{258,2},{3,259},{259,3},{4... | collective-permute-start | bytes 491528 | tf_op jit(solution)/shard_map/ppermute | solution.py:217
  6.1 10.0 %collective-permute-start.1 = (bf16[704,256]{1,0:T(8,128)(2,1)S(1)}, bf16[704,256]{1,0:T(8,128)(2,1)S(1)}, u32[]{:S(2)}, u32[]{:S(2)}) collective-permute-start(bf16[704,256]{1,0:T(8,128)(2,1)S(1)} %get-tuple-element.14), channel_id=1, source_target_pairs={{0,4},{2,6},{4,0},{6,2},{1,5},{3,7},{5,1},{7,3},{8,12},{10,14},{12... | collective-permute-start | bytes 1081352 | tf_op jit(solution)/shard_map/ppermute | solution.py:241
  16.1 1.5 %shard_map.65 = (bf16[32,11,8,128]{3,2,1,0:T(8,128)(2,1)S(1)}, s32[6,64]{1,0:T(8,128)S(1)}) custom-call(s32[3]{0:T(128)S(1)} %pad_add_fusion.place, bf16[80,1024]{1,0:T(8,128)(2,1)S(1)} %get-tuple-element.11.mine), custom_call_target="tpu_custom_call" | custom-call | tf_op jit(solution)/shard_map/pallas_call | solution.py:29
  17.6 2.7 %shard_map.66 = bf16[32,2,11,8,128]{4,3,2,1,0:T(8,128)(2,1)} custom-call(s32[3]{0:T(128)S(1)} %pad_add_fusion.place, bf16[32,11,8,128]{3,2,1,0:T(8,128)(2,1)S(1)} %get-tuple-element.13.own, bf16[80,1024]{1,0:T(8,128)(2,1)S(1)} %collective-permute-done.neighbour), custom_call_target="tpu_custom_call" | custom-call | flops 10000000000 | tf_op jit(solution)/shard_map/pallas_call | solution.py:29
  20.2 10.2 %all-to-all-start = ((bf16[32,2,11,8,128]{4,3,2,1,0:T(8,128)(2,1)}), bf16[32,2,11,8,128]{4,3,2,1,0:T(8,128)(2,1)S(1)}, u32[]{:S(2)}, u32[]{:S(2)}) async-start(bf16[32,2,11,8,128]{4,3,2,1,0:T(8,128)(2,1)} %shard_map.66), calls=%async_computation | async-start | bytes 2883584 | tf_op jit(solution)/shard_map/all_to_all | solution.py:239
  30.4 1.8 %shard_map.67 = (bf16[704,256]{1,0:T(8,128)(2,1)S(1)}, bf16[704,256]{1,0:T(8,128)(2,1)S(1)}) custom-call(s32[3]{0:T(128)S(1)} %pad_add_fusion.place, bf16[1408,256]{1,0:T(8,128)(2,1)} %bitcast.15, bf16[1408,256]{1,0:T(8,128)(2,1)} %bitcast.18, bf16[704,256]{1,0:T(8,128)(2,1)S(1)} %collective-permute-done.1._.two), custom_call_target="tpu_custom_call" | custom-call | flops 30000001024 | tf_op jit(solution)/shard_map/pallas_call | solution.py:29
  32.2 7.4 %collective-permute-start.2 = (bf16[704,256]{1,0:T(8,128)(2,1)S(1)}, bf16[704,256]{1,0:T(8,128)(2,1)S(1)}, u32[]{:S(2)}, u32[]{:S(2)}) collective-permute-start(bf16[704,256]{1,0:T(8,128)(2,1)S(1)} %get-tuple-element.15), channel_id=1, source_target_pairs={{0,2},{2,4},{4,6},{6,0},{1,3},{3,5},{5,7},{7,1},{8,10},{10,12},{12... | collective-permute-start | bytes 1081352 | tf_op jit(solution)/shard_map/ppermute | solution.py:254
  39.6 5.2 %collective-permute-start.3 = (bf16[704,256]{1,0:T(8,128)(2,1)S(1)}, bf16[704,256]{1,0:T(8,128)(2,1)S(1)}, u32[]{:S(2)}, u32[]{:S(2)}) collective-permute-start(bf16[704,256]{1,0:T(8,128)(2,1)S(1)} %get-tuple-element.16), channel_id=1, source_target_pairs={{0,6},{2,0},{4,2},{6,4},{1,7},{3,1},{5,3},{7,5},{8,14},{10,8},{12,... | collective-permute-start | bytes 1081352 | tf_op jit(solution)/shard_map/ppermute | solution.py:254
  44.8 9.6 %collective-permute-done.2.one = bf16[704,256]{1,0:T(8,128)(2,1)S(1)} collective-permute-done((bf16[704,256]{1,0:T(8,128)(2,1)S(1)}, bf16[704,256]{1,0:T(8,128)(2,1)S(1)}, u32[]{:S(2)}, u32[]{:S(2)}) %collective-permute-start.2) | collective-permute-done | bytes 360480 | tf_op jit(solution)/shard_map/ppermute | solution.py:254
  54.4 2.0 %collective-permute-done.3.three = bf16[704,256]{1,0:T(8,128)(2,1)S(1)} collective-permute-done((bf16[704,256]{1,0:T(8,128)(2,1)S(1)}, bf16[704,256]{1,0:T(8,128)(2,1)S(1)}, u32[]{:S(2)}, u32[]{:S(2)}) %collective-permute-start.3) | collective-permute-done | bytes 360480 | tf_op jit(solution)/shard_map/ppermute | solution.py:254
  56.4 1.6 %shard_map.68.weights = bf16[704,1024]{1,0:T(8,128)(2,1)S(1)} custom-call(s32[3]{0:T(128)S(1)} %pad_add_fusion.place, bf16[1408,256]{1,0:T(8,128)(2,1)} %bitcast.16, bf16[1408,256]{1,0:T(8,128)(2,1)} %bitcast.19, bf16[704,256]{1,0:T(8,128)(2,1)S(1)} %collective-permute-done.2.one, bf16[704,256]{1,0:T(8,128)(2,1)S(1)} %collective-permute-done.1._.two, ...), custom_call_target="tpu_custom_call" | custom-call | tf_op jit(solution)/shard_map/pallas_call | solution.py:29
  58.0 7.5 %all-to-all-done.rows = bf16[32,2,11,8,128]{4,3,2,1,0:T(8,128)(2,1)S(1)} async-done(((bf16[32,2,11,8,128]{4,3,2,1,0:T(8,128)(2,1)}), bf16[32,2,11,8,128]{4,3,2,1,0:T(8,128)(2,1)S(1)}, u32[]{:S(2)}, u32[]{:S(2)}) %all-to-all-start) | async-done | bytes 1441824 | tf_op jit(solution)/shard_map/all_to_all | solution.py:239
  65.5 1.3 %shard_map.70 = bf16[352,704]{1,0:T(8,128)(2,1)S(1)} custom-call(s32[3]{0:T(128)S(1)} %pad_add_fusion.place, bf16[32,2,11,8,128]{4,3,2,1,0:T(8,128)(2,1)S(1)} %all-to-all-done.rows, bf16[704,1024]{1,0:T(8,128)(2,1)S(1)} %shard_map.68.weights), custom_call_target="tpu_custom_call" | custom-call | tf_op jit(solution)/shard_map/pallas_call | solution.py:29
  66.8 1.9 %collective-permute-start.4 = (bf16[352,704]{1,0:T(8,128)(2,1)S(1)}, bf16[352,704]{1,0:T(8,128)(2,1)S(1)}, u32[]{:S(2)}, u32[]{:S(2)}) collective-permute-start(bf16[352,704]{1,0:T(8,128)(2,1)S(1)} %shard_map.70), channel_id=1, source_target_pairs={{0,1},{1,0},{2,3},{3,2},{4,5},{5,4},{6,7},{7,6},{8,9},{9,8},{10,11... | collective-permute-start | bytes 1486856 | tf_op jit(solution)/shard_map/ppermute | solution.py:274
  68.7 1.3 %shard_map.69.mine = f32[352,704]{1,0:T(8,128)S(1)} custom-call(s32[3]{0:T(128)S(1)} %pad_add_fusion.place, bf16[32,2,11,8,128]{4,3,2,1,0:T(8,128)(2,1)S(1)} %all-to-all-done.rows, bf16[704,1024]{1,0:T(8,128)(2,1)S(1)} %shard_map.68.weights), custom_call_target="tpu_custom_call" | custom-call | tf_op jit(solution)/shard_map/pallas_call | solution.py:29
  70.1 0.6 collective-permute-done.4.theirs
  70.9 23.8 %all-gather = bf16[1408,352]{1,0:T(8,128)(2,1)S(1)} all-gather(bf16[352,352]{1,0:T(8,128)(2,1)S(1)} %shard_map.71), channel_id=2, replica_groups=mesh['side'=2,'plane'=32,'chip'=4,'core'=2] {'chip'}, dimensions={0}, use_global_device_ids=true | all-gather | bytes 1239040 | tf_op jit(solution)/shard_map/all_gather | solution.py:284
  94.7 1.9 %collective-permute-start.5 = (bf16[4,352,352]{2,1,0:T(8,128)(2,1)S(1)}, bf16[4,352,352]{2,1,0:T(8,128)(2,1)S(1)}, u32[]{:S(2)}, u32[]{:S(2)}) collective-permute-start(bf16[4,352,352]{2,1,0:T(8,128)(2,1)S(1)} %bitcast.9), channel_id=1, source_target_pairs={{0,1},{1,0},{2,3},{3,2},{4,5},{5,4},{6,7},{7,6},{8,9},{9,8},{10,11... | collective-permute-start | bytes 2973704 | tf_op jit(solution)/shard_map/ppermute | solution.py:285
  96.6 0.5 shard_map.72.own
  97.1 2.1 %collective-permute-done.5.other = bf16[4,352,352]{2,1,0:T(8,128)(2,1)S(1)} collective-permute-done((bf16[4,352,352]{2,1,0:T(8,128)(2,1)S(1)}, bf16[4,352,352]{2,1,0:T(8,128)(2,1)S(1)}, u32[]{:S(2)}, u32[]{:S(2)}) %collective-permute-start.5) | collective-permute-done | bytes 991264 | tf_op jit(solution)/shard_map/ppermute | solution.py:285
  99.3 1.2 shard_map.73
  100.5 22.3 %all_to_all.10.returned = bf16[64,11,2,128]{3,2,1,0:T(2,128)(2,1)S(1)} all-to-all(bf16[64,11,2,128]{3,2,1,0:T(2,128)(2,1)S(1)} %shard_map.73), channel_id=1, replica_groups=mesh['side'=2,'plane'=32,'chip'=4,'core'=2] {'side','plane'}, dimensions={0} | all-to-all | bytes 720896 | tf_op jit(solution)/shard_map/all_to_all | solution.py:295
  122.8 1.3 %shard_map.74 = bf16[64,256]{1,0:T(8,128)(2,1)} custom-call(s32[6,64]{1,0:T(8,128)S(1)} %get-tuple-element.12.target_t, f32[6,64]{1,0:T(8,128)S(1)} %bitcast.13, bf16[64,11,2,128]{3,2,1,0:T(2,128)(2,1)S(1)} %all_to_all.10.returned), custom_call_target="tpu_custom_call" | custom-call | tf_op jit(solution)/shard_map/pallas_call | solution.py:29
  (8 shorter events, 0.4 us)
Async XLA Ops:
  1.8 15.8 %collective-permute-start = (bf16[80,1024]{1,0:T(8,128)(2,1)S(1)}, bf16[80,1024]{1,0:T(8,128)(2,1)S(1)}, u32[]{:S(2)}, u32[]{:S(2)}) collective-permute-start(bf16[80,1024]{1,0:T(8,128)(2,1)S(1)} %get-tuple-element.11.mine), channel_id=1, source_target_pairs={{0,256},{256,0},{1,257},{257,1},{2,258},{258,2},{3,259},{259,3},{4... | collective-permute-start | bytes 491528 | tf_op jit(solution)/shard_map/ppermute | solution.py:217
  6.1 24.3 %collective-permute-start.1 = (bf16[704,256]{1,0:T(8,128)(2,1)S(1)}, bf16[704,256]{1,0:T(8,128)(2,1)S(1)}, u32[]{:S(2)}, u32[]{:S(2)}) collective-permute-start(bf16[704,256]{1,0:T(8,128)(2,1)S(1)} %get-tuple-element.14), channel_id=1, source_target_pairs={{0,4},{2,6},{4,0},{6,2},{1,5},{3,7},{5,1},{7,3},{8,12},{10,14},{12... | collective-permute-start | bytes 1081352 | tf_op jit(solution)/shard_map/ppermute | solution.py:241
  20.2 45.2 %all-to-all-start = ((bf16[32,2,11,8,128]{4,3,2,1,0:T(8,128)(2,1)}), bf16[32,2,11,8,128]{4,3,2,1,0:T(8,128)(2,1)S(1)}, u32[]{:S(2)}, u32[]{:S(2)}) async-start(bf16[32,2,11,8,128]{4,3,2,1,0:T(8,128)(2,1)} %shard_map.66), calls=%async_computation | async-start | bytes 2883584 | tf_op jit(solution)/shard_map/all_to_all | solution.py:239
  32.2 22.2 %collective-permute-start.2 = (bf16[704,256]{1,0:T(8,128)(2,1)S(1)}, bf16[704,256]{1,0:T(8,128)(2,1)S(1)}, u32[]{:S(2)}, u32[]{:S(2)}) collective-permute-start(bf16[704,256]{1,0:T(8,128)(2,1)S(1)} %get-tuple-element.15), channel_id=1, source_target_pairs={{0,2},{2,4},{4,6},{6,0},{1,3},{3,5},{5,7},{7,1},{8,10},{10,12},{12... | collective-permute-start | bytes 1081352 | tf_op jit(solution)/shard_map/ppermute | solution.py:254
  39.6 16.8 %collective-permute-start.3 = (bf16[704,256]{1,0:T(8,128)(2,1)S(1)}, bf16[704,256]{1,0:T(8,128)(2,1)S(1)}, u32[]{:S(2)}, u32[]{:S(2)}) collective-permute-start(bf16[704,256]{1,0:T(8,128)(2,1)S(1)} %get-tuple-element.16), channel_id=1, source_target_pairs={{0,6},{2,0},{4,2},{6,4},{1,7},{3,1},{5,3},{7,5},{8,14},{10,8},{12,... | collective-permute-start | bytes 1081352 | tf_op jit(solution)/shard_map/ppermute | solution.py:254
  66.8 3.8 %collective-permute-start.4 = (bf16[352,704]{1,0:T(8,128)(2,1)S(1)}, bf16[352,704]{1,0:T(8,128)(2,1)S(1)}, u32[]{:S(2)}, u32[]{:S(2)}) collective-permute-start(bf16[352,704]{1,0:T(8,128)(2,1)S(1)} %shard_map.70), channel_id=1, source_target_pairs={{0,1},{1,0},{2,3},{3,2},{4,5},{5,4},{6,7},{7,6},{8,9},{9,8},{10,11... | collective-permute-start | bytes 1486856 | tf_op jit(solution)/shard_map/ppermute | solution.py:274
  70.1 26.5 %copy-start = (bf16[1,1408,256]{2,1,0:T(8,128)(2,1)S(1)}, bf16[1,1408,256]{2,1,0:T(8,128)(2,1)}, u32[]{:S(2)}) copy-start(bf16[1,1408,256]{2,1,0:T(8,128)(2,1)} %param.11) | copy-start | bytes 2162692
  94.7 4.6 %collective-permute-start.5 = (bf16[4,352,352]{2,1,0:T(8,128)(2,1)S(1)}, bf16[4,352,352]{2,1,0:T(8,128)(2,1)S(1)}, u32[]{:S(2)}, u32[]{:S(2)}) collective-permute-start(bf16[4,352,352]{2,1,0:T(8,128)(2,1)S(1)} %bitcast.9), channel_id=1, source_target_pairs={{0,1},{1,0},{2,3},{3,2},{4,5},{5,4},{6,7},{7,6},{8,9},{9,8},{10,11... | collective-permute-start | bytes 2973704 | tf_op jit(solution)/shard_map/ppermute | solution.py:285
  97.1 25.7 %copy-start.1 = (f32[64,6]{0,1:T(8,128)S(1)}, f32[64,6]{0,1:T(8,128)}, u32[]{:S(2)}) copy-start(f32[64,6]{0,1:T(8,128)} %param.8) | copy-start | bytes 4612

commit v9 on v6

--- a/solution.py
+++ b/solution.py
@@ -15,8 +15,8 @@
 TN = (((0,), (0,)), ((), ()))
 
 
+HOLD = 30_000_000_000
 PICK = 10_000_000_000
-GATHER = 40_000_000_000
 CHIPS = 4
 CORE, CHIP, SIDE = range(3)
 
@@ -49,16 +49,17 @@
     return pl.ds(pl.multiple_of(start, 16), share)
 
 
-def first_body(place, routes_hbm, tokens_hbm, w_gate, w_up, mine, one, two, three, routes_t, sems):
+def first_body(place, routes_hbm, tokens_hbm, w_gate, w_up, mine, *refs):
+    *pieces, routes_t, sems = refs
     top, rows = routes_t.shape
     cols = mine.shape[1] // CHIPS
-    share = one.shape[0] // 2
+    share = pieces[0].shape[0] // 2
     pairs = [(routes_hbm, routes_t)]
     for shift in range(CHIPS):
         block = lax.rem(place[CHIP] - shift + CHIPS, CHIPS) * 2 + place[CORE]
         columns = pl.ds(pl.multiple_of(block * cols, cols), cols)
         pairs.append((tokens_hbm.at[:, columns], mine.at[:rows, shift * cols : (shift + 1) * cols]))
-    for shift, out in enumerate((one, two, three), 1):
+    for shift, out in enumerate(pieces, 1):
         pairs.append((w_gate.at[units_of(place, shift, share), :], out.at[:share, :]))
         pairs.append((w_up.at[units_of(place, shift, share), :], out.at[share:, :]))
     copies = copy_all(pairs, sems)
@@ -66,6 +67,19 @@
     copies[0].wait()
     mine[rows : rows + top, :rows] = routes_t[...].astype(mine.dtype)
     for copy in copies[1:]:
+        copy.wait()
+
+
+def hold_body(place, w_gate, w_up, one, three, _, here, one_out, three_out, sems):
+    share = here.shape[0] // 2
+    pairs = [
+        (w.at[units_of(place, 0, share), :], here.at[n * share : (n + 1) * share, :])
+        for n, w in enumerate((w_gate, w_up))
+    ]
+    copies = copy_all(pairs, sems)
+    one_out[...] = one[...]
+    three_out[...] = three[...]
+    for copy in copies:
         copy.wait()
 
 
@@ -101,31 +115,24 @@
     outgoing[:, place[SIDE]] = own[...]
 
 
-def gather_body(place, w_gate, w_up, one, two, three, weights, sems):
-    both, cols = one.shape
-    share = both // 2
-    copies = copy_all(
-        [
-            (w.at[units_of(place, 0, share), :], weights.at[n * share : (n + 1) * share, :cols])
-            for n, w in enumerate((w_gate, w_up))
-        ],
-        sems,
-    )
-    for shift, piece in enumerate((one, two, three), 1):
-        weights[:, shift * cols : (shift + 1) * cols] = piece[...]
-    for copy in copies:
-        copy.wait()
-
-
-def gate_up_body(mine, place, rows, weights, out):
-    half = out.shape[0]
+def gate_up_body(mine, place, rows, *refs):
+    *weights, out = refs
+    half, cols = out.shape[0], weights[0].shape[1]
     for core in range(2):
         start = (core if mine else 1 - core) * (rows.shape[0] // 2)
 
         @pl.when(place[CORE] == core)
         def _():
-            flat = rows[start : start + rows.shape[0] // 2].reshape(half, weights.shape[1])
-            total = lax.dot_general(flat, weights[...], NT, preferred_element_type=jnp.float32)
+            flat = rows[start : start + rows.shape[0] // 2].reshape(half, CHIPS * cols)
+            total = functools.reduce(
+                jnp.add,
+                [
+                    lax.dot_general(
+                        flat[:, n * cols : (n + 1) * cols], w[...], NT, preferred_element_type=jnp.float32
+                    )
+                    for n, w in enumerate(weights)
+                ],
+            )
             out[...] = total.astype(out.dtype)
 
 
@@ -193,7 +200,7 @@
     place = jnp.stack([lax.axis_index(a) for a in ("core", "chip", "side")]).astype(jnp.int32)
 
     part = jax.ShapeDtypeStruct((2 * share, cols), bf16)
-    mine, *pieces = call(
+    mine, one, two, three = call(
         first_body,
         (jax.ShapeDtypeStruct((tok_count + 16, CHIPS * cols), bf16),) + (part,) * (CHIPS - 1),
         place,
@@ -203,7 +210,7 @@
         w_up[0],
         scalars=1,
         raw=4,
-        scratch=[pltpu.VMEM((top, tok_count), jnp.int32), dma((1 + CHIPS + 2 * (CHIPS - 1),))],
+        scratch=[pltpu.VMEM((top, tok_count), jnp.int32), dma((3 * CHIPS - 1,))],
     )
     neighbour = lax.ppermute(mine, "side", swap)
     sizes = (top, cap, experts, side)
@@ -228,28 +235,31 @@
         flops=PICK,
     )
     received = lax.all_to_all(outgoing, "plane", split_axis=0, concat_axis=0, tiled=True)
-    pieces = [
-        lax.ppermute(piece, "chip", [(i, (i + shift) % CHIPS) for i in range(CHIPS)])
-        for shift, piece in enumerate(pieces, 1)
-    ]
-    weights = call(
-        gather_body,
-        jax.ShapeDtypeStruct((2 * share, CHIPS * cols), bf16),
+    ring = [[(i, (i + shift) % CHIPS) for i in range(CHIPS)] for shift in range(CHIPS)]
+    two = lax.ppermute(two, "chip", ring[2])
+    here, one, three = call(
+        hold_body,
+        (part,) * 3,
         place,
         w_gate[0],
         w_up[0],
-        *pieces,
+        one,
+        three,
+        two,
         scalars=1,
         raw=2,
         scratch=[dma((2,))],
-        flops=GATHER,
-    )
+        flops=HOLD,
+    )
+    one = lax.ppermute(one, "chip", ring[1])
+    three = lax.ppermute(three, "chip", ring[3])
+    weights = (here, one, two, three)
     theirs = call(
         functools.partial(gate_up_body, False),
         jax.ShapeDtypeStruct((half, 2 * share), bf16),
         place,
         received,
-        weights,
+        *weights,
         scalars=1,
     )
     theirs = lax.ppermute(theirs, "core", swap)
@@ -258,7 +268,7 @@
         jax.ShapeDtypeStruct((half, 2 * share), jnp.float32),
         place,
         received,
-        weights,
+        *weights,
         scalars=1,
     )
     hidden = call(hidden_body, jax.ShapeDtypeStruct((half, share), bf16), mine, theirs)

time: 131 us -> 125 us (0.954)
  waiting for transfers between devices: 33.4 us -> 23.5 us
  starting transfers between devices: 36.2 us -> 40.9 us
  local copies, waits for them, and re-layouts: 1.77 us -> 0.01 us
    all_to_all x1, waiting for transfers between devices: 18.2 us -> 9.27 us  [on_device(): lax.all_to_all(outgoing, 'plane', split_axis=0, concat_axis=0, tiled=True)]
    ppermute x3, starting transfers between devices: 18 us -> 22.6 us  [the longest x1 10 us: on_device(): two = lax.ppermute(two, 'chip', ring[2])]
    unnamed x8 -> x4, local copies, waits for them, and re-layouts: 1.77 us -> 0.01 us
where the time goes in v9:
time: 125 us; the launch traced here: 124 us
  blocking collectives  45.9 us (37%)
  starting transfers between devices  40.9 us (33%)
  waiting for transfers between devices  23.5 us (19%)
  Pallas kernels  13.6 us (11%)
    all_gather x1, blocking collectives, on_device(): own = lax.all_gather(hidden, 'chip', axis=0)  23.9 us
    all_to_all x1, blocking collectives, on_device(): lax.all_to_all(produced, ('side', 'plane'), split_axis=0, concat_axis=0,...  22 us
    pallas_call x10, Pallas kernels, call(): pl.pallas_call(body, out_shape=outs, in_specs=[SMEM] * scalars + [HBM] *...  13.6 us
    all_to_all x1, starting transfers between devices, on_device(): lax.all_to_all(outgoing, 'plane', split_axis=0, concat_axis=0, tiled=True)  10.2 us
    ppermute x1, starting transfers between devices, on_device(): two = lax.ppermute(two, 'chip', ring[2])  10 us
    ppermute x1, waiting for transfers between devices, on_device(): one = lax.ppermute(one, 'chip', ring[1])  9.57 us
    all_to_all x1, waiting for transfers between devices, on_device(): lax.all_to_all(outgoing, 'plane', split_axis=0, concat_axis=0, tiled=True)  9.27 us
    ppermute x1, starting transfers between devices, on_device(): one = lax.ppermute(one, 'chip', ring[1])  7.39 us
  transfers between devices with their start and end apart: 7, of which 5 were waited for; matrix products, arithmetic and copies ran while one was open for 0% of the time, Pallas kernels for 6%

profile of v9, /device:TPU:8, one launch (start us, length us, event | category | flops | bytes accessed | tf_op | source)
XLA Modules:
  0.0 124.3 jit_solution(11616578523088502398)
XLA Ops:
  0.1 2.0 %shard_map.64 = (bf16[80,1024]{1,0:T(8,128)(2,1)S(1)}, bf16[704,256]{1,0:T(8,128)(2,1)S(1)}, bf16[704,256]{1,0:T(8,128)(2,1)S(1)}, bf16[704,256]{1,0:T(8,128)(2,1)S(1)}) custom-call(s32[3]{0:T(128)S(1)} %pad_add_fusion.place, s32[6,64]{1,0:T(8,128)} %bitcast.18, bf16[64,2048]{1,0:T(8,128)(2,1)} %tokens_hbm.1, bf16[1408,256]{1,0:T(8,128)(2,1)} %bitcast.14, ...), custom_call_target="tpu_custom_call" | custom-call | tf_op jit(solution)/shard_map/pallas_call | solution.py:29
  2.1 4.3 %collective-permute-start = (bf16[80,1024]{1,0:T(8,128)(2,1)S(1)}, bf16[80,1024]{1,0:T(8,128)(2,1)S(1)}, u32[]{:S(2)}, u32[]{:S(2)}) collective-permute-start(bf16[80,1024]{1,0:T(8,128)(2,1)S(1)} %get-tuple-element.14.mine), channel_id=1, source_target_pairs={{0,256},{256,0},{1,257},{257,1},{2,258},{258,2},{3,259},{259,3},{4... | collective-permute-start | bytes 491528 | tf_op jit(solution)/shard_map/ppermute | solution.py:215
  6.4 10.0 %collective-permute-start.1 = (bf16[704,256]{1,0:T(8,128)(2,1)S(1)}, bf16[704,256]{1,0:T(8,128)(2,1)S(1)}, u32[]{:S(2)}, u32[]{:S(2)}) collective-permute-start(bf16[704,256]{1,0:T(8,128)(2,1)S(1)} %get-tuple-element.19), channel_id=1, source_target_pairs={{0,4},{2,6},{4,0},{6,2},{1,5},{3,7},{5,1},{7,3},{8,12},{10,14},{12... | collective-permute-start | bytes 1081352 | tf_op jit(solution)/shard_map/ppermute | solution.py:239
  16.4 1.5 %shard_map.65 = (bf16[32,11,8,128]{3,2,1,0:T(8,128)(2,1)S(1)}, s32[6,64]{1,0:T(8,128)S(1)}) custom-call(s32[3]{0:T(128)S(1)} %pad_add_fusion.place, bf16[80,1024]{1,0:T(8,128)(2,1)S(1)} %get-tuple-element.14.mine), custom_call_target="tpu_custom_call" | custom-call | tf_op jit(solution)/shard_map/pallas_call | solution.py:29
  17.9 2.7 %shard_map.66 = bf16[32,2,11,8,128]{4,3,2,1,0:T(8,128)(2,1)} custom-call(s32[3]{0:T(128)S(1)} %pad_add_fusion.place, bf16[32,11,8,128]{3,2,1,0:T(8,128)(2,1)S(1)} %get-tuple-element.16.own, bf16[80,1024]{1,0:T(8,128)(2,1)S(1)} %collective-permute-done.neighbour), custom_call_target="tpu_custom_call" | custom-call | flops 10000000000 | tf_op jit(solution)/shard_map/pallas_call | solution.py:29
  20.6 10.2 %all-to-all-start = ((bf16[32,2,11,8,128]{4,3,2,1,0:T(8,128)(2,1)}), bf16[32,2,11,8,128]{4,3,2,1,0:T(8,128)(2,1)S(1)}, u32[]{:S(2)}, u32[]{:S(2)}) async-start(bf16[32,2,11,8,128]{4,3,2,1,0:T(8,128)(2,1)} %shard_map.66), calls=%async_computation | async-start | bytes 2883584 | tf_op jit(solution)/shard_map/all_to_all | solution.py:237
  30.7 1.6 %shard_map.67 = (bf16[704,256]{1,0:T(8,128)(2,1)S(1)}, bf16[704,256]{1,0:T(8,128)(2,1)S(1)}, bf16[704,256]{1,0:T(8,128)(2,1)S(1)}) custom-call(s32[3]{0:T(128)S(1)} %pad_add_fusion.place, bf16[1408,256]{1,0:T(8,128)(2,1)} %bitcast.15, bf16[1408,256]{1,0:T(8,128)(2,1)} %bitcast.17, bf16[704,256]{1,0:T(8,128)(2,1)S(1)} %get-tuple-element.17.one, ...), custom_call_target="tpu_custom_call" | custom-call | flops 30000001024 | tf_op jit(solution)/shard_map/pallas_call | solution.py:29
  32.3 7.4 %collective-permute-start.2 = (bf16[704,256]{1,0:T(8,128)(2,1)S(1)}, bf16[704,256]{1,0:T(8,128)(2,1)S(1)}, u32[]{:S(2)}, u32[]{:S(2)}) collective-permute-start(bf16[704,256]{1,0:T(8,128)(2,1)S(1)} %get-tuple-element.21), channel_id=1, source_target_pairs={{0,2},{2,4},{4,6},{6,0},{1,3},{3,5},{5,7},{7,1},{8,10},{10,12},{12... | collective-permute-start | bytes 1081352 | tf_op jit(solution)/shard_map/ppermute | solution.py:254
  39.7 5.2 %collective-permute-start.3 = (bf16[704,256]{1,0:T(8,128)(2,1)S(1)}, bf16[704,256]{1,0:T(8,128)(2,1)S(1)}, u32[]{:S(2)}, u32[]{:S(2)}) collective-permute-start(bf16[704,256]{1,0:T(8,128)(2,1)S(1)} %get-tuple-element.22), channel_id=1, source_target_pairs={{0,6},{2,0},{4,2},{6,4},{1,7},{3,1},{5,3},{7,5},{8,14},{10,8},{12,... | collective-permute-start | bytes 1081352 | tf_op jit(solution)/shard_map/ppermute | solution.py:255
  45.0 9.6 %collective-permute-done.2.refs_1_ = bf16[704,256]{1,0:T(8,128)(2,1)S(1)} collective-permute-done((bf16[704,256]{1,0:T(8,128)(2,1)S(1)}, bf16[704,256]{1,0:T(8,128)(2,1)S(1)}, u32[]{:S(2)}, u32[]{:S(2)}) %collective-permute-start.2) | collective-permute-done | bytes 360480 | tf_op jit(solution)/shard_map/ppermute | solution.py:254
  54.5 2.0 %collective-permute-done.3.refs_3_ = bf16[704,256]{1,0:T(8,128)(2,1)S(1)} collective-permute-done((bf16[704,256]{1,0:T(8,128)(2,1)S(1)}, bf16[704,256]{1,0:T(8,128)(2,1)S(1)}, u32[]{:S(2)}, u32[]{:S(2)}) %collective-permute-start.3) | collective-permute-done | bytes 360480 | tf_op jit(solution)/shard_map/ppermute | solution.py:255
  56.5 9.3 %all-to-all-done.rows = bf16[32,2,11,8,128]{4,3,2,1,0:T(8,128)(2,1)S(1)} async-done(((bf16[32,2,11,8,128]{4,3,2,1,0:T(8,128)(2,1)}), bf16[32,2,11,8,128]{4,3,2,1,0:T(8,128)(2,1)S(1)}, u32[]{:S(2)}, u32[]{:S(2)}) %all-to-all-start) | async-done | bytes 1441824 | tf_op jit(solution)/shard_map/all_to_all | solution.py:237
  65.8 1.3 %shard_map.69 = bf16[352,704]{1,0:T(8,128)(2,1)S(1)} custom-call(s32[3]{0:T(128)S(1)} %pad_add_fusion.place, bf16[32,2,11,8,128]{4,3,2,1,0:T(8,128)(2,1)S(1)} %all-to-all-done.rows, bf16[704,256]{1,0:T(8,128)(2,1)S(1)} %get-tuple-element.20.refs_0_, bf16[704,256]{1,0:T(8,128)(2,1)S(1)} %collective-permute-done.2.refs_1_, ...), custom_call_target="tpu_custom_call" | custom-call | tf_op jit(solution)/shard_map/pallas_call | solution.py:29
  67.1 1.9 %collective-permute-start.4 = (bf16[352,704]{1,0:T(8,128)(2,1)S(1)}, bf16[352,704]{1,0:T(8,128)(2,1)S(1)}, u32[]{:S(2)}, u32[]{:S(2)}) collective-permute-start(bf16[352,704]{1,0:T(8,128)(2,1)S(1)} %shard_map.69), channel_id=1, source_target_pairs={{0,1},{1,0},{2,3},{3,2},{4,5},{5,4},{6,7},{7,6},{8,9},{9,8},{10,11... | collective-permute-start | bytes 1486856 | tf_op jit(solution)/shard_map/ppermute | solution.py:265
  69.0 1.3 %shard_map.68.mine = f32[352,704]{1,0:T(8,128)S(1)} custom-call(s32[3]{0:T(128)S(1)} %pad_add_fusion.place, bf16[32,2,11,8,128]{4,3,2,1,0:T(8,128)(2,1)S(1)} %all-to-all-done.rows, bf16[704,256]{1,0:T(8,128)(2,1)S(1)} %get-tuple-element.20.refs_0_, bf16[704,256]{1,0:T(8,128)(2,1)S(1)} %collective-permute-done.2.refs_1_, ...), custom_call_target="tpu_custom_call" | custom-call | tf_op jit(solution)/shard_map/pallas_call | solution.py:29
  70.3 0.6 collective-permute-done.4.theirs
  70.9 0.3 shard_map.70
  71.2 23.9 %all-gather = bf16[1408,352]{1,0:T(8,128)(2,1)S(1)} all-gather(bf16[352,352]{1,0:T(8,128)(2,1)S(1)} %shard_map.70), channel_id=2, replica_groups=mesh['side'=2,'plane'=32,'chip'=4,'core'=2] {'chip'}, dimensions={0}, use_global_device_ids=true | all-gather | bytes 1239040 | tf_op jit(solution)/shard_map/all_gather | solution.py:275
  95.1 1.9 %collective-permute-start.5 = (bf16[4,352,352]{2,1,0:T(8,128)(2,1)S(1)}, bf16[4,352,352]{2,1,0:T(8,128)(2,1)S(1)}, u32[]{:S(2)}, u32[]{:S(2)}) collective-permute-start(bf16[4,352,352]{2,1,0:T(8,128)(2,1)S(1)} %bitcast.9), channel_id=1, source_target_pairs={{0,1},{1,0},{2,3},{3,2},{4,5},{5,4},{6,7},{7,6},{8,9},{9,8},{10,11... | collective-permute-start | bytes 2973704 | tf_op jit(solution)/shard_map/ppermute | solution.py:276
  97.0 0.5 shard_map.71.own
  97.6 2.1 %collective-permute-done.5.other = bf16[4,352,352]{2,1,0:T(8,128)(2,1)S(1)} collective-permute-done((bf16[4,352,352]{2,1,0:T(8,128)(2,1)S(1)}, bf16[4,352,352]{2,1,0:T(8,128)(2,1)S(1)}, u32[]{:S(2)}, u32[]{:S(2)}) %collective-permute-start.5) | collective-permute-done | bytes 991264 | tf_op jit(solution)/shard_map/ppermute | solution.py:276
  99.7 1.2 shard_map.72
  100.9 22.0 %all_to_all.10.returned = bf16[64,11,2,128]{3,2,1,0:T(2,128)(2,1)S(1)} all-to-all(bf16[64,11,2,128]{3,2,1,0:T(2,128)(2,1)S(1)} %shard_map.72), channel_id=1, replica_groups=mesh['side'=2,'plane'=32,'chip'=4,'core'=2] {'side','plane'}, dimensions={0} | all-to-all | bytes 720896 | tf_op jit(solution)/shard_map/all_to_all | solution.py:286
  123.0 1.3 %shard_map.73 = bf16[64,256]{1,0:T(8,128)(2,1)} custom-call(s32[6,64]{1,0:T(8,128)S(1)} %get-tuple-element.15.target_t, f32[6,64]{1,0:T(8,128)S(1)} %bitcast.13, bf16[64,11,2,128]{3,2,1,0:T(2,128)(2,1)S(1)} %all_to_all.10.returned), custom_call_target="tpu_custom_call" | custom-call | tf_op jit(solution)/shard_map/pallas_call | solution.py:29
  (7 shorter events, 0.1 us)
Async XLA Ops:
  2.1 15.8 %collective-permute-start = (bf16[80,1024]{1,0:T(8,128)(2,1)S(1)}, bf16[80,1024]{1,0:T(8,128)(2,1)S(1)}, u32[]{:S(2)}, u32[]{:S(2)}) collective-permute-start(bf16[80,1024]{1,0:T(8,128)(2,1)S(1)} %get-tuple-element.14.mine), channel_id=1, source_target_pairs={{0,256},{256,0},{1,257},{257,1},{2,258},{258,2},{3,259},{259,3},{4... | collective-permute-start | bytes 491528 | tf_op jit(solution)/shard_map/ppermute | solution.py:215
  6.4 24.3 %collective-permute-start.1 = (bf16[704,256]{1,0:T(8,128)(2,1)S(1)}, bf16[704,256]{1,0:T(8,128)(2,1)S(1)}, u32[]{:S(2)}, u32[]{:S(2)}) collective-permute-start(bf16[704,256]{1,0:T(8,128)(2,1)S(1)} %get-tuple-element.19), channel_id=1, source_target_pairs={{0,4},{2,6},{4,0},{6,2},{1,5},{3,7},{5,1},{7,3},{8,12},{10,14},{12... | collective-permute-start | bytes 1081352 | tf_op jit(solution)/shard_map/ppermute | solution.py:239
  20.6 45.2 %all-to-all-start = ((bf16[32,2,11,8,128]{4,3,2,1,0:T(8,128)(2,1)}), bf16[32,2,11,8,128]{4,3,2,1,0:T(8,128)(2,1)S(1)}, u32[]{:S(2)}, u32[]{:S(2)}) async-start(bf16[32,2,11,8,128]{4,3,2,1,0:T(8,128)(2,1)} %shard_map.66), calls=%async_computation | async-start | bytes 2883584 | tf_op jit(solution)/shard_map/all_to_all | solution.py:237
  32.3 22.2 %collective-permute-start.2 = (bf16[704,256]{1,0:T(8,128)(2,1)S(1)}, bf16[704,256]{1,0:T(8,128)(2,1)S(1)}, u32[]{:S(2)}, u32[]{:S(2)}) collective-permute-start(bf16[704,256]{1,0:T(8,128)(2,1)S(1)} %get-tuple-element.21), channel_id=1, source_target_pairs={{0,2},{2,4},{4,6},{6,0},{1,3},{3,5},{5,7},{7,1},{8,10},{10,12},{12... | collective-permute-start | bytes 1081352 | tf_op jit(solution)/shard_map/ppermute | solution.py:254
  39.7 16.8 %collective-permute-start.3 = (bf16[704,256]{1,0:T(8,128)(2,1)S(1)}, bf16[704,256]{1,0:T(8,128)(2,1)S(1)}, u32[]{:S(2)}, u32[]{:S(2)}) collective-permute-start(bf16[704,256]{1,0:T(8,128)(2,1)S(1)} %get-tuple-element.22), channel_id=1, source_target_pairs={{0,6},{2,0},{4,2},{6,4},{1,7},{3,1},{5,3},{7,5},{8,14},{10,8},{12,... | collective-permute-start | bytes 1081352 | tf_op jit(solution)/shard_map/ppermute | solution.py:255
  67.1 3.8 %collective-permute-start.4 = (bf16[352,704]{1,0:T(8,128)(2,1)S(1)}, bf16[352,704]{1,0:T(8,128)(2,1)S(1)}, u32[]{:S(2)}, u32[]{:S(2)}) collective-permute-start(bf16[352,704]{1,0:T(8,128)(2,1)S(1)} %shard_map.69), channel_id=1, source_target_pairs={{0,1},{1,0},{2,3},{3,2},{4,5},{5,4},{6,7},{7,6},{8,9},{9,8},{10,11... | collective-permute-start | bytes 1486856 | tf_op jit(solution)/shard_map/ppermute | solution.py:265
  71.2 25.8 %copy-start = (bf16[1,1408,256]{2,1,0:T(8,128)(2,1)S(1)}, bf16[1,1408,256]{2,1,0:T(8,128)(2,1)}, u32[]{:S(2)}) copy-start(bf16[1,1408,256]{2,1,0:T(8,128)(2,1)} %param.11) | copy-start | bytes 2162692
  95.1 4.6 %collective-permute-start.5 = (bf16[4,352,352]{2,1,0:T(8,128)(2,1)S(1)}, bf16[4,352,352]{2,1,0:T(8,128)(2,1)S(1)}, u32[]{:S(2)}, u32[]{:S(2)}) collective-permute-start(bf16[4,352,352]{2,1,0:T(8,128)(2,1)S(1)} %bitcast.9), channel_id=1, source_target_pairs={{0,1},{1,0},{2,3},{3,2},{4,5},{5,4},{6,7},{7,6},{8,9},{9,8},{10,11... | collective-permute-start | bytes 2973704 | tf_op jit(solution)/shard_map/ppermute | solution.py:276
  97.6 25.4 %copy-start.1 = (f32[64,6]{0,1:T(8,128)S(1)}, f32[64,6]{0,1:T(8,128)}, u32[]{:S(2)}) copy-start(f32[64,6]{0,1:T(8,128)} %param.8) | copy-start | bytes 4612

commit v10 on v9

--- a/solution.py
+++ b/solution.py
@@ -70,14 +70,14 @@
         copy.wait()
 
 
-def hold_body(place, w_gate, w_up, one, three, _, here, one_out, three_out, sems):
+def hold_body(place, w_gate, w_up, two, three, _, here, two_out, three_out, sems):
     share = here.shape[0] // 2
     pairs = [
         (w.at[units_of(place, 0, share), :], here.at[n * share : (n + 1) * share, :])
         for n, w in enumerate((w_gate, w_up))
     ]
     copies = copy_all(pairs, sems)
-    one_out[...] = one[...]
+    two_out[...] = two[...]
     three_out[...] = three[...]
     for copy in copies:
         copy.wait()
@@ -236,22 +236,22 @@
     )
     received = lax.all_to_all(outgoing, "plane", split_axis=0, concat_axis=0, tiled=True)
     ring = [[(i, (i + shift) % CHIPS) for i in range(CHIPS)] for shift in range(CHIPS)]
-    two = lax.ppermute(two, "chip", ring[2])
-    here, one, three = call(
+    one = lax.ppermute(one, "chip", ring[1])
+    here, two, three = call(
         hold_body,
         (part,) * 3,
         place,
         w_gate[0],
         w_up[0],
+        two,
+        three,
         one,
-        three,
-        two,
         scalars=1,
         raw=2,
         scratch=[dma((2,))],
         flops=HOLD,
     )
-    one = lax.ppermute(one, "chip", ring[1])
+    two = lax.ppermute(two, "chip", ring[2])
     three = lax.ppermute(three, "chip", ring[3])
     weights = (here, one, two, three)
     theirs = call(

time: 125 us -> 131 us (1.048)
  waiting for transfers between devices: 23.5 us -> 36.5 us
  starting transfers between devices: 40.9 us -> 29.3 us
  blocking collectives: 45.9 us -> 50.7 us
    ppermute x1, waiting for transfers between devices: 0.01 us -> 17.8 us  [on_device(): two = lax.ppermute(two, 'chip', ring[2])]
    all_to_all x1, waiting for transfers between devices: 9.27 us -> 0.01 us  [on_device(): lax.all_to_all(outgoing, 'plane', split_axis=0, concat_axis=0, tiled=True)]
    ppermute x1, starting transfers between devices: 10 us -> 3.02 us  [on_device(): two = lax.ppermute(two, 'chip', ring[2])]
    ppermute x1, waiting for transfers between devices: 1.96 us -> 8.94 us  [on_device(): three = lax.ppermute(three, 'chip', ring[3])]
    all_to_all x1, blocking collectives: 22 us -> 26.9 us  [on_device(): lax.all_to_all(produced, ('side', 'plane'), split_axis=0, concat_axis=0,...]
    ppermute x1, starting transfers between devices: 5.24 us -> 1.92 us  [on_device(): three = lax.ppermute(three, 'chip', ring[3])]
    ppermute x1, waiting for transfers between devices: 9.57 us -> 7.06 us  [on_device(): one = lax.ppermute(one, 'chip', ring[1])]
where the time goes in v10:
time: 131 us; the launch traced here: 130 us
  blocking collectives  50.7 us (39%)
  waiting for transfers between devices  36.5 us (28%)
  starting transfers between devices  29.3 us (22%)
  Pallas kernels  13.6 us (10%)
    all_to_all x1, blocking collectives, on_device(): lax.all_to_all(produced, ('side', 'plane'), split_axis=0, concat_axis=0,...  26.9 us
    all_gather x1, blocking collectives, on_device(): own = lax.all_gather(hidden, 'chip', axis=0)  23.8 us
    ppermute x1, waiting for transfers between devices, on_device(): two = lax.ppermute(two, 'chip', ring[2])  17.8 us
    pallas_call x10, Pallas kernels, call(): pl.pallas_call(body, out_shape=outs, in_specs=[SMEM] * scalars + [HBM] *...  13.6 us
    all_to_all x1, starting transfers between devices, on_device(): lax.all_to_all(outgoing, 'plane', split_axis=0, concat_axis=0, tiled=True)  10.2 us
    ppermute x1, waiting for transfers between devices, on_device(): three = lax.ppermute(three, 'chip', ring[3])  8.94 us
    ppermute x1, waiting for transfers between devices, on_device(): one = lax.ppermute(one, 'chip', ring[1])  7.06 us
    ppermute x1, starting transfers between devices, on_device(): one = lax.ppermute(one, 'chip', ring[1])  6.09 us
  transfers between devices with their start and end apart: 7, of which 5 were waited for; matrix products, arithmetic and copies ran while one was open for 0% of the time, Pallas kernels for 6%

profile of v10, /device:TPU:8, one launch (start us, length us, event | category | flops | bytes accessed | tf_op | source)
XLA Modules:
  0.0 130.3 jit_solution(17596843885625068187)
XLA Ops:
  0.1 2.0 %shard_map.64 = (bf16[80,1024]{1,0:T(8,128)(2,1)S(1)}, bf16[704,256]{1,0:T(8,128)(2,1)S(1)}, bf16[704,256]{1,0:T(8,128)(2,1)S(1)}, bf16[704,256]{1,0:T(8,128)(2,1)S(1)}) custom-call(s32[3]{0:T(128)S(1)} %pad_add_fusion.place, s32[6,64]{1,0:T(8,128)} %bitcast.18, bf16[64,2048]{1,0:T(8,128)(2,1)} %tokens_hbm.1, bf16[1408,256]{1,0:T(8,128)(2,1)} %bitcast.14, ...), custom_call_target="tpu_custom_call" | custom-call | tf_op jit(solution)/shard_map/pallas_call | solution.py:29
  2.1 4.3 %collective-permute-start = (bf16[80,1024]{1,0:T(8,128)(2,1)S(1)}, bf16[80,1024]{1,0:T(8,128)(2,1)S(1)}, u32[]{:S(2)}, u32[]{:S(2)}) collective-permute-start(bf16[80,1024]{1,0:T(8,128)(2,1)S(1)} %get-tuple-element.14.mine), channel_id=1, source_target_pairs={{0,256},{256,0},{1,257},{257,1},{2,258},{258,2},{3,259},{259,3},{4... | collective-permute-start | bytes 491528 | tf_op jit(solution)/shard_map/ppermute | solution.py:215
  6.4 6.1 %collective-permute-start.1 = (bf16[704,256]{1,0:T(8,128)(2,1)S(1)}, bf16[704,256]{1,0:T(8,128)(2,1)S(1)}, u32[]{:S(2)}, u32[]{:S(2)}) collective-permute-start(bf16[704,256]{1,0:T(8,128)(2,1)S(1)} %get-tuple-element.19), channel_id=1, source_target_pairs={{0,2},{2,4},{4,6},{6,0},{1,3},{3,5},{5,7},{7,1},{8,10},{10,12},{12... | collective-permute-start | bytes 1081352 | tf_op jit(solution)/shard_map/ppermute | solution.py:239
  12.5 1.5 %shard_map.65 = (bf16[32,11,8,128]{3,2,1,0:T(8,128)(2,1)S(1)}, s32[6,64]{1,0:T(8,128)S(1)}) custom-call(s32[3]{0:T(128)S(1)} %pad_add_fusion.place, bf16[80,1024]{1,0:T(8,128)(2,1)S(1)} %get-tuple-element.14.mine), custom_call_target="tpu_custom_call" | custom-call | tf_op jit(solution)/shard_map/pallas_call | solution.py:29
  14.0 2.7 %shard_map.66 = bf16[32,2,11,8,128]{4,3,2,1,0:T(8,128)(2,1)} custom-call(s32[3]{0:T(128)S(1)} %pad_add_fusion.place, bf16[32,11,8,128]{3,2,1,0:T(8,128)(2,1)S(1)} %get-tuple-element.16.own, bf16[80,1024]{1,0:T(8,128)(2,1)S(1)} %collective-permute-done.neighbour), custom_call_target="tpu_custom_call" | custom-call | flops 10000000000 | tf_op jit(solution)/shard_map/pallas_call | solution.py:29
  16.6 10.2 %all-to-all-start = ((bf16[32,2,11,8,128]{4,3,2,1,0:T(8,128)(2,1)}), bf16[32,2,11,8,128]{4,3,2,1,0:T(8,128)(2,1)S(1)}, u32[]{:S(2)}, u32[]{:S(2)}) async-start(bf16[32,2,11,8,128]{4,3,2,1,0:T(8,128)(2,1)} %shard_map.66), calls=%async_computation | async-start | bytes 2883584 | tf_op jit(solution)/shard_map/all_to_all | solution.py:237
  26.8 7.1 %collective-permute-done.1._.refs_1_ = bf16[704,256]{1,0:T(8,128)(2,1)S(1)} collective-permute-done((bf16[704,256]{1,0:T(8,128)(2,1)S(1)}, bf16[704,256]{1,0:T(8,128)(2,1)S(1)}, u32[]{:S(2)}, u32[]{:S(2)}) %collective-permute-start.1) | collective-permute-done | bytes 360480 | tf_op jit(solution)/shard_map/ppermute | solution.py:239
  33.9 1.6 %shard_map.67 = (bf16[704,256]{1,0:T(8,128)(2,1)S(1)}, bf16[704,256]{1,0:T(8,128)(2,1)S(1)}, bf16[704,256]{1,0:T(8,128)(2,1)S(1)}) custom-call(s32[3]{0:T(128)S(1)} %pad_add_fusion.place, bf16[1408,256]{1,0:T(8,128)(2,1)} %bitcast.15, bf16[1408,256]{1,0:T(8,128)(2,1)} %bitcast.17, bf16[704,256]{1,0:T(8,128)(2,1)S(1)} %get-tuple-element.17.two, ...), custom_call_target="tpu_custom_call" | custom-call | flops 30000001024 | tf_op jit(solution)/shard_map/pallas_call | solution.py:29
  35.4 3.0 %collective-permute-start.2 = (bf16[704,256]{1,0:T(8,128)(2,1)S(1)}, bf16[704,256]{1,0:T(8,128)(2,1)S(1)}, u32[]{:S(2)}, u32[]{:S(2)}) collective-permute-start(bf16[704,256]{1,0:T(8,128)(2,1)S(1)} %get-tuple-element.21), channel_id=1, source_target_pairs={{0,4},{2,6},{4,0},{6,2},{1,5},{3,7},{5,1},{7,3},{8,12},{10,14},{12... | collective-permute-start | bytes 1081352 | tf_op jit(solution)/shard_map/ppermute | solution.py:254
  38.5 1.9 %collective-permute-start.3 = (bf16[704,256]{1,0:T(8,128)(2,1)S(1)}, bf16[704,256]{1,0:T(8,128)(2,1)S(1)}, u32[]{:S(2)}, u32[]{:S(2)}) collective-permute-start(bf16[704,256]{1,0:T(8,128)(2,1)S(1)} %get-tuple-element.22), channel_id=1, source_target_pairs={{0,6},{2,0},{4,2},{6,4},{1,7},{3,1},{5,3},{7,5},{8,14},{10,8},{12,... | collective-permute-start | bytes 1081352 | tf_op jit(solution)/shard_map/ppermute | solution.py:255
  40.4 17.8 %collective-permute-done.2.refs_2_ = bf16[704,256]{1,0:T(8,128)(2,1)S(1)} collective-permute-done((bf16[704,256]{1,0:T(8,128)(2,1)S(1)}, bf16[704,256]{1,0:T(8,128)(2,1)S(1)}, u32[]{:S(2)}, u32[]{:S(2)}) %collective-permute-start.2) | collective-permute-done | bytes 360480 | tf_op jit(solution)/shard_map/ppermute | solution.py:254
  58.2 8.9 %collective-permute-done.3.refs_3_ = bf16[704,256]{1,0:T(8,128)(2,1)S(1)} collective-permute-done((bf16[704,256]{1,0:T(8,128)(2,1)S(1)}, bf16[704,256]{1,0:T(8,128)(2,1)S(1)}, u32[]{:S(2)}, u32[]{:S(2)}) %collective-permute-start.3) | collective-permute-done | bytes 360480 | tf_op jit(solution)/shard_map/ppermute | solution.py:255
  67.1 1.3 %shard_map.69 = bf16[352,704]{1,0:T(8,128)(2,1)S(1)} custom-call(s32[3]{0:T(128)S(1)} %pad_add_fusion.place, bf16[32,2,11,8,128]{4,3,2,1,0:T(8,128)(2,1)S(1)} %all-to-all-done.rows, bf16[704,256]{1,0:T(8,128)(2,1)S(1)} %get-tuple-element.20.refs_0_, bf16[704,256]{1,0:T(8,128)(2,1)S(1)} %collective-permute-done.1._.refs_1_, ...), custom_call_target="tpu_custom_call" | custom-call | tf_op jit(solution)/shard_map/pallas_call | solution.py:29
  68.4 1.9 %collective-permute-start.4 = (bf16[352,704]{1,0:T(8,128)(2,1)S(1)}, bf16[352,704]{1,0:T(8,128)(2,1)S(1)}, u32[]{:S(2)}, u32[]{:S(2)}) collective-permute-start(bf16[352,704]{1,0:T(8,128)(2,1)S(1)} %shard_map.69), channel_id=1, source_target_pairs={{0,1},{1,0},{2,3},{3,2},{4,5},{5,4},{6,7},{7,6},{8,9},{9,8},{10,11... | collective-permute-start | bytes 1486856 | tf_op jit(solution)/shard_map/ppermute | solution.py:265
  70.4 1.3 %shard_map.68.mine = f32[352,704]{1,0:T(8,128)S(1)} custom-call(s32[3]{0:T(128)S(1)} %pad_add_fusion.place, bf16[32,2,11,8,128]{4,3,2,1,0:T(8,128)(2,1)S(1)} %all-to-all-done.rows, bf16[704,256]{1,0:T(8,128)(2,1)S(1)} %get-tuple-element.20.refs_0_, bf16[704,256]{1,0:T(8,128)(2,1)S(1)} %collective-permute-done.1._.refs_1_, ...), custom_call_target="tpu_custom_call" | custom-call | tf_op jit(solution)/shard_map/pallas_call | solution.py:29
  71.7 0.6 collective-permute-done.4.theirs
  72.3 0.3 shard_map.70
  72.5 23.8 %all-gather = bf16[1408,352]{1,0:T(8,128)(2,1)S(1)} all-gather(bf16[352,352]{1,0:T(8,128)(2,1)S(1)} %shard_map.70), channel_id=2, replica_groups=mesh['side'=2,'plane'=32,'chip'=4,'core'=2] {'chip'}, dimensions={0}, use_global_device_ids=true | all-gather | bytes 1239040 | tf_op jit(solution)/shard_map/all_gather | solution.py:275
  96.3 1.9 %collective-permute-start.5 = (bf16[4,352,352]{2,1,0:T(8,128)(2,1)S(1)}, bf16[4,352,352]{2,1,0:T(8,128)(2,1)S(1)}, u32[]{:S(2)}, u32[]{:S(2)}) collective-permute-start(bf16[4,352,352]{2,1,0:T(8,128)(2,1)S(1)} %bitcast.9), channel_id=1, source_target_pairs={{0,1},{1,0},{2,3},{3,2},{4,5},{5,4},{6,7},{7,6},{8,9},{9,8},{10,11... | collective-permute-start | bytes 2973704 | tf_op jit(solution)/shard_map/ppermute | solution.py:276
  98.3 0.5 shard_map.71.own
  98.8 2.1 %collective-permute-done.5.other = bf16[4,352,352]{2,1,0:T(8,128)(2,1)S(1)} collective-permute-done((bf16[4,352,352]{2,1,0:T(8,128)(2,1)S(1)}, bf16[4,352,352]{2,1,0:T(8,128)(2,1)S(1)}, u32[]{:S(2)}, u32[]{:S(2)}) %collective-permute-start.5) | collective-permute-done | bytes 991264 | tf_op jit(solution)/shard_map/ppermute | solution.py:276
  100.9 1.2 shard_map.72
  102.2 26.9 %all_to_all.10.returned = bf16[64,11,2,128]{3,2,1,0:T(2,128)(2,1)S(1)} all-to-all(bf16[64,11,2,128]{3,2,1,0:T(2,128)(2,1)S(1)} %shard_map.72), channel_id=1, replica_groups=mesh['side'=2,'plane'=32,'chip'=4,'core'=2] {'side','plane'}, dimensions={0} | all-to-all | bytes 720896 | tf_op jit(solution)/shard_map/all_to_all | solution.py:286
  129.0 1.3 shard_map.73
  (7 shorter events, 0.1 us)
Async XLA Ops:
  2.1 11.9 %collective-permute-start = (bf16[80,1024]{1,0:T(8,128)(2,1)S(1)}, bf16[80,1024]{1,0:T(8,128)(2,1)S(1)}, u32[]{:S(2)}, u32[]{:S(2)}) collective-permute-start(bf16[80,1024]{1,0:T(8,128)(2,1)S(1)} %get-tuple-element.14.mine), channel_id=1, source_target_pairs={{0,256},{256,0},{1,257},{257,1},{2,258},{258,2},{3,259},{259,3},{4... | collective-permute-start | bytes 491528 | tf_op jit(solution)/shard_map/ppermute | solution.py:215
  6.4 27.5 %collective-permute-start.1 = (bf16[704,256]{1,0:T(8,128)(2,1)S(1)}, bf16[704,256]{1,0:T(8,128)(2,1)S(1)}, u32[]{:S(2)}, u32[]{:S(2)}) collective-permute-start(bf16[704,256]{1,0:T(8,128)(2,1)S(1)} %get-tuple-element.19), channel_id=1, source_target_pairs={{0,2},{2,4},{4,6},{6,0},{1,3},{3,5},{5,7},{7,1},{8,10},{10,12},{12... | collective-permute-start | bytes 1081352 | tf_op jit(solution)/shard_map/ppermute | solution.py:239
  16.6 50.5 %all-to-all-start = ((bf16[32,2,11,8,128]{4,3,2,1,0:T(8,128)(2,1)}), bf16[32,2,11,8,128]{4,3,2,1,0:T(8,128)(2,1)S(1)}, u32[]{:S(2)}, u32[]{:S(2)}) async-start(bf16[32,2,11,8,128]{4,3,2,1,0:T(8,128)(2,1)} %shard_map.66), calls=%async_computation | async-start | bytes 2883584 | tf_op jit(solution)/shard_map/all_to_all | solution.py:237
  35.4 22.7 %collective-permute-start.2 = (bf16[704,256]{1,0:T(8,128)(2,1)S(1)}, bf16[704,256]{1,0:T(8,128)(2,1)S(1)}, u32[]{:S(2)}, u32[]{:S(2)}) collective-permute-start(bf16[704,256]{1,0:T(8,128)(2,1)S(1)} %get-tuple-element.21), channel_id=1, source_target_pairs={{0,4},{2,6},{4,0},{6,2},{1,5},{3,7},{5,1},{7,3},{8,12},{10,14},{12... | collective-permute-start | bytes 1081352 | tf_op jit(solution)/shard_map/ppermute | solution.py:254
  38.5 28.6 %collective-permute-start.3 = (bf16[704,256]{1,0:T(8,128)(2,1)S(1)}, bf16[704,256]{1,0:T(8,128)(2,1)S(1)}, u32[]{:S(2)}, u32[]{:S(2)}) collective-permute-start(bf16[704,256]{1,0:T(8,128)(2,1)S(1)} %get-tuple-element.22), channel_id=1, source_target_pairs={{0,6},{2,0},{4,2},{6,4},{1,7},{3,1},{5,3},{7,5},{8,14},{10,8},{12,... | collective-permute-start | bytes 1081352 | tf_op jit(solution)/shard_map/ppermute | solution.py:255
  68.4 3.8 %collective-permute-start.4 = (bf16[352,704]{1,0:T(8,128)(2,1)S(1)}, bf16[352,704]{1,0:T(8,128)(2,1)S(1)}, u32[]{:S(2)}, u32[]{:S(2)}) collective-permute-start(bf16[352,704]{1,0:T(8,128)(2,1)S(1)} %shard_map.69), channel_id=1, source_target_pairs={{0,1},{1,0},{2,3},{3,2},{4,5},{5,4},{6,7},{7,6},{8,9},{9,8},{10,11... | collective-permute-start | bytes 1486856 | tf_op jit(solution)/shard_map/ppermute | solution.py:265
  72.5 25.7 %copy-start = (bf16[1,1408,256]{2,1,0:T(8,128)(2,1)S(1)}, bf16[1,1408,256]{2,1,0:T(8,128)(2,1)}, u32[]{:S(2)}) copy-start(bf16[1,1408,256]{2,1,0:T(8,128)(2,1)} %param.11) | copy-start | bytes 2162692
  96.3 4.6 %collective-permute-start.5 = (bf16[4,352,352]{2,1,0:T(8,128)(2,1)S(1)}, bf16[4,352,352]{2,1,0:T(8,128)(2,1)S(1)}, u32[]{:S(2)}, u32[]{:S(2)}) collective-permute-start(bf16[4,352,352]{2,1,0:T(8,128)(2,1)S(1)} %bitcast.9), channel_id=1, source_target_pairs={{0,1},{1,0},{2,3},{3,2},{4,5},{5,4},{6,7},{7,6},{8,9},{9,8},{10,11... | collective-permute-start | bytes 2973704 | tf_op jit(solution)/shard_map/ppermute | solution.py:276
  98.8 30.2 %copy-start.1 = (f32[64,6]{0,1:T(8,128)S(1)}, f32[64,6]{0,1:T(8,128)}, u32[]{:S(2)}) copy-start(f32[64,6]{0,1:T(8,128)} %param.8) | copy-start | bytes 4612

commit v11 on v9

--- a/solution.py
+++ b/solution.py
@@ -16,7 +16,6 @@
 
 
 HOLD = 30_000_000_000
-PICK = 10_000_000_000
 CHIPS = 4
 CORE, CHIP, SIDE = range(3)
 
@@ -59,7 +58,7 @@
         block = lax.rem(place[CHIP] - shift + CHIPS, CHIPS) * 2 + place[CORE]
         columns = pl.ds(pl.multiple_of(block * cols, cols), cols)
         pairs.append((tokens_hbm.at[:, columns], mine.at[:rows, shift * cols : (shift + 1) * cols]))
-    for shift, out in enumerate(pieces, 1):
+    for shift, out in zip((1, 3), pieces):
         pairs.append((w_gate.at[units_of(place, shift, share), :], out.at[:share, :]))
         pairs.append((w_up.at[units_of(place, shift, share), :], out.at[share:, :]))
     copies = copy_all(pairs, sems)
@@ -110,9 +109,17 @@
     out[...] = picked(*sizes, place, mine, target_t)
 
 
-def dispatch_body(sizes, place, own, neighbour, outgoing):
+def dispatch_body(sizes, place, w_gate, w_up, own, neighbour, outgoing, two, sems):
+    share = two.shape[0] // 2
+    pairs = [
+        (w.at[units_of(place, 2, share), :], two.at[n * share : (n + 1) * share, :])
+        for n, w in enumerate((w_gate, w_up))
+    ]
+    copies = copy_all(pairs, sems)
     outgoing[:, 1 - place[SIDE]] = picked(*sizes, place, neighbour)
     outgoing[:, place[SIDE]] = own[...]
+    for copy in copies:
+        copy.wait()
 
 
 def gate_up_body(mine, place, rows, *refs):
@@ -200,9 +207,9 @@
     place = jnp.stack([lax.axis_index(a) for a in ("core", "chip", "side")]).astype(jnp.int32)
 
     part = jax.ShapeDtypeStruct((2 * share, cols), bf16)
-    mine, one, two, three = call(
+    mine, one, three = call(
         first_body,
-        (jax.ShapeDtypeStruct((tok_count + 16, CHIPS * cols), bf16),) + (part,) * (CHIPS - 1),
+        (jax.ShapeDtypeStruct((tok_count + 16, CHIPS * cols), bf16),) + (part,) * 2,
         place,
         routes.T,
         tokens,
@@ -210,7 +217,7 @@
         w_up[0],
         scalars=1,
         raw=4,
-        scratch=[pltpu.VMEM((top, tok_count), jnp.int32), dma((3 * CHIPS - 1,))],
+        scratch=[pltpu.VMEM((top, tok_count), jnp.int32), dma((CHIPS + 5,))],
     )
     neighbour = lax.ppermute(mine, "side", swap)
     sizes = (top, cap, experts, side)
@@ -225,14 +232,17 @@
         mine,
         scalars=1,
     )
-    outgoing = call(
+    outgoing, two = call(
         functools.partial(dispatch_body, sizes),
-        jax.ShapeDtypeStruct((side, 2, *chunk), bf16),
-        place,
+        (jax.ShapeDtypeStruct((side, 2, *chunk), bf16), part),
+        place,
+        w_gate[0],
+        w_up[0],
         picked_own,
         neighbour,
         scalars=1,
-        flops=PICK,
+        raw=2,
+        scratch=[dma((2,))],
     )
     received = lax.all_to_all(outgoing, "plane", split_axis=0, concat_axis=0, tiled=True)
     ring = [[(i, (i + shift) % CHIPS) for i in range(CHIPS)] for shift in range(CHIPS)]

time: 125 us -> 128 us (1.024)
  starting transfers between devices: 40.9 us -> 42.9 us
    all_to_all x1, waiting for transfers between devices: 9.27 us -> 3.94 us  [on_device(): lax.all_to_all(outgoing, 'plane', split_axis=0, concat_axis=0, tiled=True)]
    ppermute x1, waiting for transfers between devices: 0.01 us -> 2.72 us  [on_device(): neighbour = lax.ppermute(mine, 'side', swap)]
    ppermute x1, starting transfers between devices: 7.39 us -> 9.42 us  [on_device(): one = lax.ppermute(one, 'chip', ring[1])]
    ppermute x1, waiting for transfers between devices: 9.57 us -> 11.2 us  [on_device(): one = lax.ppermute(one, 'chip', ring[1])]
    ppermute x1, waiting for transfers between devices: 1.96 us -> 3.37 us  [on_device(): three = lax.ppermute(three, 'chip', ring[3])]
  transfers between devices with their start and end apart: 7 -> 7, of which waited for: 5 -> 6; matrix products, arithmetic and copies ran while one was open for 0% -> 0% of each run, Pallas kernels for 6% -> 4%
where the time goes in v11:
time: 128 us
  blocking collectives  47.1 us (37%)
  starting transfers between devices  42.9 us (34%)
  waiting for transfers between devices  23.9 us (19%)
  Pallas kernels  13.5 us (11%)
    all_gather x1, blocking collectives, on_device(): own = lax.all_gather(hidden, 'chip', axis=0)  24.5 us
    all_to_all x1, blocking collectives, on_device(): lax.all_to_all(produced, ('side', 'plane'), split_axis=0, concat_axis=0,...  22.6 us
    pallas_call x10, Pallas kernels, call(): pl.pallas_call(body, out_shape=outs, in_specs=[SMEM] * scalars + [HBM] *...  13.5 us
    ppermute x1, waiting for transfers between devices, on_device(): one = lax.ppermute(one, 'chip', ring[1])  11.2 us
    ppermute x1, starting transfers between devices, on_device(): two = lax.ppermute(two, 'chip', ring[2])  10.3 us
    all_to_all x1, starting transfers between devices, on_device(): lax.all_to_all(outgoing, 'plane', split_axis=0, concat_axis=0, tiled=True)  10.2 us
    ppermute x1, starting transfers between devices, on_device(): one = lax.ppermute(one, 'chip', ring[1])  9.42 us
    ppermute x1, starting transfers between devices, on_device(): three = lax.ppermute(three, 'chip', ring[3])  4.96 us
  transfers between devices with their start and end apart: 7, of which 6 were waited for; matrix products, arithmetic and copies ran while one was open for 0% of the time, Pallas kernels for 4%

profile of v11, /device:TPU:8, one launch (start us, length us, event | category | flops | bytes accessed | tf_op | source)
XLA Modules:
  0.0 127.7 jit_solution(9515188619271624851)
XLA Ops:
  0.1 1.9 %shard_map.64 = (bf16[80,1024]{1,0:T(8,128)(2,1)S(1)}, bf16[704,256]{1,0:T(8,128)(2,1)S(1)}, bf16[704,256]{1,0:T(8,128)(2,1)S(1)}) custom-call(s32[3]{0:T(128)S(1)} %pad_add_fusion.place, s32[6,64]{1,0:T(8,128)} %bitcast.20, bf16[64,2048]{1,0:T(8,128)(2,1)} %tokens_hbm.1, bf16[1408,256]{1,0:T(8,128)(2,1)} %bitcast.14, bf16[1408,256]{1,0:T(8,128)(2,1)} %bitcast.17), custom_call_target="tpu_custom_call" | custom-call | tf_op jit(solution)/shard_map/pallas_call | solution.py:28
  2.0 4.3 %collective-permute-start = (bf16[80,1024]{1,0:T(8,128)(2,1)S(1)}, bf16[80,1024]{1,0:T(8,128)(2,1)S(1)}, u32[]{:S(2)}, u32[]{:S(2)}) collective-permute-start(bf16[80,1024]{1,0:T(8,128)(2,1)S(1)} %get-tuple-element.15.mine), channel_id=1, source_target_pairs={{0,256},{256,0},{1,257},{257,1},{2,258},{258,2},{3,259},{259,3},{4... | collective-permute-start | bytes 491528 | tf_op jit(solution)/shard_map/ppermute | solution.py:222
  6.3 1.5 %shard_map.65 = (bf16[32,11,8,128]{3,2,1,0:T(8,128)(2,1)S(1)}, s32[6,64]{1,0:T(8,128)S(1)}) custom-call(s32[3]{0:T(128)S(1)} %pad_add_fusion.place, bf16[80,1024]{1,0:T(8,128)(2,1)S(1)} %get-tuple-element.15.mine), custom_call_target="tpu_custom_call" | custom-call | tf_op jit(solution)/shard_map/pallas_call | solution.py:28
  7.7 2.7 %collective-permute-done.neighbour = bf16[80,1024]{1,0:T(8,128)(2,1)S(1)} collective-permute-done((bf16[80,1024]{1,0:T(8,128)(2,1)S(1)}, bf16[80,1024]{1,0:T(8,128)(2,1)S(1)}, u32[]{:S(2)}, u32[]{:S(2)}) %collective-permute-start) | collective-permute-done | bytes 163872 | tf_op jit(solution)/shard_map/ppermute | solution.py:222
  10.5 2.7 %shard_map.66 = (bf16[32,2,11,8,128]{4,3,2,1,0:T(8,128)(2,1)}, bf16[704,256]{1,0:T(8,128)(2,1)S(1)}) custom-call(s32[3]{0:T(128)S(1)} %pad_add_fusion.place, bf16[1408,256]{1,0:T(8,128)(2,1)} %bitcast.15, bf16[1408,256]{1,0:T(8,128)(2,1)} %bitcast.18, bf16[32,11,8,128]{3,2,1,0:T(8,128)(2,1)S(1)} %get-tuple-element.17.own, ...), custom_call_target="tpu_custom_call" | custom-call | tf_op jit(solution)/shard_map/pallas_call | solution.py:28
  13.1 10.3 %collective-permute-start.1 = (bf16[704,256]{1,0:T(8,128)(2,1)S(1)}, bf16[704,256]{1,0:T(8,128)(2,1)S(1)}, u32[]{:S(2)}, u32[]{:S(2)}) collective-permute-start(bf16[704,256]{1,0:T(8,128)(2,1)S(1)} %get-tuple-element.21), channel_id=1, source_target_pairs={{0,4},{2,6},{4,0},{6,2},{1,5},{3,7},{5,1},{7,3},{8,12},{10,14},{12... | collective-permute-start | bytes 1081352 | tf_op jit(solution)/shard_map/ppermute | solution.py:249
  23.4 10.2 %all-to-all-start = ((bf16[32,2,11,8,128]{4,3,2,1,0:T(8,128)(2,1)}), bf16[32,2,11,8,128]{4,3,2,1,0:T(8,128)(2,1)S(1)}, u32[]{:S(2)}, u32[]{:S(2)}) async-start(bf16[32,2,11,8,128]{4,3,2,1,0:T(8,128)(2,1)} %get-tuple-element.18), calls=%async_computation | async-start | bytes 2883584 | tf_op jit(solution)/shard_map/all_to_all | solution.py:247
  33.6 1.6 %shard_map.67 = (bf16[704,256]{1,0:T(8,128)(2,1)S(1)}, bf16[704,256]{1,0:T(8,128)(2,1)S(1)}, bf16[704,256]{1,0:T(8,128)(2,1)S(1)}) custom-call(s32[3]{0:T(128)S(1)} %pad_add_fusion.place, bf16[1408,256]{1,0:T(8,128)(2,1)} %bitcast.16, bf16[1408,256]{1,0:T(8,128)(2,1)} %bitcast.19, bf16[704,256]{1,0:T(8,128)(2,1)S(1)} %get-tuple-element.19.one, ...), custom_call_target="tpu_custom_call" | custom-call | flops 30000001024 | tf_op jit(solution)/shard_map/pallas_call | solution.py:28
  35.2 9.4 %collective-permute-start.2 = (bf16[704,256]{1,0:T(8,128)(2,1)S(1)}, bf16[704,256]{1,0:T(8,128)(2,1)S(1)}, u32[]{:S(2)}, u32[]{:S(2)}) collective-permute-start(bf16[704,256]{1,0:T(8,128)(2,1)S(1)} %get-tuple-element.23), channel_id=1, source_target_pairs={{0,2},{2,4},{4,6},{6,0},{1,3},{3,5},{5,7},{7,1},{8,10},{10,12},{12... | collective-permute-start | bytes 1081352 | tf_op jit(solution)/shard_map/ppermute | solution.py:264
  44.6 5.0 %collective-permute-start.3 = (bf16[704,256]{1,0:T(8,128)(2,1)S(1)}, bf16[704,256]{1,0:T(8,128)(2,1)S(1)}, u32[]{:S(2)}, u32[]{:S(2)}) collective-permute-start(bf16[704,256]{1,0:T(8,128)(2,1)S(1)} %get-tuple-element.24), channel_id=1, source_target_pairs={{0,6},{2,0},{4,2},{6,4},{1,7},{3,1},{5,3},{7,5},{8,14},{10,8},{12,... | collective-permute-start | bytes 1081352 | tf_op jit(solution)/shard_map/ppermute | solution.py:265
  49.6 11.2 %collective-permute-done.2.refs_1_ = bf16[704,256]{1,0:T(8,128)(2,1)S(1)} collective-permute-done((bf16[704,256]{1,0:T(8,128)(2,1)S(1)}, bf16[704,256]{1,0:T(8,128)(2,1)S(1)}, u32[]{:S(2)}, u32[]{:S(2)}) %collective-permute-start.2) | collective-permute-done | bytes 360480 | tf_op jit(solution)/shard_map/ppermute | solution.py:264
  60.8 3.4 %collective-permute-done.3.refs_3_ = bf16[704,256]{1,0:T(8,128)(2,1)S(1)} collective-permute-done((bf16[704,256]{1,0:T(8,128)(2,1)S(1)}, bf16[704,256]{1,0:T(8,128)(2,1)S(1)}, u32[]{:S(2)}, u32[]{:S(2)}) %collective-permute-start.3) | collective-permute-done | bytes 360480 | tf_op jit(solution)/shard_map/ppermute | solution.py:265
  64.1 3.9 %all-to-all-done.rows = bf16[32,2,11,8,128]{4,3,2,1,0:T(8,128)(2,1)S(1)} async-done(((bf16[32,2,11,8,128]{4,3,2,1,0:T(8,128)(2,1)}), bf16[32,2,11,8,128]{4,3,2,1,0:T(8,128)(2,1)S(1)}, u32[]{:S(2)}, u32[]{:S(2)}) %all-to-all-start) | async-done | bytes 1441824 | tf_op jit(solution)/shard_map/all_to_all | solution.py:247
  68.1 1.3 %shard_map.69 = bf16[352,704]{1,0:T(8,128)(2,1)S(1)} custom-call(s32[3]{0:T(128)S(1)} %pad_add_fusion.place, bf16[32,2,11,8,128]{4,3,2,1,0:T(8,128)(2,1)S(1)} %all-to-all-done.rows, bf16[704,256]{1,0:T(8,128)(2,1)S(1)} %get-tuple-element.22.refs_0_, bf16[704,256]{1,0:T(8,128)(2,1)S(1)} %collective-permute-done.2.refs_1_, ...), custom_call_target="tpu_custom_call" | custom-call | tf_op jit(solution)/shard_map/pallas_call | solution.py:28
  69.4 1.9 %collective-permute-start.4 = (bf16[352,704]{1,0:T(8,128)(2,1)S(1)}, bf16[352,704]{1,0:T(8,128)(2,1)S(1)}, u32[]{:S(2)}, u32[]{:S(2)}) collective-permute-start(bf16[352,704]{1,0:T(8,128)(2,1)S(1)} %shard_map.69), channel_id=1, source_target_pairs={{0,1},{1,0},{2,3},{3,2},{4,5},{5,4},{6,7},{7,6},{8,9},{9,8},{10,11... | collective-permute-start | bytes 1486856 | tf_op jit(solution)/shard_map/ppermute | solution.py:275
  71.3 1.3 %shard_map.68.mine = f32[352,704]{1,0:T(8,128)S(1)} custom-call(s32[3]{0:T(128)S(1)} %pad_add_fusion.place, bf16[32,2,11,8,128]{4,3,2,1,0:T(8,128)(2,1)S(1)} %all-to-all-done.rows, bf16[704,256]{1,0:T(8,128)(2,1)S(1)} %get-tuple-element.22.refs_0_, bf16[704,256]{1,0:T(8,128)(2,1)S(1)} %collective-permute-done.2.refs_1_, ...), custom_call_target="tpu_custom_call" | custom-call | tf_op jit(solution)/shard_map/pallas_call | solution.py:28
  72.6 0.6 collective-permute-done.4.theirs
  73.5 24.5 %all-gather = bf16[1408,352]{1,0:T(8,128)(2,1)S(1)} all-gather(bf16[352,352]{1,0:T(8,128)(2,1)S(1)} %shard_map.70), channel_id=2, replica_groups=mesh['side'=2,'plane'=32,'chip'=4,'core'=2] {'chip'}, dimensions={0}, use_global_device_ids=true | all-gather | bytes 1239040 | tf_op jit(solution)/shard_map/all_gather | solution.py:285
  98.0 1.9 %collective-permute-start.5 = (bf16[4,352,352]{2,1,0:T(8,128)(2,1)S(1)}, bf16[4,352,352]{2,1,0:T(8,128)(2,1)S(1)}, u32[]{:S(2)}, u32[]{:S(2)}) collective-permute-start(bf16[4,352,352]{2,1,0:T(8,128)(2,1)S(1)} %bitcast.9), channel_id=1, source_target_pairs={{0,1},{1,0},{2,3},{3,2},{4,5},{5,4},{6,7},{7,6},{8,9},{9,8},{10,11... | collective-permute-start | bytes 2973704 | tf_op jit(solution)/shard_map/ppermute | solution.py:286
  100.0 0.5 shard_map.71.own
  100.5 2.1 %collective-permute-done.5.other = bf16[4,352,352]{2,1,0:T(8,128)(2,1)S(1)} collective-permute-done((bf16[4,352,352]{2,1,0:T(8,128)(2,1)S(1)}, bf16[4,352,352]{2,1,0:T(8,128)(2,1)S(1)}, u32[]{:S(2)}, u32[]{:S(2)}) %collective-permute-start.5) | collective-permute-done | bytes 991264 | tf_op jit(solution)/shard_map/ppermute | solution.py:286
  102.6 1.2 shard_map.72
  103.8 22.6 %all_to_all.10.returned = bf16[64,11,2,128]{3,2,1,0:T(2,128)(2,1)S(1)} all-to-all(bf16[64,11,2,128]{3,2,1,0:T(2,128)(2,1)S(1)} %shard_map.72), channel_id=1, replica_groups=mesh['side'=2,'plane'=32,'chip'=4,'core'=2] {'side','plane'}, dimensions={0} | all-to-all | bytes 720896 | tf_op jit(solution)/shard_map/all_to_all | solution.py:296
  126.4 1.3 %shard_map.73 = bf16[64,256]{1,0:T(8,128)(2,1)} custom-call(s32[6,64]{1,0:T(8,128)S(1)} %get-tuple-element.16.target_t, f32[6,64]{1,0:T(8,128)S(1)} %bitcast.13, bf16[64,11,2,128]{3,2,1,0:T(2,128)(2,1)S(1)} %all_to_all.10.returned), custom_call_target="tpu_custom_call" | custom-call | tf_op jit(solution)/shard_map/pallas_call | solution.py:28
  (7 shorter events, 0.4 us)
Async XLA Ops:
  2.0 8.5 %collective-permute-start = (bf16[80,1024]{1,0:T(8,128)(2,1)S(1)}, bf16[80,1024]{1,0:T(8,128)(2,1)S(1)}, u32[]{:S(2)}, u32[]{:S(2)}) collective-permute-start(bf16[80,1024]{1,0:T(8,128)(2,1)S(1)} %get-tuple-element.15.mine), channel_id=1, source_target_pairs={{0,256},{256,0},{1,257},{257,1},{2,258},{258,2},{3,259},{259,3},{4... | collective-permute-start | bytes 491528 | tf_op jit(solution)/shard_map/ppermute | solution.py:222
  13.1 20.5 %collective-permute-start.1 = (bf16[704,256]{1,0:T(8,128)(2,1)S(1)}, bf16[704,256]{1,0:T(8,128)(2,1)S(1)}, u32[]{:S(2)}, u32[]{:S(2)}) collective-permute-start(bf16[704,256]{1,0:T(8,128)(2,1)S(1)} %get-tuple-element.21), channel_id=1, source_target_pairs={{0,4},{2,6},{4,0},{6,2},{1,5},{3,7},{5,1},{7,3},{8,12},{10,14},{12... | collective-permute-start | bytes 1081352 | tf_op jit(solution)/shard_map/ppermute | solution.py:249
  23.4 44.6 %all-to-all-start = ((bf16[32,2,11,8,128]{4,3,2,1,0:T(8,128)(2,1)}), bf16[32,2,11,8,128]{4,3,2,1,0:T(8,128)(2,1)S(1)}, u32[]{:S(2)}, u32[]{:S(2)}) async-start(bf16[32,2,11,8,128]{4,3,2,1,0:T(8,128)(2,1)} %get-tuple-element.18), calls=%async_computation | async-start | bytes 2883584 | tf_op jit(solution)/shard_map/all_to_all | solution.py:247
  35.2 25.6 %collective-permute-start.2 = (bf16[704,256]{1,0:T(8,128)(2,1)S(1)}, bf16[704,256]{1,0:T(8,128)(2,1)S(1)}, u32[]{:S(2)}, u32[]{:S(2)}) collective-permute-start(bf16[704,256]{1,0:T(8,128)(2,1)S(1)} %get-tuple-element.23), channel_id=1, source_target_pairs={{0,2},{2,4},{4,6},{6,0},{1,3},{3,5},{5,7},{7,1},{8,10},{10,12},{12... | collective-permute-start | bytes 1081352 | tf_op jit(solution)/shard_map/ppermute | solution.py:264
  44.6 19.5 %collective-permute-start.3 = (bf16[704,256]{1,0:T(8,128)(2,1)S(1)}, bf16[704,256]{1,0:T(8,128)(2,1)S(1)}, u32[]{:S(2)}, u32[]{:S(2)}) collective-permute-start(bf16[704,256]{1,0:T(8,128)(2,1)S(1)} %get-tuple-element.24), channel_id=1, source_target_pairs={{0,6},{2,0},{4,2},{6,4},{1,7},{3,1},{5,3},{7,5},{8,14},{10,8},{12,... | collective-permute-start | bytes 1081352 | tf_op jit(solution)/shard_map/ppermute | solution.py:265
  69.4 3.8 %collective-permute-start.4 = (bf16[352,704]{1,0:T(8,128)(2,1)S(1)}, bf16[352,704]{1,0:T(8,128)(2,1)S(1)}, u32[]{:S(2)}, u32[]{:S(2)}) collective-permute-start(bf16[352,704]{1,0:T(8,128)(2,1)S(1)} %shard_map.69), channel_id=1, source_target_pairs={{0,1},{1,0},{2,3},{3,2},{4,5},{5,4},{6,7},{7,6},{8,9},{9,8},{10,11... | collective-permute-start | bytes 1486856 | tf_op jit(solution)/shard_map/ppermute | solution.py:275
  73.5 26.5 %copy-start = (bf16[1,1408,256]{2,1,0:T(8,128)(2,1)S(1)}, bf16[1,1408,256]{2,1,0:T(8,128)(2,1)}, u32[]{:S(2)}) copy-start(bf16[1,1408,256]{2,1,0:T(8,128)(2,1)} %param.11) | copy-start | bytes 2162692
  98.0 4.6 %collective-permute-start.5 = (bf16[4,352,352]{2,1,0:T(8,128)(2,1)S(1)}, bf16[4,352,352]{2,1,0:T(8,128)(2,1)S(1)}, u32[]{:S(2)}, u32[]{:S(2)}) collective-permute-start(bf16[4,352,352]{2,1,0:T(8,128)(2,1)S(1)} %bitcast.9), channel_id=1, source_target_pairs={{0,1},{1,0},{2,3},{3,2},{4,5},{5,4},{6,7},{7,6},{8,9},{9,8},{10,11... | collective-permute-start | bytes 2973704 | tf_op jit(solution)/shard_map/ppermute | solution.py:286
  100.5 25.9 %copy-start.1 = (f32[64,6]{0,1:T(8,128)S(1)}, f32[64,6]{0,1:T(8,128)}, u32[]{:S(2)}) copy-start(f32[64,6]{0,1:T(8,128)} %param.8) | copy-start | bytes 4612

commit v12 on v9

--- a/solution.py
+++ b/solution.py
@@ -18,6 +18,7 @@
 HOLD = 30_000_000_000
 PICK = 10_000_000_000
 CHIPS = 4
+GROUPS = 4
 CORE, CHIP, SIDE = range(3)
 
 
@@ -137,23 +138,41 @@
 
 
 def hidden_body(mine, theirs, hidden):
-    units = hidden.shape[1]
     total = mine[...] + theirs[...].astype(jnp.float32)
+    half, units = total.shape[0], total.shape[1] // 2
     gate, up = total[:, :units], total[:, units:]
-    hidden[...] = (gate / (1 + jnp.exp(-gate)) * up).astype(jnp.bfloat16)
+    value = gate / (1 + jnp.exp(-gate)) * up
+    full = units // 128
+    rows = half // GROUPS
+    for n in range(full):
+        hidden[n * half : (n + 1) * half, :] = value[:, n * 128 : (n + 1) * 128].astype(jnp.bfloat16)
+    rest = jnp.concatenate([value[g * rows : (g + 1) * rows, full * 128 :] for g in range(GROUPS)], 1)
+    for n in range(rest.shape[1] // 128):
+        start = full * half + n * rows
+        hidden[start : start + rows, :] = rest[:, n * 128 : (n + 1) * 128].astype(jnp.bfloat16)
 
 
 def down(hidden, w_down):
-    units = hidden.shape[2]
-    total = functools.reduce(
-        jnp.add,
-        [
-            jnp.dot(
-                hidden[z], w_down[z * units : (z + 1) * units, :], preferred_element_type=jnp.float32
-            )
-            for z in range(CHIPS)
-        ],
-    )
+    units = w_down.shape[0] // CHIPS
+    full, left = units // 128, units % 128
+    half = hidden.shape[1] * 128 // units
+    rows = half // GROUPS
+    total = jnp.zeros((half, w_down.shape[1]), jnp.float32)
+    for z in range(CHIPS):
+        main = jnp.concatenate([hidden[z, n * half : (n + 1) * half, :] for n in range(full)], 1)
+        rest = [
+            hidden[z, full * half + n * rows : full * half + (n + 1) * rows, :].astype(jnp.float32)
+            for n in range(GROUPS * left // 128)
+        ]
+        rest = jnp.concatenate(rest, 1)
+        rest = jnp.concatenate([rest[:, g * left : (g + 1) * left] for g in range(GROUPS)], 0)
+        start = z * units
+        total += jnp.dot(main, w_down[start : start + full * 128, :], preferred_element_type=jnp.float32)
+        total += jnp.dot(
+            rest.astype(jnp.bfloat16),
+            w_down[start + full * 128 : start + units, :],
+            preferred_element_type=jnp.float32,
+        )
     return total.astype(jnp.bfloat16)
 
 
@@ -271,7 +290,7 @@
         *weights,
         scalars=1,
     )
-    hidden = call(hidden_body, jax.ShapeDtypeStruct((half, share), bf16), mine, theirs)
+    hidden = call(hidden_body, jax.ShapeDtypeStruct((half * share // 128, 128), bf16), mine, theirs)
     own = lax.all_gather(hidden, "chip", axis=0)
     other = lax.ppermute(own, "core", swap)
     produced = call(

time: 125 us -> 123 us (0.984)
  blocking collectives: 45.9 us -> 44.4 us
    all_gather x1, blocking collectives: 23.9 us -> 22.4 us  [on_device(): own = lax.all_gather(hidden, 'chip', axis=0)]
where the time goes in v12:
time: 123 us
  blocking collectives  44.4 us (36%)
  starting transfers between devices  40.9 us (33%)
  waiting for transfers between devices  23.3 us (19%)
  Pallas kernels  13.8 us (11%)
    all_gather x1, blocking collectives, on_device(): own = lax.all_gather(hidden, 'chip', axis=0)  22.4 us
    all_to_all x1, blocking collectives, on_device(): lax.all_to_all(produced, ('side', 'plane'), split_axis=0, concat_axis=0,...  22 us
    pallas_call x10, Pallas kernels, call(): pl.pallas_call(body, out_shape=outs, in_specs=[SMEM] * scalars + [HBM] *...  13.8 us
    all_to_all x1, starting transfers between devices, on_device(): lax.all_to_all(outgoing, 'plane', split_axis=0, concat_axis=0, tiled=True)  10.2 us
    ppermute x1, starting transfers between devices, on_device(): two = lax.ppermute(two, 'chip', ring[2])  10 us
    ppermute x1, waiting for transfers between devices, on_device(): one = lax.ppermute(one, 'chip', ring[1])  9.57 us
    all_to_all x1, waiting for transfers between devices, on_device(): lax.all_to_all(outgoing, 'plane', split_axis=0, concat_axis=0, tiled=True)  9.27 us
    ppermute x1, starting transfers between devices, on_device(): one = lax.ppermute(one, 'chip', ring[1])  7.39 us
  transfers between devices with their start and end apart: 7, of which 5 were waited for; matrix products, arithmetic and copies ran while one was open for 0% of the time, Pallas kernels for 6%

profile of v12, /device:TPU:8, one launch (start us, length us, event | category | flops | bytes accessed | tf_op | source)
XLA Modules:
  0.0 122.7 jit_solution(16469709220733362766)
XLA Ops:
  0.1 2.0 %shard_map.64 = (bf16[80,1024]{1,0:T(8,128)(2,1)S(1)}, bf16[704,256]{1,0:T(8,128)(2,1)S(1)}, bf16[704,256]{1,0:T(8,128)(2,1)S(1)}, bf16[704,256]{1,0:T(8,128)(2,1)S(1)}) custom-call(s32[3]{0:T(128)S(1)} %pad_add_fusion.place, s32[6,64]{1,0:T(8,128)} %bitcast.18, bf16[64,2048]{1,0:T(8,128)(2,1)} %tokens_hbm.1, bf16[1408,256]{1,0:T(8,128)(2,1)} %bitcast.14, ...), custom_call_target="tpu_custom_call" | custom-call | tf_op jit(solution)/shard_map/pallas_call | solution.py:30
  2.1 4.3 %collective-permute-start = (bf16[80,1024]{1,0:T(8,128)(2,1)S(1)}, bf16[80,1024]{1,0:T(8,128)(2,1)S(1)}, u32[]{:S(2)}, u32[]{:S(2)}) collective-permute-start(bf16[80,1024]{1,0:T(8,128)(2,1)S(1)} %get-tuple-element.14.mine), channel_id=1, source_target_pairs={{0,256},{256,0},{1,257},{257,1},{2,258},{258,2},{3,259},{259,3},{4... | collective-permute-start | bytes 491528 | tf_op jit(solution)/shard_map/ppermute | solution.py:234
  6.4 10.0 %collective-permute-start.1 = (bf16[704,256]{1,0:T(8,128)(2,1)S(1)}, bf16[704,256]{1,0:T(8,128)(2,1)S(1)}, u32[]{:S(2)}, u32[]{:S(2)}) collective-permute-start(bf16[704,256]{1,0:T(8,128)(2,1)S(1)} %get-tuple-element.19), channel_id=1, source_target_pairs={{0,4},{2,6},{4,0},{6,2},{1,5},{3,7},{5,1},{7,3},{8,12},{10,14},{12... | collective-permute-start | bytes 1081352 | tf_op jit(solution)/shard_map/ppermute | solution.py:258
  16.4 1.5 %shard_map.65 = (bf16[32,11,8,128]{3,2,1,0:T(8,128)(2,1)S(1)}, s32[6,64]{1,0:T(8,128)S(1)}) custom-call(s32[3]{0:T(128)S(1)} %pad_add_fusion.place, bf16[80,1024]{1,0:T(8,128)(2,1)S(1)} %get-tuple-element.14.mine), custom_call_target="tpu_custom_call" | custom-call | tf_op jit(solution)/shard_map/pallas_call | solution.py:30
  17.9 2.7 %shard_map.66 = bf16[32,2,11,8,128]{4,3,2,1,0:T(8,128)(2,1)} custom-call(s32[3]{0:T(128)S(1)} %pad_add_fusion.place, bf16[32,11,8,128]{3,2,1,0:T(8,128)(2,1)S(1)} %get-tuple-element.16.own, bf16[80,1024]{1,0:T(8,128)(2,1)S(1)} %collective-permute-done.neighbour), custom_call_target="tpu_custom_call" | custom-call | flops 10000000000 | tf_op jit(solution)/shard_map/pallas_call | solution.py:30
  20.6 10.2 %all-to-all-start = ((bf16[32,2,11,8,128]{4,3,2,1,0:T(8,128)(2,1)}), bf16[32,2,11,8,128]{4,3,2,1,0:T(8,128)(2,1)S(1)}, u32[]{:S(2)}, u32[]{:S(2)}) async-start(bf16[32,2,11,8,128]{4,3,2,1,0:T(8,128)(2,1)} %shard_map.66), calls=%async_computation | async-start | bytes 2883584 | tf_op jit(solution)/shard_map/all_to_all | solution.py:256
  30.7 1.6 %shard_map.67 = (bf16[704,256]{1,0:T(8,128)(2,1)S(1)}, bf16[704,256]{1,0:T(8,128)(2,1)S(1)}, bf16[704,256]{1,0:T(8,128)(2,1)S(1)}) custom-call(s32[3]{0:T(128)S(1)} %pad_add_fusion.place, bf16[1408,256]{1,0:T(8,128)(2,1)} %bitcast.15, bf16[1408,256]{1,0:T(8,128)(2,1)} %bitcast.17, bf16[704,256]{1,0:T(8,128)(2,1)S(1)} %get-tuple-element.17.one, ...), custom_call_target="tpu_custom_call" | custom-call | flops 30000001024 | tf_op jit(solution)/shard_map/pallas_call | solution.py:30
  32.3 7.4 %collective-permute-start.2 = (bf16[704,256]{1,0:T(8,128)(2,1)S(1)}, bf16[704,256]{1,0:T(8,128)(2,1)S(1)}, u32[]{:S(2)}, u32[]{:S(2)}) collective-permute-start(bf16[704,256]{1,0:T(8,128)(2,1)S(1)} %get-tuple-element.21), channel_id=1, source_target_pairs={{0,2},{2,4},{4,6},{6,0},{1,3},{3,5},{5,7},{7,1},{8,10},{10,12},{12... | collective-permute-start | bytes 1081352 | tf_op jit(solution)/shard_map/ppermute | solution.py:273
  39.7 5.2 %collective-permute-start.3 = (bf16[704,256]{1,0:T(8,128)(2,1)S(1)}, bf16[704,256]{1,0:T(8,128)(2,1)S(1)}, u32[]{:S(2)}, u32[]{:S(2)}) collective-permute-start(bf16[704,256]{1,0:T(8,128)(2,1)S(1)} %get-tuple-element.22), channel_id=1, source_target_pairs={{0,6},{2,0},{4,2},{6,4},{1,7},{3,1},{5,3},{7,5},{8,14},{10,8},{12,... | collective-permute-start | bytes 1081352 | tf_op jit(solution)/shard_map/ppermute | solution.py:274
  45.0 9.6 %collective-permute-done.2.refs_1_ = bf16[704,256]{1,0:T(8,128)(2,1)S(1)} collective-permute-done((bf16[704,256]{1,0:T(8,128)(2,1)S(1)}, bf16[704,256]{1,0:T(8,128)(2,1)S(1)}, u32[]{:S(2)}, u32[]{:S(2)}) %collective-permute-start.2) | collective-permute-done | bytes 360480 | tf_op jit(solution)/shard_map/ppermute | solution.py:273
  54.5 2.0 %collective-permute-done.3.refs_3_ = bf16[704,256]{1,0:T(8,128)(2,1)S(1)} collective-permute-done((bf16[704,256]{1,0:T(8,128)(2,1)S(1)}, bf16[704,256]{1,0:T(8,128)(2,1)S(1)}, u32[]{:S(2)}, u32[]{:S(2)}) %collective-permute-start.3) | collective-permute-done | bytes 360480 | tf_op jit(solution)/shard_map/ppermute | solution.py:274
  56.5 9.3 %all-to-all-done.rows = bf16[32,2,11,8,128]{4,3,2,1,0:T(8,128)(2,1)S(1)} async-done(((bf16[32,2,11,8,128]{4,3,2,1,0:T(8,128)(2,1)}), bf16[32,2,11,8,128]{4,3,2,1,0:T(8,128)(2,1)S(1)}, u32[]{:S(2)}, u32[]{:S(2)}) %all-to-all-start) | async-done | bytes 1441824 | tf_op jit(solution)/shard_map/all_to_all | solution.py:256
  65.8 1.3 %shard_map.69 = bf16[352,704]{1,0:T(8,128)(2,1)S(1)} custom-call(s32[3]{0:T(128)S(1)} %pad_add_fusion.place, bf16[32,2,11,8,128]{4,3,2,1,0:T(8,128)(2,1)S(1)} %all-to-all-done.rows, bf16[704,256]{1,0:T(8,128)(2,1)S(1)} %get-tuple-element.20.refs_0_, bf16[704,256]{1,0:T(8,128)(2,1)S(1)} %collective-permute-done.2.refs_1_, ...), custom_call_target="tpu_custom_call" | custom-call | tf_op jit(solution)/shard_map/pallas_call | solution.py:30
  67.1 1.9 %collective-permute-start.4 = (bf16[352,704]{1,0:T(8,128)(2,1)S(1)}, bf16[352,704]{1,0:T(8,128)(2,1)S(1)}, u32[]{:S(2)}, u32[]{:S(2)}) collective-permute-start(bf16[352,704]{1,0:T(8,128)(2,1)S(1)} %shard_map.69), channel_id=1, source_target_pairs={{0,1},{1,0},{2,3},{3,2},{4,5},{5,4},{6,7},{7,6},{8,9},{9,8},{10,11... | collective-permute-start | bytes 1486856 | tf_op jit(solution)/shard_map/ppermute | solution.py:284
  69.0 1.3 %shard_map.68.mine = f32[352,704]{1,0:T(8,128)S(1)} custom-call(s32[3]{0:T(128)S(1)} %pad_add_fusion.place, bf16[32,2,11,8,128]{4,3,2,1,0:T(8,128)(2,1)S(1)} %all-to-all-done.rows, bf16[704,256]{1,0:T(8,128)(2,1)S(1)} %get-tuple-element.20.refs_0_, bf16[704,256]{1,0:T(8,128)(2,1)S(1)} %collective-permute-done.2.refs_1_, ...), custom_call_target="tpu_custom_call" | custom-call | tf_op jit(solution)/shard_map/pallas_call | solution.py:30
  70.3 0.6 collective-permute-done.4.theirs
  70.9 0.3 shard_map.70
  71.2 22.4 %all-gather = bf16[3872,128]{1,0:T(8,128)(2,1)S(1)} all-gather(bf16[968,128]{1,0:T(8,128)(2,1)S(1)} %shard_map.70), channel_id=2, replica_groups=mesh['side'=2,'plane'=32,'chip'=4,'core'=2] {'chip'}, dimensions={0}, use_global_device_ids=true | all-gather | bytes 1239040 | tf_op jit(solution)/shard_map/all_gather | solution.py:294
  93.6 1.9 %collective-permute-start.5 = (bf16[4,968,128]{2,1,0:T(8,128)(2,1)S(1)}, bf16[4,968,128]{2,1,0:T(8,128)(2,1)S(1)}, u32[]{:S(2)}, u32[]{:S(2)}) collective-permute-start(bf16[4,968,128]{2,1,0:T(8,128)(2,1)S(1)} %bitcast.9), channel_id=1, source_target_pairs={{0,1},{1,0},{2,3},{3,2},{4,5},{5,4},{6,7},{7,6},{8,9},{9,8},{10,11... | collective-permute-start | bytes 2973704 | tf_op jit(solution)/shard_map/ppermute | solution.py:295
  95.6 0.6 shard_map.71.own
  96.2 1.9 %collective-permute-done.5.other = bf16[4,968,128]{2,1,0:T(8,128)(2,1)S(1)} collective-permute-done((bf16[4,968,128]{2,1,0:T(8,128)(2,1)S(1)}, bf16[4,968,128]{2,1,0:T(8,128)(2,1)S(1)}, u32[]{:S(2)}, u32[]{:S(2)}) %collective-permute-start.5) | collective-permute-done | bytes 991264 | tf_op jit(solution)/shard_map/ppermute | solution.py:295
  98.1 1.3 %shard_map.72 = bf16[64,11,2,128]{3,2,1,0:T(2,128)(2,1)S(1)} custom-call(s32[3]{0:T(128)S(1)} %pad_add_fusion.place, bf16[352,256]{1,0:T(8,128)(2,1)S(1)} %shard_map.71.own, bf16[4,968,128]{2,1,0:T(8,128)(2,1)S(1)} %collective-permute-done.5.other, bf16[1408,256]{1,0:T(8,128)(2,1)S(1)} %bitcast.12), custom_call_target="tpu_custom_call" | custom-call | tf_op jit(solution)/shard_map/pallas_call | solution.py:30
  99.4 22.0 %all_to_all.10.returned = bf16[64,11,2,128]{3,2,1,0:T(2,128)(2,1)S(1)} all-to-all(bf16[64,11,2,128]{3,2,1,0:T(2,128)(2,1)S(1)} %shard_map.72), channel_id=1, replica_groups=mesh['side'=2,'plane'=32,'chip'=4,'core'=2] {'side','plane'}, dimensions={0} | all-to-all | bytes 720896 | tf_op jit(solution)/shard_map/all_to_all | solution.py:305
  121.4 1.3 %shard_map.73 = bf16[64,256]{1,0:T(8,128)(2,1)} custom-call(s32[6,64]{1,0:T(8,128)S(1)} %get-tuple-element.15.target_t, f32[6,64]{1,0:T(8,128)S(1)} %bitcast.13, bf16[64,11,2,128]{3,2,1,0:T(2,128)(2,1)S(1)} %all_to_all.10.returned), custom_call_target="tpu_custom_call" | custom-call | tf_op jit(solution)/shard_map/pallas_call | solution.py:30
  (7 shorter events, 0.1 us)
Async XLA Ops:
  2.1 15.8 %collective-permute-start = (bf16[80,1024]{1,0:T(8,128)(2,1)S(1)}, bf16[80,1024]{1,0:T(8,128)(2,1)S(1)}, u32[]{:S(2)}, u32[]{:S(2)}) collective-permute-start(bf16[80,1024]{1,0:T(8,128)(2,1)S(1)} %get-tuple-element.14.mine), channel_id=1, source_target_pairs={{0,256},{256,0},{1,257},{257,1},{2,258},{258,2},{3,259},{259,3},{4... | collective-permute-start | bytes 491528 | tf_op jit(solution)/shard_map/ppermute | solution.py:234
  6.4 24.3 %collective-permute-start.1 = (bf16[704,256]{1,0:T(8,128)(2,1)S(1)}, bf16[704,256]{1,0:T(8,128)(2,1)S(1)}, u32[]{:S(2)}, u32[]{:S(2)}) collective-permute-start(bf16[704,256]{1,0:T(8,128)(2,1)S(1)} %get-tuple-element.19), channel_id=1, source_target_pairs={{0,4},{2,6},{4,0},{6,2},{1,5},{3,7},{5,1},{7,3},{8,12},{10,14},{12... | collective-permute-start | bytes 1081352 | tf_op jit(solution)/shard_map/ppermute | solution.py:258
  20.6 45.2 %all-to-all-start = ((bf16[32,2,11,8,128]{4,3,2,1,0:T(8,128)(2,1)}), bf16[32,2,11,8,128]{4,3,2,1,0:T(8,128)(2,1)S(1)}, u32[]{:S(2)}, u32[]{:S(2)}) async-start(bf16[32,2,11,8,128]{4,3,2,1,0:T(8,128)(2,1)} %shard_map.66), calls=%async_computation | async-start | bytes 2883584 | tf_op jit(solution)/shard_map/all_to_all | solution.py:256
  32.3 22.2 %collective-permute-start.2 = (bf16[704,256]{1,0:T(8,128)(2,1)S(1)}, bf16[704,256]{1,0:T(8,128)(2,1)S(1)}, u32[]{:S(2)}, u32[]{:S(2)}) collective-permute-start(bf16[704,256]{1,0:T(8,128)(2,1)S(1)} %get-tuple-element.21), channel_id=1, source_target_pairs={{0,2},{2,4},{4,6},{6,0},{1,3},{3,5},{5,7},{7,1},{8,10},{10,12},{12... | collective-permute-start | bytes 1081352 | tf_op jit(solution)/shard_map/ppermute | solution.py:273
  39.7 16.8 %collective-permute-start.3 = (bf16[704,256]{1,0:T(8,128)(2,1)S(1)}, bf16[704,256]{1,0:T(8,128)(2,1)S(1)}, u32[]{:S(2)}, u32[]{:S(2)}) collective-permute-start(bf16[704,256]{1,0:T(8,128)(2,1)S(1)} %get-tuple-element.22), channel_id=1, source_target_pairs={{0,6},{2,0},{4,2},{6,4},{1,7},{3,1},{5,3},{7,5},{8,14},{10,8},{12,... | collective-permute-start | bytes 1081352 | tf_op jit(solution)/shard_map/ppermute | solution.py:274
  67.1 3.8 %collective-permute-start.4 = (bf16[352,704]{1,0:T(8,128)(2,1)S(1)}, bf16[352,704]{1,0:T(8,128)(2,1)S(1)}, u32[]{:S(2)}, u32[]{:S(2)}) collective-permute-start(bf16[352,704]{1,0:T(8,128)(2,1)S(1)} %shard_map.69), channel_id=1, source_target_pairs={{0,1},{1,0},{2,3},{3,2},{4,5},{5,4},{6,7},{7,6},{8,9},{9,8},{10,11... | collective-permute-start | bytes 1486856 | tf_op jit(solution)/shard_map/ppermute | solution.py:284
  70.3 25.2 %copy-start = (bf16[1,1408,256]{2,1,0:T(8,128)(2,1)S(1)}, bf16[1,1408,256]{2,1,0:T(8,128)(2,1)}, u32[]{:S(2)}) copy-start(bf16[1,1408,256]{2,1,0:T(8,128)(2,1)} %param.11) | copy-start | bytes 2162692
  93.6 4.5 %collective-permute-start.5 = (bf16[4,968,128]{2,1,0:T(8,128)(2,1)S(1)}, bf16[4,968,128]{2,1,0:T(8,128)(2,1)S(1)}, u32[]{:S(2)}, u32[]{:S(2)}) collective-permute-start(bf16[4,968,128]{2,1,0:T(8,128)(2,1)S(1)} %bitcast.9), channel_id=1, source_target_pairs={{0,1},{1,0},{2,3},{3,2},{4,5},{5,4},{6,7},{7,6},{8,9},{9,8},{10,11... | collective-permute-start | bytes 2973704 | tf_op jit(solution)/shard_map/ppermute | solution.py:295
  96.2 25.2 %copy-start.1 = (f32[64,6]{0,1:T(8,128)S(1)}, f32[64,6]{0,1:T(8,128)}, u32[]{:S(2)}) copy-start(f32[64,6]{0,1:T(8,128)} %param.8) | copy-start | bytes 4612

commit v13 on v12

--- a/solution.py
+++ b/solution.py
@@ -50,19 +50,24 @@
     return pl.ds(pl.multiple_of(start, 16), share)
 
 
+def slices(place, w_gate, w_up, shift, out):
+    share = out.shape[0] // 2
+    return [
+        (w.at[units_of(place, shift, share), :], out.at[n * share : (n + 1) * share, :])
+        for n, w in enumerate((w_gate, w_up))
+    ]
+
+
 def first_body(place, routes_hbm, tokens_hbm, w_gate, w_up, mine, *refs):
-    *pieces, routes_t, sems = refs
+    two, routes_t, sems = refs
     top, rows = routes_t.shape
     cols = mine.shape[1] // CHIPS
-    share = pieces[0].shape[0] // 2
     pairs = [(routes_hbm, routes_t)]
     for shift in range(CHIPS):
         block = lax.rem(place[CHIP] - shift + CHIPS, CHIPS) * 2 + place[CORE]
         columns = pl.ds(pl.multiple_of(block * cols, cols), cols)
         pairs.append((tokens_hbm.at[:, columns], mine.at[:rows, shift * cols : (shift + 1) * cols]))
-    for shift, out in enumerate(pieces, 1):
-        pairs.append((w_gate.at[units_of(place, shift, share), :], out.at[:share, :]))
-        pairs.append((w_up.at[units_of(place, shift, share), :], out.at[share:, :]))
+    pairs += slices(place, w_gate, w_up, 2, two)
     copies = copy_all(pairs, sems)
     mine[rows:, :] = jnp.zeros((mine.shape[0] - rows, mine.shape[1]), mine.dtype)
     copies[0].wait()
@@ -72,12 +77,7 @@
 
 
 def hold_body(place, w_gate, w_up, one, three, _, here, one_out, three_out, sems):
-    share = here.shape[0] // 2
-    pairs = [
-        (w.at[units_of(place, 0, share), :], here.at[n * share : (n + 1) * share, :])
-        for n, w in enumerate((w_gate, w_up))
-    ]
-    copies = copy_all(pairs, sems)
+    copies = copy_all(slices(place, w_gate, w_up, 0, here), sems)
     one_out[...] = one[...]
     three_out[...] = three[...]
     for copy in copies:
@@ -107,13 +107,13 @@
     return rows_out.astype(jnp.bfloat16).reshape(side, cap, block.shape[1] // 128, 128)
 
 
-def own_body(sizes, place, mine, out, target_t):
-    out[...] = picked(*sizes, place, mine, target_t)
-
-
-def dispatch_body(sizes, place, own, neighbour, outgoing):
+def dispatch_body(sizes, place, w_gate, w_up, mine, neighbour, outgoing, target_t, one, three, sems):
+    pairs = slices(place, w_gate, w_up, 1, one) + slices(place, w_gate, w_up, 3, three)
+    copies = copy_all(pairs, sems)
+    outgoing[:, place[SIDE]] = picked(*sizes, place, mine, target_t)
     outgoing[:, 1 - place[SIDE]] = picked(*sizes, place, neighbour)
-    outgoing[:, place[SIDE]] = own[...]
+    for copy in copies:
+        copy.wait()
 
 
 def gate_up_body(mine, place, rows, *refs):
@@ -219,9 +219,9 @@
     place = jnp.stack([lax.axis_index(a) for a in ("core", "chip", "side")]).astype(jnp.int32)
 
     part = jax.ShapeDtypeStruct((2 * share, cols), bf16)
-    mine, one, two, three = call(
+    mine, two = call(
         first_body,
-        (jax.ShapeDtypeStruct((tok_count + 16, CHIPS * cols), bf16),) + (part,) * (CHIPS - 1),
+        (jax.ShapeDtypeStruct((tok_count + 16, CHIPS * cols), bf16),) + (part,),
         place,
         routes.T,
         tokens,
@@ -229,28 +229,27 @@
         w_up[0],
         scalars=1,
         raw=4,
-        scratch=[pltpu.VMEM((top, tok_count), jnp.int32), dma((3 * CHIPS - 1,))],
+        scratch=[pltpu.VMEM((top, tok_count), jnp.int32), dma((CHIPS + 3,))],
     )
     neighbour = lax.ppermute(mine, "side", swap)
     sizes = (top, cap, experts, side)
     chunk = (cap, CHIPS * cols // 128, 128)
-    picked_own, target_t = call(
-        functools.partial(own_body, sizes),
+    outgoing, target_t, one, three = call(
+        functools.partial(dispatch_body, sizes),
         (
-            jax.ShapeDtypeStruct((side, *chunk), bf16),
+            jax.ShapeDtypeStruct((side, 2, *chunk), bf16),
             jax.ShapeDtypeStruct((top, tok_count), jnp.int32),
+            part,
+            part,
         ),
         place,
+        w_gate[0],
+        w_up[0],
         mine,
-        scalars=1,
-    )
-    outgoing = call(
-        functools.partial(dispatch_body, sizes),
-        jax.ShapeDtypeStruct((side, 2, *chunk), bf16),
-        place,
-        picked_own,
         neighbour,
         scalars=1,
+        raw=2,
+        scratch=[dma((4,))],
         flops=PICK,
     )
     received = lax.all_to_all(outgoing, "plane", split_axis=0, concat_axis=0, tiled=True)

time: 123 us -> 123 us (level)
  starting transfers between devices: 40.9 us -> 42.4 us
  waiting for transfers between devices: 23.3 us -> 21.9 us
    ppermute x1, waiting for transfers between devices: 9.57 us -> 7.2 us  [on_device(): one = lax.ppermute(one, 'chip', ring[1])]
    ppermute x1, starting transfers between devices: 5.24 us -> 6.5 us  [on_device(): three = lax.ppermute(three, 'chip', ring[3])]
    pallas_call x10 -> x9, Pallas kernels: 13.8 us -> 13.3 us  [call(): pl.pallas_call(body, out_shape=outs, in_specs=[SMEM] * scalars + [HBM] *...]
where the time goes in v13:
time: 123 us; the launch traced here: 122 us
  blocking collectives  44.7 us (36%)
  starting transfers between devices  42.4 us (34%)
  waiting for transfers between devices  21.9 us (18%)
  Pallas kernels  13.3 us (11%)
    all_gather x1, blocking collectives, on_device(): own = lax.all_gather(hidden, 'chip', axis=0)  22.8 us
    all_to_all x1, blocking collectives, on_device(): lax.all_to_all(produced, ('side', 'plane'), split_axis=0, concat_axis=0,...  22 us
    pallas_call x9, Pallas kernels, call(): pl.pallas_call(body, out_shape=outs, in_specs=[SMEM] * scalars + [HBM] *...  13.3 us
    all_to_all x1, starting transfers between devices, on_device(): lax.all_to_all(outgoing, 'plane', split_axis=0, concat_axis=0, tiled=True)  10.2 us
    ppermute x1, starting transfers between devices, on_device(): two = lax.ppermute(two, 'chip', ring[2])  10 us
    all_to_all x1, waiting for transfers between devices, on_device(): lax.all_to_all(outgoing, 'plane', split_axis=0, concat_axis=0, tiled=True)  9.08 us
    ppermute x1, starting transfers between devices, on_device(): one = lax.ppermute(one, 'chip', ring[1])  7.58 us
    ppermute x1, waiting for transfers between devices, on_device(): one = lax.ppermute(one, 'chip', ring[1])  7.2 us
  transfers between devices with their start and end apart: 7, of which 5 were waited for; matrix products, arithmetic and copies ran while one was open for 0% of the time, Pallas kernels for 6%

profile of v13, /device:TPU:8, one launch (start us, length us, event | category | flops | bytes accessed | tf_op | source)
XLA Modules:
  0.0 122.5 jit_solution(18126270446392973380)
XLA Ops:
  0.0 0.1 pad_add_fusion.place
  0.1 1.7 %shard_map.64 = (bf16[80,1024]{1,0:T(8,128)(2,1)S(1)}, bf16[704,256]{1,0:T(8,128)(2,1)S(1)}) custom-call(s32[3]{0:T(128)S(1)} %pad_add_fusion.place, s32[6,64]{1,0:T(8,128)} %bitcast.20, bf16[64,2048]{1,0:T(8,128)(2,1)} %tokens_hbm.1, bf16[1408,256]{1,0:T(8,128)(2,1)} %bitcast.14, bf16[1408,256]{1,0:T(8,128)(2,1)} %bitcast.17), custom_call_target="tpu_custom_call" | custom-call | tf_op jit(solution)/shard_map/pallas_call | solution.py:30
  1.8 4.3 %collective-permute-start = (bf16[80,1024]{1,0:T(8,128)(2,1)S(1)}, bf16[80,1024]{1,0:T(8,128)(2,1)S(1)}, u32[]{:S(2)}, u32[]{:S(2)}) collective-permute-start(bf16[80,1024]{1,0:T(8,128)(2,1)S(1)} %get-tuple-element.14.mine), channel_id=1, source_target_pairs={{0,256},{256,0},{1,257},{257,1},{2,258},{258,2},{3,259},{259,3},{4... | collective-permute-start | bytes 491528 | tf_op jit(solution)/shard_map/ppermute | solution.py:234
  6.1 10.0 %collective-permute-start.1 = (bf16[704,256]{1,0:T(8,128)(2,1)S(1)}, bf16[704,256]{1,0:T(8,128)(2,1)S(1)}, u32[]{:S(2)}, u32[]{:S(2)}) collective-permute-start(bf16[704,256]{1,0:T(8,128)(2,1)S(1)} %get-tuple-element.19), channel_id=1, source_target_pairs={{0,4},{2,6},{4,0},{6,2},{1,5},{3,7},{5,1},{7,3},{8,12},{10,14},{12... | collective-permute-start | bytes 1081352 | tf_op jit(solution)/shard_map/ppermute | solution.py:257
  16.1 3.9 %shard_map.65 = (bf16[32,2,11,8,128]{4,3,2,1,0:T(8,128)(2,1)}, s32[6,64]{1,0:T(8,128)S(1)}, bf16[704,256]{1,0:T(8,128)(2,1)S(1)}, bf16[704,256]{1,0:T(8,128)(2,1)S(1)}) custom-call(s32[3]{0:T(128)S(1)} %pad_add_fusion.place, bf16[1408,256]{1,0:T(8,128)(2,1)} %bitcast.15, bf16[1408,256]{1,0:T(8,128)(2,1)} %bitcast.18, ...), custom_call_target="tpu_custom_call" | custom-call | flops 10000000000 | tf_op jit(solution)/shard_map/pallas_call | solution.py:30
  20.0 10.2 %all-to-all-start = ((bf16[32,2,11,8,128]{4,3,2,1,0:T(8,128)(2,1)}), bf16[32,2,11,8,128]{4,3,2,1,0:T(8,128)(2,1)S(1)}, u32[]{:S(2)}, u32[]{:S(2)}) async-start(bf16[32,2,11,8,128]{4,3,2,1,0:T(8,128)(2,1)} %get-tuple-element.16), calls=%async_computation | async-start | bytes 2883584 | tf_op jit(solution)/shard_map/all_to_all | solution.py:255
  30.2 1.6 %shard_map.66 = (bf16[704,256]{1,0:T(8,128)(2,1)S(1)}, bf16[704,256]{1,0:T(8,128)(2,1)S(1)}, bf16[704,256]{1,0:T(8,128)(2,1)S(1)}) custom-call(s32[3]{0:T(128)S(1)} %pad_add_fusion.place, bf16[1408,256]{1,0:T(8,128)(2,1)} %bitcast.16, bf16[1408,256]{1,0:T(8,128)(2,1)} %bitcast.19, bf16[704,256]{1,0:T(8,128)(2,1)S(1)} %get-tuple-element.17.one, ...), custom_call_target="tpu_custom_call" | custom-call | flops 30000001024 | tf_op jit(solution)/shard_map/pallas_call | solution.py:30
  31.8 7.6 %collective-permute-start.2 = (bf16[704,256]{1,0:T(8,128)(2,1)S(1)}, bf16[704,256]{1,0:T(8,128)(2,1)S(1)}, u32[]{:S(2)}, u32[]{:S(2)}) collective-permute-start(bf16[704,256]{1,0:T(8,128)(2,1)S(1)} %get-tuple-element.21), channel_id=1, source_target_pairs={{0,2},{2,4},{4,6},{6,0},{1,3},{3,5},{5,7},{7,1},{8,10},{10,12},{12... | collective-permute-start | bytes 1081352 | tf_op jit(solution)/shard_map/ppermute | solution.py:272
  39.4 6.5 %collective-permute-start.3 = (bf16[704,256]{1,0:T(8,128)(2,1)S(1)}, bf16[704,256]{1,0:T(8,128)(2,1)S(1)}, u32[]{:S(2)}, u32[]{:S(2)}) collective-permute-start(bf16[704,256]{1,0:T(8,128)(2,1)S(1)} %get-tuple-element.22), channel_id=1, source_target_pairs={{0,6},{2,0},{4,2},{6,4},{1,7},{3,1},{5,3},{7,5},{8,14},{10,8},{12,... | collective-permute-start | bytes 1081352 | tf_op jit(solution)/shard_map/ppermute | solution.py:273
  45.9 7.2 %collective-permute-done.2.refs_1_ = bf16[704,256]{1,0:T(8,128)(2,1)S(1)} collective-permute-done((bf16[704,256]{1,0:T(8,128)(2,1)S(1)}, bf16[704,256]{1,0:T(8,128)(2,1)S(1)}, u32[]{:S(2)}, u32[]{:S(2)}) %collective-permute-start.2) | collective-permute-done | bytes 360480 | tf_op jit(solution)/shard_map/ppermute | solution.py:272
  53.1 3.1 %collective-permute-done.3.refs_3_ = bf16[704,256]{1,0:T(8,128)(2,1)S(1)} collective-permute-done((bf16[704,256]{1,0:T(8,128)(2,1)S(1)}, bf16[704,256]{1,0:T(8,128)(2,1)S(1)}, u32[]{:S(2)}, u32[]{:S(2)}) %collective-permute-start.3) | collective-permute-done | bytes 360480 | tf_op jit(solution)/shard_map/ppermute | solution.py:273
  56.2 9.1 %all-to-all-done.rows = bf16[32,2,11,8,128]{4,3,2,1,0:T(8,128)(2,1)S(1)} async-done(((bf16[32,2,11,8,128]{4,3,2,1,0:T(8,128)(2,1)}), bf16[32,2,11,8,128]{4,3,2,1,0:T(8,128)(2,1)S(1)}, u32[]{:S(2)}, u32[]{:S(2)}) %all-to-all-start) | async-done | bytes 1441824 | tf_op jit(solution)/shard_map/all_to_all | solution.py:255
  65.3 1.3 %shard_map.68 = bf16[352,704]{1,0:T(8,128)(2,1)S(1)} custom-call(s32[3]{0:T(128)S(1)} %pad_add_fusion.place, bf16[32,2,11,8,128]{4,3,2,1,0:T(8,128)(2,1)S(1)} %all-to-all-done.rows, bf16[704,256]{1,0:T(8,128)(2,1)S(1)} %get-tuple-element.20.refs_0_, bf16[704,256]{1,0:T(8,128)(2,1)S(1)} %collective-permute-done.2.refs_1_, ...), custom_call_target="tpu_custom_call" | custom-call | tf_op jit(solution)/shard_map/pallas_call | solution.py:30
  66.6 1.9 %collective-permute-start.4 = (bf16[352,704]{1,0:T(8,128)(2,1)S(1)}, bf16[352,704]{1,0:T(8,128)(2,1)S(1)}, u32[]{:S(2)}, u32[]{:S(2)}) collective-permute-start(bf16[352,704]{1,0:T(8,128)(2,1)S(1)} %shard_map.68), channel_id=1, source_target_pairs={{0,1},{1,0},{2,3},{3,2},{4,5},{5,4},{6,7},{7,6},{8,9},{9,8},{10,11... | collective-permute-start | bytes 1486856 | tf_op jit(solution)/shard_map/ppermute | solution.py:283
  68.5 1.3 %shard_map.67.mine = f32[352,704]{1,0:T(8,128)S(1)} custom-call(s32[3]{0:T(128)S(1)} %pad_add_fusion.place, bf16[32,2,11,8,128]{4,3,2,1,0:T(8,128)(2,1)S(1)} %all-to-all-done.rows, bf16[704,256]{1,0:T(8,128)(2,1)S(1)} %get-tuple-element.20.refs_0_, bf16[704,256]{1,0:T(8,128)(2,1)S(1)} %collective-permute-done.2.refs_1_, ...), custom_call_target="tpu_custom_call" | custom-call | tf_op jit(solution)/shard_map/pallas_call | solution.py:30
  69.8 0.6 collective-permute-done.4.theirs
  70.4 0.3 shard_map.69
  70.7 22.8 %all-gather = bf16[3872,128]{1,0:T(8,128)(2,1)S(1)} all-gather(bf16[968,128]{1,0:T(8,128)(2,1)S(1)} %shard_map.69), channel_id=2, replica_groups=mesh['side'=2,'plane'=32,'chip'=4,'core'=2] {'chip'}, dimensions={0}, use_global_device_ids=true | all-gather | bytes 1239040 | tf_op jit(solution)/shard_map/all_gather | solution.py:293
  93.5 1.9 %collective-permute-start.5 = (bf16[4,968,128]{2,1,0:T(8,128)(2,1)S(1)}, bf16[4,968,128]{2,1,0:T(8,128)(2,1)S(1)}, u32[]{:S(2)}, u32[]{:S(2)}) collective-permute-start(bf16[4,968,128]{2,1,0:T(8,128)(2,1)S(1)} %bitcast.9), channel_id=1, source_target_pairs={{0,1},{1,0},{2,3},{3,2},{4,5},{5,4},{6,7},{7,6},{8,9},{9,8},{10,11... | collective-permute-start | bytes 2973704 | tf_op jit(solution)/shard_map/ppermute | solution.py:294
  95.4 0.6 shard_map.70.own
  96.0 1.9 %collective-permute-done.5.other = bf16[4,968,128]{2,1,0:T(8,128)(2,1)S(1)} collective-permute-done((bf16[4,968,128]{2,1,0:T(8,128)(2,1)S(1)}, bf16[4,968,128]{2,1,0:T(8,128)(2,1)S(1)}, u32[]{:S(2)}, u32[]{:S(2)}) %collective-permute-start.5) | collective-permute-done | bytes 991264 | tf_op jit(solution)/shard_map/ppermute | solution.py:294
  97.9 1.3 %shard_map.71 = bf16[64,11,2,128]{3,2,1,0:T(2,128)(2,1)S(1)} custom-call(s32[3]{0:T(128)S(1)} %pad_add_fusion.place, bf16[352,256]{1,0:T(8,128)(2,1)S(1)} %shard_map.70.own, bf16[4,968,128]{2,1,0:T(8,128)(2,1)S(1)} %collective-permute-done.5.other, bf16[1408,256]{1,0:T(8,128)(2,1)S(1)} %bitcast.12), custom_call_target="tpu_custom_call" | custom-call | tf_op jit(solution)/shard_map/pallas_call | solution.py:30
  99.2 22.0 %all_to_all.10.returned = bf16[64,11,2,128]{3,2,1,0:T(2,128)(2,1)S(1)} all-to-all(bf16[64,11,2,128]{3,2,1,0:T(2,128)(2,1)S(1)} %shard_map.71), channel_id=1, replica_groups=mesh['side'=2,'plane'=32,'chip'=4,'core'=2] {'side','plane'}, dimensions={0} | all-to-all | bytes 720896 | tf_op jit(solution)/shard_map/all_to_all | solution.py:304
  121.2 1.3 %shard_map.72 = bf16[64,256]{1,0:T(8,128)(2,1)} custom-call(s32[6,64]{1,0:T(8,128)S(1)} %get-tuple-element.15.target_t, f32[6,64]{1,0:T(8,128)S(1)} %bitcast.13, bf16[64,11,2,128]{3,2,1,0:T(2,128)(2,1)S(1)} %all_to_all.10.returned), custom_call_target="tpu_custom_call" | custom-call | tf_op jit(solution)/shard_map/pallas_call | solution.py:30
  (6 shorter events, 0.0 us)
Async XLA Ops:
  1.8 14.3 %collective-permute-start = (bf16[80,1024]{1,0:T(8,128)(2,1)S(1)}, bf16[80,1024]{1,0:T(8,128)(2,1)S(1)}, u32[]{:S(2)}, u32[]{:S(2)}) collective-permute-start(bf16[80,1024]{1,0:T(8,128)(2,1)S(1)} %get-tuple-element.14.mine), channel_id=1, source_target_pairs={{0,256},{256,0},{1,257},{257,1},{2,258},{258,2},{3,259},{259,3},{4... | collective-permute-start | bytes 491528 | tf_op jit(solution)/shard_map/ppermute | solution.py:234
  6.1 24.1 %collective-permute-start.1 = (bf16[704,256]{1,0:T(8,128)(2,1)S(1)}, bf16[704,256]{1,0:T(8,128)(2,1)S(1)}, u32[]{:S(2)}, u32[]{:S(2)}) collective-permute-start(bf16[704,256]{1,0:T(8,128)(2,1)S(1)} %get-tuple-element.19), channel_id=1, source_target_pairs={{0,4},{2,6},{4,0},{6,2},{1,5},{3,7},{5,1},{7,3},{8,12},{10,14},{12... | collective-permute-start | bytes 1081352 | tf_op jit(solution)/shard_map/ppermute | solution.py:257
  20.0 45.2 %all-to-all-start = ((bf16[32,2,11,8,128]{4,3,2,1,0:T(8,128)(2,1)}), bf16[32,2,11,8,128]{4,3,2,1,0:T(8,128)(2,1)S(1)}, u32[]{:S(2)}, u32[]{:S(2)}) async-start(bf16[32,2,11,8,128]{4,3,2,1,0:T(8,128)(2,1)} %get-tuple-element.16), calls=%async_computation | async-start | bytes 2883584 | tf_op jit(solution)/shard_map/all_to_all | solution.py:255
  31.8 21.3 %collective-permute-start.2 = (bf16[704,256]{1,0:T(8,128)(2,1)S(1)}, bf16[704,256]{1,0:T(8,128)(2,1)S(1)}, u32[]{:S(2)}, u32[]{:S(2)}) collective-permute-start(bf16[704,256]{1,0:T(8,128)(2,1)S(1)} %get-tuple-element.21), channel_id=1, source_target_pairs={{0,2},{2,4},{4,6},{6,0},{1,3},{3,5},{5,7},{7,1},{8,10},{10,12},{12... | collective-permute-start | bytes 1081352 | tf_op jit(solution)/shard_map/ppermute | solution.py:272
  39.4 16.8 %collective-permute-start.3 = (bf16[704,256]{1,0:T(8,128)(2,1)S(1)}, bf16[704,256]{1,0:T(8,128)(2,1)S(1)}, u32[]{:S(2)}, u32[]{:S(2)}) collective-permute-start(bf16[704,256]{1,0:T(8,128)(2,1)S(1)} %get-tuple-element.22), channel_id=1, source_target_pairs={{0,6},{2,0},{4,2},{6,4},{1,7},{3,1},{5,3},{7,5},{8,14},{10,8},{12,... | collective-permute-start | bytes 1081352 | tf_op jit(solution)/shard_map/ppermute | solution.py:273
  66.6 3.8 %collective-permute-start.4 = (bf16[352,704]{1,0:T(8,128)(2,1)S(1)}, bf16[352,704]{1,0:T(8,128)(2,1)S(1)}, u32[]{:S(2)}, u32[]{:S(2)}) collective-permute-start(bf16[352,704]{1,0:T(8,128)(2,1)S(1)} %shard_map.68), channel_id=1, source_target_pairs={{0,1},{1,0},{2,3},{3,2},{4,5},{5,4},{6,7},{7,6},{8,9},{9,8},{10,11... | collective-permute-start | bytes 1486856 | tf_op jit(solution)/shard_map/ppermute | solution.py:283
  69.8 25.6 %copy-start = (bf16[1,1408,256]{2,1,0:T(8,128)(2,1)S(1)}, bf16[1,1408,256]{2,1,0:T(8,128)(2,1)}, u32[]{:S(2)}) copy-start(bf16[1,1408,256]{2,1,0:T(8,128)(2,1)} %param.11) | copy-start | bytes 2162692
  93.5 4.5 %collective-permute-start.5 = (bf16[4,968,128]{2,1,0:T(8,128)(2,1)S(1)}, bf16[4,968,128]{2,1,0:T(8,128)(2,1)S(1)}, u32[]{:S(2)}, u32[]{:S(2)}) collective-permute-start(bf16[4,968,128]{2,1,0:T(8,128)(2,1)S(1)} %bitcast.9), channel_id=1, source_target_pairs={{0,1},{1,0},{2,3},{3,2},{4,5},{5,4},{6,7},{7,6},{8,9},{9,8},{10,11... | collective-permute-start | bytes 2973704 | tf_op jit(solution)/shard_map/ppermute | solution.py:294
  96.0 25.2 %copy-start.1 = (f32[64,6]{0,1:T(8,128)S(1)}, f32[64,6]{0,1:T(8,128)}, u32[]{:S(2)}) copy-start(f32[64,6]{0,1:T(8,128)} %param.8) | copy-start | bytes 4612

commit v14 on v13

--- a/solution.py
+++ b/solution.py
@@ -19,7 +19,7 @@
 PICK = 10_000_000_000
 CHIPS = 4
 GROUPS = 4
-CORE, CHIP, SIDE = range(3)
+CORE, CHIP = range(2)
 
 
 def call(body, outs, *operands, scalars=0, raw=0, scratch=(), flops=None, out_space=VMEM):
@@ -84,9 +84,9 @@
         copy.wait()
 
 
-def picked(top, cap, experts, side, place, block, target_t=None):
+def picked(top, cap, experts, block, target_t):
     rows = block.shape[0] - 16
-    slots = side * cap
+    slots = experts * cap
     routes_t = block[rows:, :rows].astype(jnp.float32).astype(jnp.int32)
     expert_ids = lax.broadcasted_iota(jnp.int32, (experts, rows), 0)
     chosen = [(routes_t[k : k + 1, :] == expert_ids).astype(jnp.float32) for k in range(top)]
@@ -100,18 +100,16 @@
     for k in range(top):
         slot = jnp.sum(chosen[k] * before, axis=0, keepdims=True).astype(jnp.int32)
         target = routes_t[k : k + 1, :] * cap + slot
-        if target_t is not None:
-            target_t[k : k + 1, :] = target
-        picker += (slot_ids == target - place[SIDE] * slots).astype(jnp.float32)
+        target_t[k : k + 1, :] = target
+        picker += (slot_ids == target).astype(jnp.float32)
     rows_out = jnp.dot(picker.astype(jnp.bfloat16), block[:rows, :], preferred_element_type=jnp.float32)
-    return rows_out.astype(jnp.bfloat16).reshape(side, cap, block.shape[1] // 128, 128)
-
-
-def dispatch_body(sizes, place, w_gate, w_up, mine, neighbour, outgoing, target_t, one, three, sems):
+    return rows_out.astype(jnp.bfloat16).reshape(experts, cap, block.shape[1] // 128, 128)
+
+
+def dispatch_body(sizes, place, w_gate, w_up, mine, outgoing, target_t, one, three, sems):
     pairs = slices(place, w_gate, w_up, 1, one) + slices(place, w_gate, w_up, 3, three)
     copies = copy_all(pairs, sems)
-    outgoing[:, place[SIDE]] = picked(*sizes, place, mine, target_t)
-    outgoing[:, 1 - place[SIDE]] = picked(*sizes, place, neighbour)
+    outgoing[...] = picked(*sizes, mine, target_t)
     for copy in copies:
         copy.wait()
 
@@ -181,12 +179,10 @@
 
 
 def down_body(place, own, other, w_down, out):
-    blocks, cap = out.shape[:2]
-    part = blocks // 4
+    cap = out.shape[1]
+    part = out.shape[0] // 2
     for value, which in ((own[...], place[CORE]), (down(other, w_down), 1 - place[CORE])):
-        value = value.reshape(part, 2, cap, *out.shape[2:])
-        for side in range(2):
-            out[pl.ds(side * (blocks // 2) + which * part, part)] = value[:, side]
+        out[pl.ds(which * part, part)] = value.reshape(part, cap, *out.shape[2:])
 
 
 def combine_body(target_t, weight_t, returned, out):
@@ -207,8 +203,7 @@
 def on_device(tokens, routes, route_weight, w_gate, w_up, w_down):
     tok_count, top = routes.shape
     _, units, cols = w_gate.shape
-    side = lax.axis_size("plane")
-    experts = 2 * side
+    experts = lax.axis_size("wide")
     cap = max(2, (11 * tok_count + experts - 1) // experts)
     slots = experts * cap
     share = units // CHIPS
@@ -216,7 +211,7 @@
     bf16 = jnp.bfloat16
     dma = pltpu.SemaphoreType.DMA
     swap = [(0, 1), (1, 0)]
-    place = jnp.stack([lax.axis_index(a) for a in ("core", "chip", "side")]).astype(jnp.int32)
+    place = jnp.stack([lax.axis_index(a) for a in ("core", "chip")]).astype(jnp.int32)
 
     part = jax.ShapeDtypeStruct((2 * share, cols), bf16)
     mine, two = call(
@@ -231,13 +226,12 @@
         raw=4,
         scratch=[pltpu.VMEM((top, tok_count), jnp.int32), dma((CHIPS + 3,))],
     )
-    neighbour = lax.ppermute(mine, "side", swap)
-    sizes = (top, cap, experts, side)
+    sizes = (top, cap, experts)
     chunk = (cap, CHIPS * cols // 128, 128)
     outgoing, target_t, one, three = call(
         functools.partial(dispatch_body, sizes),
         (
-            jax.ShapeDtypeStruct((side, 2, *chunk), bf16),
+            jax.ShapeDtypeStruct((experts, *chunk), bf16),
             jax.ShapeDtypeStruct((top, tok_count), jnp.int32),
             part,
             part,
@@ -246,13 +240,12 @@
         w_gate[0],
         w_up[0],
         mine,
-        neighbour,
         scalars=1,
         raw=2,
         scratch=[dma((4,))],
         flops=PICK,
     )
-    received = lax.all_to_all(outgoing, "plane", split_axis=0, concat_axis=0, tiled=True)
+    received = lax.all_to_all(outgoing, "wide", split_axis=0, concat_axis=0, tiled=True)
     ring = [[(i, (i + shift) % CHIPS) for i in range(CHIPS)] for shift in range(CHIPS)]
     two = lax.ppermute(two, "chip", ring[2])
     here, one, three = call(
@@ -301,7 +294,7 @@
         w_down[0],
         scalars=1,
     )
-    returned = lax.all_to_all(produced, ("side", "plane"), split_axis=0, concat_axis=0, tiled=True)
+    returned = lax.all_to_all(produced, "wide", split_axis=0, concat_axis=0, tiled=True)
     return call(
         combine_body,
         jax.ShapeDtypeStruct((tok_count, cols), bf16),
@@ -312,10 +305,8 @@
 
 
 def solution(mesh):
-    fine = Mesh(
-        mesh.devices.reshape(2, mesh.shape["wide"] // 2, CHIPS, 2), ("side", "plane", "chip", "core")
-    )
-    wide, narrow = ("side", "plane"), ("chip", "core")
+    fine = Mesh(mesh.devices.reshape(mesh.shape["wide"], CHIPS, 2), ("wide", "chip", "core"))
+    wide, narrow = "wide", ("chip", "core")
     return jax.shard_map(
         on_device,
         mesh=fine,

time: 123 us -> 126 us (1.024)
  starting transfers between devices: 42.4 us -> 38.6 us
  blocking collectives: 44.7 us -> 48.3 us
  waiting for transfers between devices: 21.9 us -> 25.3 us
    ppermute x1, waiting for transfers between devices: 7.2 us -> 21.5 us  [on_device(): one = lax.ppermute(one, 'chip', ring[1])]
    all_to_all x1, waiting for transfers between devices: 9.08 us -> 1.22 us  [on_device(): lax.all_to_all(outgoing, 'wide', split_axis=0, concat_axis=0, tiled=True)]
    ppermute x1 -> x0, starting transfers between devices: 4.28 us -> none  [on_device(): neighbour = lax.ppermute(mine, 'side', swap)]
    ppermute x1, waiting for transfers between devices: 3.07 us -> 0.01 us  [on_device(): three = lax.ppermute(three, 'chip', ring[3])]
    all_to_all x1, blocking collectives: 22 us -> 24.8 us  [on_device(): lax.all_to_all(produced, 'wide', split_axis=0, concat_axis=0, tiled=True)]
    ppermute x1, starting transfers between devices: 7.58 us -> 5.59 us  [on_device(): one = lax.ppermute(one, 'chip', ring[1])]
    all_to_all x1, starting transfers between devices: 10.2 us -> 11.5 us  [on_device(): lax.all_to_all(outgoing, 'wide', split_axis=0, concat_axis=0, tiled=True)]
  transfers between devices with their start and end apart: 7 -> 6, of which waited for: 5 -> 4; matrix products, arithmetic and copies ran while one was open for 0% -> 0% of each run, Pallas kernels for 6% -> 5%
where the time goes in v14:
time: 126 us; the launch traced here: 125 us
  blocking collectives  48.3 us (38%)
  starting transfers between devices  38.6 us (31%)
  waiting for transfers between devices  25.3 us (20%)
  Pallas kernels  12.8 us (10%)
    all_to_all x1, blocking collectives, on_device(): lax.all_to_all(produced, 'wide', split_axis=0, concat_axis=0, tiled=True)  24.8 us
    all_gather x1, blocking collectives, on_device(): own = lax.all_gather(hidden, 'chip', axis=0)  23.5 us
    ppermute x1, waiting for transfers between devices, on_device(): one = lax.ppermute(one, 'chip', ring[1])  21.5 us
    pallas_call x9, Pallas kernels, call(): pl.pallas_call(body, out_shape=outs, in_specs=[SMEM] * scalars + [HBM] *...  12.8 us
    all_to_all x1, starting transfers between devices, on_device(): lax.all_to_all(outgoing, 'wide', split_axis=0, concat_axis=0, tiled=True)  11.5 us
    ppermute x1, starting transfers between devices, on_device(): two = lax.ppermute(two, 'chip', ring[2])  10.9 us
    ppermute x1, starting transfers between devices, on_device(): three = lax.ppermute(three, 'chip', ring[3])  6.75 us
    ppermute x1, starting transfers between devices, on_device(): one = lax.ppermute(one, 'chip', ring[1])  5.59 us
  transfers between devices with their start and end apart: 6, of which 4 were waited for; matrix products, arithmetic and copies ran while one was open for 0% of the time, Pallas kernels for 5%

profile of v14, /device:TPU:8, one launch (start us, length us, event | category | flops | bytes accessed | tf_op | source)
XLA Modules:
  0.0 125.1 jit_solution(10043470138751300989)
XLA Ops:
  0.0 0.1 pad_add_fusion.place
  0.1 1.7 %shard_map.64 = (bf16[80,1024]{1,0:T(8,128)(2,1)S(1)}, bf16[704,256]{1,0:T(8,128)(2,1)S(1)}) custom-call(s32[2]{0:T(128)S(1)} %pad_add_fusion.place, s32[6,64]{1,0:T(8,128)} %bitcast.19, bf16[64,2048]{1,0:T(8,128)(2,1)} %tokens_hbm.1, bf16[1408,256]{1,0:T(8,128)(2,1)} %bitcast.13, bf16[1408,256]{1,0:T(8,128)(2,1)} %bitcast.16), custom_call_target="tpu_custom_call" | custom-call | tf_op jit(solution)/shard_map/pallas_call | solution.py:30
  1.8 10.9 %collective-permute-start = (bf16[704,256]{1,0:T(8,128)(2,1)S(1)}, bf16[704,256]{1,0:T(8,128)(2,1)S(1)}, u32[]{:S(2)}, u32[]{:S(2)}) collective-permute-start(bf16[704,256]{1,0:T(8,128)(2,1)S(1)} %get-tuple-element.19), channel_id=1, source_target_pairs={{0,4},{2,6},{4,0},{6,2},{1,5},{3,7},{5,1},{7,3},{8,12},{10,14},{12... | collective-permute-start | bytes 1081352 | tf_op jit(solution)/shard_map/ppermute | solution.py:250
  12.7 3.4 %shard_map.65 = (bf16[64,11,8,128]{3,2,1,0:T(8,128)(2,1)}, s32[6,64]{1,0:T(8,128)S(1)}, bf16[704,256]{1,0:T(8,128)(2,1)S(1)}, bf16[704,256]{1,0:T(8,128)(2,1)S(1)}) custom-call(s32[2]{0:T(128)S(1)} %pad_add_fusion.place, bf16[1408,256]{1,0:T(8,128)(2,1)} %bitcast.14, bf16[1408,256]{1,0:T(8,128)(2,1)} %bitcast.17, bf16[80,1024]{1,0:T(8,128)(2,1)S(1)} %get-tuple-element.14.mine), custom_call_target="tpu_custom_call" | custom-call | flops 10000000000 | tf_op jit(solution)/shard_map/pallas_call | solution.py:30
  16.1 11.5 %all-to-all-start = ((bf16[64,11,8,128]{3,2,1,0:T(8,128)(2,1)}), bf16[64,11,8,128]{3,2,1,0:T(8,128)(2,1)S(1)}, u32[]{:S(2)}, u32[]{:S(2)}) async-start(bf16[64,11,8,128]{3,2,1,0:T(8,128)(2,1)} %get-tuple-element.16), calls=%async_computation | async-start | bytes 2883584 | tf_op jit(solution)/shard_map/all_to_all | solution.py:248
  27.6 1.6 %shard_map.66 = (bf16[704,256]{1,0:T(8,128)(2,1)S(1)}, bf16[704,256]{1,0:T(8,128)(2,1)S(1)}, bf16[704,256]{1,0:T(8,128)(2,1)S(1)}) custom-call(s32[2]{0:T(128)S(1)} %pad_add_fusion.place, bf16[1408,256]{1,0:T(8,128)(2,1)} %bitcast.15, bf16[1408,256]{1,0:T(8,128)(2,1)} %bitcast.18, bf16[704,256]{1,0:T(8,128)(2,1)S(1)} %get-tuple-element.17.one, ...), custom_call_target="tpu_custom_call" | custom-call | flops 30000001024 | tf_op jit(solution)/shard_map/pallas_call | solution.py:30
  29.2 5.6 %collective-permute-start.1 = (bf16[704,256]{1,0:T(8,128)(2,1)S(1)}, bf16[704,256]{1,0:T(8,128)(2,1)S(1)}, u32[]{:S(2)}, u32[]{:S(2)}) collective-permute-start(bf16[704,256]{1,0:T(8,128)(2,1)S(1)} %get-tuple-element.21), channel_id=1, source_target_pairs={{0,2},{2,4},{4,6},{6,0},{1,3},{3,5},{5,7},{7,1},{8,10},{10,12},{12... | collective-permute-start | bytes 1081352 | tf_op jit(solution)/shard_map/ppermute | solution.py:265
  34.8 6.7 %collective-permute-start.2 = (bf16[704,256]{1,0:T(8,128)(2,1)S(1)}, bf16[704,256]{1,0:T(8,128)(2,1)S(1)}, u32[]{:S(2)}, u32[]{:S(2)}) collective-permute-start(bf16[704,256]{1,0:T(8,128)(2,1)S(1)} %get-tuple-element.22), channel_id=1, source_target_pairs={{0,6},{2,0},{4,2},{6,4},{1,7},{3,1},{5,3},{7,5},{8,14},{10,8},{12,... | collective-permute-start | bytes 1081352 | tf_op jit(solution)/shard_map/ppermute | solution.py:266
  41.5 21.5 %collective-permute-done.1.refs_1_ = bf16[704,256]{1,0:T(8,128)(2,1)S(1)} collective-permute-done((bf16[704,256]{1,0:T(8,128)(2,1)S(1)}, bf16[704,256]{1,0:T(8,128)(2,1)S(1)}, u32[]{:S(2)}, u32[]{:S(2)}) %collective-permute-start.1) | collective-permute-done | bytes 360480 | tf_op jit(solution)/shard_map/ppermute | solution.py:265
  63.1 1.2 all-to-all-done.rows
  64.3 1.3 %shard_map.68 = bf16[352,704]{1,0:T(8,128)(2,1)S(1)} custom-call(s32[2]{0:T(128)S(1)} %pad_add_fusion.place, bf16[64,11,8,128]{3,2,1,0:T(8,128)(2,1)S(1)} %all-to-all-done.rows, bf16[704,256]{1,0:T(8,128)(2,1)S(1)} %get-tuple-element.20.refs_0_, bf16[704,256]{1,0:T(8,128)(2,1)S(1)} %collective-permute-done.1.refs_1_, ...), custom_call_target="tpu_custom_call" | custom-call | tf_op jit(solution)/shard_map/pallas_call | solution.py:30
  65.6 1.9 %collective-permute-start.3 = (bf16[352,704]{1,0:T(8,128)(2,1)S(1)}, bf16[352,704]{1,0:T(8,128)(2,1)S(1)}, u32[]{:S(2)}, u32[]{:S(2)}) collective-permute-start(bf16[352,704]{1,0:T(8,128)(2,1)S(1)} %shard_map.68), channel_id=1, source_target_pairs={{0,1},{1,0},{2,3},{3,2},{4,5},{5,4},{6,7},{7,6},{8,9},{9,8},{10,11... | collective-permute-start | bytes 1486856 | tf_op jit(solution)/shard_map/ppermute | solution.py:276
  67.5 1.3 %shard_map.67.mine = f32[352,704]{1,0:T(8,128)S(1)} custom-call(s32[2]{0:T(128)S(1)} %pad_add_fusion.place, bf16[64,11,8,128]{3,2,1,0:T(8,128)(2,1)S(1)} %all-to-all-done.rows, bf16[704,256]{1,0:T(8,128)(2,1)S(1)} %get-tuple-element.20.refs_0_, bf16[704,256]{1,0:T(8,128)(2,1)S(1)} %collective-permute-done.1.refs_1_, ...), custom_call_target="tpu_custom_call" | custom-call | tf_op jit(solution)/shard_map/pallas_call | solution.py:30
  68.8 0.0 copy-start
  68.9 0.6 collective-permute-done.3.theirs
  69.4 0.3 shard_map.69
  69.7 23.5 %all-gather = bf16[3872,128]{1,0:T(8,128)(2,1)S(1)} all-gather(bf16[968,128]{1,0:T(8,128)(2,1)S(1)} %shard_map.69), channel_id=2, replica_groups=mesh['wide'=64,'chip'=4,'core'=2] {'chip'}, dimensions={0}, use_global_device_ids=true | all-gather | bytes 1239040 | tf_op jit(solution)/shard_map/all_gather | solution.py:286
  93.2 1.9 %collective-permute-start.4 = (bf16[4,968,128]{2,1,0:T(8,128)(2,1)S(1)}, bf16[4,968,128]{2,1,0:T(8,128)(2,1)S(1)}, u32[]{:S(2)}, u32[]{:S(2)}) collective-permute-start(bf16[4,968,128]{2,1,0:T(8,128)(2,1)S(1)} %bitcast.8), channel_id=1, source_target_pairs={{0,1},{1,0},{2,3},{3,2},{4,5},{5,4},{6,7},{7,6},{8,9},{9,8},{10,11... | collective-permute-start | bytes 2973704 | tf_op jit(solution)/shard_map/ppermute | solution.py:287
  95.1 0.6 shard_map.70.own
  95.7 0.0 copy-start.1
  95.7 1.9 %collective-permute-done.4.other = bf16[4,968,128]{2,1,0:T(8,128)(2,1)S(1)} collective-permute-done((bf16[4,968,128]{2,1,0:T(8,128)(2,1)S(1)}, bf16[4,968,128]{2,1,0:T(8,128)(2,1)S(1)}, u32[]{:S(2)}, u32[]{:S(2)}) %collective-permute-start.4) | collective-permute-done | bytes 991264 | tf_op jit(solution)/shard_map/ppermute | solution.py:287
  97.7 1.3 %shard_map.71 = bf16[64,11,2,128]{3,2,1,0:T(2,128)(2,1)S(1)} custom-call(s32[2]{0:T(128)S(1)} %pad_add_fusion.place, bf16[352,256]{1,0:T(8,128)(2,1)S(1)} %shard_map.70.own, bf16[4,968,128]{2,1,0:T(8,128)(2,1)S(1)} %collective-permute-done.4.other, bf16[1408,256]{1,0:T(8,128)(2,1)S(1)} %bitcast.11), custom_call_target="tpu_custom_call" | custom-call | tf_op jit(solution)/shard_map/pallas_call | solution.py:30
  99.0 24.8 %all_to_all.10.returned = bf16[64,11,2,128]{3,2,1,0:T(2,128)(2,1)S(1)} all-to-all(bf16[64,11,2,128]{3,2,1,0:T(2,128)(2,1)S(1)} %shard_map.71), channel_id=1, replica_groups=mesh['wide'=64,'chip'=4,'core'=2] {'wide'}, dimensions={0} | all-to-all | bytes 720896 | tf_op jit(solution)/shard_map/all_to_all | solution.py:297
  123.8 1.3 %shard_map.72 = bf16[64,256]{1,0:T(8,128)(2,1)} custom-call(s32[6,64]{1,0:T(8,128)S(1)} %get-tuple-element.15.target_t, f32[6,64]{1,0:T(8,128)S(1)} %bitcast.12, bf16[64,11,2,128]{3,2,1,0:T(2,128)(2,1)S(1)} %all_to_all.10.returned), custom_call_target="tpu_custom_call" | custom-call | tf_op jit(solution)/shard_map/pallas_call | solution.py:30
  (4 shorter events, 0.0 us)
Async XLA Ops:
  1.8 25.8 %collective-permute-start = (bf16[704,256]{1,0:T(8,128)(2,1)S(1)}, bf16[704,256]{1,0:T(8,128)(2,1)S(1)}, u32[]{:S(2)}, u32[]{:S(2)}) collective-permute-start(bf16[704,256]{1,0:T(8,128)(2,1)S(1)} %get-tuple-element.19), channel_id=1, source_target_pairs={{0,4},{2,6},{4,0},{6,2},{1,5},{3,7},{5,1},{7,3},{8,12},{10,14},{12... | collective-permute-start | bytes 1081352 | tf_op jit(solution)/shard_map/ppermute | solution.py:250
  16.1 48.2 %all-to-all-start = ((bf16[64,11,8,128]{3,2,1,0:T(8,128)(2,1)}), bf16[64,11,8,128]{3,2,1,0:T(8,128)(2,1)S(1)}, u32[]{:S(2)}, u32[]{:S(2)}) async-start(bf16[64,11,8,128]{3,2,1,0:T(8,128)(2,1)} %get-tuple-element.16), calls=%async_computation | async-start | bytes 2883584 | tf_op jit(solution)/shard_map/all_to_all | solution.py:248
  29.2 33.9 %collective-permute-start.1 = (bf16[704,256]{1,0:T(8,128)(2,1)S(1)}, bf16[704,256]{1,0:T(8,128)(2,1)S(1)}, u32[]{:S(2)}, u32[]{:S(2)}) collective-permute-start(bf16[704,256]{1,0:T(8,128)(2,1)S(1)} %get-tuple-element.21), channel_id=1, source_target_pairs={{0,2},{2,4},{4,6},{6,0},{1,3},{3,5},{5,7},{7,1},{8,10},{10,12},{12... | collective-permute-start | bytes 1081352 | tf_op jit(solution)/shard_map/ppermute | solution.py:265
  34.8 28.3 %collective-permute-start.2 = (bf16[704,256]{1,0:T(8,128)(2,1)S(1)}, bf16[704,256]{1,0:T(8,128)(2,1)S(1)}, u32[]{:S(2)}, u32[]{:S(2)}) collective-permute-start(bf16[704,256]{1,0:T(8,128)(2,1)S(1)} %get-tuple-element.22), channel_id=1, source_target_pairs={{0,6},{2,0},{4,2},{6,4},{1,7},{3,1},{5,3},{7,5},{8,14},{10,8},{12,... | collective-permute-start | bytes 1081352 | tf_op jit(solution)/shard_map/ppermute | solution.py:266
  65.6 3.8 %collective-permute-start.3 = (bf16[352,704]{1,0:T(8,128)(2,1)S(1)}, bf16[352,704]{1,0:T(8,128)(2,1)S(1)}, u32[]{:S(2)}, u32[]{:S(2)}) collective-permute-start(bf16[352,704]{1,0:T(8,128)(2,1)S(1)} %shard_map.68), channel_id=1, source_target_pairs={{0,1},{1,0},{2,3},{3,2},{4,5},{5,4},{6,7},{7,6},{8,9},{9,8},{10,11... | collective-permute-start | bytes 1486856 | tf_op jit(solution)/shard_map/ppermute | solution.py:276
  68.8 26.3 %copy-start = (bf16[1,1408,256]{2,1,0:T(8,128)(2,1)S(1)}, bf16[1,1408,256]{2,1,0:T(8,128)(2,1)}, u32[]{:S(2)}) copy-start(bf16[1,1408,256]{2,1,0:T(8,128)(2,1)} %param.11) | copy-start | bytes 2162692
  93.2 4.5 %collective-permute-start.4 = (bf16[4,968,128]{2,1,0:T(8,128)(2,1)S(1)}, bf16[4,968,128]{2,1,0:T(8,128)(2,1)S(1)}, u32[]{:S(2)}, u32[]{:S(2)}) collective-permute-start(bf16[4,968,128]{2,1,0:T(8,128)(2,1)S(1)} %bitcast.8), channel_id=1, source_target_pairs={{0,1},{1,0},{2,3},{3,2},{4,5},{5,4},{6,7},{7,6},{8,9},{9,8},{10,11... | collective-permute-start | bytes 2973704 | tf_op jit(solution)/shard_map/ppermute | solution.py:287
  95.7 28.1 %copy-start.1 = (f32[64,6]{0,1:T(8,128)S(1)}, f32[64,6]{0,1:T(8,128)}, u32[]{:S(2)}) copy-start(f32[64,6]{0,1:T(8,128)} %param.8) | copy-start | bytes 4612

commit v15 on v13

--- a/solution.py
+++ b/solution.py
@@ -77,7 +77,12 @@
 
 
 def hold_body(place, w_gate, w_up, one, three, _, here, one_out, three_out, sems):
-    copies = copy_all(slices(place, w_gate, w_up, 0, here), sems)
+    share = here.shape[0] // 2
+    pairs = [
+        (w.at[units_of(place, 0, share), :], here.at[n * share : (n + 1) * share, :])
+        for n, w in enumerate((w_gate, w_up))
+    ]
+    copies = copy_all(pairs, sems)
     one_out[...] = one[...]
     three_out[...] = three[...]
     for copy in copies:
@@ -107,13 +112,17 @@
     return rows_out.astype(jnp.bfloat16).reshape(side, cap, block.shape[1] // 128, 128)
 
 
-def dispatch_body(sizes, place, w_gate, w_up, mine, neighbour, outgoing, target_t, one, three, sems):
+def own_body(sizes, place, w_gate, w_up, mine, out, target_t, one, three, sems):
     pairs = slices(place, w_gate, w_up, 1, one) + slices(place, w_gate, w_up, 3, three)
     copies = copy_all(pairs, sems)
-    outgoing[:, place[SIDE]] = picked(*sizes, place, mine, target_t)
-    outgoing[:, 1 - place[SIDE]] = picked(*sizes, place, neighbour)
+    out[...] = picked(*sizes, place, mine, target_t)
     for copy in copies:
         copy.wait()
+
+
+def dispatch_body(sizes, place, own, neighbour, outgoing):
+    outgoing[:, 1 - place[SIDE]] = picked(*sizes, place, neighbour)
+    outgoing[:, place[SIDE]] = own[...]
 
 
 def gate_up_body(mine, place, rows, *refs):
@@ -176,8 +185,15 @@
     return total.astype(jnp.bfloat16)
 
 
-def down_own_body(own, w_down, out):
+def down_own_body(own, w_down, target_t, weight_t, out, high, low):
     out[...] = down(own, w_down)
+    top = target_t.shape[0]
+    slot_ids = lax.broadcasted_iota(jnp.int32, high.shape, 0)
+    spread = jnp.zeros(high.shape, jnp.float32)
+    for k in range(top):
+        spread += jnp.where(slot_ids == target_t[k : k + 1, :], weight_t[k : k + 1, :], 0.0)
+    high[...] = spread.astype(jnp.bfloat16)
+    low[...] = (spread - high[...].astype(jnp.float32)).astype(jnp.bfloat16)
 
 
 def down_body(place, own, other, w_down, out):
@@ -189,18 +205,10 @@
             out[pl.ds(side * (blocks // 2) + which * part, part)] = value[:, side]
 
 
-def combine_body(target_t, weight_t, returned, out):
-    top, rows = target_t.shape
-    slots = returned.shape[0] * returned.shape[1]
-    slot_ids = lax.broadcasted_iota(jnp.int32, (slots, rows), 0)
-    spread = jnp.zeros((slots, rows), jnp.float32)
-    for k in range(top):
-        spread += jnp.where(slot_ids == target_t[k : k + 1, :], weight_t[k : k + 1, :], 0.0)
-    high = spread.astype(jnp.bfloat16)
-    low = (spread - high.astype(jnp.float32)).astype(jnp.bfloat16)
-    flat = returned[...].reshape(slots, out.shape[1])
-    total = lax.dot_general(high, flat, TN, preferred_element_type=jnp.float32)
-    total += lax.dot_general(low, flat, TN, preferred_element_type=jnp.float32)
+def combine_body(high, low, returned, out):
+    flat = returned[...].reshape(high.shape[0], out.shape[1])
+    total = lax.dot_general(high[...], flat, TN, preferred_element_type=jnp.float32)
+    total += lax.dot_general(low[...], flat, TN, preferred_element_type=jnp.float32)
     out[...] = total.astype(jnp.bfloat16)
 
 
@@ -234,10 +242,10 @@
     neighbour = lax.ppermute(mine, "side", swap)
     sizes = (top, cap, experts, side)
     chunk = (cap, CHIPS * cols // 128, 128)
-    outgoing, target_t, one, three = call(
-        functools.partial(dispatch_body, sizes),
+    picked_own, target_t, one, three = call(
+        functools.partial(own_body, sizes),
         (
-            jax.ShapeDtypeStruct((side, 2, *chunk), bf16),
+            jax.ShapeDtypeStruct((side, *chunk), bf16),
             jax.ShapeDtypeStruct((top, tok_count), jnp.int32),
             part,
             part,
@@ -246,10 +254,17 @@
         w_gate[0],
         w_up[0],
         mine,
-        neighbour,
         scalars=1,
         raw=2,
         scratch=[dma((4,))],
+    )
+    outgoing = call(
+        functools.partial(dispatch_body, sizes),
+        jax.ShapeDtypeStruct((side, 2, *chunk), bf16),
+        place,
+        picked_own,
+        neighbour,
+        scalars=1,
         flops=PICK,
     )
     received = lax.all_to_all(outgoing, "plane", split_axis=0, concat_axis=0, tiled=True)
@@ -292,23 +307,26 @@
     hidden = call(hidden_body, jax.ShapeDtypeStruct((half * share // 128, 128), bf16), mine, theirs)
     own = lax.all_gather(hidden, "chip", axis=0)
     other = lax.ppermute(own, "core", swap)
+    spread = jax.ShapeDtypeStruct((slots, tok_count), bf16)
+    down_own, high, low = call(
+        down_own_body,
+        (jax.ShapeDtypeStruct((half, cols), bf16), spread, spread),
+        own,
+        w_down[0],
+        target_t,
+        route_weight.T,
+    )
     produced = call(
         down_body,
         jax.ShapeDtypeStruct((experts, cap, cols // 128, 128), bf16),
         place,
-        call(down_own_body, jax.ShapeDtypeStruct((half, cols), bf16), own, w_down[0]),
+        down_own,
         other,
         w_down[0],
         scalars=1,
     )
     returned = lax.all_to_all(produced, ("side", "plane"), split_axis=0, concat_axis=0, tiled=True)
-    return call(
-        combine_body,
-        jax.ShapeDtypeStruct((tok_count, cols), bf16),
-        target_t,
-        route_weight.T,
-        returned,
-    )
+    return call(combine_body, jax.ShapeDtypeStruct((tok_count, cols), bf16), high, low, returned)
 
 
 def solution(mesh):

time: 123 us -> 123 us (level)
  starting transfers between devices: 42.4 us -> 40.4 us
  waiting for transfers between devices: 21.9 us -> 23.3 us
    ppermute x1, waiting for transfers between devices: 7.2 us -> 9.59 us  [on_device(): one = lax.ppermute(one, 'chip', ring[1])]
    ppermute x1, starting transfers between devices: 6.5 us -> 5.22 us  [on_device(): three = lax.ppermute(three, 'chip', ring[3])]
    pallas_call x9 -> x10, Pallas kernels: 13.3 us -> 14.4 us  [call(): pl.pallas_call(body, out_shape=outs, in_specs=[SMEM] * scalars + [HBM] *...]
  transfers between devices with their start and end apart: 7 -> 7, of which waited for: 5 -> 5; matrix products, arithmetic and copies ran while one was open for 0% -> 0% of each run, Pallas kernels for 6% -> 7%
where the time goes in v15:
time: 123 us
  blocking collectives  44.4 us (36%)
  starting transfers between devices  40.4 us (33%)
  waiting for transfers between devices  23.3 us (19%)
  Pallas kernels  14.4 us (12%)
    all_gather x1, blocking collectives, on_device(): own = lax.all_gather(hidden, 'chip', axis=0)  22.4 us
    all_to_all x1, blocking collectives, on_device(): lax.all_to_all(produced, ('side', 'plane'), split_axis=0, concat_axis=0,...  22 us
    pallas_call x10, Pallas kernels, call(): pl.pallas_call(body, out_shape=outs, in_specs=[SMEM] * scalars + [HBM] *...  14.4 us
    all_to_all x1, starting transfers between devices, on_device(): lax.all_to_all(outgoing, 'plane', split_axis=0, concat_axis=0, tiled=True)  10.2 us
    ppermute x1, starting transfers between devices, on_device(): two = lax.ppermute(two, 'chip', ring[2])  10 us
    all_to_all x1, waiting for transfers between devices, on_device(): lax.all_to_all(outgoing, 'plane', split_axis=0, concat_axis=0, tiled=True)  9.86 us
    ppermute x1, waiting for transfers between devices, on_device(): one = lax.ppermute(one, 'chip', ring[1])  9.59 us
    ppermute x1, starting transfers between devices, on_device(): one = lax.ppermute(one, 'chip', ring[1])  6.81 us
  transfers between devices with their start and end apart: 7, of which 5 were waited for; matrix products, arithmetic and copies ran while one was open for 0% of the time, Pallas kernels for 7%

profile of v15, /device:TPU:8, one launch (start us, length us, event | category | flops | bytes accessed | tf_op | source)
XLA Modules:
  0.0 122.7 jit_solution(12618539253975764461)
XLA Ops:
  0.1 1.7 %shard_map.64 = (bf16[80,1024]{1,0:T(8,128)(2,1)S(1)}, bf16[704,256]{1,0:T(8,128)(2,1)S(1)}) custom-call(s32[3]{0:T(128)S(1)} %pad_add_fusion.place, s32[6,64]{1,0:T(8,128)} %bitcast.20, bf16[64,2048]{1,0:T(8,128)(2,1)} %tokens_hbm.1, bf16[1408,256]{1,0:T(8,128)(2,1)} %bitcast.14, bf16[1408,256]{1,0:T(8,128)(2,1)} %bitcast.17), custom_call_target="tpu_custom_call" | custom-call | tf_op jit(solution)/shard_map/pallas_call | solution.py:30
  1.8 4.3 %collective-permute-start = (bf16[80,1024]{1,0:T(8,128)(2,1)S(1)}, bf16[80,1024]{1,0:T(8,128)(2,1)S(1)}, u32[]{:S(2)}, u32[]{:S(2)}) collective-permute-start(bf16[80,1024]{1,0:T(8,128)(2,1)S(1)} %get-tuple-element.17.mine), channel_id=1, source_target_pairs={{0,256},{256,0},{1,257},{257,1},{2,258},{258,2},{3,259},{259,3},{4... | collective-permute-start | bytes 491528 | tf_op jit(solution)/shard_map/ppermute | solution.py:242
  6.1 10.0 %collective-permute-start.1 = (bf16[704,256]{1,0:T(8,128)(2,1)S(1)}, bf16[704,256]{1,0:T(8,128)(2,1)S(1)}, u32[]{:S(2)}, u32[]{:S(2)}) collective-permute-start(bf16[704,256]{1,0:T(8,128)(2,1)S(1)} %get-tuple-element.21), channel_id=1, source_target_pairs={{0,4},{2,6},{4,0},{6,2},{1,5},{3,7},{5,1},{7,3},{8,12},{10,14},{12... | collective-permute-start | bytes 1081352 | tf_op jit(solution)/shard_map/ppermute | solution.py:272
  16.1 2.0 %shard_map.65 = (bf16[32,11,8,128]{3,2,1,0:T(8,128)(2,1)S(1)}, s32[6,64]{1,0:T(8,128)S(1)}, bf16[704,256]{1,0:T(8,128)(2,1)S(1)}, bf16[704,256]{1,0:T(8,128)(2,1)S(1)}) custom-call(s32[3]{0:T(128)S(1)} %pad_add_fusion.place, bf16[1408,256]{1,0:T(8,128)(2,1)} %bitcast.15, bf16[1408,256]{1,0:T(8,128)(2,1)} %bitcast.18, bf16[80,1024]{1,0:T(8,128)(2,1)S(1)} %get-tuple-element.17.mine), custom_call_target="tpu_custom_call" | custom-call | tf_op jit(solution)/shard_map/pallas_call | solution.py:30
  18.2 2.7 %shard_map.66 = bf16[32,2,11,8,128]{4,3,2,1,0:T(8,128)(2,1)} custom-call(s32[3]{0:T(128)S(1)} %pad_add_fusion.place, bf16[32,11,8,128]{3,2,1,0:T(8,128)(2,1)S(1)} %get-tuple-element.18.own, bf16[80,1024]{1,0:T(8,128)(2,1)S(1)} %collective-permute-done.neighbour), custom_call_target="tpu_custom_call" | custom-call | flops 10000000000 | tf_op jit(solution)/shard_map/pallas_call | solution.py:30
  20.8 10.2 %all-to-all-start = ((bf16[32,2,11,8,128]{4,3,2,1,0:T(8,128)(2,1)}), bf16[32,2,11,8,128]{4,3,2,1,0:T(8,128)(2,1)S(1)}, u32[]{:S(2)}, u32[]{:S(2)}) async-start(bf16[32,2,11,8,128]{4,3,2,1,0:T(8,128)(2,1)} %shard_map.66), calls=%async_computation | async-start | bytes 2883584 | tf_op jit(solution)/shard_map/all_to_all | solution.py:270
  31.0 1.6 %shard_map.67 = (bf16[704,256]{1,0:T(8,128)(2,1)S(1)}, bf16[704,256]{1,0:T(8,128)(2,1)S(1)}, bf16[704,256]{1,0:T(8,128)(2,1)S(1)}) custom-call(s32[3]{0:T(128)S(1)} %pad_add_fusion.place, bf16[1408,256]{1,0:T(8,128)(2,1)} %bitcast.16, bf16[1408,256]{1,0:T(8,128)(2,1)} %bitcast.19, bf16[704,256]{1,0:T(8,128)(2,1)S(1)} %get-tuple-element.19.one, ...), custom_call_target="tpu_custom_call" | custom-call | flops 30000001024 | tf_op jit(solution)/shard_map/pallas_call | solution.py:30
  32.6 6.8 %collective-permute-start.2 = (bf16[704,256]{1,0:T(8,128)(2,1)S(1)}, bf16[704,256]{1,0:T(8,128)(2,1)S(1)}, u32[]{:S(2)}, u32[]{:S(2)}) collective-permute-start(bf16[704,256]{1,0:T(8,128)(2,1)S(1)} %get-tuple-element.23), channel_id=1, source_target_pairs={{0,2},{2,4},{4,6},{6,0},{1,3},{3,5},{5,7},{7,1},{8,10},{10,12},{12... | collective-permute-start | bytes 1081352 | tf_op jit(solution)/shard_map/ppermute | solution.py:287
  39.4 5.2 %collective-permute-start.3 = (bf16[704,256]{1,0:T(8,128)(2,1)S(1)}, bf16[704,256]{1,0:T(8,128)(2,1)S(1)}, u32[]{:S(2)}, u32[]{:S(2)}) collective-permute-start(bf16[704,256]{1,0:T(8,128)(2,1)S(1)} %get-tuple-element.24), channel_id=1, source_target_pairs={{0,6},{2,0},{4,2},{6,4},{1,7},{3,1},{5,3},{7,5},{8,14},{10,8},{12,... | collective-permute-start | bytes 1081352 | tf_op jit(solution)/shard_map/ppermute | solution.py:288
  44.6 9.6 %collective-permute-done.2.refs_1_ = bf16[704,256]{1,0:T(8,128)(2,1)S(1)} collective-permute-done((bf16[704,256]{1,0:T(8,128)(2,1)S(1)}, bf16[704,256]{1,0:T(8,128)(2,1)S(1)}, u32[]{:S(2)}, u32[]{:S(2)}) %collective-permute-start.2) | collective-permute-done | bytes 360480 | tf_op jit(solution)/shard_map/ppermute | solution.py:287
  54.2 1.9 %collective-permute-done.3.refs_3_ = bf16[704,256]{1,0:T(8,128)(2,1)S(1)} collective-permute-done((bf16[704,256]{1,0:T(8,128)(2,1)S(1)}, bf16[704,256]{1,0:T(8,128)(2,1)S(1)}, u32[]{:S(2)}, u32[]{:S(2)}) %collective-permute-start.3) | collective-permute-done | bytes 360480 | tf_op jit(solution)/shard_map/ppermute | solution.py:288
  56.2 9.9 %all-to-all-done.rows = bf16[32,2,11,8,128]{4,3,2,1,0:T(8,128)(2,1)S(1)} async-done(((bf16[32,2,11,8,128]{4,3,2,1,0:T(8,128)(2,1)}), bf16[32,2,11,8,128]{4,3,2,1,0:T(8,128)(2,1)S(1)}, u32[]{:S(2)}, u32[]{:S(2)}) %all-to-all-start) | async-done | bytes 1441824 | tf_op jit(solution)/shard_map/all_to_all | solution.py:270
  66.0 1.3 %shard_map.69 = bf16[352,704]{1,0:T(8,128)(2,1)S(1)} custom-call(s32[3]{0:T(128)S(1)} %pad_add_fusion.place, bf16[32,2,11,8,128]{4,3,2,1,0:T(8,128)(2,1)S(1)} %all-to-all-done.rows, bf16[704,256]{1,0:T(8,128)(2,1)S(1)} %get-tuple-element.22.refs_0_, bf16[704,256]{1,0:T(8,128)(2,1)S(1)} %collective-permute-done.2.refs_1_, ...), custom_call_target="tpu_custom_call" | custom-call | tf_op jit(solution)/shard_map/pallas_call | solution.py:30
  67.4 1.9 %collective-permute-start.4 = (bf16[352,704]{1,0:T(8,128)(2,1)S(1)}, bf16[352,704]{1,0:T(8,128)(2,1)S(1)}, u32[]{:S(2)}, u32[]{:S(2)}) collective-permute-start(bf16[352,704]{1,0:T(8,128)(2,1)S(1)} %shard_map.69), channel_id=1, source_target_pairs={{0,1},{1,0},{2,3},{3,2},{4,5},{5,4},{6,7},{7,6},{8,9},{9,8},{10,11... | collective-permute-start | bytes 1486856 | tf_op jit(solution)/shard_map/ppermute | solution.py:298
  69.3 1.3 %shard_map.68.mine = f32[352,704]{1,0:T(8,128)S(1)} custom-call(s32[3]{0:T(128)S(1)} %pad_add_fusion.place, bf16[32,2,11,8,128]{4,3,2,1,0:T(8,128)(2,1)S(1)} %all-to-all-done.rows, bf16[704,256]{1,0:T(8,128)(2,1)S(1)} %get-tuple-element.22.refs_0_, bf16[704,256]{1,0:T(8,128)(2,1)S(1)} %collective-permute-done.2.refs_1_, ...), custom_call_target="tpu_custom_call" | custom-call | tf_op jit(solution)/shard_map/pallas_call | solution.py:30
  70.6 0.6 collective-permute-done.4.theirs
  71.2 0.3 shard_map.70
  71.5 22.4 %all-gather = bf16[3872,128]{1,0:T(8,128)(2,1)S(1)} all-gather(bf16[968,128]{1,0:T(8,128)(2,1)S(1)} %shard_map.70), channel_id=2, replica_groups=mesh['side'=2,'plane'=32,'chip'=4,'core'=2] {'chip'}, dimensions={0}, use_global_device_ids=true | all-gather | bytes 1239040 | tf_op jit(solution)/shard_map/all_gather | solution.py:308
  93.9 1.9 %collective-permute-start.5 = (bf16[4,968,128]{2,1,0:T(8,128)(2,1)S(1)}, bf16[4,968,128]{2,1,0:T(8,128)(2,1)S(1)}, u32[]{:S(2)}, u32[]{:S(2)}) collective-permute-start(bf16[4,968,128]{2,1,0:T(8,128)(2,1)S(1)} %bitcast.9), channel_id=1, source_target_pairs={{0,1},{1,0},{2,3},{3,2},{4,5},{5,4},{6,7},{7,6},{8,9},{9,8},{10,11... | collective-permute-start | bytes 2973704 | tf_op jit(solution)/shard_map/ppermute | solution.py:309
  95.8 1.1 shard_map.71
  97.0 1.4 %collective-permute-done.5.other = bf16[4,968,128]{2,1,0:T(8,128)(2,1)S(1)} collective-permute-done((bf16[4,968,128]{2,1,0:T(8,128)(2,1)S(1)}, bf16[4,968,128]{2,1,0:T(8,128)(2,1)S(1)}, u32[]{:S(2)}, u32[]{:S(2)}) %collective-permute-start.5) | collective-permute-done | bytes 991264 | tf_op jit(solution)/shard_map/ppermute | solution.py:309
  98.3 1.3 %shard_map.72 = bf16[64,11,2,128]{3,2,1,0:T(2,128)(2,1)S(1)} custom-call(s32[3]{0:T(128)S(1)} %pad_add_fusion.place, bf16[352,256]{1,0:T(8,128)(2,1)S(1)} %get-tuple-element.28.own, bf16[4,968,128]{2,1,0:T(8,128)(2,1)S(1)} %collective-permute-done.5.other, bf16[1408,256]{1,0:T(8,128)(2,1)S(1)} %bitcast.12), custom_call_target="tpu_custom_call" | custom-call | tf_op jit(solution)/shard_map/pallas_call | solution.py:30
  99.6 22.0 %all_to_all.10.returned = bf16[64,11,2,128]{3,2,1,0:T(2,128)(2,1)S(1)} all-to-all(bf16[64,11,2,128]{3,2,1,0:T(2,128)(2,1)S(1)} %shard_map.72), channel_id=1, replica_groups=mesh['side'=2,'plane'=32,'chip'=4,'core'=2] {'side','plane'}, dimensions={0} | all-to-all | bytes 720896 | tf_op jit(solution)/shard_map/all_to_all | solution.py:328
  121.7 1.1 shard_map.73
  (7 shorter events, 0.1 us)
Async XLA Ops:
  1.8 16.4 %collective-permute-start = (bf16[80,1024]{1,0:T(8,128)(2,1)S(1)}, bf16[80,1024]{1,0:T(8,128)(2,1)S(1)}, u32[]{:S(2)}, u32[]{:S(2)}) collective-permute-start(bf16[80,1024]{1,0:T(8,128)(2,1)S(1)} %get-tuple-element.17.mine), channel_id=1, source_target_pairs={{0,256},{256,0},{1,257},{257,1},{2,258},{258,2},{3,259},{259,3},{4... | collective-permute-start | bytes 491528 | tf_op jit(solution)/shard_map/ppermute | solution.py:242
  6.1 24.9 %collective-permute-start.1 = (bf16[704,256]{1,0:T(8,128)(2,1)S(1)}, bf16[704,256]{1,0:T(8,128)(2,1)S(1)}, u32[]{:S(2)}, u32[]{:S(2)}) collective-permute-start(bf16[704,256]{1,0:T(8,128)(2,1)S(1)} %get-tuple-element.21), channel_id=1, source_target_pairs={{0,4},{2,6},{4,0},{6,2},{1,5},{3,7},{5,1},{7,3},{8,12},{10,14},{12... | collective-permute-start | bytes 1081352 | tf_op jit(solution)/shard_map/ppermute | solution.py:272
  20.8 45.2 %all-to-all-start = ((bf16[32,2,11,8,128]{4,3,2,1,0:T(8,128)(2,1)}), bf16[32,2,11,8,128]{4,3,2,1,0:T(8,128)(2,1)S(1)}, u32[]{:S(2)}, u32[]{:S(2)}) async-start(bf16[32,2,11,8,128]{4,3,2,1,0:T(8,128)(2,1)} %shard_map.66), calls=%async_computation | async-start | bytes 2883584 | tf_op jit(solution)/shard_map/all_to_all | solution.py:270
  32.6 21.6 %collective-permute-start.2 = (bf16[704,256]{1,0:T(8,128)(2,1)S(1)}, bf16[704,256]{1,0:T(8,128)(2,1)S(1)}, u32[]{:S(2)}, u32[]{:S(2)}) collective-permute-start(bf16[704,256]{1,0:T(8,128)(2,1)S(1)} %get-tuple-element.23), channel_id=1, source_target_pairs={{0,2},{2,4},{4,6},{6,0},{1,3},{3,5},{5,7},{7,1},{8,10},{10,12},{12... | collective-permute-start | bytes 1081352 | tf_op jit(solution)/shard_map/ppermute | solution.py:287
  39.4 16.8 %collective-permute-start.3 = (bf16[704,256]{1,0:T(8,128)(2,1)S(1)}, bf16[704,256]{1,0:T(8,128)(2,1)S(1)}, u32[]{:S(2)}, u32[]{:S(2)}) collective-permute-start(bf16[704,256]{1,0:T(8,128)(2,1)S(1)} %get-tuple-element.24), channel_id=1, source_target_pairs={{0,6},{2,0},{4,2},{6,4},{1,7},{3,1},{5,3},{7,5},{8,14},{10,8},{12,... | collective-permute-start | bytes 1081352 | tf_op jit(solution)/shard_map/ppermute | solution.py:288
  67.4 3.8 %collective-permute-start.4 = (bf16[352,704]{1,0:T(8,128)(2,1)S(1)}, bf16[352,704]{1,0:T(8,128)(2,1)S(1)}, u32[]{:S(2)}, u32[]{:S(2)}) collective-permute-start(bf16[352,704]{1,0:T(8,128)(2,1)S(1)} %shard_map.69), channel_id=1, source_target_pairs={{0,1},{1,0},{2,3},{3,2},{4,5},{5,4},{6,7},{7,6},{8,9},{9,8},{10,11... | collective-permute-start | bytes 1486856 | tf_op jit(solution)/shard_map/ppermute | solution.py:298
  70.6 25.2 %copy-start = (bf16[1,1408,256]{2,1,0:T(8,128)(2,1)S(1)}, bf16[1,1408,256]{2,1,0:T(8,128)(2,1)}, u32[]{:S(2)}) copy-start(bf16[1,1408,256]{2,1,0:T(8,128)(2,1)} %param.11) | copy-start | bytes 2162692
  70.6 25.2 %copy-start.1 = (f32[64,6]{0,1:T(8,128)S(1)}, f32[64,6]{0,1:T(8,128)}, u32[]{:S(2)}) copy-start(f32[64,6]{0,1:T(8,128)} %param.8) | copy-start | bytes 4612
  93.9 4.5 %collective-permute-start.5 = (bf16[4,968,128]{2,1,0:T(8,128)(2,1)S(1)}, bf16[4,968,128]{2,1,0:T(8,128)(2,1)S(1)}, u32[]{:S(2)}, u32[]{:S(2)}) collective-permute-start(bf16[4,968,128]{2,1,0:T(8,128)(2,1)S(1)} %bitcast.9), channel_id=1, source_target_pairs={{0,1},{1,0},{2,3},{3,2},{4,5},{5,4},{6,7},{7,6},{8,9},{9,8},{10,11... | collective-permute-start | bytes 2973704 | tf_op jit(solution)/shard_map/ppermute | solution.py:309
